TPU v7x, 256 devices: a whole 4x4x8 slice. The times are simulated.
256 devices in a mesh: section: 16 (over y_lo, z), dp: 16 (over x, y_hi, core).
Axes of the slice: x: 4, y: 4 (y_hi: 2, y_lo: 2; y = y_hi * 2 + y_lo), z: 8, core: 2. Of those that a mesh axis runs over, the one named last changes fastest.
Arguments:
- entering: bfloat16 [16, 2048, 8192], P('section', 'dp'), may hold values from -6 to 6
- returning: bfloat16 [16, 2048, 8192], P('section', 'dp'), may hold values from -6 to 6
- adapter_down: bfloat16 [2, 16, 64, 8192], P(None, 'section'), may hold values from -0.0625 to 0.0625
- adapter_up: bfloat16 [2, 16, 64, 8192], P(None, 'section'), may hold values from -0.75 to 0.75
- stashed: float32 [16, 3, 64, 2048], P('section', None, None, 'dp'), may hold values from -6 to 6
- doc_ids: int32 [16, 2048], P(None, 'dp'), may hold values from 0 to 31, never falling along the last dimension, each value on 1 to 256 neighbouring positions
- input_factor: float32 [16, 8192, 1024], P('section', 'dp'), may hold values from -3 to 3
- output_factor: float32 [2, 16, 64, 64], P(None, 'section'), may hold values from -3 to 3
Outputs:
- input_factor_new: float32 [16, 8192, 1024], P('section', 'dp')
- output_factor_new: float32 [2, 16, 64, 64], P(None, 'section')
Inputs may be any that keep to these rules, and one draw needn't show every extreme that they name: `doc_ids`: each row packs 32 documents in order: document numbers never fall along a row, every document has 1 to 256 tokens, and some document of every row has exactly 256.
All inputs are finite; a program needn't handle non-finite values.
Results may differ from a plain program's by a relative error of at most 0.0044.
Values may be sent and summed in bfloat16 or wider, within the bound.
No kernel may reach another device: no remote copies, remote signals or barrier semaphores. Data moves between devices by JAX's collectives and lax.ppermute only.
A program may use at most 128 MiB of HBM per device.

v0:
```python
import jax
import jax.numpy as jnp
from jax import lax
from jax.sharding import PartitionSpec as P


def from_behind(block, axis, distance):
    devices = range(lax.axis_size(axis))
    route = [((i - distance) % len(devices), i) for i in devices]
    return lax.ppermute(block, axis, route)


def select_span(weights, span_id):
    return lax.dynamic_index_in_dim(weights[:, 0], span_id, 0, keepdims=False)


def shards(
    entering, returning, adapter_down, adapter_up, stashed, doc_ids, input_factor, output_factor
):
    section_index = lax.axis_index("section")
    section_count = lax.axis_size("section")
    replicas = lax.axis_size("dp")
    tok_rows = entering.shape[1]
    model_width = entering.shape[2]
    steps_count = stashed.shape[1]
    block_size = input_factor.shape[2]
    doc_range = jnp.arange(2 * replicas, dtype=jnp.int32)
    onehot = (doc_ids[:, :, None] == doc_range[None, None, :]).astype(jnp.int32)
    local_counts = jnp.sum(onehot, axis=1)
    counts = lax.psum(local_counts, "dp").astype(jnp.float32)
    doc_length = jnp.sum(onehot.astype(jnp.float32) * counts[:, None, :], axis=2)
    weight = jnp.sqrt(tok_rows / doc_length)
    current = entering[0]
    pieces = []
    for step_idx in range(steps_count):
        anchor = (section_index - step_idx) % section_count
        span_id = (anchor < section_count // 2).astype(jnp.int32) + (
            section_index < step_idx
        ).astype(jnp.int32)
        row_scale = jnp.sqrt(lax.dynamic_index_in_dim(weight, anchor, 0, keepdims=False))
        pieces.append((row_scale[:, None] * current.astype(jnp.float32)).astype(jnp.bfloat16))
        if step_idx + 1 < steps_count:
            down_proj = select_span(adapter_down, span_id)
            up_proj = select_span(adapter_up, span_id)
            pre_act = jnp.einsum(
                "td,rd->tr", current, down_proj, preferred_element_type=jnp.float32
            )
            gated = jax.nn.silu(pre_act).astype(jnp.bfloat16)
            mixed = jnp.dot(gated, up_proj, preferred_element_type=jnp.float32)
            result = (current.astype(jnp.float32) + mixed).astype(jnp.bfloat16)
            current = from_behind(result, "section", 1)
    stacked_rows = jnp.concatenate(pieces, axis=0)
    row_total = stacked_rows.shape[0]
    grouped = stacked_rows.reshape(row_total, model_width // block_size, block_size)
    products = jnp.einsum("tki,tkj->kij", grouped, grouped, preferred_element_type=jnp.float32)
    summed = lax.psum_scatter(
        products.reshape(model_width, block_size).astype(jnp.bfloat16),
        "dp",
        scatter_dimension=0,
        tiled=True,
    ).astype(jnp.float32)
    norm_count = steps_count * tok_rows * replicas
    input_factor_new = 0.75 * input_factor + 0.25 * summed[None] / norm_count
    gradient = returning[0]
    rank_size = stashed.shape[2]
    curv_zero = jnp.zeros((rank_size, rank_size), jnp.float32)
    curv_one = jnp.zeros((rank_size, rank_size), jnp.float32)
    steps_zero = jnp.float32(0.0)
    steps_one = jnp.float32(0.0)
    for step_idx in range(steps_count):
        span_id = (section_index + step_idx < section_count).astype(jnp.int32)
        down_proj = select_span(adapter_down, span_id)
        up_proj = select_span(adapter_up, span_id)
        stash_now = stashed[0, step_idx].T
        grad_act = jnp.einsum("td,rd->tr", gradient, up_proj, preferred_element_type=jnp.float32)
        sigmoid_z = jax.nn.sigmoid(stash_now)
        grad_pre = (grad_act * sigmoid_z * (1.0 + stash_now * (1.0 - sigmoid_z))).astype(
            jnp.bfloat16
        )
        outer = jnp.dot(grad_pre.T, grad_pre, preferred_element_type=jnp.float32)
        in_second = span_id.astype(jnp.float32)
        curv_one = curv_one + outer * in_second
        curv_zero = curv_zero + outer * (1.0 - in_second)
        steps_one = steps_one + in_second
        steps_zero = steps_zero + (1.0 - in_second)
        if step_idx + 1 < steps_count:
            branch = jnp.dot(grad_pre, down_proj, preferred_element_type=jnp.float32)
            passed = (gradient.astype(jnp.float32) + branch).astype(jnp.bfloat16)
            gradient = from_behind(passed, "section", -1)
    curv_total = lax.psum(jnp.stack([curv_zero, curv_one]), "dp")
    step_totals = jnp.stack([steps_zero, steps_one])
    tokens_all = tok_rows * replicas
    divisor = (jnp.maximum(step_totals, 1.0) * tokens_all)[:, None, None]
    updated = 0.75 * output_factor[:, 0] + 0.25 * curv_total / divisor
    output_factor_new = jnp.where((step_totals > 0.0)[:, None, None], updated, output_factor[:, 0])[
        :, None
    ]
    return (input_factor_new, output_factor_new)


def solution(mesh):
    in_specs = (
        P("section", "dp", None),
        P("section", "dp", None),
        P(None, "section", None, None),
        P(None, "section", None, None),
        P("section", None, None, "dp"),
        P(None, "dp"),
        P("section", "dp", None),
        P(None, "section", None, None),
    )
    out_specs = (P("section", "dp", None), P(None, "section", None, None))
    return jax.shard_map(shards, mesh=mesh, in_specs=in_specs, out_specs=out_specs, check_vma=False)
```

profile of v0, /device:TPU:1, one launch (start us, length us, event | category | flops | bytes accessed | tf_op | source)
XLA Modules:
  0.0 359.5 jit_solution(15739634982547837906)
XLA Ops:
  7.2 0.0 copy-start
  7.2 0.0 reduce-scatter.2.cloned.1.call-start
  7.2 1.5 copy-done
  8.8 0.0 copy-start.4
  8.8 6.4 %fusion = bf16[128,8192]{1,0:T(8,128)(2,1)} fusion(bf16[1,128,8192]{2,1,0:T(8,128)(2,1)} %param.8, bf16[2,1,64,8192]{3,2,1,0:T(8,128)(2,1)} %param.11, s32[]{:T(128)S(6)} %select_n.53, bf16[2,1,64,8192]{3,2,1,0:T(8,128)(2,1)S(1)} %copy-done), kind=kOutput, calls=%fused_computation.4 | convolution fusion | flops 271622144 | bytes 8389632 | tf_op jit(solution)/shard_map/dot_general | solution.py:49
  15.1 2.5 collective-permute-start
  17.6 0.0 copy-done.4
  17.6 0.3 convert_reduce_fusion
  17.9 12.9 %psum.14 = s32[16,32]{1,0:T(8,128)S(1)} all-reduce(s32[16,32]{1,0:T(8,128)S(1)} %convert_reduce_fusion), channel_id=1, replica_groups=mesh['section'=16,'dp'=16] {'dp'}, use_global_device_ids=true, to_apply=%region_1.0 | all-reduce | flops 512 | bytes 4096 | tf_op jit(solution)/shard_map/psum | solution.py:30
  30.9 0.1 fusion.56
  31.1 37.2 %collective-permute-done = bf16[128,8192]{1,0:T(8,128)(2,1)} collective-permute-done((bf16[128,8192]{1,0:T(8,128)(2,1)}, bf16[128,8192]{1,0:T(8,128)(2,1)}, u32[]{:S(2)}, u32[]{:S(2)}) %collective-permute-start) | collective-permute-done | bytes 2097184 | tf_op jit(solution)/shard_map/ppermute | solution.py:10
  68.2 6.4 %fusion.1 = bf16[128,8192]{1,0:T(8,128)(2,1)} fusion(bf16[128,8192]{1,0:T(8,128)(2,1)} %collective-permute-done, bf16[2,1,64,8192]{3,2,1,0:T(8,128)(2,1)} %param.11, s32[]{:T(128)S(6)} %select_n.56, bf16[2,1,64,8192]{3,2,1,0:T(8,128)(2,1)S(1)} %copy-done), kind=kOutput, calls=%fused_computation.5 | convolution fusion | flops 271622144 | bytes 8389632 | tf_op jit(solution)/shard_map/dot_general | solution.py:49
  74.6 0.0 collective-permute-start.1
  74.6 2.0 fusion.5
  76.6 2.0 fusion.6
  78.7 44.1 %collective-permute-done.1 = bf16[128,8192]{1,0:T(8,128)(2,1)S(1)} collective-permute-done((bf16[128,8192]{1,0:T(8,128)(2,1)}, bf16[128,8192]{1,0:T(8,128)(2,1)S(1)}, u32[]{:S(2)}, u32[]{:S(2)}) %collective-permute-start.1) | collective-permute-done | bytes 2097184 | tf_op jit(solution)/shard_map/ppermute | solution.py:10
  122.8 0.4 multiply_convert_fusion
  123.2 7.0 %pad_maximum_fusion = bf16[384,8192]{1,0:T(8,128)(2,1)} fusion(bf16[128,8192]{1,0:T(8,128)(2,1)S(1)} %multiply_convert_fusion, bf16[128,8192]{1,0:T(8,128)(2,1)S(1)} %fusion.6, bf16[128,8192]{1,0:T(8,128)(2,1)S(1)} %fusion.5), kind=kLoop, calls=%fused_computation.9 | loop fusion | flops 18874368 | bytes 12582912 | tf_op jit(solution)/shard_map/concatenate | solution.py:52
  130.2 16.0 %convolution_convert_fusion = bf16[8,1024,1024]{2,1,0:T(8,128)(2,1)} fusion(bf16[48,8,8,1024]{3,2,1,0:T(8,128)(2,1)} %bitcast.174), kind=kOutput, calls=%fused_computation | convolution fusion | flops 6450839552 | bytes 23068672 | tf_op jit(solution)/shard_map/tki,tkj->kij/dot_general | solution.py:55
  146.2 0.0 copy-start.2
  146.2 0.0 reduce-scatter.2.cloned.1.call-update
  146.3 0.9 copy-done.2
  147.1 0.0 copy-start.1
  147.1 2.9 fusion.25
  150.0 0.0 copy-done.1
  150.1 2.1 fusion.2
  152.1 0.0 collective-permute-start.2
  152.1 45.2 %collective-permute-done.2 = bf16[128,8192]{1,0:T(8,128)(2,1)} collective-permute-done((bf16[128,8192]{1,0:T(8,128)(2,1)}, bf16[128,8192]{1,0:T(8,128)(2,1)}, u32[]{:S(2)}, u32[]{:S(2)}) %collective-permute-start.2) | collective-permute-done | bytes 2097184 | tf_op jit(solution)/shard_map/ppermute | solution.py:10
  197.4 2.7 fusion.30
  200.1 3.7 %add_convert_fusion = bf16[128,8192]{1,0:T(8,128)(2,1)} fusion(bf16[128,8192]{1,0:T(8,128)(2,1)} %collective-permute-done.2, bf16[128,64]{0,1:T(8,128)(2,1)S(1)} %fusion.30, bf16[2,1,64,8192]{3,2,1,0:T(8,128)(2,1)S(1)} %copy-done, s32[]{:T(128)S(6)} %select_n.58), kind=kOutput, calls=%fused_computation.14 | convolution fusion | flops 137363456 | bytes 5259268 | tf_op jit(solution)/shard_map/dot_general | solution.py:87
  203.7 0.0 copy-start.3
  203.7 2.4 collective-permute-start.3
  206.1 0.1 broadcast_compare_fusion
  206.2 0.1 maximum_multiply_fusion
  206.3 0.1 fusion.111
  206.4 0.1 fusion.112
  206.5 42.0 %collective-permute-done.3 = bf16[128,8192]{1,0:T(8,128)(2,1)} collective-permute-done((bf16[128,8192]{1,0:T(8,128)(2,1)}, bf16[128,8192]{1,0:T(8,128)(2,1)}, u32[]{:S(2)}, u32[]{:S(2)}) %collective-permute-start.3) | collective-permute-done | bytes 2097184 | tf_op jit(solution)/shard_map/ppermute | solution.py:10
  248.5 4.5 %add_bitcast_fusion.1 = (f32[1,64,64]{2,1,0:T(8,128)S(1)}, f32[1,64,64]{2,1,0:T(8,128)S(1)}) fusion(f32[64,64]{1,0:T(8,128)S(1)} %fusion.112, f32[64,64]{1,0:T(8,128)S(1)} %fusion.111, f32[]{:T(128)S(6)} %sub.31, f32[]{:T(128)S(6)} %sub.30, f32[]{:T(128)S(6)} %sub.29, f32[]{:T(128)S(6)} %convert_element_type.126, f32[]{:T(128)S(6)} %convert_element_type.124, ...), kind=kOutput, calls=%fused_computation.82 | convolution fusion | flops 135380992 | bytes 3276828 | tf_op jit(solution)/shard_map/dot_general | solution.py:80
  253.0 62.9 %psum.15 = f32[2,64,64]{2,1,0:T(8,128)S(1)} all-reduce(f32[2,64,64]{2,1,0:T(8,128)S(1)} %pad_maximum_fusion.1), channel_id=1, replica_groups=mesh['section'=16,'dp'=16] {'dp'}, use_global_device_ids=true, to_apply=%region_4.5 | all-reduce | flops 8192 | bytes 65536 | tf_op jit(solution)/shard_map/psum | solution.py:90
  315.9 0.0 copy-done.3
  315.9 0.7 fusion.58
  316.6 32.2 %reduce-scatter.2.cloned.1.call-done = bf16[512,1024]{1,0:T(8,128)(2,1)} async-done(((bf16[8192,1024]{1,0:T(8,128)(2,1)}), bf16[512,1024]{1,0:T(8,128)(2,1)}) %reduce-scatter.2.cloned.1.call-update) | async-done | bytes 1048592 | tf_op jit(solution)/shard_map/reduce_scatter | solution.py:56
  348.9 3.7 %bitcast_add_fusion = f32[1,512,1024]{2,1,0:T(8,128)} fusion(bf16[512,1024]{1,0:T(8,128)(2,1)} %reduce-scatter.2.cloned.1.call-done, f32[1,512,1024]{2,1,0:T(8,128)} %param.14), kind=kLoop, calls=%fused_computation.18 | loop fusion | flops 2097152 | bytes 5242880 | tf_op jit(solution)/shard_map/add | solution.py:63
  (4 shorter events, 0.0 us)
Async XLA Ops:
  7.2 1.6 copy-start
  7.2 341.7 %reduce-scatter.2.cloned.1.call-start = ((), (), s32[]{:S(2)}) async-start(), calls=%async_computation.1 | async-start | bytes 17825792 | tf_op jit(solution)/shard_map/reduce_scatter | solution.py:56
  8.8 8.8 %copy-start.4 = (s32[16,128]{1,0:T(8,128)S(1)}, s32[16,128]{1,0:T(8,128)}, u32[]{:S(2)}) copy-start(s32[16,128]{1,0:T(8,128)} %param.13) | copy-start | bytes 24580
  15.1 53.1 %collective-permute-start = (bf16[128,8192]{1,0:T(8,128)(2,1)}, bf16[128,8192]{1,0:T(8,128)(2,1)}, u32[]{:S(2)}, u32[]{:S(2)}) collective-permute-start(bf16[128,8192]{1,0:T(8,128)(2,1)} %fusion), channel_id=1, source_target_pairs={{240,0},{0,16},{16,32},{32,48},{48,64},{64,80},{80,96},{96,112},{1... | collective-permute-start | bytes 6291464 | tf_op jit(solution)/shard_map/ppermute | solution.py:10
  74.6 48.2 %collective-permute-start.1 = (bf16[128,8192]{1,0:T(8,128)(2,1)}, bf16[128,8192]{1,0:T(8,128)(2,1)S(1)}, u32[]{:S(2)}, u32[]{:S(2)}) collective-permute-start(bf16[128,8192]{1,0:T(8,128)(2,1)} %fusion.1), channel_id=1, source_target_pairs={{240,0},{0,16},{16,32},{32,48},{48,64},{64,80},{80,96},{96,112},{1... | collective-permute-start | bytes 6291464 | tf_op jit(solution)/shard_map/ppermute | solution.py:10
  146.2 0.9 copy-start.2
  147.1 2.9 copy-start.1
  152.1 45.2 %collective-permute-start.2 = (bf16[128,8192]{1,0:T(8,128)(2,1)}, bf16[128,8192]{1,0:T(8,128)(2,1)}, u32[]{:S(2)}, u32[]{:S(2)}) collective-permute-start(bf16[128,8192]{1,0:T(8,128)(2,1)} %fusion.2), channel_id=1, source_target_pairs={{16,0},{32,16},{48,32},{64,48},{80,64},{96,80},{112,96},{128,112},... | collective-permute-start | bytes 6291464 | tf_op jit(solution)/shard_map/ppermute | solution.py:10
  203.7 112.2 %copy-start.3 = (f32[2,1,64,64]{3,2,1,0:T(8,128)S(1)}, f32[2,1,64,64]{3,2,1,0:T(8,128)}, u32[]{:S(2)}) copy-start(f32[2,1,64,64]{3,2,1,0:T(8,128)} %param.15) | copy-start | bytes 98308
  203.7 44.8 %collective-permute-start.3 = (bf16[128,8192]{1,0:T(8,128)(2,1)}, bf16[128,8192]{1,0:T(8,128)(2,1)}, u32[]{:S(2)}, u32[]{:S(2)}) collective-permute-start(bf16[128,8192]{1,0:T(8,128)(2,1)} %add_convert_fusion), channel_id=1, source_target_pairs={{16,0},{32,16},{48,32},{64,48},{80,64},{96,80},{112,96},{128,112},... | collective-permute-start | bytes 6291464 | tf_op jit(solution)/shard_map/ppermute | solution.py:10
Sparse Core Ops, SparseCore 0:
  146.4 202.4 reduce-scatter.1
where the time goes:
time: 360 us; the launch traced here: 359 us
  waiting for transfers between devices  201 us (56%)
  blocking collectives  75.8 us (21%)
  matrix products  44.8 us (12%)
  other arithmetic  16.6 us (5%)
  between operations  14.2 us (4%)
  starting transfers between devices  4.87 us (1%)
    ppermute x4, waiting for transfers between devices, from_behind(): return lax.ppermute(block, axis, route)  168 us
    psum x1, blocking collectives, shards(): curv_total = lax.psum(jnp.stack([curv_zero, curv_one]), 'dp')  62.9 us
    reduce_scatter x1, waiting for transfers between devices, shards(): lax.psum_scatter(products.reshape(model_width, block_size).astype(jnp.bfl...  32.2 us
    dot_general x1, matrix products, shards(): jnp.einsum('tki,tkj->kij', grouped, grouped, preferred_element_type=jnp.f...  16 us
    psum x1, blocking collectives, shards(): counts = lax.psum(local_counts, 'dp').astype(jnp.float32)  12.9 us
    dot_general x2, matrix products, shards(): mixed = jnp.dot(gated, up_proj, preferred_element_type=jnp.float32)  12.7 us
  transfers between devices with their start and end apart: 5, of which 5 were waited for; matrix products, arithmetic and copies ran while one was open for 6% of the time, Pallas kernels for 0%

commit v1 on v0

v1 whole, which is shorter than its diff:
```python
import jax
import jax.numpy as jnp
from jax import lax
from jax.sharding import PartitionSpec as P

F32 = jnp.float32
BF16 = jnp.bfloat16


def shift(block, axis, distance):
    count = lax.axis_size(axis)
    return lax.ppermute(block, axis, [(i, (i + distance) % count) for i in range(count)])


def swap_cores(block):
    count = lax.axis_size("dp")
    return lax.ppermute(block, "dp", [(i, i ^ 1) for i in range(count)])


def gather_dp(block):
    count = lax.axis_size("dp")
    return lax.all_to_all(jnp.broadcast_to(block[None], (count,) + block.shape), "dp", 0, 0)


def pick(weights, span_id):
    return lax.dynamic_index_in_dim(weights[:, 0], span_id, 0, keepdims=False)


def nt(a, b):
    return lax.dot_general(a, b, (((1,), (1,)), ((), ())), preferred_element_type=F32)


def shards(
    entering, returning, adapter_down, adapter_up, stashed, doc_ids, input_factor, output_factor
):
    sec = lax.axis_index("section")
    rep = lax.axis_index("dp")
    sections = lax.axis_size("section")
    replicas = lax.axis_size("dp")
    core = rep % 2
    tok = entering.shape[1]
    width = entering.shape[2]
    steps_count = stashed.shape[1]
    rank = stashed.shape[2]
    block = input_factor.shape[2]
    rows = input_factor.shape[1]
    half = width // 2
    tokens = tok * replicas

    def first(home):
        return (home < sections // 2).astype(jnp.int32)

    x0 = entering[0]
    grad0 = returning[0]

    with jax.named_scope("columns"):
        split = x0.reshape(tok, replicas, rows).transpose(1, 0, 2)
        own = lax.all_to_all(split, "dp", 0, 0).reshape(tokens, rows)
        other = swap_cores(own)

    with jax.named_scope("weights"):
        f_span = first((sec - 1) % sections) + (sec == 0).astype(jnp.int32)
        down_f = lax.dynamic_slice_in_dim(pick(adapter_down, f_span), core * half, half, 1)
        up_f = lax.dynamic_slice_in_dim(pick(adapter_up, f_span), (rep // 2) * block, block, 1)
        ahead = shift(jnp.concatenate([down_f, up_f], axis=1), "section", -1)
        up1_cols = ahead[:, half:]
        b1 = (sec + 1 < sections).astype(jnp.int32)
        b2 = (sec + 2 < sections).astype(jnp.int32)
        up_b1 = lax.dynamic_slice_in_dim(pick(adapter_up, b1), core * half, half, 1)
        down_b1 = lax.dynamic_slice_in_dim(pick(adapter_down, b1), core * half, half, 1)
        up_b2 = lax.dynamic_slice_in_dim(pick(adapter_up, b2), core * half, half, 1)
        behind1 = shift(jnp.concatenate([up_b1, down_b1], axis=0), "section", 1)
        behind2 = shift(up_b2, "section", 2)
        stash1 = shift(stashed[0, 1], "section", 1)
        stash2 = shift(stashed[0, 2], "section", 2)
        ahead_mine = ahead[:, :half]
        ahead_sib = swap_cores(ahead_mine)
        down1_lo = jnp.where(core == 0, ahead_mine, ahead_sib)
        down1_hi = jnp.where(core == 0, ahead_sib, ahead_mine)
        mine = jnp.concatenate([behind1, behind2], axis=0)
        sib = swap_cores(mine)
        back_lo = jnp.where(core == 0, mine, sib)
        back_hi = jnp.where(core == 0, sib, mine)

    with jax.named_scope("gates"):
        c0 = first(sec)
        up0 = pick(adapter_up, c0)
        gate0 = jax.nn.silu(nt(x0, pick(adapter_down, c0))).astype(BF16)
        ids = pick(doc_ids[:, None], sec).astype(BF16)
        sent = jnp.concatenate([gate0, jnp.broadcast_to(ids[:, None], (tok, rank))], axis=1)
        got0 = gather_dp(sent).reshape(tokens, 2 * rank)
        x1 = (x0.astype(F32) + jnp.dot(gate0, up0, preferred_element_type=F32)).astype(BF16)
        z1 = nt(x1[:, :half], down1_lo) + nt(x1[:, half:], down1_hi)
        gate1 = jax.nn.silu(z1).astype(BF16)
        got1 = gather_dp(gate1).reshape(tokens, rank)

    with jax.named_scope("scale"):
        docs = jnp.arange(2 * replicas, dtype=jnp.int32).astype(F32)
        onehot = (got0[:, rank:rank + 1].astype(F32) == docs[None, :]).astype(F32)
        counts = jnp.sum(onehot, axis=0, keepdims=True)
        length = jnp.sum(onehot * counts, axis=1, keepdims=True)
        scale = jnp.sqrt(jnp.sqrt(tok / length))

    with jax.named_scope("grams"):
        up0_cols = lax.dynamic_slice_in_dim(up0, (rep // 2) * block, block, 1)
        lo = jnp.where(core == 0, own, other)
        hi = jnp.where(core == 0, other, own)
        a0 = jnp.concatenate([lo, hi], axis=1)
        g0 = got0[:, :rank]
        a1 = (a0.astype(F32) + jnp.dot(g0, up0_cols, preferred_element_type=F32)).astype(BF16)
        a2 = (a1.astype(F32) + jnp.dot(got1, up1_cols, preferred_element_type=F32)).astype(BF16)

        def gram(act):
            scaled = (scale * act.astype(F32)).astype(BF16)
            mine_cols = lax.dynamic_slice_in_dim(scaled, core * rows, rows, 1)
            return lax.dot_general(
                mine_cols, scaled, (((0,), (0,)), ((), ())), preferred_element_type=F32
            )

        here = gram(a0)
        from1 = shift(gram(a1).astype(BF16), "section", 1).astype(F32)
        from2 = shift(gram(a2).astype(BF16), "section", 2).astype(F32)
        norm_count = steps_count * tokens
        input_factor_new = 0.75 * input_factor + 0.25 * (here + from1 + from2)[None] / norm_count

    with jax.named_scope("backward"):
        b0 = (sec < sections).astype(jnp.int32)
        upb0 = pick(adapter_up, b0)
        downb0 = pick(adapter_down, b0)
        proj0 = nt(upb0, grad0)
        r2 = 2 * rank
        ups_lo = jnp.concatenate([back_lo[:rank], back_lo[r2:]], axis=0)
        ups_hi = jnp.concatenate([back_hi[:rank], back_hi[r2:]], axis=0)
        proj12 = nt(ups_lo, grad0[:, :half]) + nt(ups_hi, grad0[:, half:])
        m0 = nt(ups_lo, downb0[:, :half]) + nt(ups_hi, downb0[:, half:])
        m12 = nt(back_lo[r2:], back_lo[rank:r2]) + nt(back_hi[r2:], back_hi[rank:r2])

        def dz_of(grad_act, q):
            sigma = jax.nn.sigmoid(q)
            return (grad_act * sigma * (1.0 + q * (1.0 - sigma))).astype(BF16)

        def exact(m, d):
            return jnp.dot(m, d.astype(F32), precision=lax.Precision.HIGHEST)

        dz0 = dz_of(proj0, stashed[0, 0])
        dz1 = dz_of(proj12[:rank] + exact(m0[:rank], dz0), stash1)
        dz2 = dz_of(proj12[rank:] + exact(m0[rank:], dz0) + exact(m12, dz1), stash2)
        outer0 = nt(dz0, dz0)
        outer1 = shift(nt(dz1, dz1), "section", -1)
        outer2 = shift(nt(dz2, dz2), "section", -2)
        f1 = b1.astype(F32)
        f2 = b2.astype(F32)
        curv = jnp.stack([outer1 * (1.0 - f1) + outer2 * (1.0 - f2), outer0 + outer1 * f1 + outer2 * f2])
        step_totals = jnp.stack([2.0 - f1 - f2, 1.0 + f1 + f2])
        curv_total = jnp.sum(gather_dp(curv.reshape(rank, 2 * rank)), axis=0).reshape(2, rank, rank)
        divisor = (jnp.maximum(step_totals, 1.0) * tokens)[:, None, None]
        updated = 0.75 * output_factor[:, 0] + 0.25 * curv_total / divisor
        output_factor_new = jnp.where(
            (step_totals > 0.0)[:, None, None], updated, output_factor[:, 0]
        )[:, None]
    return (input_factor_new, output_factor_new)


def solution(mesh):
    in_specs = (
        P("section", "dp", None),
        P("section", "dp", None),
        P(None, "section", None, None),
        P(None, "section", None, None),
        P("section", None, None, "dp"),
        P(None, "dp"),
        P("section", "dp", None),
        P(None, "section", None, None),
    )
    out_specs = (P("section", "dp", None), P(None, "section", None, None))
    return jax.shard_map(shards, mesh=mesh, in_specs=in_specs, out_specs=out_specs, check_vma=False)
```

time: 360 us -> 203 us (0.56)
  waiting for transfers between devices: 201 us -> 87.5 us
  blocking collectives: 75.8 us -> 0 us
  starting transfers between devices: 4.87 us -> 47.3 us
  local copies, waits for them, and re-layouts: 2.43 us -> 20.6 us
  between operations: 14.2 us -> 1 us
  other arithmetic: 16.6 us -> 8.3 us
  matrix products: 44.8 us -> 37.6 us
    ppermute x4 -> x12, waiting for transfers between devices: 168 us -> 50.1 us  [the longest x9 49 us: shift(): lax.ppermute(block, axis, [(i, (i + distance) % count) for i in range(cou...]
    psum x2 -> x0, blocking collectives: 75.8 us -> none  [the longest x1 62.9 us: shards(): curv_total = lax.psum(jnp.stack([curv_zero, curv_one]), 'dp')]
    all_to_all x0 -> x4, waiting for transfers between devices: none -> 37.3 us  [the longest x3 20.1 us: gather_dp(): lax.all_to_all(jnp.broadcast_to(block[None], (count,) + block.shape), 'dp...]
    reduce_scatter x1 -> x0, waiting for transfers between devices: 32.2 us -> none  [shards(): lax.psum_scatter(products.reshape(model_width, block_size).astype(jnp.bfl...]
    all_to_all x0 -> x4, starting transfers between devices: none -> 29.4 us  [the longest x3 21.2 us: gather_dp(): lax.all_to_all(jnp.broadcast_to(block[None], (count,) + block.shape), 'dp...]
    ppermute x4 -> x12, starting transfers between devices: 4.83 us -> 17.9 us  [the longest x9 16.1 us: shift(): lax.ppermute(block, axis, [(i, (i + distance) % count) for i in range(cou...]
    dot_general x10 -> x22, matrix products: 44.8 us -> 37.6 us  [the longest x3 14.1 us: gram(): lax.dot_general(mine_cols, scaled, (((0,), (0,)), ((), ())), preferred_el...]
    concatenate x1 -> x3, other arithmetic: 7 us -> 2 us  [the longest x1 1.03 us: shards(): behind1 = shift(jnp.concatenate([up_b1, down_b1], axis=0), 'section', 1)]
  transfers between devices with their start and end apart: 5 -> 16, of which waited for: 5 -> 8; matrix products, arithmetic and copies ran while one was open for 6% -> 23% of each run, Pallas kernels for 0% -> 0%
where the time goes in v1:
time: 203 us; the launch traced here: 202 us
  waiting for transfers between devices  87.5 us (43%)
  starting transfers between devices  47.3 us (23%)
  matrix products  37.6 us (19%)
  local copies, waits for them, and re-layouts  20.6 us (10%)
  other arithmetic  8.3 us (4%)
    ppermute x9, waiting for transfers between devices, shift(): lax.ppermute(block, axis, [(i, (i + distance) % count) for i in range(cou...  49 us
    all_to_all x3, starting transfers between devices, gather_dp(): lax.all_to_all(jnp.broadcast_to(block[None], (count,) + block.shape), 'dp...  21.2 us
    all_to_all x3, waiting for transfers between devices, gather_dp(): lax.all_to_all(jnp.broadcast_to(block[None], (count,) + block.shape), 'dp...  20.1 us
    all_to_all x1, waiting for transfers between devices, shards(): own = lax.all_to_all(split, 'dp', 0, 0).reshape(tokens, rows)  17.3 us
    ppermute x9, starting transfers between devices, shift(): lax.ppermute(block, axis, [(i, (i + distance) % count) for i in range(cou...  16.1 us
    dot_general x3, matrix products, gram(): lax.dot_general(mine_cols, scaled, (((0,), (0,)), ((), ())), preferred_el...  14.1 us
    dot_general x13, matrix products, nt(): lax.dot_general(a, b, (((1,), (1,)), ((), ())), preferred_element_type=F32)  11.2 us
    all_to_all x1, starting transfers between devices, shards(): own = lax.all_to_all(split, 'dp', 0, 0).reshape(tokens, rows)  8.18 us
  transfers between devices with their start and end apart: 16, of which 8 were waited for; matrix products, arithmetic and copies ran while one was open for 23% of the time, Pallas kernels for 0%

profile of v1, /device:TPU:1, one launch (start us, length us, event | category | flops | bytes accessed | tf_op | source)
XLA Modules:
  0.0 202.3 jit_solution(13865313941146041154)
XLA Ops:
  0.7 1.7 dynamic-slice_bitcast_fusion.2
  2.6 1.2 dynamic-slice_bitcast_fusion.1
  3.8 1.0 pad_maximum_fusion.1
  4.8 2.5 %collective-permute-start.5 = (bf16[128,4096]{1,0:T(8,128)(2,1)}, bf16[128,4096]{1,0:T(8,128)(2,1)}, u32[]{:S(2)}, u32[]{:S(2)}) collective-permute-start(bf16[128,4096]{1,0:T(8,128)(2,1)} %pad_maximum_fusion.1), channel_id=1, source_target_pairs={{0,16},{16,32},{32,48},{48,64},{64,80},{80,96},{96,112},{112,128},... | collective-permute-start | bytes 3145736 | tf_op jit(solution)/shard_map/weights/ppermute | solution.py:12
  7.3 3.0 %collective-permute-start.6 = (bf16[64,4096]{1,0:T(8,128)(2,1)}, bf16[64,4096]{1,0:T(8,128)(2,1)}, u32[]{:S(2)}, u32[]{:S(2)}) collective-permute-start(bf16[64,4096]{1,0:T(8,128)(2,1)} %get-tuple-element.6), channel_id=1, source_target_pairs={{0,32},{16,48},{32,64},{48,80},{64,96},{80,112},{96,128},{112,144}... | collective-permute-start | bytes 1572872 | tf_op jit(solution)/shard_map/weights/ppermute | solution.py:12
  10.3 2.9 %collective-permute-start.8 = (f32[64,128]{1,0:T(8,128)S(1)}, f32[64,128]{1,0:T(8,128)S(1)}, u32[]{:S(2)}, u32[]{:S(2)}) collective-permute-start(f32[64,128]{1,0:T(8,128)S(1)} %get-tuple-element.15), channel_id=1, source_target_pairs={{0,16},{16,32},{32,48},{48,64},{64,80},{80,96},{96,112},{112,128},... | collective-permute-start | bytes 98312 | tf_op jit(solution)/shard_map/weights/ppermute | solution.py:12
  13.2 1.2 collective-permute-start.10
  14.4 2.1 %multiply_convert_fusion.2 = bf16[128,64]{0,1:T(8,128)(2,1)S(1)} fusion(bf16[1,128,8192]{2,1,0:T(8,128)(2,1)S(1)} %copy-done, bf16[2,1,64,8192]{3,2,1,0:T(8,128)(2,1)} %param.10, s32[]{:T(128)S(6)} %select_n.108), kind=kOutput, calls=%fused_computation.106 | convolution fusion | flops 134258688 | bytes 3162116 | tf_op jit(solution)/shard_map/gates/dot_general | solution.py:30
  17.2 0.9 broadcast_in_dim.16
  18.1 8.8 %all-to-all-start = ((bf16[16,128,128]{1,2,0:T(8,128)(2,1)}), bf16[16,128,128]{1,2,0:T(8,128)(2,1)S(1)}, u32[]{:S(2)}, u32[]{:S(2)}) async-start(bf16[16,128,128]{1,2,0:T(8,128)(2,1)} %broadcast_in_dim.16), calls=%async_computation | async-start | bytes 1048576 | tf_op jit(solution)/shard_map/gates/all_to_all | solution.py:22
  26.9 1.0 dynamic-slice_bitcast_fusion.5
  27.9 1.0 pad_maximum_fusion.8
  28.9 2.2 %collective-permute-start.2 = (bf16[64,5120]{1,0:T(8,128)(2,1)}, bf16[64,5120]{1,0:T(8,128)(2,1)}, u32[]{:S(2)}, u32[]{:S(2)}) collective-permute-start(bf16[64,5120]{1,0:T(8,128)(2,1)} %pad_maximum_fusion.8), channel_id=1, source_target_pairs={{0,240},{16,0},{32,16},{48,32},{64,48},{80,64},{96,80},{112,96},{1... | collective-permute-start | bytes 1966088 | tf_op jit(solution)/shard_map/weights/ppermute | solution.py:12
  31.1 2.9 %fusion.29 = bf16[64,128]{1,0:T(8,128)(2,1)S(1)} fusion(bf16[2,1,64,8192]{3,2,1,0:T(8,128)(2,1)} %param.11, s32[]{:T(128)S(6)} %select_n.134, f32[1,3,64,128]{3,2,1,0:T(8,128)S(1)} %copy-done.7, bf16[1,128,8192]{2,1,0:T(8,128)(2,1)} %param.9), kind=kOutput, calls=%fused_computation.42 | convolution fusion | flops 134291456 | bytes 3194884 | tf_op jit(solution)/shard_map/backward/dot_general | solution.py:30
  34.0 2.1 %fusion = bf16[128,8192]{1,0:T(8,128)(2,1)} fusion(bf16[128,64]{0,1:T(8,128)(2,1)S(1)} %multiply_convert_fusion.2, bf16[1,128,8192]{2,1,0:T(8,128)(2,1)S(1)} %copy-done, bf16[2,1,64,8192]{3,2,1,0:T(8,128)(2,1)S(1)} %copy-done.2, s32[]{:T(128)S(6)} %select_n.108), kind=kOutput, calls=%fused_computation.5 | convolution fusion | flops 137363456 | bytes 5259268 | tf_op jit(solution)/shard_map/gates/dot_general | solution.py:92
  36.1 0.8 copy.24
  36.9 2.5 %copy.30 = bf16[128,16,512]{2,0,1:T(8,128)(2,1)} copy(bf16[128,16,512]{2,1,0:T(8,128)(2,1)S(1)} %bitcast.110) | data formatting | bytes 4194304 | tf_op jit(solution)/shard_map/columns/reshape;squeeze | solution.py:57
  39.4 9.4 %collective-permute-done.5 = bf16[128,4096]{1,0:T(8,128)(2,1)} collective-permute-done((bf16[128,4096]{1,0:T(8,128)(2,1)}, bf16[128,4096]{1,0:T(8,128)(2,1)}, u32[]{:S(2)}, u32[]{:S(2)}) %collective-permute-start.5) | collective-permute-done | bytes 1048608 | tf_op jit(solution)/shard_map/weights/ppermute | solution.py:12
  48.9 2.3 %constant_dynamic-update-slice_fusion.1 = bf16[192,4096]{1,0:T(8,128)(2,1)} fusion(bf16[128,4096]{1,0:T(8,128)(2,1)} %collective-permute-done.5), kind=kLoop, calls=%fused_computation.110 | loop fusion | bytes 2097152
  51.2 2.8 %all-to-all-done = bf16[16,128,128]{1,2,0:T(8,128)(2,1)S(1)} async-done(((bf16[16,128,128]{1,2,0:T(8,128)(2,1)}), bf16[16,128,128]{1,2,0:T(8,128)(2,1)S(1)}, u32[]{:S(2)}, u32[]{:S(2)}) %all-to-all-start) | async-done | bytes 524320 | tf_op jit(solution)/shard_map/gates/all_to_all | solution.py:22
  54.0 8.2 %all-to-all-start.1 = ((bf16[16,128,512]{2,1,0:T(8,128)(2,1)}), bf16[16,128,512]{2,1,0:T(8,128)(2,1)S(1)}, u32[]{:S(2)}, u32[]{:S(2)}) async-start(bf16[16,128,512]{2,1,0:T(8,128)(2,1)} %bitcast.108), calls=%async_computation.1 | async-start | bytes 4194304 | tf_op jit(solution)/shard_map/columns/all_to_all | solution.py:58
  62.2 1.9 constant_dynamic-update-slice_fusion
  64.1 0.8 collective-permute-start.7
  64.9 2.4 %dynamic-slice_bitcast_fusion = bf16[64,8192]{1,0:T(8,128)(2,1)} fusion(bf16[2,1,64,8192]{3,2,1,0:T(8,128)(2,1)} %param.10, s32[]{:T(128)S(6)} %select_n.134), kind=kLoop, calls=%fused_computation.59 | loop fusion | bytes 2097156 | tf_op jit(solution)/shard_map/backward/jit(dynamic_index_in_dim)/squeeze | solution.py:26
  67.6 1.1 slice.97
  69.5 1.2 collective-permute-done.3
  70.7 0.9 copy-done.10
  71.5 1.8 fusion.35
  73.4 17.3 %all-to-all-done.1 = bf16[16,128,512]{2,1,0:T(8,128)(2,1)S(1)} async-done(((bf16[16,128,512]{2,1,0:T(8,128)(2,1)}), bf16[16,128,512]{2,1,0:T(8,128)(2,1)S(1)}, u32[]{:S(2)}, u32[]{:S(2)}) %all-to-all-start.1) | async-done | bytes 2097184 | tf_op jit(solution)/shard_map/columns/all_to_all | solution.py:58
  90.6 0.9 collective-permute-start
  91.5 2.1 %broadcast_select_fusion.3 = (bf16[192,4096]{1,0:T(8,128)(2,1)S(1)}, bf16[192,4096]{1,0:T(8,128)(2,1)S(1)}) fusion(bf16[192,4096]{1,0:T(8,128)(2,1)} %constant_dynamic-update-slice_fusion, bf16[192,4096]{1,0:T(8,128)(2,1)} %collective-permute-done.7, pred[]{:T(512)S(6)} %eq.37), kind=kLoop, calls=%fused_computation.25 | loop fusion | flops 1572864 | bytes 6291457 | tf_op jit(solution)/shard_map/weights/jit(_where)/select_n | solution.py:82
  93.8 1.4 copy-done.4
  98.8 1.5 multiply_convert_fusion.1
  100.3 0.8 broadcast_in_dim.17
  101.1 5.1 %all-to-all-start.2 = ((bf16[16,128,64]{1,2,0:T(8,128)(2,1)}), bf16[16,128,64]{1,2,0:T(8,128)(2,1)S(1)}, u32[]{:S(2)}, u32[]{:S(2)}) async-start(bf16[16,128,64]{1,2,0:T(8,128)(2,1)} %broadcast_in_dim.17), calls=%async_computation.2 | async-start | bytes 524288 | tf_op jit(solution)/shard_map/gates/all_to_all | solution.py:22
  106.3 1.9 broadcast_select_fusion.1
  108.2 6.5 %fusion.1 = (bf16[2048,1024]{1,0:T(8,128)(2,1)}, bf16[2048,1024]{1,0:T(8,128)(2,1)}, bf16[2048,1024]{1,0:T(8,128)(2,1)}) fusion(f32[2048]{0:T(1024)S(1)} %sqrt_sqrt_fusion, bf16[2048,512]{1,0:T(8,128)(2,1)S(1)} %get-tuple-element.3, bf16[2048,512]{1,0:T(8,128)(2,1)S(1)} %get-tuple-element.2, bf16[2,1,64,8192]{3,2,1,0:T(8,128)(2,1)} %param.11, ...), kind=kOutput, calls=%fused_computation.6 | convolution fusion | flops 291504128 | bytes 17440776 | tf_op jit(solution)/shard_map/grams/dot_general | solution.py:110
  115.1 3.1 %multiply_convert_fusion = bf16[2048,1024]{1,0:T(8,128)(2,1)S(1)} fusion(f32[2048]{0:T(1024)S(1)} %sqrt_sqrt_fusion, bf16[2048,1024]{1,0:T(8,128)(2,1)} %get-tuple-element.20, bf16[64,5120]{1,0:T(8,128)(2,1)} %collective-permute-done.2, bf16[16,128,64]{1,2,0:T(8,128)(2,1)S(1)} %all-to-all-done.2), kind=kOutput, calls=%fused_computation.10 | convolution fusion | flops 281018368 | bytes 8790016 | tf_op jit(solution)/shard_map/grams/dot_general | solution.py:111
  118.2 3.4 %fusion.16 = bf16[512,1024]{1,0:T(8,128)(2,1)} fusion(bf16[2048,1024]{1,0:T(8,128)(2,1)S(1)} %multiply_convert_fusion, s32[]{:T(128)S(6)} %select_n.114), kind=kOutput, calls=%fused_computation.27 | convolution fusion | flops 2148007936 | bytes 7340036 | tf_op jit(solution)/shard_map/grams/dot_general | solution.py:116
  121.6 2.6 %collective-permute-start.4 = (bf16[512,1024]{1,0:T(8,128)(2,1)}, bf16[512,1024]{1,0:T(8,128)(2,1)}, u32[]{:S(2)}, u32[]{:S(2)}) collective-permute-start(bf16[512,1024]{1,0:T(8,128)(2,1)} %fusion.16), channel_id=1, source_target_pairs={{0,32},{16,48},{32,64},{48,80},{64,96},{80,112},{96,128},{112,144}... | collective-permute-start | bytes 3145736 | tf_op jit(solution)/shard_map/grams/ppermute | solution.py:12
  124.1 3.4 %fusion.13 = bf16[512,1024]{1,0:T(8,128)(2,1)} fusion(bf16[2048,1024]{1,0:T(8,128)(2,1)S(1)} %copy-done.3, s32[]{:T(128)S(6)} %select_n.114), kind=kOutput, calls=%fused_computation.26 | convolution fusion | flops 2148007936 | bytes 7340036 | tf_op jit(solution)/shard_map/grams/dot_general | solution.py:116
  127.5 1.7 collective-permute-start.1
  129.3 0.9 broadcast_in_dim.20
  130.2 7.4 %all-to-all-start.3 = ((f32[16,64,128]{2,1,0:T(8,128)}), f32[16,64,128]{2,1,0:T(8,128)S(1)}, u32[]{:S(2)}, u32[]{:S(2)}) async-start(f32[16,64,128]{2,1,0:T(8,128)} %broadcast_in_dim.20), calls=%async_computation.3 | async-start | bytes 1048576 | tf_op jit(solution)/shard_map/backward/all_to_all | solution.py:22
  137.7 16.9 %all-to-all-done.3 = f32[16,64,128]{2,1,0:T(8,128)S(1)} async-done(((f32[16,64,128]{2,1,0:T(8,128)}), f32[16,64,128]{2,1,0:T(8,128)S(1)}, u32[]{:S(2)}, u32[]{:S(2)}) %all-to-all-start.3) | async-done | bytes 524320 | tf_op jit(solution)/shard_map/backward/all_to_all | solution.py:22
  155.4 17.0 %collective-permute-done.4 = bf16[512,1024]{1,0:T(8,128)(2,1)} collective-permute-done((bf16[512,1024]{1,0:T(8,128)(2,1)}, bf16[512,1024]{1,0:T(8,128)(2,1)}, u32[]{:S(2)}, u32[]{:S(2)}) %collective-permute-start.4) | collective-permute-done | bytes 1048608 | tf_op jit(solution)/shard_map/grams/ppermute | solution.py:12
  172.5 22.5 %collective-permute-done.1 = bf16[512,1024]{1,0:T(8,128)(2,1)} collective-permute-done((bf16[512,1024]{1,0:T(8,128)(2,1)}, bf16[512,1024]{1,0:T(8,128)(2,1)}, u32[]{:S(2)}, u32[]{:S(2)}) %collective-permute-start.1) | collective-permute-done | bytes 1048608 | tf_op jit(solution)/shard_map/grams/ppermute | solution.py:12
  195.0 7.3 %bitcast_add_fusion = f32[1,512,1024]{2,1,0:T(8,128)} fusion(bf16[512,1024]{1,0:T(8,128)(2,1)} %collective-permute-done.4, bf16[512,1024]{1,0:T(8,128)(2,1)} %collective-permute-done.1, f32[1,512,1024]{2,1,0:T(8,128)S(1)} %copy-done.9, bf16[2048,1024]{1,0:T(8,128)(2,1)} %get-tuple-element.18, s32[]{:T(128)S(6)} %select_n.114), kind=kOutput, calls=%fused_computation.12 | convolution fusion | flops 2151153664 | bytes 12582916 | tf_op jit(solution)/shard_map/grams/dot_general | solution.py:116
  (65 shorter events, 7.2 us)
Async XLA Ops:
  0.7 1.9 copy-start.1
  2.6 7.7 %copy-start.7 = (f32[1,3,64,128]{3,2,1,0:T(8,128)S(1)}, f32[1,3,64,128]{3,2,1,0:T(8,128)}, u32[]{:S(2)}) copy-start(f32[1,3,64,128]{3,2,1,0:T(8,128)} %param.12) | copy-start | bytes 294916
  2.6 11.8 %copy-start = (bf16[1,128,8192]{2,1,0:T(8,128)(2,1)S(1)}, bf16[1,128,8192]{2,1,0:T(8,128)(2,1)}, u32[]{:S(2)}) copy-start(bf16[1,128,8192]{2,1,0:T(8,128)(2,1)} %param.8) | copy-start | bytes 6291460
  4.8 44.0 %collective-permute-start.5 = (bf16[128,4096]{1,0:T(8,128)(2,1)}, bf16[128,4096]{1,0:T(8,128)(2,1)}, u32[]{:S(2)}, u32[]{:S(2)}) collective-permute-start(bf16[128,4096]{1,0:T(8,128)(2,1)} %pad_maximum_fusion.1), channel_id=1, source_target_pairs={{0,16},{16,32},{32,48},{48,64},{64,80},{80,96},{96,112},{112,128},... | collective-permute-start | bytes 3145736 | tf_op jit(solution)/shard_map/weights/ppermute | solution.py:12
  7.3 54.9 %collective-permute-start.6 = (bf16[64,4096]{1,0:T(8,128)(2,1)}, bf16[64,4096]{1,0:T(8,128)(2,1)}, u32[]{:S(2)}, u32[]{:S(2)}) collective-permute-start(bf16[64,4096]{1,0:T(8,128)(2,1)} %get-tuple-element.6), channel_id=1, source_target_pairs={{0,32},{16,48},{32,64},{48,80},{64,96},{80,112},{96,128},{112,144}... | collective-permute-start | bytes 1572872 | tf_op jit(solution)/shard_map/weights/ppermute | solution.py:12
  10.3 86.8 %collective-permute-start.8 = (f32[64,128]{1,0:T(8,128)S(1)}, f32[64,128]{1,0:T(8,128)S(1)}, u32[]{:S(2)}, u32[]{:S(2)}) collective-permute-start(f32[64,128]{1,0:T(8,128)S(1)} %get-tuple-element.15), channel_id=1, source_target_pairs={{0,16},{16,32},{32,48},{48,64},{64,80},{80,96},{96,112},{112,128},... | collective-permute-start | bytes 98312 | tf_op jit(solution)/shard_map/weights/ppermute | solution.py:12
  13.2 85.0 %collective-permute-start.10 = (f32[64,128]{1,0:T(8,128)S(1)}, f32[64,128]{1,0:T(8,128)S(1)}, u32[]{:S(2)}, u32[]{:S(2)}) collective-permute-start(f32[64,128]{1,0:T(8,128)S(1)} %get-tuple-element.14), channel_id=1, source_target_pairs={{0,32},{16,48},{32,64},{48,80},{64,96},{80,112},{96,128},{112,144}... | collective-permute-start | bytes 98312 | tf_op jit(solution)/shard_map/weights/ppermute | solution.py:12
  18.1 35.9 %all-to-all-start = ((bf16[16,128,128]{1,2,0:T(8,128)(2,1)}), bf16[16,128,128]{1,2,0:T(8,128)(2,1)S(1)}, u32[]{:S(2)}, u32[]{:S(2)}) async-start(bf16[16,128,128]{1,2,0:T(8,128)(2,1)} %broadcast_in_dim.16), calls=%async_computation | async-start | bytes 1048576 | tf_op jit(solution)/shard_map/gates/all_to_all | solution.py:22
  28.9 38.7 %collective-permute-start.2 = (bf16[64,5120]{1,0:T(8,128)(2,1)}, bf16[64,5120]{1,0:T(8,128)(2,1)}, u32[]{:S(2)}, u32[]{:S(2)}) collective-permute-start(bf16[64,5120]{1,0:T(8,128)(2,1)} %pad_maximum_fusion.8), channel_id=1, source_target_pairs={{0,240},{16,0},{32,16},{48,32},{64,48},{80,64},{96,80},{112,96},{1... | collective-permute-start | bytes 1966088 | tf_op jit(solution)/shard_map/weights/ppermute | solution.py:12
  31.1 2.9 %copy-start.2 = (bf16[2,1,64,8192]{3,2,1,0:T(8,128)(2,1)S(1)}, bf16[2,1,64,8192]{3,2,1,0:T(8,128)(2,1)}, u32[]{:S(2)}) copy-start(bf16[2,1,64,8192]{3,2,1,0:T(8,128)(2,1)} %param.11) | copy-start | bytes 6291460
  54.0 36.6 %all-to-all-start.1 = ((bf16[16,128,512]{2,1,0:T(8,128)(2,1)}), bf16[16,128,512]{2,1,0:T(8,128)(2,1)S(1)}, u32[]{:S(2)}, u32[]{:S(2)}) async-start(bf16[16,128,512]{2,1,0:T(8,128)(2,1)} %bitcast.108), calls=%async_computation.1 | async-start | bytes 4194304 | tf_op jit(solution)/shard_map/columns/all_to_all | solution.py:58
  64.1 27.4 %collective-permute-start.7 = (bf16[192,4096]{1,0:T(8,128)(2,1)}, bf16[192,4096]{1,0:T(8,128)(2,1)}, u32[]{:S(2)}, u32[]{:S(2)}) collective-permute-start(bf16[192,4096]{1,0:T(8,128)(2,1)} %constant_dynamic-update-slice_fusion), channel_id=1, source_target_pairs={{0,1},{1,0},{2,3},{3,2},{4,5},{5,4},{6,7},{7,6},{8,9},{9,8},{10,11... | collective-permute-start | bytes 4718600 | tf_op jit(solution)/shard_map/weights/ppermute | solution.py:17
  68.7 2.0 collective-permute-start.3
  70.7 0.9 copy-start.10
  90.6 15.7 %collective-permute-start = (bf16[2048,512]{1,0:T(8,128)(2,1)S(1)}, bf16[2048,512]{1,0:T(8,128)(2,1)}, u32[]{:S(2)}, u32[]{:S(2)}) collective-permute-start(bf16[2048,512]{1,0:T(8,128)(2,1)S(1)} %bitcast.111), channel_id=1, source_target_pairs={{0,1},{1,0},{2,3},{3,2},{4,5},{5,4},{6,7},{7,6},{8,9},{9,8},{10,11... | collective-permute-start | bytes 6291464 | tf_op jit(solution)/shard_map/columns/ppermute | solution.py:17
  93.6 1.6 copy-start.4
  93.8 1.9 copy-start.6
  97.1 1.6 copy-start.5
  97.1 1.7 copy-start.11
  98.5 7.6 %collective-permute-start.11 = (f32[64,64]{1,0:T(8,128)S(1)}, f32[64,64]{1,0:T(8,128)S(1)}, u32[]{:S(2)}, u32[]{:S(2)}) collective-permute-start(f32[64,64]{1,0:T(8,128)S(1)} %fusion.99), channel_id=1, source_target_pairs={{0,224},{16,240},{32,0},{48,16},{64,32},{80,48},{96,64},{112,80},{... | collective-permute-start | bytes 49160 | tf_op jit(solution)/shard_map/backward/ppermute | solution.py:12
  98.7 7.5 %collective-permute-start.9 = (f32[64,64]{1,0:T(8,128)S(1)}, f32[64,64]{1,0:T(8,128)S(1)}, u32[]{:S(2)}, u32[]{:S(2)}) collective-permute-start(f32[64,64]{1,0:T(8,128)S(1)} %fusion.98), channel_id=1, source_target_pairs={{0,240},{16,0},{32,16},{48,32},{64,48},{80,64},{96,80},{112,96},{1... | collective-permute-start | bytes 49160 | tf_op jit(solution)/shard_map/backward/ppermute | solution.py:12
  101.1 14.0 %all-to-all-start.2 = ((bf16[16,128,64]{1,2,0:T(8,128)(2,1)}), bf16[16,128,64]{1,2,0:T(8,128)(2,1)S(1)}, u32[]{:S(2)}, u32[]{:S(2)}) async-start(bf16[16,128,64]{1,2,0:T(8,128)(2,1)} %broadcast_in_dim.17), calls=%async_computation.2 | async-start | bytes 524288 | tf_op jit(solution)/shard_map/gates/all_to_all | solution.py:22
  118.2 5.9 %copy-start.3 = (bf16[2048,1024]{1,0:T(8,128)(2,1)S(1)}, bf16[2048,1024]{1,0:T(8,128)(2,1)}, u32[]{:S(2)}) copy-start(bf16[2048,1024]{1,0:T(8,128)(2,1)} %get-tuple-element.19) | copy-start | bytes 12582916
  121.6 50.9 %collective-permute-start.4 = (bf16[512,1024]{1,0:T(8,128)(2,1)}, bf16[512,1024]{1,0:T(8,128)(2,1)}, u32[]{:S(2)}, u32[]{:S(2)}) collective-permute-start(bf16[512,1024]{1,0:T(8,128)(2,1)} %fusion.16), channel_id=1, source_target_pairs={{0,32},{16,48},{32,64},{48,80},{64,96},{80,112},{96,128},{112,144}... | collective-permute-start | bytes 3145736 | tf_op jit(solution)/shard_map/grams/ppermute | solution.py:12
  127.5 27.2 %copy-start.8 = (f32[2,1,64,64]{3,2,1,0:T(8,128)S(1)}, f32[2,1,64,64]{3,2,1,0:T(8,128)}, u32[]{:S(2)}) copy-start(f32[2,1,64,64]{3,2,1,0:T(8,128)} %param.15) | copy-start | bytes 98308
  127.5 67.5 %copy-start.9 = (f32[1,512,1024]{2,1,0:T(8,128)S(1)}, f32[1,512,1024]{2,1,0:T(8,128)}, u32[]{:S(2)}) copy-start(f32[1,512,1024]{2,1,0:T(8,128)} %param.14) | copy-start | bytes 6291460
  127.5 67.4 %collective-permute-start.1 = (bf16[512,1024]{1,0:T(8,128)(2,1)}, bf16[512,1024]{1,0:T(8,128)(2,1)}, u32[]{:S(2)}, u32[]{:S(2)}) collective-permute-start(bf16[512,1024]{1,0:T(8,128)(2,1)} %fusion.13), channel_id=1, source_target_pairs={{0,16},{16,32},{32,48},{48,64},{64,80},{80,96},{96,112},{112,128},... | collective-permute-start | bytes 3145736 | tf_op jit(solution)/shard_map/grams/ppermute | solution.py:12
  130.2 24.4 %all-to-all-start.3 = ((f32[16,64,128]{2,1,0:T(8,128)}), f32[16,64,128]{2,1,0:T(8,128)S(1)}, u32[]{:S(2)}, u32[]{:S(2)}) async-start(f32[16,64,128]{2,1,0:T(8,128)} %broadcast_in_dim.20), calls=%async_computation.3 | async-start | bytes 1048576 | tf_op jit(solution)/shard_map/backward/all_to_all | solution.py:22

commit v2 on v1

--- a/solution.py
+++ b/solution.py
@@ -1,6 +1,10 @@
+import functools
+
 import jax
 import jax.numpy as jnp
 from jax import lax
+from jax.experimental import pallas as pl
+from jax.experimental.pallas import tpu as pltpu
 from jax.sharding import PartitionSpec as P
 
 F32 = jnp.float32
@@ -22,12 +26,172 @@
     return lax.all_to_all(jnp.broadcast_to(block[None], (count,) + block.shape), "dp", 0, 0)
 
 
+def gather_chips(block):
+    chips = lax.axis_size("dp") // 2
+    return jnp.stack([block] + [shift(block, "dp", 2 * m) for m in range(1, chips)])
+
+
 def pick(weights, span_id):
     return lax.dynamic_index_in_dim(weights[:, 0], span_id, 0, keepdims=False)
 
 
 def nt(a, b):
     return lax.dot_general(a, b, (((1,), (1,)), ((), ())), preferred_element_type=F32)
+
+
+def tn(a, b):
+    return lax.dot_general(a, b, (((0,), (0,)), ((), ())), preferred_element_type=F32)
+
+
+def gram_kernel(steps, where, own, other, mine, sibs, up0_own, up0_oth, up1_own, up1_oth, table, *rest):
+    outs, accs = rest[: len(steps)], rest[len(steps):]
+    core = where[1]
+    rank = up0_own.shape[2]
+    hlf = own.shape[2] // 2
+    rows = own.shape[2]
+
+    @pl.when(pl.program_id(0) == 0)
+    def _():
+        for acc in accs:
+            acc[...] = jnp.zeros_like(acc)
+
+    gates = jnp.concatenate([mine[0], sibs[0]], axis=0)
+    ids = gates[:, 2 * rank:].astype(F32)
+    lane = lax.broadcasted_iota(jnp.int32, ids.shape, 1).astype(F32)
+    scale = jnp.sum(jnp.where(ids == lane, table[...], 0.0), axis=1, keepdims=True)
+    g0, g1 = gates[:, :rank], gates[:, rank:2 * rank]
+
+    def rebuilt(ref, up0, up1):
+        act = jnp.concatenate([ref[core], ref[1 - core]], axis=0)
+        acts = [act]
+        for gate, up in ((g0, up0), (g1, up1))[: max(steps)]:
+            add = jnp.dot(gate, up, preferred_element_type=F32)
+            act = (act.astype(F32) + add).astype(BF16)
+            acts.append(act)
+        return [(scale * acts[j].astype(F32)).astype(BF16) for j in steps]
+
+    r_all = rebuilt(own, up0_own[0, 0], up1_own[...])
+    q_all = rebuilt(other, up0_oth[0, 0], up1_oth[...])
+    for acc, r, q in zip(accs, r_all, q_all):
+        acc[:, :rows] += tn(r[:, :hlf], r)
+        acc[:, rows:rows + hlf] += tn(r[:, hlf:], r[:, hlf:])
+
+        @pl.when(core == 0)
+        def _():
+            acc[:, rows + hlf:] += tn(r[:, :hlf], q)
+
+        @pl.when(core == 1)
+        def _():
+            acc[:, rows + hlf:] += tn(q[:, hlf:], r)
+
+    @pl.when(pl.program_id(0) == pl.num_programs(0) - 1)
+    def _():
+        for out, acc in zip(outs, accs):
+            out[...] = acc[...].astype(out.dtype)
+
+
+def grams(steps, dtypes, where, own, other, mine, sibs, adapter_up, up1, table):
+    chips, tok, lanes = mine.shape
+    rows = own.shape[2]
+    rank = adapter_up.shape[2]
+    packed = (rows // 2, rows * 5 // 2)
+    tokens = own.shape[0] * tok
+    one_up = lambda pick_cols: pl.BlockSpec(
+        (1, 1, rank, rows), lambda i, w: (w[2], 0, 0, pick_cols(w))
+    )
+    cols = pl.BlockSpec((2, tok, rows), lambda i, w: (i, 0, 0))
+    gate = pl.BlockSpec((1, tok, lanes), lambda i, w: ((w[0] + chips - i) % chips, 0, 0))
+    spec = pltpu.PrefetchScalarGridSpec(
+        num_scalar_prefetch=1,
+        grid=(chips,),
+        in_specs=[
+            cols,
+            cols,
+            gate,
+            gate,
+            one_up(lambda w: 2 * w[0] + w[1]),
+            one_up(lambda w: 2 * w[0] + 1 - w[1]),
+            pl.BlockSpec((rank, rows), lambda i, w: (0, w[1])),
+            pl.BlockSpec((rank, rows), lambda i, w: (0, 1 - w[1])),
+            pl.BlockSpec((1, lanes - 2 * rank), lambda i, w: (0, 0)),
+        ],
+        out_specs=[pl.BlockSpec(packed, lambda i, w: (0, 0)) for _ in steps],
+        scratch_shapes=[pltpu.VMEM(packed, F32) for _ in steps],
+    )
+    return pl.pallas_call(
+        functools.partial(gram_kernel, steps),
+        grid_spec=spec,
+        out_shape=[jax.ShapeDtypeStruct(packed, d) for d in dtypes],
+        compiler_params=pltpu.CompilerParams(dimension_semantics=("arbitrary",)),
+        cost_estimate=pl.CostEstimate(
+            flops=2 * tokens * packed[0] * packed[1] * len(steps),
+            transcendentals=0,
+            bytes_accessed=2 * own.size * 2,
+        ),
+    )(where, own, other, mine, sibs, adapter_up, adapter_up, up1, up1, table)
+
+
+def update_kernel(factor_scale, where, old, here, came, cross, out):
+    i = pl.program_id(0)
+    core = where[1]
+    hlf = out.shape[0]
+    rows = 2 * hlf
+
+    def put(lo, hi, val):
+        out[:, lo:hi] = 0.75 * old[:, lo:hi] + factor_scale * val
+
+    def packed(lo, hi):
+        return here[:, lo:hi] + came[:, lo:hi].astype(F32)
+
+    for c in range(2):
+        base = c * rows
+
+        @pl.when(jnp.logical_and(core == c, i == 0))
+        def _():
+            put(base, base + rows, packed(0, rows))
+
+        @pl.when(jnp.logical_and(core == c, i == 1))
+        def _():
+            put(base, base + hlf, packed(hlf, rows).T)
+            put(base + hlf, base + rows, packed(rows, rows + hlf))
+
+    @pl.when(jnp.logical_and(core == 0, i == 0))
+    def _():
+        put(rows, 2 * rows, packed(rows + hlf, 2 * rows + hlf))
+
+    @pl.when(jnp.logical_and(core == 0, i == 1))
+    def _():
+        put(rows, 2 * rows, cross[...])
+
+    for k in range(2):
+        a, b = k * hlf, (k + 1) * hlf
+
+        @pl.when(jnp.logical_and(core == 1, i == k))
+        def _():
+            put(0, hlf, cross[:, a:b].T)
+            put(hlf, rows, packed(rows + hlf + a, rows + hlf + b).T)
+
+
+def update(factor_scale, where, old, here, came, cross):
+    total, block = old.shape
+    hlf = total // 2
+    whole = lambda x: pl.BlockSpec(x.shape, lambda i, w: (0, 0))
+    part = pl.BlockSpec((hlf, block), lambda i, w: (i, 0))
+    spec = pltpu.PrefetchScalarGridSpec(
+        num_scalar_prefetch=1,
+        grid=(2,),
+        in_specs=[part, whole(here), whole(came), whole(cross)],
+        out_specs=part,
+    )
+    return pl.pallas_call(
+        functools.partial(update_kernel, factor_scale),
+        grid_spec=spec,
+        out_shape=jax.ShapeDtypeStruct(old.shape, F32),
+        compiler_params=pltpu.CompilerParams(dimension_semantics=("arbitrary",)),
+        cost_estimate=pl.CostEstimate(
+            flops=4 * old.size, transcendentals=0, bytes_accessed=12 * old.size
+        ),
+    )(where, old, here, came, cross)
 
 
 def shards(
@@ -55,7 +219,7 @@
 
     with jax.named_scope("columns"):
         split = x0.reshape(tok, replicas, rows).transpose(1, 0, 2)
-        own = lax.all_to_all(split, "dp", 0, 0).reshape(tokens, rows)
+        own = lax.all_to_all(split, "dp", 0, 0)
         other = swap_cores(own)
 
     with jax.named_scope("weights"):
@@ -86,42 +250,33 @@
         c0 = first(sec)
         up0 = pick(adapter_up, c0)
         gate0 = jax.nn.silu(nt(x0, pick(adapter_down, c0))).astype(BF16)
-        ids = pick(doc_ids[:, None], sec).astype(BF16)
-        sent = jnp.concatenate([gate0, jnp.broadcast_to(ids[:, None], (tok, rank))], axis=1)
-        got0 = gather_dp(sent).reshape(tokens, 2 * rank)
         x1 = (x0.astype(F32) + jnp.dot(gate0, up0, preferred_element_type=F32)).astype(BF16)
         z1 = nt(x1[:, :half], down1_lo) + nt(x1[:, half:], down1_hi)
         gate1 = jax.nn.silu(z1).astype(BF16)
-        got1 = gather_dp(gate1).reshape(tokens, rank)
+        ids = jnp.broadcast_to(pick(doc_ids[:, None], sec).astype(BF16)[:, None], (tok, 2 * rank))
+        gates = gather_chips(jnp.concatenate([gate0, gate1, ids], axis=1))
+        gates_sib = swap_cores(gates)
 
     with jax.named_scope("scale"):
-        docs = jnp.arange(2 * replicas, dtype=jnp.int32).astype(F32)
-        onehot = (got0[:, rank:rank + 1].astype(F32) == docs[None, :]).astype(F32)
-        counts = jnp.sum(onehot, axis=0, keepdims=True)
-        length = jnp.sum(onehot * counts, axis=1, keepdims=True)
-        scale = jnp.sqrt(jnp.sqrt(tok / length))
-
-    with jax.named_scope("grams"):
-        up0_cols = lax.dynamic_slice_in_dim(up0, (rep // 2) * block, block, 1)
-        lo = jnp.where(core == 0, own, other)
-        hi = jnp.where(core == 0, other, own)
-        a0 = jnp.concatenate([lo, hi], axis=1)
-        g0 = got0[:, :rank]
-        a1 = (a0.astype(F32) + jnp.dot(g0, up0_cols, preferred_element_type=F32)).astype(BF16)
-        a2 = (a1.astype(F32) + jnp.dot(got1, up1_cols, preferred_element_type=F32)).astype(BF16)
-
-        def gram(act):
-            scaled = (scale * act.astype(F32)).astype(BF16)
-            mine_cols = lax.dynamic_slice_in_dim(scaled, core * rows, rows, 1)
-            return lax.dot_general(
-                mine_cols, scaled, (((0,), (0,)), ((), ())), preferred_element_type=F32
-            )
-
-        here = gram(a0)
-        from1 = shift(gram(a1).astype(BF16), "section", 1).astype(F32)
-        from2 = shift(gram(a2).astype(BF16), "section", 2).astype(F32)
-        norm_count = steps_count * tokens
-        input_factor_new = 0.75 * input_factor + 0.25 * (here + from1 + from2)[None] / norm_count
+        lane = jnp.arange(2 * rank, dtype=jnp.int32).astype(F32)
+
+        def tally(held):
+            return jnp.sum((held[:, :, 2 * rank:].astype(F32) == lane).astype(F32), axis=(0, 1))
+
+        counts = jnp.maximum(tally(gates) + tally(gates_sib), 1.0)
+        table = jnp.sqrt(jnp.sqrt(tok / counts))[None]
+
+    with jax.named_scope("factor"):
+        where = jnp.stack([rep // 2, core, c0])
+        common = (where, own, other, gates, gates_sib, adapter_up, up1_cols, table)
+        (step2,) = grams((2,), (BF16,), *common)
+        step0, step1 = grams((0, 1), (F32, F32), *common)
+        from2 = shift(step2, "section", 1)
+        from1 = shift((step1 + from2.astype(F32)).astype(BF16), "section", 1)
+        cut = rows + rows // 2
+        cross = swap_cores(step0[:, cut:] + from1[:, cut:].astype(F32))
+        factor_scale = 0.25 / (steps_count * tokens)
+        input_factor_new = update(factor_scale, where, input_factor[0], step0, from1, cross)[None]
 
     with jax.named_scope("backward"):
         b0 = (sec < sections).astype(jnp.int32)

time: 203 us -> 175 us (0.86)
  waiting for transfers between devices: 87.5 us -> 29.7 us
  Pallas kernels: 0 us -> 29.5 us
  matrix products: 37.6 us -> 11.5 us
  starting transfers between devices: 47.3 us -> 70.8 us
    pallas_call x0 -> x3, Pallas kernels: none -> 29.5 us  [the longest x2 25.1 us: grams(): pl.pallas_call(functools.partial(gram_kernel, steps), grid_spec=spec, out...]
    ppermute x9 -> x16, waiting for transfers between devices: 49 us -> 21.7 us  [shift(): lax.ppermute(block, axis, [(i, (i + distance) % count) for i in range(cou...]
    dot_general x5 -> x0, matrix products: 23.7 us -> none  [the longest x3 14.1 us: gram(): lax.dot_general(mine_cols, scaled, (((0,), (0,)), ((), ())), preferred_el...]
    ppermute x9 -> x16, starting transfers between devices: 16.1 us -> 37.7 us  [shift(): lax.ppermute(block, axis, [(i, (i + distance) % count) for i in range(cou...]
    all_to_all x1, waiting for transfers between devices: 17.3 us -> 0.01 us  [shards(): own = lax.all_to_all(split, 'dp', 0, 0)]
    ppermute x3 -> x5, starting transfers between devices: 1.8 us -> 14.5 us  [swap_cores(): return lax.ppermute(block, 'dp', [(i, i ^ 1) for i in range(count)])]
    all_to_all x3 -> x1, waiting for transfers between devices: 20.1 us -> 7.98 us  [gather_dp(): lax.all_to_all(jnp.broadcast_to(block[None], (count,) + block.shape), 'dp...]
    all_to_all x3 -> x1, starting transfers between devices: 21.2 us -> 9.59 us  [gather_dp(): lax.all_to_all(jnp.broadcast_to(block[None], (count,) + block.shape), 'dp...]
  transfers between devices with their start and end apart: 16 -> 23, of which waited for: 8 -> 9; matrix products, arithmetic and copies ran while one was open for 23% -> 20% of each run, Pallas kernels for 0% -> 14%
where the time goes in v2:
time: 175 us; the launch traced here: 174 us
  starting transfers between devices  70.8 us (40%)
  waiting for transfers between devices  29.7 us (17%)
  Pallas kernels  29.5 us (17%)
  local copies, waits for them, and re-layouts  22.4 us (13%)
  matrix products  11.5 us (7%)
  other arithmetic  9.12 us (5%)
    ppermute x16, starting transfers between devices, shift(): lax.ppermute(block, axis, [(i, (i + distance) % count) for i in range(cou...  37.7 us
    pallas_call x2, Pallas kernels, grams(): pl.pallas_call(functools.partial(gram_kernel, steps), grid_spec=spec, out...  25.1 us
    ppermute x16, waiting for transfers between devices, shift(): lax.ppermute(block, axis, [(i, (i + distance) % count) for i in range(cou...  21.7 us
    ppermute x5, starting transfers between devices, swap_cores(): return lax.ppermute(block, 'dp', [(i, i ^ 1) for i in range(count)])  14.5 us
    all_to_all x1, starting transfers between devices, gather_dp(): lax.all_to_all(jnp.broadcast_to(block[None], (count,) + block.shape), 'dp...  9.59 us
    unnamed x36, local copies, waits for them, and re-layouts  9.13 us
    all_to_all x1, starting transfers between devices, shards(): own = lax.all_to_all(split, 'dp', 0, 0)  9.03 us
    all_to_all x1, waiting for transfers between devices, gather_dp(): lax.all_to_all(jnp.broadcast_to(block[None], (count,) + block.shape), 'dp...  7.98 us
  transfers between devices with their start and end apart: 23, of which 9 were waited for; matrix products, arithmetic and copies ran while one was open for 20% of the time, Pallas kernels for 14%

profile of v2, /device:TPU:1, one launch (start us, length us, event | category | flops | bytes accessed | tf_op | source)
XLA Modules:
  0.0 174.0 jit_solution(10075081446525744550)
XLA Ops:
  0.7 1.7 dynamic-slice_bitcast_fusion.2
  2.5 1.2 dynamic-slice_bitcast_fusion.1
  3.7 1.1 pad_maximum_fusion
  4.8 2.5 %collective-permute-start.14 = (bf16[128,4096]{1,0:T(8,128)(2,1)}, bf16[128,4096]{1,0:T(8,128)(2,1)}, u32[]{:S(2)}, u32[]{:S(2)}) collective-permute-start(bf16[128,4096]{1,0:T(8,128)(2,1)} %pad_maximum_fusion), channel_id=1, source_target_pairs={{0,16},{16,32},{32,48},{48,64},{64,80},{80,96},{96,112},{112,128},... | collective-permute-start | bytes 3145736 | tf_op jit(solution)/shard_map/weights/ppermute | solution.py:16
  7.3 3.0 %collective-permute-start.15 = (bf16[64,4096]{1,0:T(8,128)(2,1)}, bf16[64,4096]{1,0:T(8,128)(2,1)}, u32[]{:S(2)}, u32[]{:S(2)}) collective-permute-start(bf16[64,4096]{1,0:T(8,128)(2,1)} %get-tuple-element.10), channel_id=1, source_target_pairs={{0,32},{16,48},{32,64},{48,80},{64,96},{80,112},{96,128},{112,144}... | collective-permute-start | bytes 1572872 | tf_op jit(solution)/shard_map/weights/ppermute | solution.py:16
  10.9 2.8 %collective-permute-start.17 = (f32[64,128]{1,0:T(8,128)}, f32[64,128]{1,0:T(8,128)}, u32[]{:S(2)}, u32[]{:S(2)}) collective-permute-start(f32[64,128]{1,0:T(8,128)} %get-tuple-element.19), channel_id=1, source_target_pairs={{0,16},{16,32},{32,48},{48,64},{64,80},{80,96},{96,112},{112,128},... | collective-permute-start | bytes 98312 | tf_op jit(solution)/shard_map/weights/ppermute | solution.py:16
  13.7 1.2 collective-permute-start.19
  15.1 2.9 %collective-permute-start.1 = (bf16[64,5120]{1,0:T(8,128)(2,1)S(1)}, bf16[64,5120]{1,0:T(8,128)(2,1)S(1)}, u32[]{:S(2)}, u32[]{:S(2)}) collective-permute-start(bf16[64,5120]{1,0:T(8,128)(2,1)S(1)} %pad_maximum_fusion.7), channel_id=1, source_target_pairs={{0,240},{16,0},{32,16},{48,32},{64,48},{80,64},{96,80},{112,96},{1... | collective-permute-start | bytes 1966088 | tf_op jit(solution)/shard_map/weights/ppermute | solution.py:16
  18.0 4.1 %copy.24 = bf16[1,128,8192]{1,2,0:T(8,128)(2,1)} copy(bf16[1,128,8192]{2,1,0:T(8,128)(2,1)} %param.8) | data formatting | bytes 4194304 | tf_op args[0]
  22.1 3.9 %copy.25 = bf16[128,16,512]{2,0,1:T(8,128)(2,1)} copy(bf16[128,16,512]{0,2,1:T(8,128)(2,1)} %bitcast.108) | data formatting | bytes 4194304 | tf_op jit(solution)/shard_map/columns/reshape;squeeze | solution.py:221
  26.0 9.0 %all-to-all-start = ((bf16[16,128,512]{2,1,0:T(8,128)(2,1)}), bf16[16,128,512]{2,1,0:T(8,128)(2,1)}, u32[]{:S(2)}, u32[]{:S(2)}) async-start(bf16[16,128,512]{2,1,0:T(8,128)(2,1)} %bitcast.107), calls=%async_computation | async-start | bytes 4194304 | tf_op jit(solution)/shard_map/columns/all_to_all | solution.py:222
  35.0 2.8 %multiply_convert_fusion.1 = bf16[128,64]{1,0:T(8,128)(2,1)S(1)} fusion(bf16[1,128,8192]{2,1,0:T(8,128)(2,1)} %param.8, bf16[2,1,64,8192]{3,2,1,0:T(8,128)(2,1)} %param.10, s32[]{:T(128)S(6)} %select_n.90), kind=kOutput, calls=%fused_computation.75 | convolution fusion | flops 134258688 | bytes 3162116 | tf_op jit(solution)/shard_map/gates/dot_general | solution.py:39
  37.8 2.1 %fusion = bf16[128,8192]{1,0:T(8,128)(2,1)} fusion(bf16[128,64]{1,0:T(8,128)(2,1)S(1)} %multiply_convert_fusion.1, bf16[1,128,8192]{2,1,0:T(8,128)(2,1)S(1)} %copy-done.1, bf16[2,1,64,8192]{3,2,1,0:T(8,128)(2,1)S(1)} %copy-done, s32[]{:T(128)S(6)} %select_n.90), kind=kOutput, calls=%fused_computation.1 | convolution fusion | flops 137363456 | bytes 5275652 | tf_op jit(solution)/shard_map/gates/dot_general | solution.py:253
  40.9 2.7 %constant_dynamic-update-slice_fusion.1 = bf16[192,4096]{1,0:T(8,128)(2,1)} fusion(bf16[128,4096]{1,0:T(8,128)(2,1)} %collective-permute-done.14), kind=kLoop, calls=%fused_computation.89 | loop fusion | bytes 2097152
  43.6 11.2 %collective-permute-done.15 = bf16[64,4096]{1,0:T(8,128)(2,1)} collective-permute-done((bf16[64,4096]{1,0:T(8,128)(2,1)}, bf16[64,4096]{1,0:T(8,128)(2,1)}, u32[]{:S(2)}, u32[]{:S(2)}) %collective-permute-start.15) | collective-permute-done | bytes 524320 | tf_op jit(solution)/shard_map/weights/ppermute | solution.py:16
  54.8 1.9 %constant_dynamic-update-slice_fusion = bf16[192,4096]{1,0:T(8,128)(2,1)} fusion(bf16[192,4096]{1,0:T(8,128)(2,1)} %constant_dynamic-update-slice_fusion.1, bf16[64,4096]{1,0:T(8,128)(2,1)} %collective-permute-done.15), kind=kLoop, calls=%fused_computation.88 | loop fusion | bytes 1048576 | tf_op jit(solution)/shard_map/weights/concatenate | solution.py:244
  56.6 8.7 %collective-permute-start.16 = (bf16[192,4096]{1,0:T(8,128)(2,1)}, bf16[192,4096]{1,0:T(8,128)(2,1)}, u32[]{:S(2)}, u32[]{:S(2)}) collective-permute-start(bf16[192,4096]{1,0:T(8,128)(2,1)} %constant_dynamic-update-slice_fusion), channel_id=1, source_target_pairs={{0,1},{1,0},{2,3},{3,2},{4,5},{5,4},{6,7},{7,6},{8,9},{9,8},{10,11... | collective-permute-start | bytes 4718600 | tf_op jit(solution)/shard_map/weights/ppermute | solution.py:21
  66.4 4.4 %collective-permute-start.3 = (bf16[128,256]{1,0:T(8,128)(2,1)S(1)}, bf16[128,256]{1,0:T(8,128)(2,1)S(1)}, u32[]{:S(2)}, u32[]{:S(2)}) collective-permute-start(bf16[128,256]{1,0:T(8,128)(2,1)S(1)} %pad_maximum_fusion.8), channel_id=1, source_target_pairs={{0,2},{1,3},{2,4},{3,5},{4,6},{5,7},{6,8},{7,9},{8,10},{9,11},{10,... | collective-permute-start | bytes 196616 | tf_op jit(solution)/shard_map/gates/ppermute | solution.py:16
  71.6 2.7 %collective-permute-done.3 = bf16[128,256]{1,0:T(8,128)(2,1)S(1)} collective-permute-done((bf16[128,256]{1,0:T(8,128)(2,1)S(1)}, bf16[128,256]{1,0:T(8,128)(2,1)S(1)}, u32[]{:S(2)}, u32[]{:S(2)}) %collective-permute-start.3) | collective-permute-done | bytes 65568 | tf_op jit(solution)/shard_map/gates/ppermute | solution.py:16
  74.4 2.1 %collective-permute-start.5 = (bf16[128,256]{1,0:T(8,128)(2,1)S(1)}, bf16[128,256]{1,0:T(8,128)(2,1)S(1)}, u32[]{:S(2)}, u32[]{:S(2)}) collective-permute-start(bf16[128,256]{1,0:T(8,128)(2,1)S(1)} %pad_maximum_fusion.8), channel_id=1, source_target_pairs={{0,6},{1,7},{2,8},{3,9},{4,10},{5,11},{6,12},{7,13},{8,14},{9,15},... | collective-permute-start | bytes 196616 | tf_op jit(solution)/shard_map/gates/ppermute | solution.py:16
  76.5 2.9 %collective-permute-start.6 = (bf16[128,256]{1,0:T(8,128)(2,1)S(1)}, bf16[128,256]{1,0:T(8,128)(2,1)S(1)}, u32[]{:S(2)}, u32[]{:S(2)}) collective-permute-start(bf16[128,256]{1,0:T(8,128)(2,1)S(1)} %pad_maximum_fusion.8), channel_id=1, source_target_pairs={{0,8},{1,9},{2,10},{3,11},{4,12},{5,13},{6,14},{7,15},{8,0},{9,1},... | collective-permute-start | bytes 196616 | tf_op jit(solution)/shard_map/gates/ppermute | solution.py:16
  79.4 2.0 %collective-permute-done.5 = bf16[128,256]{1,0:T(8,128)(2,1)S(1)} collective-permute-done((bf16[128,256]{1,0:T(8,128)(2,1)S(1)}, bf16[128,256]{1,0:T(8,128)(2,1)S(1)}, u32[]{:S(2)}, u32[]{:S(2)}) %collective-permute-start.5) | collective-permute-done | bytes 65568 | tf_op jit(solution)/shard_map/gates/ppermute | solution.py:16
  81.4 2.6 %collective-permute-start.7 = (bf16[128,256]{1,0:T(8,128)(2,1)S(1)}, bf16[128,256]{1,0:T(8,128)(2,1)S(1)}, u32[]{:S(2)}, u32[]{:S(2)}) collective-permute-start(bf16[128,256]{1,0:T(8,128)(2,1)S(1)} %pad_maximum_fusion.8), channel_id=1, source_target_pairs={{0,10},{1,11},{2,12},{3,13},{4,14},{5,15},{6,0},{7,1},{8,2},{9,3},... | collective-permute-start | bytes 196616 | tf_op jit(solution)/shard_map/gates/ppermute | solution.py:16
  84.0 2.2 %collective-permute-start.8 = (bf16[128,256]{1,0:T(8,128)(2,1)S(1)}, bf16[128,256]{1,0:T(8,128)(2,1)S(1)}, u32[]{:S(2)}, u32[]{:S(2)}) collective-permute-start(bf16[128,256]{1,0:T(8,128)(2,1)S(1)} %pad_maximum_fusion.8), channel_id=1, source_target_pairs={{0,12},{1,13},{2,14},{3,15},{4,0},{5,1},{6,2},{7,3},{8,4},{9,5},{1... | collective-permute-start | bytes 196616 | tf_op jit(solution)/shard_map/gates/ppermute | solution.py:16
  86.9 5.0 %collective-permute-start.9 = (bf16[128,256]{1,0:T(8,128)(2,1)S(1)}, bf16[128,256]{1,0:T(8,128)(2,1)S(1)}, u32[]{:S(2)}, u32[]{:S(2)}) collective-permute-start(bf16[128,256]{1,0:T(8,128)(2,1)S(1)} %pad_maximum_fusion.8), channel_id=1, source_target_pairs={{0,14},{1,15},{2,0},{3,1},{4,2},{5,3},{6,4},{7,5},{8,6},{9,7},{10,... | collective-permute-start | bytes 196616 | tf_op jit(solution)/shard_map/gates/ppermute | solution.py:16
  91.9 1.3 collective-permute-done.9
  93.2 3.8 %collective-permute-start.10 = (bf16[8,128,256]{2,1,0:T(8,128)(2,1)S(1)}, bf16[8,128,256]{2,1,0:T(8,128)(2,1)S(1)}, u32[]{:S(2)}, u32[]{:S(2)}) collective-permute-start(bf16[8,128,256]{2,1,0:T(8,128)(2,1)S(1)} %bitcast_dynamic-update-slice_fusion.mine), channel_id=1, source_target_pairs={{0,1},{1,0},{2,3},{3,2},{4,5},{5,4},{6,7},{7,6},{8,9},{9,8},{10,11... | collective-permute-start | bytes 1572872 | tf_op jit(solution)/shard_map/gates/ppermute | solution.py:21
  97.0 1.0 dynamic-slice_bitcast_fusion
  98.6 0.9 fusion.11
  99.5 1.6 slice.105.up1_own.up1_oth
  101.9 2.1 %broadcast_select_fusion.1 = (bf16[192,4096]{1,0:T(8,128)(2,1)S(1)}, bf16[192,4096]{1,0:T(8,128)(2,1)S(1)}) fusion(bf16[192,4096]{1,0:T(8,128)(2,1)} %constant_dynamic-update-slice_fusion, bf16[192,4096]{1,0:T(8,128)(2,1)} %collective-permute-done.16, pred[]{:T(512)S(6)} %eq.28), kind=kLoop, calls=%fused_computation.5 | loop fusion | flops 1572864 | bytes 6291457 | tf_op jit(solution)/shard_map/weights/jit(_where)/select_n | solution.py:246
  104.2 1.0 copy-done.9
  107.4 1.0 fusion.12
  109.0 10.4 %factor.4 = bf16[256,1280]{1,0:T(8,128)(2,1)} custom-call(s32[3]{0:T(128)} %pad_add_fusion.where, bf16[16,128,512]{2,1,0:T(8,128)(2,1)} %all-to-all-done.own, bf16[16,128,512]{2,1,0:T(8,128)(2,1)} %collective-permute-done.other, bf16[8,128,256]{2,1,0:T(8,128)(2,1)} %copy-done.6, bf16[8,128,256]{2,1,0:T(8,128)(2,1)} %copy-done.8, ...), custom_call_target="tpu_custom_call" | custom-call | flops 1342177280 | bytes 4194304 | tf_op jit(solution)/shard_map/factor/pallas_call | solution.py:121
  119.4 1.7 collective-permute-start.11
  121.4 0.9 fusion.13
  122.3 14.7 %factor.3 = (f32[256,1280]{1,0:T(8,128)}, f32[256,1280]{1,0:T(8,128)}) custom-call(s32[3]{0:T(128)} %pad_add_fusion.where, bf16[16,128,512]{2,1,0:T(8,128)(2,1)} %all-to-all-done.own, bf16[16,128,512]{2,1,0:T(8,128)(2,1)} %collective-permute-done.other, bf16[8,128,256]{2,1,0:T(8,128)(2,1)} %copy-done.6, bf16[8,128,256]{2,1,0:T(8,128)(2,1)} %copy-done.8, ...), custom_call_target="tpu_custom_call" | custom-call | flops 2684354560 | bytes 4194304 | tf_op jit(solution)/shard_map/factor/pallas_call | solution.py:121
  137.7 1.4 add_convert_fusion
  139.5 2.4 %collective-permute-start.20 = (f32[64,64]{1,0:T(8,128)S(1)}, f32[64,64]{1,0:T(8,128)S(1)}, u32[]{:S(2)}, u32[]{:S(2)}) collective-permute-start(f32[64,64]{1,0:T(8,128)S(1)} %fusion.69), channel_id=1, source_target_pairs={{0,224},{16,240},{32,0},{48,16},{64,32},{80,48},{96,64},{112,80},{... | collective-permute-start | bytes 49160 | tf_op jit(solution)/shard_map/backward/ppermute | solution.py:16
  141.8 1.3 collective-permute-start.18
  143.2 3.0 %collective-permute-done.18 = f32[64,64]{1,0:T(8,128)S(1)} collective-permute-done((f32[64,64]{1,0:T(8,128)S(1)}, f32[64,64]{1,0:T(8,128)S(1)}, u32[]{:S(2)}, u32[]{:S(2)}) %collective-permute-start.18) | collective-permute-done | bytes 16416 | tf_op jit(solution)/shard_map/backward/ppermute | solution.py:16
  146.4 0.8 broadcast_in_dim.34
  147.3 9.6 %all-to-all-start.1 = ((f32[16,64,128]{2,1,0:T(8,128)}), f32[16,64,128]{2,1,0:T(8,128)S(1)}, u32[]{:S(2)}, u32[]{:S(2)}) async-start(f32[16,64,128]{2,1,0:T(8,128)} %broadcast_in_dim.34), calls=%async_computation.1 | async-start | bytes 1048576 | tf_op jit(solution)/shard_map/backward/all_to_all | solution.py:26
  156.9 1.3 convert_add_fusion
  158.3 1.6 collective-permute-start.13
  160.0 8.0 %all-to-all-done.1 = f32[16,64,128]{2,1,0:T(8,128)S(1)} async-done(((f32[16,64,128]{2,1,0:T(8,128)}), f32[16,64,128]{2,1,0:T(8,128)S(1)}, u32[]{:S(2)}, u32[]{:S(2)}) %all-to-all-start.1) | async-done | bytes 524320 | tf_op jit(solution)/shard_map/backward/all_to_all | solution.py:26
  168.8 0.8 copy-done.11
  169.7 4.3 %factor.5 = f32[512,1024]{1,0:T(8,128)} custom-call(s32[3]{0:T(128)} %pad_add_fusion.where, f32[512,1024]{1,0:T(8,128)} %bitcast.111, f32[256,1280]{1,0:T(8,128)} %get-tuple-element.4.here, bf16[256,1280]{1,0:T(8,128)(2,1)} %copy-done.7, f32[256,512]{1,0:T(8,128)} %copy-done.11), custom_call_target="tpu_custom_call" | custom-call | flops 2097152 | bytes 6291456 | tf_op jit(solution)/shard_map/factor/pallas_call | solution.py:186
  (87 shorter events, 11.3 us)
Async XLA Ops:
  0.6 1.9 %copy-start = (bf16[2,1,64,8192]{3,2,1,0:T(8,128)(2,1)S(1)}, bf16[2,1,64,8192]{3,2,1,0:T(8,128)(2,1)}, u32[]{:S(2)}) copy-start(bf16[2,1,64,8192]{3,2,1,0:T(8,128)(2,1)} %up0_oth.3) | copy-start | bytes 6291460
  2.5 7.7 %copy-start.12 = (f32[1,3,64,128]{3,2,1,0:T(8,128)S(1)}, f32[1,3,64,128]{3,2,1,0:T(8,128)}, u32[]{:S(2)}) copy-start(f32[1,3,64,128]{3,2,1,0:T(8,128)} %param.12) | copy-start | bytes 294916
  4.8 36.1 %collective-permute-start.14 = (bf16[128,4096]{1,0:T(8,128)(2,1)}, bf16[128,4096]{1,0:T(8,128)(2,1)}, u32[]{:S(2)}, u32[]{:S(2)}) collective-permute-start(bf16[128,4096]{1,0:T(8,128)(2,1)} %pad_maximum_fusion), channel_id=1, source_target_pairs={{0,16},{16,32},{32,48},{48,64},{64,80},{80,96},{96,112},{112,128},... | collective-permute-start | bytes 3145736 | tf_op jit(solution)/shard_map/weights/ppermute | solution.py:16
  7.3 47.5 %collective-permute-start.15 = (bf16[64,4096]{1,0:T(8,128)(2,1)}, bf16[64,4096]{1,0:T(8,128)(2,1)}, u32[]{:S(2)}, u32[]{:S(2)}) collective-permute-start(bf16[64,4096]{1,0:T(8,128)(2,1)} %get-tuple-element.10), channel_id=1, source_target_pairs={{0,32},{16,48},{32,64},{48,80},{64,96},{80,112},{96,128},{112,144}... | collective-permute-start | bytes 1572872 | tf_op jit(solution)/shard_map/weights/ppermute | solution.py:16
  10.9 96.5 %collective-permute-start.17 = (f32[64,128]{1,0:T(8,128)}, f32[64,128]{1,0:T(8,128)}, u32[]{:S(2)}, u32[]{:S(2)}) collective-permute-start(f32[64,128]{1,0:T(8,128)} %get-tuple-element.19), channel_id=1, source_target_pairs={{0,16},{16,32},{32,48},{48,64},{64,80},{80,96},{96,112},{112,128},... | collective-permute-start | bytes 98312 | tf_op jit(solution)/shard_map/weights/ppermute | solution.py:16
  13.7 107.6 %collective-permute-start.19 = (f32[64,128]{1,0:T(8,128)}, f32[64,128]{1,0:T(8,128)}, u32[]{:S(2)}, u32[]{:S(2)}) collective-permute-start(f32[64,128]{1,0:T(8,128)} %get-tuple-element.18), channel_id=1, source_target_pairs={{0,32},{16,48},{32,64},{48,80},{64,96},{80,112},{96,128},{112,144}... | collective-permute-start | bytes 98312 | tf_op jit(solution)/shard_map/weights/ppermute | solution.py:16
  15.1 25.5 %collective-permute-start.1 = (bf16[64,5120]{1,0:T(8,128)(2,1)S(1)}, bf16[64,5120]{1,0:T(8,128)(2,1)S(1)}, u32[]{:S(2)}, u32[]{:S(2)}) collective-permute-start(bf16[64,5120]{1,0:T(8,128)(2,1)S(1)} %pad_maximum_fusion.7), channel_id=1, source_target_pairs={{0,240},{16,0},{32,16},{48,32},{64,48},{80,64},{96,80},{112,96},{1... | collective-permute-start | bytes 1966088 | tf_op jit(solution)/shard_map/weights/ppermute | solution.py:16
  26.0 75.8 %all-to-all-start = ((bf16[16,128,512]{2,1,0:T(8,128)(2,1)}), bf16[16,128,512]{2,1,0:T(8,128)(2,1)}, u32[]{:S(2)}, u32[]{:S(2)}) async-start(bf16[16,128,512]{2,1,0:T(8,128)(2,1)} %bitcast.107), calls=%async_computation | async-start | bytes 4194304 | tf_op jit(solution)/shard_map/columns/all_to_all | solution.py:222
  35.0 2.8 %copy-start.1 = (bf16[1,128,8192]{2,1,0:T(8,128)(2,1)S(1)}, bf16[1,128,8192]{2,1,0:T(8,128)(2,1)}, u32[]{:S(2)}) copy-start(bf16[1,128,8192]{2,1,0:T(8,128)(2,1)} %param.8) | copy-start | bytes 6291460
  40.6 24.8 %copy-start.5 = (bf16[128,8192]{1,0:T(8,128)(2,1)S(1)}, bf16[128,8192]{1,0:T(8,128)(2,1)}, u32[]{:S(2)}) copy-start(bf16[128,8192]{1,0:T(8,128)(2,1)} %fusion) | copy-start | bytes 6291460
  40.6 25.2 %copy-start.10 = (bf16[64,5120]{1,0:T(8,128)(2,1)}, bf16[64,5120]{1,0:T(8,128)(2,1)S(1)}, u32[]{:S(2)}) copy-start(bf16[64,5120]{1,0:T(8,128)(2,1)S(1)} %collective-permute-done.1) | copy-start | bytes 1966084
  40.6 24.7 %collective-permute-start.2 = (bf16[64,4096]{1,0:T(8,128)(2,1)S(1)}, bf16[64,4096]{1,0:T(8,128)(2,1)S(1)}, u32[]{:S(2)}, u32[]{:S(2)}) collective-permute-start(bf16[64,4096]{1,0:T(8,128)(2,1)S(1)} %slice.103), channel_id=1, source_target_pairs={{0,1},{1,0},{2,3},{3,2},{4,5},{5,4},{6,7},{7,6},{8,9},{9,8},{10,11... | collective-permute-start | bytes 1572872 | tf_op jit(solution)/shard_map/weights/ppermute | solution.py:21
  56.6 45.3 %collective-permute-start.16 = (bf16[192,4096]{1,0:T(8,128)(2,1)}, bf16[192,4096]{1,0:T(8,128)(2,1)}, u32[]{:S(2)}, u32[]{:S(2)}) collective-permute-start(bf16[192,4096]{1,0:T(8,128)(2,1)} %constant_dynamic-update-slice_fusion), channel_id=1, source_target_pairs={{0,1},{1,0},{2,3},{3,2},{4,5},{5,4},{6,7},{7,6},{8,9},{9,8},{10,11... | collective-permute-start | bytes 4718600 | tf_op jit(solution)/shard_map/weights/ppermute | solution.py:21
  65.8 31.2 %copy-start.2 = (bf16[2,1,64,8192]{3,2,1,0:T(8,128)(2,1)S(1)}, bf16[2,1,64,8192]{3,2,1,0:T(8,128)(2,1)}, u32[]{:S(2)}) copy-start(bf16[2,1,64,8192]{3,2,1,0:T(8,128)(2,1)} %param.10) | copy-start | bytes 6291460
  66.2 32.4 %copy-start.3 = (bf16[1,128,8192]{2,1,0:T(8,128)(2,1)S(1)}, bf16[1,128,8192]{2,1,0:T(8,128)(2,1)}, u32[]{:S(2)}) copy-start(bf16[1,128,8192]{2,1,0:T(8,128)(2,1)} %param.9) | copy-start | bytes 6291460
  66.4 7.9 %collective-permute-start.3 = (bf16[128,256]{1,0:T(8,128)(2,1)S(1)}, bf16[128,256]{1,0:T(8,128)(2,1)S(1)}, u32[]{:S(2)}, u32[]{:S(2)}) collective-permute-start(bf16[128,256]{1,0:T(8,128)(2,1)S(1)} %pad_maximum_fusion.8), channel_id=1, source_target_pairs={{0,2},{1,3},{2,4},{3,5},{4,6},{5,7},{6,8},{7,9},{8,10},{9,11},{10,... | collective-permute-start | bytes 196616 | tf_op jit(solution)/shard_map/gates/ppermute | solution.py:16
  70.9 5.6 %collective-permute-start.4 = (bf16[128,256]{1,0:T(8,128)(2,1)S(1)}, bf16[128,256]{1,0:T(8,128)(2,1)S(1)}, u32[]{:S(2)}, u32[]{:S(2)}) collective-permute-start(bf16[128,256]{1,0:T(8,128)(2,1)S(1)} %pad_maximum_fusion.8), channel_id=1, source_target_pairs={{0,4},{1,5},{2,6},{3,7},{4,8},{5,9},{6,10},{7,11},{8,12},{9,13},{1... | collective-permute-start | bytes 196616 | tf_op jit(solution)/shard_map/gates/ppermute | solution.py:16
  74.4 7.0 %collective-permute-start.5 = (bf16[128,256]{1,0:T(8,128)(2,1)S(1)}, bf16[128,256]{1,0:T(8,128)(2,1)S(1)}, u32[]{:S(2)}, u32[]{:S(2)}) collective-permute-start(bf16[128,256]{1,0:T(8,128)(2,1)S(1)} %pad_maximum_fusion.8), channel_id=1, source_target_pairs={{0,6},{1,7},{2,8},{3,9},{4,10},{5,11},{6,12},{7,13},{8,14},{9,15},... | collective-permute-start | bytes 196616 | tf_op jit(solution)/shard_map/gates/ppermute | solution.py:16
  76.5 7.6 %collective-permute-start.6 = (bf16[128,256]{1,0:T(8,128)(2,1)S(1)}, bf16[128,256]{1,0:T(8,128)(2,1)S(1)}, u32[]{:S(2)}, u32[]{:S(2)}) collective-permute-start(bf16[128,256]{1,0:T(8,128)(2,1)S(1)} %pad_maximum_fusion.8), channel_id=1, source_target_pairs={{0,8},{1,9},{2,10},{3,11},{4,12},{5,13},{6,14},{7,15},{8,0},{9,1},... | collective-permute-start | bytes 196616 | tf_op jit(solution)/shard_map/gates/ppermute | solution.py:16
  81.4 5.5 %collective-permute-start.7 = (bf16[128,256]{1,0:T(8,128)(2,1)S(1)}, bf16[128,256]{1,0:T(8,128)(2,1)S(1)}, u32[]{:S(2)}, u32[]{:S(2)}) collective-permute-start(bf16[128,256]{1,0:T(8,128)(2,1)S(1)} %pad_maximum_fusion.8), channel_id=1, source_target_pairs={{0,10},{1,11},{2,12},{3,13},{4,14},{5,15},{6,0},{7,1},{8,2},{9,3},... | collective-permute-start | bytes 196616 | tf_op jit(solution)/shard_map/gates/ppermute | solution.py:16
  84.0 7.8 %collective-permute-start.8 = (bf16[128,256]{1,0:T(8,128)(2,1)S(1)}, bf16[128,256]{1,0:T(8,128)(2,1)S(1)}, u32[]{:S(2)}, u32[]{:S(2)}) collective-permute-start(bf16[128,256]{1,0:T(8,128)(2,1)S(1)} %pad_maximum_fusion.8), channel_id=1, source_target_pairs={{0,12},{1,13},{2,14},{3,15},{4,0},{5,1},{6,2},{7,3},{8,4},{9,5},{1... | collective-permute-start | bytes 196616 | tf_op jit(solution)/shard_map/gates/ppermute | solution.py:16
  86.9 6.3 %collective-permute-start.9 = (bf16[128,256]{1,0:T(8,128)(2,1)S(1)}, bf16[128,256]{1,0:T(8,128)(2,1)S(1)}, u32[]{:S(2)}, u32[]{:S(2)}) collective-permute-start(bf16[128,256]{1,0:T(8,128)(2,1)S(1)} %pad_maximum_fusion.8), channel_id=1, source_target_pairs={{0,14},{1,15},{2,0},{3,1},{4,2},{5,3},{6,4},{7,5},{8,6},{9,7},{10,... | collective-permute-start | bytes 196616 | tf_op jit(solution)/shard_map/gates/ppermute | solution.py:16
  93.2 7.9 %copy-start.6 = (bf16[8,128,256]{2,1,0:T(8,128)(2,1)}, bf16[8,128,256]{2,1,0:T(8,128)(2,1)S(1)}, u32[]{:S(2)}) copy-start(bf16[8,128,256]{2,1,0:T(8,128)(2,1)S(1)} %bitcast_dynamic-update-slice_fusion.mine) | copy-start | bytes 1572868
  93.2 7.9 %collective-permute-start.10 = (bf16[8,128,256]{2,1,0:T(8,128)(2,1)S(1)}, bf16[8,128,256]{2,1,0:T(8,128)(2,1)S(1)}, u32[]{:S(2)}, u32[]{:S(2)}) collective-permute-start(bf16[8,128,256]{2,1,0:T(8,128)(2,1)S(1)} %bitcast_dynamic-update-slice_fusion.mine), channel_id=1, source_target_pairs={{0,1},{1,0},{2,3},{3,2},{4,5},{5,4},{6,7},{7,6},{8,9},{9,8},{10,11... | collective-permute-start | bytes 1572872 | tf_op jit(solution)/shard_map/gates/ppermute | solution.py:21
  101.1 2.9 %copy-start.8 = (bf16[8,128,256]{2,1,0:T(8,128)(2,1)}, bf16[8,128,256]{2,1,0:T(8,128)(2,1)S(1)}, u32[]{:S(2)}) copy-start(bf16[8,128,256]{2,1,0:T(8,128)(2,1)S(1)} %collective-permute-done.10.sibs) | copy-start | bytes 1572868
  101.8 7.1 %collective-permute-start = (bf16[16,128,512]{2,1,0:T(8,128)(2,1)}, bf16[16,128,512]{2,1,0:T(8,128)(2,1)}, u32[]{:S(2)}, u32[]{:S(2)}) collective-permute-start(bf16[16,128,512]{2,1,0:T(8,128)(2,1)} %all-to-all-done.own), channel_id=1, source_target_pairs={{0,1},{1,0},{2,3},{3,2},{4,5},{5,4},{6,7},{7,6},{8,9},{9,8},{10,11... | collective-permute-start | bytes 6291464 | tf_op jit(solution)/shard_map/columns/ppermute | solution.py:21
  104.1 1.2 copy-start.9
  104.2 1.8 %copy-start.4 = (bf16[1,128,8192]{2,1,0:T(8,128)(2,1)S(1)}, bf16[1,128,8192]{2,1,0:T(8,128)(2,1)}, u32[]{:S(2)}) copy-start(bf16[1,128,8192]{2,1,0:T(8,128)(2,1)} %param.9) | copy-start | bytes 6291460
  119.4 18.3 %collective-permute-start.11 = (bf16[256,1280]{1,0:T(8,128)(2,1)}, bf16[256,1280]{1,0:T(8,128)(2,1)S(1)}, u32[]{:S(2)}, u32[]{:S(2)}) collective-permute-start(bf16[256,1280]{1,0:T(8,128)(2,1)} %factor.4), channel_id=1, source_target_pairs={{0,16},{16,32},{32,48},{48,64},{64,80},{80,96},{96,112},{112,128},... | collective-permute-start | bytes 1966088 | tf_op jit(solution)/shard_map/factor/ppermute | solution.py:16
  139.1 29.0 %copy-start.13 = (f32[2,1,64,64]{3,2,1,0:T(8,128)S(1)}, f32[2,1,64,64]{3,2,1,0:T(8,128)}, u32[]{:S(2)}) copy-start(f32[2,1,64,64]{3,2,1,0:T(8,128)} %param.15) | copy-start | bytes 98308
  139.1 17.8 %collective-permute-start.12 = (bf16[256,1280]{1,0:T(8,128)(2,1)S(1)}, bf16[256,1280]{1,0:T(8,128)(2,1)S(1)}, u32[]{:S(2)}, u32[]{:S(2)}) collective-permute-start(bf16[256,1280]{1,0:T(8,128)(2,1)S(1)} %add_convert_fusion), channel_id=1, source_target_pairs={{0,16},{16,32},{32,48},{48,64},{64,80},{80,96},{96,112},{112,128},... | collective-permute-start | bytes 1966088 | tf_op jit(solution)/shard_map/factor/ppermute | solution.py:16
  139.5 3.7 %collective-permute-start.20 = (f32[64,64]{1,0:T(8,128)S(1)}, f32[64,64]{1,0:T(8,128)S(1)}, u32[]{:S(2)}, u32[]{:S(2)}) collective-permute-start(f32[64,64]{1,0:T(8,128)S(1)} %fusion.69), channel_id=1, source_target_pairs={{0,224},{16,240},{32,0},{48,16},{64,32},{80,48},{96,64},{112,80},{... | collective-permute-start | bytes 49160 | tf_op jit(solution)/shard_map/backward/ppermute | solution.py:16
  141.8 4.4 %collective-permute-start.18 = (f32[64,64]{1,0:T(8,128)S(1)}, f32[64,64]{1,0:T(8,128)S(1)}, u32[]{:S(2)}, u32[]{:S(2)}) collective-permute-start(f32[64,64]{1,0:T(8,128)S(1)} %fusion.68), channel_id=1, source_target_pairs={{0,240},{16,0},{32,16},{48,32},{64,48},{80,64},{96,80},{112,96},{1... | collective-permute-start | bytes 49160 | tf_op jit(solution)/shard_map/backward/ppermute | solution.py:16
  147.3 20.7 %all-to-all-start.1 = ((f32[16,64,128]{2,1,0:T(8,128)}), f32[16,64,128]{2,1,0:T(8,128)S(1)}, u32[]{:S(2)}, u32[]{:S(2)}) async-start(f32[16,64,128]{2,1,0:T(8,128)} %broadcast_in_dim.34), calls=%async_computation.1 | async-start | bytes 1048576 | tf_op jit(solution)/shard_map/backward/all_to_all | solution.py:26
  156.9 11.9 %copy-start.7 = (bf16[256,1280]{1,0:T(8,128)(2,1)}, bf16[256,1280]{1,0:T(8,128)(2,1)S(1)}, u32[]{:S(2)}) copy-start(bf16[256,1280]{1,0:T(8,128)(2,1)S(1)} %collective-permute-done.12.came) | copy-start | bytes 1966084
  158.3 10.5 %collective-permute-start.13 = (f32[256,512]{1,0:T(8,128)S(1)}, f32[256,512]{1,0:T(8,128)S(1)}, u32[]{:S(2)}, u32[]{:S(2)}) collective-permute-start(f32[256,512]{1,0:T(8,128)S(1)} %convert_add_fusion), channel_id=1, source_target_pairs={{0,1},{1,0},{2,3},{3,2},{4,5},{5,4},{6,7},{7,6},{8,9},{9,8},{10,11... | collective-permute-start | bytes 1572872 | tf_op jit(solution)/shard_map/factor/ppermute | solution.py:21
  168.8 0.8 copy-start.11

commit v3 on v1

v3 whole, which is shorter than its diff:
```python
import functools

import jax
import jax.numpy as jnp
from jax import lax
from jax.experimental import pallas as pl
from jax.experimental.pallas import tpu as pltpu
from jax.sharding import PartitionSpec as P

F32 = jnp.float32
BF16 = jnp.bfloat16
ANY = pl.BlockSpec(memory_space=pl.ANY)


def shift(block, axis, distance):
    count = lax.axis_size(axis)
    return lax.ppermute(block, axis, [(i, (i + distance) % count) for i in range(count)])


def swap_cores(block):
    count = lax.axis_size("dp")
    return lax.ppermute(block, "dp", [(i, i ^ 1) for i in range(count)])


def nt(a, b):
    return lax.dot_general(a, b, (((1,), (1,)), ((), ())), preferred_element_type=F32)


def tn(a, b):
    return lax.dot_general(a, b, (((0,), (0,)), ((), ())), preferred_element_type=F32)


def call(kernel, where, operands, in_specs, outs, out_specs, grid, scratch, cost, aliases={}):
    spec = pltpu.PrefetchScalarGridSpec(
        num_scalar_prefetch=1,
        grid=grid,
        in_specs=in_specs,
        out_specs=out_specs,
        scratch_shapes=list(scratch),
    )
    flops, moved = cost
    return pl.pallas_call(
        kernel,
        grid_spec=spec,
        out_shape=outs,
        input_output_aliases=aliases,
        compiler_params=pltpu.CompilerParams(dimension_semantics=("arbitrary",) * len(grid)),
        cost_estimate=pl.CostEstimate(flops=flops, transcendentals=0, bytes_accessed=moved),
    )(where, *operands)


def tie_kernel(x, *rest):
    del x, rest


def tie(x, *after):
    hbm = pl.BlockSpec(memory_space=pltpu.HBM)
    return pl.pallas_call(
        tie_kernel,
        in_specs=[hbm] + [ANY] * len(after),
        out_specs=hbm,
        out_shape=jax.ShapeDtypeStruct(x.shape, x.dtype),
        input_output_aliases={0: 0},
        cost_estimate=pl.CostEstimate(flops=0, transcendentals=0, bytes_accessed=0),
    )(x, *after)


CHIP, CORE, SEC, C0, F1, B1, B2 = range(7)


def split_kernel(where, x, down, ids, out, gate, acc):
    i = pl.program_id(0)
    pieces, _, cols = out.shape
    tok, rank = gate.shape

    @pl.when(i == 0)
    def _():
        acc[...] = jnp.zeros_like(acc)

    acc[...] += nt(x[...], down[0, 0])
    row = ids[pl.ds(where[SEC], 1), :].astype(F32)
    row = jnp.broadcast_to(row, (out.shape[1] - tok, tok)).astype(BF16)
    for k in range(pieces):
        out[k, :tok, :] = x[:, k * cols:(k + 1) * cols]
        out[k, tok:, :tok] = row
        out[k, tok:, tok:] = jnp.zeros((out.shape[1] - tok, cols - tok), BF16)

    @pl.when(i == pl.num_programs(0) - 1)
    def _():
        z = acc[...]
        gate[...] = (z * jax.nn.sigmoid(z)).astype(BF16)


def split(where, x, adapter_down, doc_ids, pieces, extra):
    tok, width = x.shape
    rank = adapter_down.shape[2]
    cols = width // pieces
    grid = 4
    each = width // grid
    return call(
        split_kernel,
        where,
        (x, adapter_down, doc_ids),
        [
            pl.BlockSpec((tok, each), lambda i, w: (0, i)),
            pl.BlockSpec((1, 1, rank, each), lambda i, w: (w[C0], 0, 0, i)),
            pl.BlockSpec(doc_ids.shape, lambda i, w: (0, 0)),
        ],
        [
            jax.ShapeDtypeStruct((pieces, tok + extra, cols), BF16),
            jax.ShapeDtypeStruct((tok, rank), BF16),
        ],
        [
            pl.BlockSpec((pieces // grid, tok + extra, cols), lambda i, w: (i, 0, 0)),
            pl.BlockSpec((tok, rank), lambda i, w: (0, 0)),
        ],
        (grid,),
        [pltpu.VMEM((tok, rank), F32)],
        (2 * x.size * rank, 5 * x.size),
    )


def pack_kernel(where, up_f, down_f, up_b1, down_b1, up_b2, after, ahead, behind1, behind2):
    rank, cols = up_f.shape[2:]
    ahead[:, :cols] = up_f[0, 0]
    ahead[:, cols:] = down_f[0, 0]
    behind1[:rank] = up_b1[0, 0]
    behind1[rank:] = down_b1[0, 0]
    behind2[...] = up_b2[0, 0]


def pack(where, adapter_down, adapter_up, block, after):
    rank, width = adapter_down.shape[2:]
    half = width // 2
    part = lambda span: pl.BlockSpec(
        (1, 1, rank, half), lambda i, w: (w[span], 0, 0, w[CORE])
    )
    shapes = ((rank, block + half), (2 * rank, half), (rank, half))
    return call(
        pack_kernel,
        where,
        (adapter_up, adapter_down, adapter_up, adapter_down, adapter_up, after),
        [
            pl.BlockSpec((1, 1, rank, block), lambda i, w: (w[F1], 0, 0, w[CHIP])),
            part(F1),
            part(B1),
            part(B1),
            part(B2),
            ANY,
        ],
        [jax.ShapeDtypeStruct(shape, BF16) for shape in shapes],
        [pl.BlockSpec(shape, lambda i, w: (0, 0)) for shape in shapes],
        (1,),
        (),
        (0, 10 * rank * half * 2),
    )


def gate_kernel(where, xm, xs, um, us, dm, ds, gate0, after1, after2, sent, acc):
    i = pl.program_id(0)
    rank = gate0.shape[1]

    @pl.when(i == 0)
    def _():
        acc[...] = jnp.zeros_like(acc)

    for x, u, d in ((xm, um, dm), (xs, us, ds)):
        add = jnp.dot(gate0[...], u[0, 0], preferred_element_type=F32)
        acc[...] += nt((x[...].astype(F32) + add).astype(BF16), d[...])

    @pl.when(i == pl.num_programs(0) - 1)
    def _():
        z = acc[...]
        gate1 = (z * jax.nn.sigmoid(z)).astype(BF16)
        both = jnp.concatenate([gate0[...], gate1], axis=1)
        for k in range(sent.shape[0]):
            sent[k] = both


def gates(where, x, adapter_up, ahead_mine, ahead_sib, gate0, replicas, *after):
    tok, width = x.shape
    rank = gate0.shape[1]
    each = ahead_mine.shape[1] - width // 2
    grid = width // 2 // each
    x_spec = lambda side: pl.BlockSpec((tok, each), lambda i, w: (0, side(w) * grid + i))
    u_spec = lambda side: pl.BlockSpec(
        (1, 1, rank, each), lambda i, w: (w[C0], 0, 0, side(w) * grid + i)
    )
    mine, sib = (lambda w: w[CORE]), (lambda w: 1 - w[CORE])
    d_spec = pl.BlockSpec((rank, each), lambda i, w: (0, i + 1))
    shape = (replicas, tok, 2 * rank)
    return call(
        gate_kernel,
        where,
        (x, x, adapter_up, adapter_up, ahead_mine, ahead_sib, gate0, *after),
        [
            x_spec(mine),
            x_spec(sib),
            u_spec(mine),
            u_spec(sib),
            d_spec,
            d_spec,
            pl.BlockSpec((tok, rank), lambda i, w: (0, 0)),
            ANY,
            ANY,
        ],
        jax.ShapeDtypeStruct(shape, BF16),
        pl.BlockSpec(shape, lambda i, w: (0, 0, 0)),
        (grid,),
        [pltpu.VMEM((tok, rank), F32)],
        (4 * x.size * rank, 5 * x.size),
    )


def gram_kernel(step, where, own, other, ids, *rest):
    ups, (out, acc) = rest[:-2], rest[-2:]
    core = where[CORE]
    pieces, _, rows = own.shape
    tok = ids.shape[2]
    hlf = rows // 2
    i = pl.program_id(0)

    @pl.when(i == 0)
    def _():
        acc[...] = jnp.zeros_like(acc)

    same = lax.broadcasted_iota(jnp.int32, (tok, tok), 0) == lax.broadcasted_iota(
        jnp.int32, (tok, tok), 1
    )
    everyone = ids[:, 0, :].astype(F32)
    scales = []
    for k in range(pieces):
        mine = own[k, tok:tok + 1, :tok].astype(F32)
        column = jnp.sum(jnp.where(same, mine, 0.0), axis=1, keepdims=True)
        hits = jnp.zeros((tok, tok), F32)
        for m in range(everyone.shape[0]):
            hits += (column == everyone[m:m + 1, :]).astype(F32)
        scales.append(jnp.sqrt(jnp.sqrt(tok / jnp.sum(hits, axis=1, keepdims=True))))
    scale = jnp.concatenate(scales, axis=0)

    def rebuilt(ref, up):
        act = jnp.concatenate([ref[k, :tok, :] for k in range(pieces)], axis=0).astype(F32)
        if step:
            add = jnp.dot(gate, up, preferred_element_type=F32)
            act = (act + add).astype(BF16).astype(F32)
        return (scale * act).astype(BF16)

    if step == 0:
        up_own = up_oth = None
    else:
        got = ups[0]
        gate = jnp.concatenate([got[k] for k in range(pieces)], axis=0)
        if step == 1:
            gate = gate[:, :gate.shape[1] // 2]
            up_own, up_oth = ups[1][0, 0], ups[2][0, 0]
        else:
            up_own = jnp.concatenate([ups[1][0, 0], ups[3][...]], axis=0)
            up_oth = jnp.concatenate([ups[2][0, 0], ups[4][...]], axis=0)
    r = rebuilt(own, up_own)
    q = rebuilt(other, up_oth)
    acc[:, :rows] += tn(r[:, :hlf], r)
    acc[:, rows:rows + hlf] += tn(r[:, hlf:], r[:, hlf:])

    @pl.when(core == 0)
    def _():
        acc[:, rows + hlf:] += tn(r[:, :hlf], q)

    @pl.when(core == 1)
    def _():
        acc[:, rows + hlf:] += tn(q[:, hlf:], r)

    @pl.when(i == pl.num_programs(0) - 1)
    def _():
        out[...] = acc[...].astype(out.dtype)


def gram(step, dtype, where, own, other, got=None, adapter_up=None, up1=None, after=None):
    replicas, long, rows = own.shape
    tok = long - 8
    grid = 4
    pieces = replicas // grid
    packed = (rows // 2, rows * 5 // 2)
    cols = pl.BlockSpec((pieces, long, rows), lambda i, w: (i, 0, 0))
    operands = [own, other, own]
    specs = [cols, cols, pl.BlockSpec((replicas, 8, tok), lambda i, w: (0, tok // 8, 0))]
    if step:
        rank = adapter_up.shape[2]
        up = lambda side: pl.BlockSpec(
            (1, 1, rank, rows), lambda i, w: (w[C0], 0, 0, 2 * w[CHIP] + side(w))
        )
        mine, sib = (lambda w: w[CORE]), (lambda w: 1 - w[CORE])
        operands += [got, adapter_up, adapter_up]
        specs += [pl.BlockSpec((pieces, tok, 2 * rank), lambda i, w: (i, 0, 0)), up(mine), up(sib)]
    if step == 2:
        one = lambda side: pl.BlockSpec((rank, rows), lambda i, w: (0, side(w)))
        operands += [up1, up1]
        specs += [one(mine), one(sib)]
    if after is not None:
        operands.append(after)
        specs.append(ANY)
    return call(
        functools.partial(gram_kernel, step),
        where,
        operands,
        specs,
        jax.ShapeDtypeStruct(packed, dtype),
        pl.BlockSpec(packed, lambda i, w: (0, 0)),
        (grid,),
        [pltpu.VMEM(packed, F32)],
        (2 * replicas * tok * packed[0] * packed[1], 4 * own.size),
    )


def back_kernel(where, gm, gs, um, us, dm, ds, b1m, b1s, b2m, b2s, q0, q1, q2, after, *rest):
    outs, (proj, m0, m12) = rest[:3], rest[3:]
    i = pl.program_id(0)
    rank = b2m.shape[0]

    @pl.when(i == 0)
    def _():
        for acc in (proj, m0, m12):
            acc[...] = jnp.zeros_like(acc)

    for g, u, d, b1, b2 in ((gm, um, dm, b1m, b2m), (gs, us, ds, b1s, b2s)):
        two = jnp.concatenate([b1[:rank], b2[...]], axis=0)
        proj[:rank] += nt(u[0, 0], g[...])
        proj[rank:] += nt(two, g[...])
        m0[...] += nt(two, d[0, 0])
        m12[...] += nt(b2[...], b1[rank:])

    def dz_of(grad_act, q):
        sigma = jax.nn.sigmoid(q)
        return (grad_act * sigma * (1.0 + q * (1.0 - sigma))).astype(BF16)

    def exact(m, d):
        return jnp.dot(
            m, d.astype(F32), precision=lax.Precision.HIGHEST, preferred_element_type=F32
        )

    @pl.when(i == pl.num_programs(0) - 1)
    def _():
        dz0 = dz_of(proj[:rank], q0[0, 0])
        dz1 = dz_of(proj[rank:2 * rank] + exact(m0[:rank], dz0), q1[...])
        dz2 = dz_of(proj[2 * rank:] + exact(m0[rank:], dz0) + exact(m12[...], dz1), q2[...])
        for out, dz in zip(outs, (dz0, dz1, dz2)):
            out[...] = nt(dz, dz)


def back(where, grad, adapter_down, adapter_up, b1, b1s, b2, b2s, stashed, q1, q2, after):
    tok, width = grad.shape
    rank = adapter_up.shape[2]
    grid = 4
    each = width // 2 // grid
    mine, sib = (lambda w: w[CORE]), (lambda w: 1 - w[CORE])
    g_spec = lambda side: pl.BlockSpec((tok, each), lambda i, w: (0, side(w) * grid + i))
    a_spec = lambda side: pl.BlockSpec(
        (1, 1, rank, each), lambda i, w: (1, 0, 0, side(w) * grid + i)
    )
    got = lambda x: pl.BlockSpec((x.shape[0], each), lambda i, w: (0, i))
    q_spec = pl.BlockSpec((rank, tok), lambda i, w: (0, 0))
    return call(
        back_kernel,
        where,
        (
            grad, grad, adapter_up, adapter_up, adapter_down, adapter_down,
            b1, b1s, b2, b2s, stashed, q1, q2, after,
        ),
        [
            g_spec(mine), g_spec(sib), a_spec(mine), a_spec(sib), a_spec(mine), a_spec(sib),
            got(b1), got(b1s), got(b2), got(b2s),
            pl.BlockSpec((1, 1, rank, tok), lambda i, w: (0, 0, 0, 0)), q_spec, q_spec, ANY,
        ],
        [jax.ShapeDtypeStruct((rank, rank), F32)] * 3,
        [pl.BlockSpec((rank, rank), lambda i, w: (0, 0))] * 3,
        (grid,),
        [
            pltpu.VMEM((3 * rank, tok), F32),
            pltpu.VMEM((2 * rank, rank), F32),
            pltpu.VMEM((rank, rank), F32),
        ],
        (12 * grad.size * rank, 8 * grad.size),
    )


def merge_kernel(a, b, after, out):
    out[...] = (a[...] + b[...].astype(F32)).astype(BF16)


def merge(a, b, after):
    grid = 2
    part = pl.BlockSpec((a.shape[0] // grid, a.shape[1]), lambda i: (i, 0))
    return pl.pallas_call(
        merge_kernel,
        grid=(grid,),
        in_specs=[part, part, ANY],
        out_specs=part,
        out_shape=jax.ShapeDtypeStruct(a.shape, BF16),
        compiler_params=pltpu.CompilerParams(dimension_semantics=("arbitrary",)),
        cost_estimate=pl.CostEstimate(flops=a.size, transcendentals=0, bytes_accessed=8 * a.size),
    )(a, b, after)


def square_kernel(factor_scale, where, old, here, came, out):
    i = pl.program_id(0)
    hlf = out.shape[0]
    rows = 2 * hlf

    def put(lo, hi, val):
        out[:, lo:hi] = 0.75 * old[:, lo:hi] + factor_scale * val

    def packed(lo, hi):
        return here[:, lo:hi] + came[:, lo:hi].astype(F32)

    @pl.when(i == 0)
    def _():
        put(0, rows, packed(0, rows))

    @pl.when(i == 1)
    def _():
        put(0, hlf, packed(hlf, rows).T)
        put(hlf, rows, packed(rows, rows + hlf))


def cross_kernel(factor_scale, where, old, mine, sib, done, out):
    i = pl.program_id(0)
    core = where[CORE]
    hlf = out.shape[0]

    def put(lo, hi, val):
        out[:, lo:hi] = 0.75 * old[:, lo:hi] + factor_scale * val

    for k, part in enumerate((mine, sib)):
        @pl.when(jnp.logical_and(core == 0, i == k))
        def _():
            put(0, 2 * hlf, part[...])

    for k in range(2):
        a, b = k * hlf, (k + 1) * hlf

        @pl.when(jnp.logical_and(core == 1, i == k))
        def _():
            put(0, hlf, sib[:, a:b].T)
            put(hlf, 2 * hlf, mine[:, a:b].T)


def update(factor_scale, where, old, here, came, mine, sib):
    total, block = old.shape
    hlf = total // 2
    whole = lambda x: pl.BlockSpec(x.shape, lambda i, w: (0, 0))
    own = pl.BlockSpec((hlf, total), lambda i, w: (i, w[CORE]))
    oth = pl.BlockSpec((hlf, total), lambda i, w: (i, 1 - w[CORE]))
    shape = jax.ShapeDtypeStruct(old.shape, F32)
    cost = (2 * old.size, 6 * old.size)
    done = call(
        functools.partial(square_kernel, factor_scale), where, (old, here, came),
        [own, whole(here), whole(came)], shape, own, (2,), (), cost,
    )
    return call(
        functools.partial(cross_kernel, factor_scale), where, (old, mine, sib, done),
        [oth, whole(mine), whole(sib), ANY], shape, oth, (2,), (), cost, {4: 0},
    )


def shards(
    entering, returning, adapter_down, adapter_up, stashed, doc_ids, input_factor, output_factor
):
    sec = lax.axis_index("section")
    rep = lax.axis_index("dp")
    sections = lax.axis_size("section")
    replicas = lax.axis_size("dp")
    tok = entering.shape[1]
    steps_count = stashed.shape[1]
    rank = stashed.shape[2]
    rows, block = input_factor.shape[1:]
    tokens = tok * replicas

    def first(home):
        return (home < sections // 2).astype(jnp.int32)

    x0 = entering[0]
    f1 = first((sec + sections - 1) % sections) + (sec == 0).astype(jnp.int32)
    b1 = (sec + 1 < sections).astype(jnp.int32)
    b2 = (sec + 2 < sections).astype(jnp.int32)
    where = jnp.stack([rep // 2, rep % 2, sec, first(sec), f1, b1, b2]).astype(jnp.int32)

    with jax.named_scope("weights"):
        pieces, gate0 = split(where, x0, adapter_down, doc_ids, replicas, 8)
        ahead, behind1, behind2 = pack(where, adapter_down, adapter_up, block, gate0)
        ahead = shift(ahead, "section", -1)
        ahead_sib = swap_cores(ahead)
        behind1 = shift(behind1, "section", 1)
        behind2 = shift(behind2, "section", 2)
        stash1 = shift(stashed[0, 1], "section", 1)
        stash2 = shift(stashed[0, 2], "section", 2)
        behind1_sib = swap_cores(behind1)
        behind2_sib = swap_cores(behind2)

    with jax.named_scope("gates"):
        sent = gates(where, x0, adapter_up, ahead, ahead_sib, gate0, replicas, stash1, stash2)

    with jax.named_scope("columns"):
        own = tie(lax.all_to_all(pieces, "dp", 0, 0), sent)
        other = swap_cores(own)
        got = lax.all_to_all(sent, "dp", 0, 0)

    with jax.named_scope("factor"):
        step0 = gram(0, F32, where, own, other)
        step2 = gram(2, BF16, where, own, other, got, adapter_up, ahead, step0)
        from2 = shift(step2, "section", 1)
        step1 = gram(1, F32, where, own, other, got, adapter_up, None, step2)

    with jax.named_scope("backward"):
        outer0, outer1, outer2 = back(
            where, returning[0], adapter_down, adapter_up, behind1, behind1_sib, behind2,
            behind2_sib, stashed, stash1, stash2, step1,
        )

    with jax.named_scope("factor"):
        from1 = shift(merge(step1, from2, outer0), "section", 1)
        cut = rows + rows // 2
        mine = step0[:, cut:] + from1[:, cut:].astype(F32)
        sib = swap_cores(mine)
        factor_scale = 0.25 / (steps_count * tokens)
        input_factor_new = update(
            factor_scale, where, input_factor[0], step0, from1, mine, sib
        )[None]

    with jax.named_scope("backward"):
        outer1 = shift(outer1, "section", -1)
        outer2 = shift(outer2, "section", -2)
        g1 = b1.astype(F32)
        g2 = b2.astype(F32)
        curv = jnp.concatenate(
            [
                outer1 * (1.0 - g1) + outer2 * (1.0 - g2),
                outer0 + outer1 * g1 + outer2 * g2,
            ],
            axis=1,
        )
        curv_all = lax.all_to_all(
            jnp.broadcast_to(curv[None], (replicas,) + curv.shape), "dp", 0, 0
        )
        curv_total = jnp.sum(curv_all, axis=0)
        curv_total = jnp.stack([curv_total[:, :rank], curv_total[:, rank:]])
        step_totals = jnp.stack([2.0 - g1 - g2, 1.0 + g1 + g2])
        divisor = (jnp.maximum(step_totals, 1.0) * tokens)[:, None, None]
        updated = 0.75 * output_factor[:, 0] + 0.25 * curv_total / divisor
        output_factor_new = jnp.where(
            (step_totals > 0.0)[:, None, None], updated, output_factor[:, 0]
        )[:, None]
    return (input_factor_new, output_factor_new)


def solution(mesh):
    in_specs = (
        P("section", "dp", None),
        P("section", "dp", None),
        P(None, "section", None, None),
        P(None, "section", None, None),
        P("section", None, None, "dp"),
        P(None, "dp"),
        P("section", "dp", None),
        P(None, "section", None, None),
    )
    out_specs = (P("section", "dp", None), P(None, "section", None, None))
    return jax.shard_map(shards, mesh=mesh, in_specs=in_specs, out_specs=out_specs, check_vma=False)
```

time: 203 us -> 198 us (0.975)
  Pallas kernels: 0 us -> 61.1 us
  matrix products: 37.6 us -> 0 us
  local copies, waits for them, and re-layouts: 20.6 us -> 10.4 us
  starting transfers between devices: 47.3 us -> 37.8 us
  other arithmetic: 8.3 us -> 2.34 us
  waiting for transfers between devices: 87.5 us -> 84.5 us
    pallas_call x0 -> x11, Pallas kernels: none -> 61.1 us  [the longest x9 58.8 us: call(): pl.pallas_call(kernel, grid_spec=spec, out_shape=outs, input_output_alias...]
    dot_general x22 -> x0, matrix products: 37.6 us -> none  [the longest x3 14.1 us: gram(): lax.dot_general(mine_cols, scaled, (((0,), (0,)), ((), ())), preferred_el...]
    all_to_all x4 -> x3, waiting for transfers between devices: 37.3 us -> 5.86 us  [the longest x1 5.85 us: shards(): lax.all_to_all(jnp.broadcast_to(curv[None], (replicas,) + curv.shape), 'd...]
    ppermute x9, waiting for transfers between devices: 49 us -> 78.6 us  [shift(): lax.ppermute(block, axis, [(i, (i + distance) % count) for i in range(cou...]
    all_to_all x4 -> x3, starting transfers between devices: 29.4 us -> 21.1 us  [the longest x1 8.45 us: shards(): own = tie(lax.all_to_all(pieces, 'dp', 0, 0), sent)]
    ppermute x9, starting transfers between devices: 16.1 us -> 10.4 us  [shift(): lax.ppermute(block, axis, [(i, (i + distance) % count) for i in range(cou...]
    ppermute x3 -> x5, starting transfers between devices: 1.8 us -> 6.34 us  [swap_cores(): return lax.ppermute(block, 'dp', [(i, i ^ 1) for i in range(count)])]
    select_n x2 -> x0, other arithmetic: 3.96 us -> none  [the longest x1 2.09 us: shards(): back_lo = jnp.where(core == 0, mine, sib)]
  transfers between devices with their start and end apart: 16 -> 17, of which waited for: 8 -> 7; matrix products, arithmetic and copies ran while one was open for 23% -> 2% of each run, Pallas kernels for 0% -> 26%
where the time goes in v3:
time: 198 us; the launch traced here: 197 us
  waiting for transfers between devices  84.5 us (43%)
  Pallas kernels  61.1 us (31%)
  starting transfers between devices  37.8 us (19%)
  local copies, waits for them, and re-layouts  10.4 us (5%)
  other arithmetic  2.34 us (1%)
    ppermute x9, waiting for transfers between devices, shift(): lax.ppermute(block, axis, [(i, (i + distance) % count) for i in range(cou...  78.6 us
    pallas_call x9, Pallas kernels, call(): pl.pallas_call(kernel, grid_spec=spec, out_shape=outs, input_output_alias...  58.8 us
    ppermute x9, starting transfers between devices, shift(): lax.ppermute(block, axis, [(i, (i + distance) % count) for i in range(cou...  10.4 us
    all_to_all x1, starting transfers between devices, shards(): own = tie(lax.all_to_all(pieces, 'dp', 0, 0), sent)  8.45 us
    unnamed x34, local copies, waits for them, and re-layouts  8.11 us
    all_to_all x1, starting transfers between devices, shards(): lax.all_to_all(jnp.broadcast_to(curv[None], (replicas,) + curv.shape), 'd...  7.32 us
    ppermute x5, starting transfers between devices, swap_cores(): return lax.ppermute(block, 'dp', [(i, i ^ 1) for i in range(count)])  6.34 us
    all_to_all x1, waiting for transfers between devices, shards(): lax.all_to_all(jnp.broadcast_to(curv[None], (replicas,) + curv.shape), 'd...  5.85 us
  transfers between devices with their start and end apart: 17, of which 7 were waited for; matrix products, arithmetic and copies ran while one was open for 2% of the time, Pallas kernels for 26%

profile of v3, /device:TPU:1, one launch (start us, length us, event | category | flops | bytes accessed | tf_op | source)
XLA Modules:
  0.0 197.0 jit_solution(1545921261242395303)
XLA Ops:
  0.7 0.6 stack.53.where
  1.2 5.2 %weights.2 = (bf16[16,136,512]{2,1,0:T(8,128)(2,1)}, bf16[128,64]{1,0:T(8,128)(2,1)}) custom-call(s32[7]{0:T(128)} %stack.53.where, bf16[128,8192]{1,0:T(8,128)(2,1)} %bitcast.21, bf16[2,1,64,8192]{3,2,1,0:T(8,128)(2,1)} %ds.1, s32[16,128]{1,0:T(8,128)} %ids.1), custom_call_target="tpu_custom_call" | custom-call | flops 134217728 | bytes 5242880 | tf_op jit(solution)/shard_map/weights/pallas_call | solution.py:42
  6.4 8.5 %all-to-all-start = ((bf16[16,136,512]{2,1,0:T(8,128)(2,1)}), bf16[16,136,512]{2,1,0:T(8,128)(2,1)S(1)}, u32[]{:S(2)}, u32[]{:S(2)}) async-start(bf16[16,136,512]{2,1,0:T(8,128)(2,1)} %get-tuple-element.10), calls=%async_computation | async-start | bytes 4456448 | tf_op jit(solution)/shard_map/columns/all_to_all | solution.py:502
  14.9 3.6 %weights.3 = (bf16[64,5120]{1,0:T(8,128)(2,1)}, bf16[128,4096]{1,0:T(8,128)(2,1)}, bf16[64,4096]{1,0:T(8,128)(2,1)}) custom-call(s32[7]{0:T(128)} %stack.53.where, bf16[2,1,64,8192]{3,2,1,0:T(8,128)(2,1)} %us.3, bf16[2,1,64,8192]{3,2,1,0:T(8,128)(2,1)} %ds.1, bf16[2,1,64,8192]{3,2,1,0:T(8,128)(2,1)} %us.3, bf16[2,1,64,8192]{3,2,1,0:T(8,128)(2,1)} %ds.1, ...), custom_call_target="tpu_custom_call" | custom-call | bytes 5242880 | tf_op jit(solution)/shard_map/weights/pallas_call | solution.py:42
  18.5 5.7 %collective-permute-start = (bf16[64,5120]{1,0:T(8,128)(2,1)}, bf16[64,5120]{1,0:T(8,128)(2,1)S(1)}, u32[]{:S(2)}, u32[]{:S(2)}) collective-permute-start(bf16[64,5120]{1,0:T(8,128)(2,1)} %get-tuple-element.12), channel_id=1, source_target_pairs={{0,240},{16,0},{32,16},{48,32},{64,48},{80,64},{96,80},{112,96},{1... | collective-permute-start | bytes 1966088 | tf_op jit(solution)/shard_map/weights/ppermute | solution.py:17
  24.2 25.9 %collective-permute-done.dm.rest_3_.rest_4_ = bf16[64,5120]{1,0:T(8,128)(2,1)S(1)} collective-permute-done((bf16[64,5120]{1,0:T(8,128)(2,1)}, bf16[64,5120]{1,0:T(8,128)(2,1)S(1)}, u32[]{:S(2)}, u32[]{:S(2)}) %collective-permute-start) | collective-permute-done | bytes 655392 | tf_op jit(solution)/shard_map/weights/ppermute | solution.py:17
  50.2 1.4 collective-permute-start.1
  51.6 0.8 slice_bitcast_fusion.2
  52.3 0.1 collective-permute-start.3
  52.4 9.6 %collective-permute-done.2.after1.q1 = f32[64,128]{1,0:T(8,128)S(1)} collective-permute-done((f32[64,128]{1,0:T(8,128)S(1)}, f32[64,128]{1,0:T(8,128)S(1)}, u32[]{:S(2)}, u32[]{:S(2)}) %collective-permute-start.2) | collective-permute-done | bytes 32800 | tf_op jit(solution)/shard_map/weights/ppermute | solution.py:17
  62.0 0.6 copy-done.12
  62.6 0.8 collective-permute-done.3.after2.q2
  63.4 0.6 copy-done.13
  64.0 0.8 copy-done.7
  64.8 5.9 %gates.1.rest_0_ = bf16[16,128,128]{2,1,0:T(8,128)(2,1)} custom-call(s32[7]{0:T(128)} %stack.53.where, bf16[128,8192]{1,0:T(8,128)(2,1)} %bitcast.22, bf16[128,8192]{1,0:T(8,128)(2,1)} %bitcast.23, bf16[2,1,64,8192]{3,2,1,0:T(8,128)(2,1)} %us.3, bf16[2,1,64,8192]{3,2,1,0:T(8,128)(2,1)} %us.3, bf16[64,5120]{1,0:T(8,128)(2,1)} %copy-done.2, ...), custom_call_target="tpu_custom_call" | custom-call | flops 268435456 | bytes 5242880 | tf_op jit(solution)/shard_map/gates/pallas_call | solution.py:42
  70.7 1.4 copy-done
  72.1 1.8 collective-permute-start.4
  73.9 5.3 %all-to-all-start.1 = ((bf16[16,128,128]{2,1,0:T(8,128)(2,1)}), bf16[16,128,128]{2,1,0:T(8,128)(2,1)S(1)}, u32[]{:S(2)}, u32[]{:S(2)}) async-start(bf16[16,128,128]{2,1,0:T(8,128)(2,1)} %gates.1.rest_0_), calls=%async_computation.1 | async-start | bytes 1048576 | tf_op jit(solution)/shard_map/columns/all_to_all | solution.py:504
  79.2 37.4 %collective-permute-done.6.b1m = bf16[128,4096]{1,0:T(8,128)(2,1)} collective-permute-done((bf16[128,4096]{1,0:T(8,128)(2,1)}, bf16[128,4096]{1,0:T(8,128)(2,1)}, u32[]{:S(2)}, u32[]{:S(2)}) %collective-permute-start.6) | collective-permute-done | bytes 1048608 | tf_op jit(solution)/shard_map/weights/ppermute | solution.py:17
  116.6 1.2 collective-permute-start.7
  117.8 1.4 copy-done.1
  119.2 9.3 %factor.6.rest_5_.here = f32[256,1280]{1,0:T(8,128)} custom-call(s32[7]{0:T(128)} %stack.53.where, bf16[16,136,512]{2,1,0:T(8,128)(2,1)} %columns.1.own.ids, bf16[16,136,512]{2,1,0:T(8,128)(2,1)} %copy-done.1, bf16[16,136,512]{2,1,0:T(8,128)(2,1)} %columns.1.own.ids), custom_call_target="tpu_custom_call" | custom-call | flops 1342177280 | bytes 4456448 | tf_op jit(solution)/shard_map/factor/pallas_call | solution.py:42
  128.5 0.8 copy-done.3
  129.3 10.3 %factor.7.rest_3_ = bf16[256,1280]{1,0:T(8,128)(2,1)} custom-call(s32[7]{0:T(128)} %stack.53.where, bf16[16,136,512]{2,1,0:T(8,128)(2,1)} %columns.1.own.ids, bf16[16,136,512]{2,1,0:T(8,128)(2,1)} %copy-done.1, bf16[16,136,512]{2,1,0:T(8,128)(2,1)} %columns.1.own.ids, bf16[16,128,128]{2,1,0:T(8,128)(2,1)} %copy-done.3, bf16[2,1,64,8192]{3,2,1,0:T(8,128)(2,1)} %us.3, ...), custom_call_target="tpu_custom_call" | custom-call | flops 1342177280 | bytes 4456448 | tf_op jit(solution)/shard_map/factor/pallas_call | solution.py:42
  139.7 0.3 collective-permute-start.9
  139.9 10.5 %factor.8.after.a = f32[256,1280]{1,0:T(8,128)} custom-call(s32[7]{0:T(128)} %stack.53.where, bf16[16,136,512]{2,1,0:T(8,128)(2,1)} %columns.1.own.ids, bf16[16,136,512]{2,1,0:T(8,128)(2,1)} %copy-done.1, bf16[16,136,512]{2,1,0:T(8,128)(2,1)} %columns.1.own.ids, bf16[16,128,128]{2,1,0:T(8,128)(2,1)} %copy-done.3, bf16[2,1,64,8192]{3,2,1,0:T(8,128)(2,1)} %us.3, ...), custom_call_target="tpu_custom_call" | custom-call | flops 1342177280 | bytes 4456448 | tf_op jit(solution)/shard_map/factor/pallas_call | solution.py:42
  150.5 0.8 copy-done.9
  151.2 7.2 %backward.1 = (f32[64,64]{1,0:T(8,128)}, f32[64,64]{1,0:T(8,128)}, f32[64,64]{1,0:T(8,128)}) custom-call(s32[7]{0:T(128)} %stack.53.where, bf16[128,8192]{1,0:T(8,128)(2,1)} %bitcast.24, bf16[128,8192]{1,0:T(8,128)(2,1)} %bitcast.25, bf16[2,1,64,8192]{3,2,1,0:T(8,128)(2,1)} %us.3, bf16[2,1,64,8192]{3,2,1,0:T(8,128)(2,1)} %us.3, bf16[2,1,64,8192]{3,2,1,0:T(8,128)(2,1)} %ds.1, ...), custom_call_target="tpu_custom_call" | custom-call | flops 805306368 | bytes 8388608 | tf_op jit(solution)/shard_map/backward/pallas_call | solution.py:42
  158.5 0.0 copy-start.11
  158.5 0.9 copy-done.6
  159.3 2.3 %factor.9 = bf16[256,1280]{1,0:T(8,128)(2,1)} custom-call(f32[256,1280]{1,0:T(8,128)} %factor.8.after.a, bf16[256,1280]{1,0:T(8,128)(2,1)} %copy-done.6, f32[64,64]{1,0:T(8,128)} %get-tuple-element.15.after), custom_call_target="tpu_custom_call" | custom-call | flops 327680 | bytes 2621440 | tf_op jit(solution)/shard_map/factor/pallas_call | solution.py:392
  161.6 3.6 %collective-permute-start.12 = (f32[64,64]{1,0:T(8,128)S(1)}, f32[64,64]{1,0:T(8,128)S(1)}, u32[]{:S(2)}, u32[]{:S(2)}) collective-permute-start(f32[64,64]{1,0:T(8,128)S(1)} %copy-done.16), channel_id=1, source_target_pairs={{0,240},{16,0},{32,16},{48,32},{64,48},{80,64},{96,80},{112,96},{1... | collective-permute-start | bytes 49160 | tf_op jit(solution)/shard_map/backward/ppermute | solution.py:17
  165.2 1.1 collective-permute-start.13
  166.3 2.9 %collective-permute-done.13 = f32[64,64]{1,0:T(8,128)S(1)} collective-permute-done((f32[64,64]{1,0:T(8,128)S(1)}, f32[64,64]{1,0:T(8,128)S(1)}, u32[]{:S(2)}, u32[]{:S(2)}) %collective-permute-start.13) | collective-permute-done | bytes 16416 | tf_op jit(solution)/shard_map/backward/ppermute | solution.py:17
  169.2 0.1 pad_maximum_fusion
  169.2 0.8 broadcast_in_dim.22
  170.1 7.3 %all-to-all-start.2 = ((f32[16,64,128]{2,1,0:T(8,128)}), f32[16,64,128]{2,1,0:T(8,128)S(1)}, u32[]{:S(2)}, u32[]{:S(2)}) async-start(f32[16,64,128]{2,1,0:T(8,128)} %broadcast_in_dim.22), calls=%async_computation.2 | async-start | bytes 1048576 | tf_op jit(solution)/shard_map/backward/all_to_all | solution.py:540
  177.4 0.1 broadcast_compare_fusion
  177.5 2.1 %collective-permute-done.10.came = bf16[256,1280]{1,0:T(8,128)(2,1)S(1)} collective-permute-done((bf16[256,1280]{1,0:T(8,128)(2,1)}, bf16[256,1280]{1,0:T(8,128)(2,1)S(1)}, u32[]{:S(2)}, u32[]{:S(2)}) %collective-permute-start.10) | collective-permute-done | bytes 655392 | tf_op jit(solution)/shard_map/factor/ppermute | solution.py:17
  179.6 1.3 slice_add_fusion.mine
  181.0 1.7 collective-permute-start.11
  182.6 0.1 maximum_multiply_fusion.1
  182.7 5.9 %all-to-all-done.2 = f32[16,64,128]{2,1,0:T(8,128)S(1)} async-done(((f32[16,64,128]{2,1,0:T(8,128)}), f32[16,64,128]{2,1,0:T(8,128)S(1)}, u32[]{:S(2)}, u32[]{:S(2)}) %all-to-all-start.2) | async-done | bytes 524320 | tf_op jit(solution)/shard_map/backward/all_to_all | solution.py:540
  188.6 0.1 slice_bitcast_fusion.1
  188.7 0.7 fusion.2
  189.4 3.5 %factor.10.done = f32[512,1024]{1,0:T(8,128)} custom-call(s32[7]{0:T(128)} %stack.53.where, f32[512,1024]{1,0:T(8,128)} %bitcast.26, f32[256,1280]{1,0:T(8,128)} %factor.6.rest_5_.here, bf16[256,1280]{1,0:T(8,128)(2,1)} %copy-done.5), custom_call_target="tpu_custom_call" | custom-call | flops 1048576 | bytes 3145728 | tf_op jit(solution)/shard_map/factor/pallas_call | solution.py:42
  192.9 0.8 copy-done.10
  193.7 3.3 %factor.11 = f32[512,1024]{1,0:T(8,128)} custom-call(s32[7]{0:T(128)} %stack.53.where, f32[512,1024]{1,0:T(8,128)} %bitcast.27, f32[256,512]{1,0:T(8,128)} %copy-done.4, f32[256,512]{1,0:T(8,128)} %copy-done.10, f32[512,1024]{1,0:T(8,128)} %factor.10.done), custom_call_target="tpu_custom_call", output_to_operand_aliasing={{}: (4, {})} | custom-call | flops 1048576 | bytes 3145728 | tf_op jit(solution)/shard_map/factor/pallas_call | solution.py:42
  (42 shorter events, 0.1 us)
Async XLA Ops:
  6.4 64.3 %all-to-all-start = ((bf16[16,136,512]{2,1,0:T(8,128)(2,1)}), bf16[16,136,512]{2,1,0:T(8,128)(2,1)S(1)}, u32[]{:S(2)}, u32[]{:S(2)}) async-start(bf16[16,136,512]{2,1,0:T(8,128)(2,1)} %get-tuple-element.10), calls=%async_computation | async-start | bytes 4456448 | tf_op jit(solution)/shard_map/columns/all_to_all | solution.py:502
  18.5 31.6 %collective-permute-start = (bf16[64,5120]{1,0:T(8,128)(2,1)}, bf16[64,5120]{1,0:T(8,128)(2,1)S(1)}, u32[]{:S(2)}, u32[]{:S(2)}) collective-permute-start(bf16[64,5120]{1,0:T(8,128)(2,1)} %get-tuple-element.12), channel_id=1, source_target_pairs={{0,240},{16,0},{32,16},{48,32},{64,48},{80,64},{96,80},{112,96},{1... | collective-permute-start | bytes 1966088 | tf_op jit(solution)/shard_map/weights/ppermute | solution.py:17
  50.2 13.8 %copy-start.2 = (bf16[64,5120]{1,0:T(8,128)(2,1)}, bf16[64,5120]{1,0:T(8,128)(2,1)S(1)}, u32[]{:S(2)}) copy-start(bf16[64,5120]{1,0:T(8,128)(2,1)S(1)} %collective-permute-done.dm.rest_3_.rest_4_) | copy-start | bytes 1966084
  50.2 13.8 %collective-permute-start.1 = (bf16[64,5120]{1,0:T(8,128)(2,1)S(1)}, bf16[64,5120]{1,0:T(8,128)(2,1)S(1)}, u32[]{:S(2)}, u32[]{:S(2)}) collective-permute-start(bf16[64,5120]{1,0:T(8,128)(2,1)S(1)} %collective-permute-done.dm.rest_3_.rest_4_), channel_id=1, source_target_pairs={{0,1},{1,0},{2,3},{3,2},{4,5},{5,4},{6,7},{7,6},{8,9},{9,8},{10,11... | collective-permute-start | bytes 1966088 | tf_op jit(solution)/shard_map/weights/ppermute | solution.py:22
  52.3 9.7 %collective-permute-start.2 = (f32[64,128]{1,0:T(8,128)S(1)}, f32[64,128]{1,0:T(8,128)S(1)}, u32[]{:S(2)}, u32[]{:S(2)}) collective-permute-start(f32[64,128]{1,0:T(8,128)S(1)} %get-tuple-element.19), channel_id=1, source_target_pairs={{0,16},{16,32},{32,48},{48,64},{64,80},{80,96},{96,112},{112,128},... | collective-permute-start | bytes 98312 | tf_op jit(solution)/shard_map/weights/ppermute | solution.py:17
  52.3 11.0 %collective-permute-start.3 = (f32[64,128]{1,0:T(8,128)S(1)}, f32[64,128]{1,0:T(8,128)S(1)}, u32[]{:S(2)}, u32[]{:S(2)}) collective-permute-start(f32[64,128]{1,0:T(8,128)S(1)} %get-tuple-element.18), channel_id=1, source_target_pairs={{0,32},{16,48},{32,64},{48,80},{64,96},{80,112},{96,128},{112,144}... | collective-permute-start | bytes 98312 | tf_op jit(solution)/shard_map/weights/ppermute | solution.py:17
  62.0 0.6 copy-start.12
  63.4 0.6 copy-start.13
  64.0 0.8 copy-start.7
  70.7 1.4 copy-start
  72.1 45.7 %collective-permute-start.4 = (bf16[16,136,512]{2,1,0:T(8,128)(2,1)}, bf16[16,136,512]{2,1,0:T(8,128)(2,1)S(1)}, u32[]{:S(2)}, u32[]{:S(2)}) collective-permute-start(bf16[16,136,512]{2,1,0:T(8,128)(2,1)} %columns.1.own.ids), channel_id=1, source_target_pairs={{0,1},{1,0},{2,3},{3,2},{4,5},{5,4},{6,7},{7,6},{8,9},{9,8},{10,11... | collective-permute-start | bytes 6684680 | tf_op jit(solution)/shard_map/columns/ppermute | solution.py:22
  73.9 42.7 %collective-permute-start.6 = (bf16[128,4096]{1,0:T(8,128)(2,1)}, bf16[128,4096]{1,0:T(8,128)(2,1)}, u32[]{:S(2)}, u32[]{:S(2)}) collective-permute-start(bf16[128,4096]{1,0:T(8,128)(2,1)} %get-tuple-element.13), channel_id=1, source_target_pairs={{0,16},{16,32},{32,48},{48,64},{64,80},{80,96},{96,112},{112,128},... | collective-permute-start | bytes 3145736 | tf_op jit(solution)/shard_map/weights/ppermute | solution.py:17
  73.9 54.5 %all-to-all-start.1 = ((bf16[16,128,128]{2,1,0:T(8,128)(2,1)}), bf16[16,128,128]{2,1,0:T(8,128)(2,1)S(1)}, u32[]{:S(2)}, u32[]{:S(2)}) async-start(bf16[16,128,128]{2,1,0:T(8,128)(2,1)} %gates.1.rest_0_), calls=%async_computation.1 | async-start | bytes 1048576 | tf_op jit(solution)/shard_map/columns/all_to_all | solution.py:504
  79.2 60.4 %collective-permute-start.8 = (bf16[64,4096]{1,0:T(8,128)(2,1)}, bf16[64,4096]{1,0:T(8,128)(2,1)S(1)}, u32[]{:S(2)}, u32[]{:S(2)}) collective-permute-start(bf16[64,4096]{1,0:T(8,128)(2,1)} %get-tuple-element.14), channel_id=1, source_target_pairs={{0,32},{16,48},{32,64},{48,80},{64,96},{80,112},{96,128},{112,144}... | collective-permute-start | bytes 1572872 | tf_op jit(solution)/shard_map/weights/ppermute | solution.py:17
  116.6 33.8 %collective-permute-start.7 = (bf16[128,4096]{1,0:T(8,128)(2,1)}, bf16[128,4096]{1,0:T(8,128)(2,1)}, u32[]{:S(2)}, u32[]{:S(2)}) collective-permute-start(bf16[128,4096]{1,0:T(8,128)(2,1)} %collective-permute-done.6.b1m), channel_id=1, source_target_pairs={{0,1},{1,0},{2,3},{3,2},{4,5},{5,4},{6,7},{7,6},{8,9},{9,8},{10,11... | collective-permute-start | bytes 3145736 | tf_op jit(solution)/shard_map/weights/ppermute | solution.py:22
  117.8 1.4 copy-start.1
  128.5 0.8 copy-start.3
  139.6 18.8 %collective-permute-start.5 = (bf16[256,1280]{1,0:T(8,128)(2,1)}, bf16[256,1280]{1,0:T(8,128)(2,1)S(1)}, u32[]{:S(2)}, u32[]{:S(2)}) collective-permute-start(bf16[256,1280]{1,0:T(8,128)(2,1)} %factor.7.rest_3_), channel_id=1, source_target_pairs={{0,16},{16,32},{32,48},{48,64},{64,80},{80,96},{96,112},{112,128},... | collective-permute-start | bytes 1966088 | tf_op jit(solution)/shard_map/factor/ppermute | solution.py:17
  139.6 10.8 %copy-start.8 = (bf16[64,4096]{1,0:T(8,128)(2,1)}, bf16[64,4096]{1,0:T(8,128)(2,1)S(1)}, u32[]{:S(2)}) copy-start(bf16[64,4096]{1,0:T(8,128)(2,1)S(1)} %collective-permute-done.8.b2m) | copy-start | bytes 1572868
  139.7 10.8 %collective-permute-start.9 = (bf16[64,4096]{1,0:T(8,128)(2,1)S(1)}, bf16[64,4096]{1,0:T(8,128)(2,1)S(1)}, u32[]{:S(2)}, u32[]{:S(2)}) collective-permute-start(bf16[64,4096]{1,0:T(8,128)(2,1)S(1)} %collective-permute-done.8.b2m), channel_id=1, source_target_pairs={{0,1},{1,0},{2,3},{3,2},{4,5},{5,4},{6,7},{7,6},{8,9},{9,8},{10,11... | collective-permute-start | bytes 1572872 | tf_op jit(solution)/shard_map/weights/ppermute | solution.py:22
  150.4 0.8 copy-start.9
  158.5 3.2 %copy-start.16 = (f32[64,64]{1,0:T(8,128)S(1)}, f32[64,64]{1,0:T(8,128)}, u32[]{:S(2)}) copy-start(f32[64,64]{1,0:T(8,128)} %get-tuple-element.16) | copy-start | bytes 49156
  158.5 6.7 %copy-start.15 = (f32[64,64]{1,0:T(8,128)S(1)}, f32[64,64]{1,0:T(8,128)}, u32[]{:S(2)}) copy-start(f32[64,64]{1,0:T(8,128)} %get-tuple-element.17) | copy-start | bytes 49156
  158.5 10.7 %copy-start.11 = (f32[64,64]{1,0:T(8,128)S(1)}, f32[64,64]{1,0:T(8,128)}, u32[]{:S(2)}) copy-start(f32[64,64]{1,0:T(8,128)} %get-tuple-element.15.after) | copy-start | bytes 49156
  158.5 0.9 copy-start.6
  161.6 27.1 %copy-start.14 = (f32[2,1,64,64]{3,2,1,0:T(8,128)S(1)}, f32[2,1,64,64]{3,2,1,0:T(8,128)}, u32[]{:S(2)}) copy-start(f32[2,1,64,64]{3,2,1,0:T(8,128)} %param.15) | copy-start | bytes 98308
  161.6 18.0 %collective-permute-start.10 = (bf16[256,1280]{1,0:T(8,128)(2,1)}, bf16[256,1280]{1,0:T(8,128)(2,1)S(1)}, u32[]{:S(2)}, u32[]{:S(2)}) collective-permute-start(bf16[256,1280]{1,0:T(8,128)(2,1)} %factor.9), channel_id=1, source_target_pairs={{0,16},{16,32},{32,48},{48,64},{64,80},{80,96},{96,112},{112,128},... | collective-permute-start | bytes 1966088 | tf_op jit(solution)/shard_map/factor/ppermute | solution.py:17
  161.6 4.7 %collective-permute-start.12 = (f32[64,64]{1,0:T(8,128)S(1)}, f32[64,64]{1,0:T(8,128)S(1)}, u32[]{:S(2)}, u32[]{:S(2)}) collective-permute-start(f32[64,64]{1,0:T(8,128)S(1)} %copy-done.16), channel_id=1, source_target_pairs={{0,240},{16,0},{32,16},{48,32},{64,48},{80,64},{96,80},{112,96},{1... | collective-permute-start | bytes 49160 | tf_op jit(solution)/shard_map/backward/ppermute | solution.py:17
  165.2 4.0 %collective-permute-start.13 = (f32[64,64]{1,0:T(8,128)S(1)}, f32[64,64]{1,0:T(8,128)S(1)}, u32[]{:S(2)}, u32[]{:S(2)}) collective-permute-start(f32[64,64]{1,0:T(8,128)S(1)} %copy-done.15), channel_id=1, source_target_pairs={{0,224},{16,240},{32,0},{48,16},{64,32},{80,48},{96,64},{112,80},{... | collective-permute-start | bytes 49160 | tf_op jit(solution)/shard_map/backward/ppermute | solution.py:17
  170.1 18.5 %all-to-all-start.2 = ((f32[16,64,128]{2,1,0:T(8,128)}), f32[16,64,128]{2,1,0:T(8,128)S(1)}, u32[]{:S(2)}, u32[]{:S(2)}) async-start(f32[16,64,128]{2,1,0:T(8,128)} %broadcast_in_dim.22), calls=%async_computation.2 | async-start | bytes 1048576 | tf_op jit(solution)/shard_map/backward/all_to_all | solution.py:540
  179.6 9.8 %copy-start.5 = (bf16[256,1280]{1,0:T(8,128)(2,1)}, bf16[256,1280]{1,0:T(8,128)(2,1)S(1)}, u32[]{:S(2)}) copy-start(bf16[256,1280]{1,0:T(8,128)(2,1)S(1)} %collective-permute-done.10.came) | copy-start | bytes 1966084
  180.9 11.9 %copy-start.4 = (f32[256,512]{1,0:T(8,128)}, f32[256,512]{1,0:T(8,128)S(1)}, u32[]{:S(2)}) copy-start(f32[256,512]{1,0:T(8,128)S(1)} %slice_add_fusion.mine) | copy-start | bytes 1572868
  181.0 11.9 %collective-permute-start.11 = (f32[256,512]{1,0:T(8,128)S(1)}, f32[256,512]{1,0:T(8,128)S(1)}, u32[]{:S(2)}, u32[]{:S(2)}) collective-permute-start(f32[256,512]{1,0:T(8,128)S(1)} %slice_add_fusion.mine), channel_id=1, source_target_pairs={{0,1},{1,0},{2,3},{3,2},{4,5},{5,4},{6,7},{7,6},{8,9},{9,8},{10,11... | collective-permute-start | bytes 1572872 | tf_op jit(solution)/shard_map/factor/ppermute | solution.py:22
  192.9 0.8 copy-start.10

commit v4 on v3

v4 whole, which is shorter than its diff:
```python
import functools

import jax
import jax.numpy as jnp
from jax import lax
from jax.experimental import pallas as pl
from jax.experimental.pallas import tpu as pltpu
from jax.sharding import PartitionSpec as P

F32 = jnp.float32
BF16 = jnp.bfloat16
ANY = pl.BlockSpec(memory_space=pl.ANY)


def shift(block, axis, distance):
    count = lax.axis_size(axis)
    return lax.ppermute(block, axis, [(i, (i + distance) % count) for i in range(count)])


def swap_cores(block):
    count = lax.axis_size("dp")
    return lax.ppermute(block, "dp", [(i, i ^ 1) for i in range(count)])


def nt(a, b):
    return lax.dot_general(a, b, (((1,), (1,)), ((), ())), preferred_element_type=F32)


def tn(a, b):
    return lax.dot_general(a, b, (((0,), (0,)), ((), ())), preferred_element_type=F32)


def call(kernel, where, operands, in_specs, outs, out_specs, grid, scratch, cost, aliases={}):
    spec = pltpu.PrefetchScalarGridSpec(
        num_scalar_prefetch=1,
        grid=grid,
        in_specs=in_specs,
        out_specs=out_specs,
        scratch_shapes=list(scratch),
    )
    flops, moved = cost
    return pl.pallas_call(
        kernel,
        grid_spec=spec,
        out_shape=outs,
        input_output_aliases=aliases,
        compiler_params=pltpu.CompilerParams(dimension_semantics=("arbitrary",) * len(grid)),
        cost_estimate=pl.CostEstimate(flops=flops, transcendentals=0, bytes_accessed=moved),
    )(where, *operands)


def tie_kernel(x, *rest):
    del x, rest


def tie(x, *after, space=pltpu.HBM):
    spec = pl.BlockSpec(memory_space=space)
    return pl.pallas_call(
        tie_kernel,
        in_specs=[spec] + [ANY] * len(after),
        out_specs=spec,
        out_shape=jax.ShapeDtypeStruct(x.shape, x.dtype),
        input_output_aliases={0: 0},
        compiler_params=pltpu.CompilerParams(vmem_limit_bytes=8 << 20),
        cost_estimate=pl.CostEstimate(flops=0, transcendentals=0, bytes_accessed=0),
    )(x, *after)


CHIP, CORE, SEC, C0, F1, B1, B2 = range(7)


def split_kernel(where, x, down, ids, after, out, gate, acc):
    i = pl.program_id(0)
    pieces, _, cols = out.shape
    tok, rank = gate.shape

    @pl.when(i == 0)
    def _():
        acc[...] = jnp.zeros_like(acc)

    acc[...] += nt(x[...], down[0, 0])
    row = ids[pl.ds(where[SEC], 1), :].astype(F32)
    row = jnp.broadcast_to(row, (out.shape[1] - tok, tok)).astype(BF16)
    for k in range(pieces):
        out[k, :tok, :] = x[:, k * cols:(k + 1) * cols]
        out[k, tok:, :tok] = row
        out[k, tok:, tok:] = jnp.zeros((out.shape[1] - tok, cols - tok), BF16)

    @pl.when(i == pl.num_programs(0) - 1)
    def _():
        z = acc[...]
        gate[...] = (z * jax.nn.sigmoid(z)).astype(BF16)


def split(where, x, adapter_down, doc_ids, pieces, extra, after):
    tok, width = x.shape
    rank = adapter_down.shape[2]
    cols = width // pieces
    grid = 4
    each = width // grid
    return call(
        split_kernel,
        where,
        (x, adapter_down, doc_ids, after),
        [
            pl.BlockSpec((tok, each), lambda i, w: (0, i)),
            pl.BlockSpec((1, 1, rank, each), lambda i, w: (w[C0], 0, 0, i)),
            pl.BlockSpec(doc_ids.shape, lambda i, w: (0, 0)),
            ANY,
        ],
        [
            jax.ShapeDtypeStruct((pieces, tok + extra, cols), BF16),
            jax.ShapeDtypeStruct((tok, rank), BF16),
        ],
        [
            pl.BlockSpec((pieces // grid, tok + extra, cols), lambda i, w: (i, 0, 0)),
            pl.BlockSpec((tok, rank), lambda i, w: (0, 0)),
        ],
        (grid,),
        [pltpu.VMEM((tok, rank), F32)],
        (2 * x.size * rank, 5 * x.size),
    )


def pack_kernel(where, up_f, down_f, up_b1, up_b2, ahead, behind1, behind2):
    cols = up_f.shape[3]
    ahead[:, :cols] = up_f[0, 0]
    ahead[:, cols:] = down_f[0, 0]
    behind1[...] = up_b1[0, 0]
    behind2[...] = up_b2[0, 0]


def pack(where, adapter_down, adapter_up, block):
    rank, width = adapter_down.shape[2:]
    half = width // 2
    part = lambda span: pl.BlockSpec((1, 1, rank, half), lambda i, w: (w[span], 0, 0, w[CORE]))
    shapes = ((rank, block + half), (rank, half), (rank, half))
    return call(
        pack_kernel,
        where,
        (adapter_up, adapter_down, adapter_up, adapter_up),
        [
            pl.BlockSpec((1, 1, rank, block), lambda i, w: (w[F1], 0, 0, w[CHIP])),
            part(F1),
            part(B1),
            part(B2),
        ],
        [jax.ShapeDtypeStruct(shape, BF16) for shape in shapes],
        [pl.BlockSpec(shape, lambda i, w: (0, 0)) for shape in shapes],
        (1,),
        (),
        (0, 8 * rank * half * 2),
    )


def gate_kernel(
    where, xm, xs, um, us, dm, ds, gate0, u0o, u0s, u1o, u1s, sent, ups_o, ups_s, acc
):
    i = pl.program_id(0)
    rank = gate0.shape[1]

    @pl.when(i == 0)
    def _():
        acc[...] = jnp.zeros_like(acc)
        for out, zero, one in ((ups_o, u0o, u1o), (ups_s, u0s, u1s)):
            out[:rank] = zero[0, 0]
            out[rank:] = one[...]

    for x, u, d in ((xm, um, dm), (xs, us, ds)):
        add = jnp.dot(gate0[...], u[0, 0], preferred_element_type=F32)
        acc[...] += nt((x[...].astype(F32) + add).astype(BF16), d[...])

    @pl.when(i == pl.num_programs(0) - 1)
    def _():
        z = acc[...]
        gate1 = (z * jax.nn.sigmoid(z)).astype(BF16)
        both = jnp.concatenate([gate0[...], gate1], axis=1)
        for k in range(sent.shape[0]):
            sent[k] = both


def gates(where, x, adapter_up, ahead_mine, ahead_sib, gate0, replicas, rows):
    tok, width = x.shape
    rank = gate0.shape[1]
    each = ahead_mine.shape[1] - width // 2
    grid = width // 2 // each
    mine, sib = (lambda w: w[CORE]), (lambda w: 1 - w[CORE])
    x_spec = lambda side: pl.BlockSpec((tok, each), lambda i, w: (0, side(w) * grid + i))
    u_spec = lambda side: pl.BlockSpec(
        (1, 1, rank, each), lambda i, w: (w[C0], 0, 0, side(w) * grid + i)
    )
    d_spec = pl.BlockSpec((rank, each), lambda i, w: (0, i + 1))
    u0 = lambda side: pl.BlockSpec(
        (1, 1, rank, rows), lambda i, w: (w[C0], 0, 0, 2 * w[CHIP] + side(w))
    )
    u1 = lambda side: pl.BlockSpec((rank, rows), lambda i, w: (0, side(w)))
    shapes = ((replicas, tok, 2 * rank), (2 * rank, rows), (2 * rank, rows))
    return call(
        gate_kernel,
        where,
        (
            x, x, adapter_up, adapter_up, ahead_mine, ahead_sib, gate0,
            adapter_up, adapter_up, ahead_mine, ahead_mine,
        ),
        [
            x_spec(mine), x_spec(sib), u_spec(mine), u_spec(sib), d_spec, d_spec,
            pl.BlockSpec((tok, rank), lambda i, w: (0, 0)),
            u0(mine), u0(sib), u1(mine), u1(sib),
        ],
        [jax.ShapeDtypeStruct(shape, BF16) for shape in shapes],
        [
            pl.BlockSpec(shapes[0], lambda i, w: (0, 0, 0)),
            pl.BlockSpec(shapes[1], lambda i, w: (0, 0)),
            pl.BlockSpec(shapes[2], lambda i, w: (0, 0)),
        ],
        (grid,),
        [pltpu.VMEM((tok, rank), F32)],
        (4 * x.size * rank, 5 * x.size),
    )


def local(kernel, where, operands, outs, scratch=(), after=(), aliases={}, out_specs=None):
    vmem = pl.BlockSpec(memory_space=pltpu.VMEM)
    out_vmem = [vmem] * len(outs) if isinstance(outs, list) else vmem
    return pl.pallas_call(
        kernel,
        in_specs=[pl.BlockSpec(memory_space=pltpu.SMEM)]
        + [vmem] * len(operands)
        + [ANY] * len(after),
        out_specs=out_specs or out_vmem,
        out_shape=outs,
        scratch_shapes=list(scratch),
        input_output_aliases=aliases,
        compiler_params=pltpu.CompilerParams(vmem_limit_bytes=24 << 20),
        cost_estimate=pl.CostEstimate(
            flops=0, transcendentals=0, bytes_accessed=2 * sum(x.size for x in operands)
        ),
    )(where, *operands, *after)


def scale_columns(own, tok):
    replicas = own.shape[0]
    ids = [own[k, tok:tok + 1, :tok].astype(F32) for k in range(replicas)]
    doc = lax.broadcasted_iota(jnp.int32, (2 * replicas, tok), 0).astype(F32)
    hits = jnp.zeros((2 * replicas, tok), F32)
    for row in ids:
        hits += (doc == row).astype(F32)
    count = jnp.maximum(jnp.sum(hits, axis=1, keepdims=True), 1.0)
    table = jnp.sqrt(jnp.sqrt(tok / count))
    scales = [jnp.sum(jnp.where(doc == row, table, 0.0), axis=0, keepdims=True) for row in ids]
    return jnp.concatenate(scales + [jnp.zeros((tok - replicas, tok), F32)], axis=0).T


def gram_kernel(step, where, own, other, *rest):
    if step:
        got, ups_own, ups_oth = rest[:3]
    rest = rest[3 if step else 0:]
    core = where[CORE]
    replicas, long, rows = own.shape
    tok = long - 8
    hlf = rows // 2
    per = 4
    if step == 2:
        out, acc = rest[-2:]
    else:
        out = acc = rest[-1]
    columns = scale_columns(own, tok)

    for i in range(replicas // per):
        ks = range(i * per, (i + 1) * per)

        def rebuilt(ref, ups):
            act = jnp.concatenate([ref[k, :tok, :] for k in ks], axis=0).astype(F32)
            if step:
                rank = ups.shape[0] // 2 * step
                gate = jnp.concatenate([got[k] for k in ks], axis=0)[:, :rank]
                add = jnp.dot(gate, ups[:rank], preferred_element_type=F32)
                act = (act + add).astype(BF16).astype(F32)
            scale = [jnp.broadcast_to(columns[:, k:k + 1], (tok, rows)) for k in ks]
            return (jnp.concatenate(scale, axis=0) * act).astype(BF16)

        def put(lo, hi, val):
            acc[:, lo:hi] = val if i == 0 else acc[:, lo:hi] + val

        r = rebuilt(own, ups_own if step else None)
        q = rebuilt(other, ups_oth if step else None)
        put(0, rows, tn(r[:, :hlf], r))
        put(rows, rows + hlf, tn(r[:, hlf:], r[:, hlf:]))

        @pl.when(core == 0)
        def _():
            put(rows + hlf, 2 * rows + hlf, tn(r[:, :hlf], q))

        @pl.when(core == 1)
        def _():
            put(rows + hlf, 2 * rows + hlf, tn(q[:, hlf:], r))

    if step == 2:
        out[...] = acc[...].astype(BF16)


def gram(step, where, own, other, ups=(), after=()):
    rows = own.shape[2]
    packed = (rows // 2, rows * 5 // 2)
    return local(
        functools.partial(gram_kernel, step),
        where,
        (own, other, *ups),
        jax.ShapeDtypeStruct(packed, BF16 if step == 2 else F32),
        [pltpu.VMEM(packed, F32)] if step == 2 else [],
        after,
    )


def project_kernel(where, *refs):
    ins, stash, (proj, m0, by1, by2) = refs[:16], refs[16], refs[17:]
    i = pl.program_id(0)
    rank = stash.shape[2]

    @pl.when(i == 0)
    def _():
        for acc in (proj, m0, by1, by2):
            acc[...] = jnp.zeros_like(acc)
        by1[:rank] = stash[0, 1]
        by2[:rank] = stash[0, 2]

    for g, u, d, d1, u2, b1, b2, a in (ins[0::2], ins[1::2]):
        two = jnp.concatenate([b1[...], b2[...]], axis=0)
        proj[:rank] += nt(u[0, 0], g[...])
        proj[rank:] += nt(two, g[...])
        m0[...] += nt(two, d[0, 0])
        by1[rank:, :rank] += nt(b1[...], d1[0, 0])
        by2[rank:, :rank] += nt(u2[0, 0], a[...])


def project(where, grad, adapter_down, adapter_up, b1, b1s, b2, b2s, ahead, ahead_sib, stashed):
    tok, width = grad.shape
    rank = adapter_up.shape[2]
    each = ahead.shape[1] - width // 2
    grid = width // 2 // each
    mine, sib = (lambda w: w[CORE]), (lambda w: 1 - w[CORE])

    def half(span, side):
        return pl.BlockSpec(
            (1, 1, rank, each), lambda i, w: (span(w), 0, 0, side(w) * grid + i)
        )

    def weights(span):
        return [half(span, mine), half(span, sib)]

    g_spec = lambda side: pl.BlockSpec((tok, each), lambda i, w: (0, side(w) * grid + i))
    got = lambda skip: pl.BlockSpec((rank, each), lambda i, w: (0, i + skip))
    one = lambda w: 1
    shapes = ((3 * rank, tok), (2 * rank, rank), (2 * rank, tok), (2 * rank, tok))
    return call(
        project_kernel,
        where,
        (
            grad, grad, adapter_up, adapter_up, adapter_down, adapter_down,
            adapter_down, adapter_down, adapter_up, adapter_up,
            b1, b1s, b2, b2s, ahead, ahead_sib, stashed,
        ),
        [g_spec(mine), g_spec(sib)]
        + weights(one)
        + weights(one)
        + weights(lambda w: w[B1])
        + weights(lambda w: w[B2])
        + [got(0)] * 4
        + [got(1)] * 2
        + [pl.BlockSpec(stashed.shape, lambda i, w: (0, 0, 0, 0))],
        [jax.ShapeDtypeStruct(shape, F32) for shape in shapes],
        [pl.BlockSpec(shape, lambda i, w: (0, 0)) for shape in shapes],
        (grid,),
        (),
        (14 * grad.size * rank, 12 * grad.size),
    )


def back_kernel(where, proj, m0, by1, by2, q0, *rest):
    outs = rest[-3:]
    rank = m0.shape[1]

    def dz_of(grad_act, q):
        sigma = jax.nn.sigmoid(q)
        return (grad_act * sigma * (1.0 + q * (1.0 - sigma))).astype(BF16)

    def exact(m, d):
        return jnp.dot(
            m, d.astype(F32), precision=lax.Precision.HIGHEST, preferred_element_type=F32
        )

    m12 = jnp.where(where[SEC] == 0, by2[rank:, :rank], by1[rank:, :rank])
    dz0 = dz_of(proj[:rank], q0[0, 0])
    dz1 = dz_of(proj[rank:2 * rank] + exact(m0[:rank], dz0), by1[:rank])
    dz2 = dz_of(proj[2 * rank:] + exact(m0[rank:], dz0) + exact(m12, dz1), by2[:rank])
    for out, dz in zip(outs, (dz0, dz1, dz2)):
        out[...] = nt(dz, dz)


def back(where, proj, m0, by1, by2, stashed, after):
    rank = m0.shape[1]
    return local(
        back_kernel,
        where,
        (proj, m0, by1, by2, stashed),
        [jax.ShapeDtypeStruct((rank, rank), F32)] * 3,
        (),
        (after,),
    )


def merge_kernel(where, a, b, *rest):
    rest[-1][...] = (a[...] + b[...].astype(F32)).astype(BF16)


def merge(where, a, b, after):
    return local(merge_kernel, where, (a, b), jax.ShapeDtypeStruct(a.shape, BF16), (), after)


def put_rows(factor_scale, old, out, buf, sems, first_col, pieces):
    hlf = buf.shape[0] // 2
    cols = pl.ds(pl.multiple_of(first_col, 2 * hlf), 2 * hlf)
    sent = []
    for i, values in enumerate(pieces):
        rows = pl.ds(i * hlf, hlf)
        at = 0
        for value in values():
            here = slice(at, at + value.shape[1])
            was = old[rows, pl.ds(pl.multiple_of(first_col + at, hlf), value.shape[1])]
            buf[rows, here] = 0.75 * was + factor_scale * value
            at += value.shape[1]
        copy = pltpu.make_async_copy(buf.at[rows], out.at[rows, cols], sems.at[i])
        copy.start()
        sent.append(copy)
    for copy in sent:
        copy.wait()


def square_kernel(factor_scale, where, old, here, came, after, out, buf, sems):
    hlf = here.shape[0]
    rows = 2 * hlf

    def packed(lo, hi):
        return here[:, lo:hi] + came[:, lo:hi].astype(F32)

    put_rows(
        factor_scale, old, out, buf, sems, where[CORE] * rows,
        (
            lambda: [packed(0, hlf), packed(hlf, rows)],
            lambda: [packed(hlf, rows).T, packed(rows, rows + hlf)],
        ),
    )


def cross_kernel(factor_scale, where, old, mine, sib, done, out, buf, sems):
    core = where[CORE]
    hlf, rows = mine.shape

    def put(pieces):
        put_rows(factor_scale, old, out, buf, sems, (1 - core) * rows, pieces)

    @pl.when(core == 0)
    def _():
        put(tuple((lambda part=part: [part[:, :hlf], part[:, hlf:]]) for part in (mine, sib)))

    @pl.when(core == 1)
    def _():
        put(
            tuple(
                (lambda a=a: [sib[:, a:a + hlf].T, mine[:, a:a + hlf].T]) for a in (0, hlf)
            )
        )


def update(factor_scale, where, old, here, came, mine, sib, after):
    total = old.shape[0]
    shape = jax.ShapeDtypeStruct(old.shape, F32)
    scratch = [pltpu.VMEM((total, total), F32), pltpu.SemaphoreType.DMA((2,))]
    done = local(
        functools.partial(square_kernel, factor_scale), where, (old, here, came), shape, scratch,
        (after,), out_specs=ANY,
    )
    return local(
        functools.partial(cross_kernel, factor_scale), where, (old, mine, sib), shape, scratch,
        (done,), {4: 0}, ANY,
    )


def shards(
    entering, returning, adapter_down, adapter_up, stashed, doc_ids, input_factor, output_factor
):
    sec = lax.axis_index("section")
    rep = lax.axis_index("dp")
    sections = lax.axis_size("section")
    replicas = lax.axis_size("dp")
    tok = entering.shape[1]
    steps_count = stashed.shape[1]
    rank = stashed.shape[2]
    rows, block = input_factor.shape[1:]
    tokens = tok * replicas

    def first(home):
        return (home < sections // 2).astype(jnp.int32)

    x0 = entering[0]
    f1 = first((sec + sections - 1) % sections) + (sec == 0).astype(jnp.int32)
    b1 = (sec + 1 < sections).astype(jnp.int32)
    b2 = (sec + 2 < sections).astype(jnp.int32)
    where = jnp.stack([rep // 2, rep % 2, sec, first(sec), f1, b1, b2]).astype(jnp.int32)

    with jax.named_scope("weights"):
        ahead, behind1, behind2 = pack(where, adapter_down, adapter_up, block)
        pieces, gate0 = split(where, x0, adapter_down, doc_ids, replicas, 8, ahead)
        ahead = shift(ahead, "section", -1)
        ahead_sib = swap_cores(ahead)
        behind1 = shift(behind1, "section", 1)
        behind2 = shift(behind2, "section", 2)
        behind1_sib = swap_cores(behind1)
        behind2_sib = swap_cores(behind2)

    with jax.named_scope("gates"):
        sent, ups_own, ups_oth = gates(
            where, x0, adapter_up, ahead, ahead_sib, gate0, replicas, rows
        )
        sent = tie(sent, behind1_sib, behind2_sib)

    with jax.named_scope("columns"):
        own = tie(lax.all_to_all(pieces, "dp", 0, 0), sent, space=pltpu.VMEM)
        other = swap_cores(own)
        got = lax.all_to_all(sent, "dp", 0, 0)

    with jax.named_scope("backward"):
        proj, m0, by1, by2 = project(
            where, returning[0], adapter_down, adapter_up, behind1, behind1_sib, behind2,
            behind2_sib, ahead, ahead_sib, stashed,
        )
        by1 = shift(by1, "section", 1)
        by2 = shift(by2, "section", 2)

    with jax.named_scope("factor"):
        ups = (got, ups_own, ups_oth)
        step0 = gram(0, where, own, other, (), (proj,))
        step2 = gram(2, where, own, other, ups, (step0, by1, by2))
        from2 = shift(step2, "section", 1)

    with jax.named_scope("backward"):
        outer0, outer1, outer2 = back(where, proj, m0, by1, by2, stashed, step2)

        outer1 = shift(outer1, "section", -1)
        outer2 = shift(outer2, "section", -2)

    with jax.named_scope("factor"):
        step1 = gram(1, where, own, other, ups, (outer0,))
        from1 = shift(merge(where, step1, from2, (outer1, outer2)), "section", 1)

    with jax.named_scope("backward"):
        g1 = b1.astype(F32)
        g2 = b2.astype(F32)
        curv = jnp.concatenate(
            [
                outer1 * (1.0 - g1) + outer2 * (1.0 - g2),
                outer0 + outer1 * g1 + outer2 * g2,
            ],
            axis=1,
        )
        curv_all = lax.all_to_all(
            jnp.broadcast_to(curv[None], (replicas,) + curv.shape), "dp", 0, 0
        )

    with jax.named_scope("factor"):
        cut = rows + rows // 2
        mine = step0[:, cut:] + from1[:, cut:].astype(F32)
        sib = swap_cores(mine)
        factor_scale = 0.25 / (steps_count * tokens)
        input_factor_new = update(
            factor_scale, where, input_factor[0], step0, from1, mine, sib, curv_all
        )[None]

    with jax.named_scope("backward"):
        curv_total = jnp.sum(curv_all, axis=0)
        curv_total = jnp.stack([curv_total[:, :rank], curv_total[:, rank:]])
        step_totals = jnp.stack([2.0 - g1 - g2, 1.0 + g1 + g2])
        divisor = (jnp.maximum(step_totals, 1.0) * tokens)[:, None, None]
        updated = 0.75 * output_factor[:, 0] + 0.25 * curv_total / divisor
        output_factor_new = jnp.where(
            (step_totals > 0.0)[:, None, None], updated, output_factor[:, 0]
        )[:, None]
    return (input_factor_new, output_factor_new)


def solution(mesh):
    in_specs = (
        P("section", "dp", None),
        P("section", "dp", None),
        P(None, "section", None, None),
        P(None, "section", None, None),
        P("section", None, None, "dp"),
        P(None, "dp"),
        P("section", "dp", None),
        P(None, "section", None, None),
    )
    out_specs = (P("section", "dp", None), P(None, "section", None, None))
    return jax.shard_map(shards, mesh=mesh, in_specs=in_specs, out_specs=out_specs, check_vma=False)
```

time: 198 us -> 174 us (0.88)
  waiting for transfers between devices: 84.5 us -> 55.4 us
  starting transfers between devices: 37.8 us -> 54.1 us
  Pallas kernels: 61.1 us -> 47.4 us
  other arithmetic: 2.34 us -> 5.61 us
    pallas_call x9 -> x4, Pallas kernels: 58.8 us -> 22.1 us  [call(): pl.pallas_call(kernel, grid_spec=spec, out_shape=outs, input_output_alias...]
    ppermute x9, waiting for transfers between devices: 78.6 us -> 53.9 us  [shift(): lax.ppermute(block, axis, [(i, (i + distance) % count) for i in range(cou...]
    pallas_call x2 -> x9, Pallas kernels: 2.26 us -> 25.3 us  [the longest x7 25.3 us: local(): pl.pallas_call(kernel, in_specs=[pl.BlockSpec(memory_space=pltpu.SMEM)] +...]
    ppermute x9, starting transfers between devices: 10.4 us -> 22.1 us  [shift(): lax.ppermute(block, axis, [(i, (i + distance) % count) for i in range(cou...]
    all_to_all x1, waiting for transfers between devices: 5.85 us -> 1.51 us  [shards(): lax.all_to_all(jnp.broadcast_to(curv[None], (replicas,) + curv.shape), 'd...]
    ppermute x5, starting transfers between devices: 6.34 us -> 8.74 us  [swap_cores(): return lax.ppermute(block, 'dp', [(i, i ^ 1) for i in range(count)])]
    unnamed x34 -> x46, local copies, waits for them, and re-layouts: 8.11 us -> 7.47 us
  transfers between devices with their start and end apart: 17 -> 17, of which waited for: 7 -> 5; matrix products, arithmetic and copies ran while one was open for 2% -> 4% of each run, Pallas kernels for 26% -> 17%
where the time goes in v4:
time: 174 us; the launch traced here: 173 us
  waiting for transfers between devices  55.4 us (32%)
  starting transfers between devices  54.1 us (31%)
  Pallas kernels  47.4 us (27%)
  local copies, waits for them, and re-layouts  9.07 us (5%)
  other arithmetic  5.61 us (3%)
    ppermute x9, waiting for transfers between devices, shift(): lax.ppermute(block, axis, [(i, (i + distance) % count) for i in range(cou...  53.9 us
    pallas_call x7, Pallas kernels, local(): pl.pallas_call(kernel, in_specs=[pl.BlockSpec(memory_space=pltpu.SMEM)] +...  25.3 us
    pallas_call x4, Pallas kernels, call(): pl.pallas_call(kernel, grid_spec=spec, out_shape=outs, input_output_alias...  22.1 us
    ppermute x9, starting transfers between devices, shift(): lax.ppermute(block, axis, [(i, (i + distance) % count) for i in range(cou...  22.1 us
    ppermute x5, starting transfers between devices, swap_cores(): return lax.ppermute(block, 'dp', [(i, i ^ 1) for i in range(count)])  8.74 us
    all_to_all x1, starting transfers between devices, shards(): own = tie(lax.all_to_all(pieces, 'dp', 0, 0), sent, space=pltpu.VMEM)  8.66 us
    all_to_all x1, starting transfers between devices, shards(): lax.all_to_all(jnp.broadcast_to(curv[None], (replicas,) + curv.shape), 'd...  8.22 us
    unnamed x46, local copies, waits for them, and re-layouts  7.47 us
  transfers between devices with their start and end apart: 17, of which 5 were waited for; matrix products, arithmetic and copies ran while one was open for 4% of the time, Pallas kernels for 17%

profile of v4, /device:TPU:1, one launch (start us, length us, event | category | flops | bytes accessed | tf_op | source)
XLA Modules:
  0.0 172.7 jit_solution(9878269692540959402)
XLA Ops:
  0.7 0.7 stack.53.where
  1.4 3.3 %weights.2 = (bf16[64,5120]{1,0:T(8,128)(2,1)}, bf16[64,4096]{1,0:T(8,128)(2,1)}, bf16[64,4096]{1,0:T(8,128)(2,1)}) custom-call(s32[7]{0:T(128)} %stack.53.where, bf16[2,1,64,8192]{3,2,1,0:T(8,128)(2,1)} %refs_9_.1, bf16[2,1,64,8192]{3,2,1,0:T(8,128)(2,1)} %refs_7_.1, bf16[2,1,64,8192]{3,2,1,0:T(8,128)(2,1)} %refs_9_.1, bf16[2,1,64,8192]{3,2,1,0:T(8,128)(2,1)} %refs_9_.1), custom_call_target="tpu_custom_call" | custom-call | bytes 4194304 | tf_op jit(solution)/shard_map/weights/pallas_call | solution.py:42
  4.6 5.2 %weights.3 = (bf16[16,136,512]{2,1,0:T(8,128)(2,1)}, bf16[128,64]{1,0:T(8,128)(2,1)}) custom-call(s32[7]{0:T(128)} %stack.53.where, bf16[128,8192]{1,0:T(8,128)(2,1)} %bitcast.19, bf16[2,1,64,8192]{3,2,1,0:T(8,128)(2,1)} %refs_7_.1, s32[16,128]{1,0:T(8,128)} %ids.1, bf16[64,5120]{1,0:T(8,128)(2,1)} %get-tuple-element.17.after), custom_call_target="tpu_custom_call" | custom-call | flops 134217728 | bytes 5242880 | tf_op jit(solution)/shard_map/weights/pallas_call | solution.py:42
  9.8 8.7 %all-to-all-start = ((bf16[16,136,512]{2,1,0:T(8,128)(2,1)}), bf16[16,136,512]{2,1,0:T(8,128)(2,1)S(1)}, u32[]{:S(2)}, u32[]{:S(2)}) async-start(bf16[16,136,512]{2,1,0:T(8,128)(2,1)} %get-tuple-element.18), calls=%async_computation | async-start | bytes 4456448 | tf_op jit(solution)/shard_map/columns/all_to_all | solution.py:528
  18.5 5.7 %collective-permute-start = (bf16[64,5120]{1,0:T(8,128)(2,1)S(1)}, bf16[64,5120]{1,0:T(8,128)(2,1)S(1)}, u32[]{:S(2)}, u32[]{:S(2)}) collective-permute-start(bf16[64,5120]{1,0:T(8,128)(2,1)S(1)} %copy-done.21), channel_id=1, source_target_pairs={{0,240},{16,0},{32,16},{48,32},{64,48},{80,64},{96,80},{112,96},{1... | collective-permute-start | bytes 1966088 | tf_op jit(solution)/shard_map/weights/ppermute | solution.py:17
  24.2 24.6 %collective-permute-done.dm.u1o.u1s.refs_14_ = bf16[64,5120]{1,0:T(8,128)(2,1)S(1)} collective-permute-done((bf16[64,5120]{1,0:T(8,128)(2,1)S(1)}, bf16[64,5120]{1,0:T(8,128)(2,1)S(1)}, u32[]{:S(2)}, u32[]{:S(2)}) %collective-permute-start) | collective-permute-done | bytes 655392 | tf_op jit(solution)/shard_map/weights/ppermute | solution.py:17
  48.8 1.2 collective-permute-start.1
  50.0 15.9 %collective-permute-done.2.refs_10_ = bf16[64,4096]{1,0:T(8,128)(2,1)} collective-permute-done((bf16[64,4096]{1,0:T(8,128)(2,1)}, bf16[64,4096]{1,0:T(8,128)(2,1)}, u32[]{:S(2)}, u32[]{:S(2)}) %collective-permute-start.2) | collective-permute-done | bytes 524320 | tf_op jit(solution)/shard_map/weights/ppermute | solution.py:17
  65.9 2.0 %collective-permute-start.3 = (bf16[64,4096]{1,0:T(8,128)(2,1)}, bf16[64,4096]{1,0:T(8,128)(2,1)S(1)}, u32[]{:S(2)}, u32[]{:S(2)}) collective-permute-start(bf16[64,4096]{1,0:T(8,128)(2,1)} %collective-permute-done.2.refs_10_), channel_id=1, source_target_pairs={{0,1},{1,0},{2,3},{3,2},{4,5},{5,4},{6,7},{7,6},{8,9},{9,8},{10,11... | collective-permute-start | bytes 1572872 | tf_op jit(solution)/shard_map/weights/ppermute | solution.py:22
  67.9 0.1 collective-permute-start.5
  68.0 0.8 copy-done.20
  68.8 6.2 %gates.2 = (bf16[16,128,128]{2,1,0:T(8,128)(2,1)}, bf16[128,512]{1,0:T(8,128)(2,1)}, bf16[128,512]{1,0:T(8,128)(2,1)}) custom-call(s32[7]{0:T(128)} %stack.53.where, bf16[128,8192]{1,0:T(8,128)(2,1)} %bitcast.20, bf16[128,8192]{1,0:T(8,128)(2,1)} %bitcast.21, bf16[2,1,64,8192]{3,2,1,0:T(8,128)(2,1)} %refs_9_.1, bf16[2,1,64,8192]{3,2,1,0:T(8,128)(2,1)} %refs_9_.1, ...), custom_call_target="tpu_custom_call" | custom-call | flops 268435456 | bytes 5242880 | tf_op jit(solution)/shard_map/gates/pallas_call | solution.py:42
  75.1 0.7 copy-done.1
  75.8 0.2 copy-done.2
  76.0 0.4 collective-permute-start.6
  76.5 6.3 %all-to-all-start.1 = ((bf16[16,128,128]{2,1,0:T(8,128)(2,1)}), bf16[16,128,128]{2,1,0:T(8,128)(2,1)}, u32[]{:S(2)}, u32[]{:S(2)}) async-start(bf16[16,128,128]{2,1,0:T(8,128)(2,1)} %gates.3.rest_0_), calls=%async_computation.1 | async-start | bytes 1048576 | tf_op jit(solution)/shard_map/columns/all_to_all | solution.py:530
  82.8 7.4 %backward.2 = (f32[192,128]{1,0:T(8,128)}, f32[128,64]{1,0:T(8,128)}, f32[128,128]{1,0:T(8,128)}, f32[128,128]{1,0:T(8,128)}) custom-call(s32[7]{0:T(128)} %stack.53.where, bf16[128,8192]{1,0:T(8,128)(2,1)} %bitcast.23, bf16[128,8192]{1,0:T(8,128)(2,1)} %bitcast.24, bf16[2,1,64,8192]{3,2,1,0:T(8,128)(2,1)} %refs_9_.1, bf16[2,1,64,8192]{3,2,1,0:T(8,128)(2,1)} %refs_9_.1, ...), custom_call_target="tpu_custom_call" | custom-call | flops 939524096 | bytes 12582912 | tf_op jit(solution)/shard_map/backward/pallas_call | solution.py:42
  90.3 10.3 %collective-permute-start.7 = (f32[128,128]{1,0:T(8,128)}, f32[128,128]{1,0:T(8,128)S(1)}, u32[]{:S(2)}, u32[]{:S(2)}) collective-permute-start(f32[128,128]{1,0:T(8,128)} %get-tuple-element.27), channel_id=1, source_target_pairs={{0,16},{16,32},{32,48},{48,64},{64,80},{80,96},{96,112},{112,128},... | collective-permute-start | bytes 196616 | tf_op jit(solution)/shard_map/backward/ppermute | solution.py:17
  100.6 0.9 copy-done.7
  101.5 5.8 %factor.6.rest_3_.here = f32[256,1280]{1,0:T(8,128)S(1)} custom-call(s32[7]{0:T(128)S(1)} %copy-done.17, bf16[16,136,512]{2,1,0:T(8,128)(2,1)S(1)} %columns.1.own, bf16[16,136,512]{2,1,0:T(8,128)(2,1)} %collective-permute-done.6.other, f32[192,128]{1,0:T(8,128)S(1)} %copy-done.7), custom_call_target="tpu_custom_call" | custom-call | bytes 4456448 | tf_op jit(solution)/shard_map/factor/pallas_call | solution.py:225
  107.3 0.6 copy-done.9
  107.9 0.6 copy-done.11
  108.5 0.9 copy-done.3
  109.4 0.9 copy-done.5
  110.3 0.8 copy-done.10
  111.2 0.8 copy-done.12
  112.0 6.3 %factor.7.rest_0_ = bf16[256,1280]{1,0:T(8,128)(2,1)S(1)} custom-call(s32[7]{0:T(128)S(1)} %copy-done.17, bf16[16,136,512]{2,1,0:T(8,128)(2,1)S(1)} %columns.1.own, bf16[16,136,512]{2,1,0:T(8,128)(2,1)} %collective-permute-done.6.other, bf16[16,128,128]{2,1,0:T(8,128)(2,1)} %all-to-all-done.1.rest_0_, bf16[128,512]{1,0:T(8,128)(2,1)S(1)} %copy-done.3, ...), custom_call_target="tpu_custom_call" | custom-call | bytes 5242880 | tf_op jit(solution)/shard_map/factor/pallas_call | solution.py:225
  118.3 0.2 collective-permute-start.9
  118.5 1.0 backward.3
  119.5 3.5 %collective-permute-start.10 = (f32[64,64]{1,0:T(8,128)S(1)}, f32[64,64]{1,0:T(8,128)S(1)}, u32[]{:S(2)}, u32[]{:S(2)}) collective-permute-start(f32[64,64]{1,0:T(8,128)S(1)} %get-tuple-element.30), channel_id=1, source_target_pairs={{0,240},{16,0},{32,16},{48,32},{64,48},{80,64},{96,80},{112,96},{1... | collective-permute-start | bytes 49160 | tf_op jit(solution)/shard_map/backward/ppermute | solution.py:17
  123.0 2.4 %collective-permute-start.11 = (f32[64,64]{1,0:T(8,128)S(1)}, f32[64,64]{1,0:T(8,128)S(1)}, u32[]{:S(2)}, u32[]{:S(2)}) collective-permute-start(f32[64,64]{1,0:T(8,128)S(1)} %get-tuple-element.31), channel_id=1, source_target_pairs={{0,224},{16,240},{32,0},{48,16},{64,32},{80,48},{96,64},{112,80},{... | collective-permute-start | bytes 49160 | tf_op jit(solution)/shard_map/backward/ppermute | solution.py:17
  125.3 6.1 %factor.8.a = f32[256,1280]{1,0:T(8,128)S(1)} custom-call(s32[7]{0:T(128)S(1)} %copy-done.17, bf16[16,136,512]{2,1,0:T(8,128)(2,1)S(1)} %columns.1.own, bf16[16,136,512]{2,1,0:T(8,128)(2,1)} %collective-permute-done.6.other, bf16[16,128,128]{2,1,0:T(8,128)(2,1)} %all-to-all-done.1.rest_0_, bf16[128,512]{1,0:T(8,128)(2,1)S(1)} %copy-done.4, ...), custom_call_target="tpu_custom_call" | custom-call | bytes 5242880 | tf_op jit(solution)/shard_map/factor/pallas_call | solution.py:225
  131.5 4.8 %collective-permute-done.9.b = bf16[256,1280]{1,0:T(8,128)(2,1)S(1)} collective-permute-done((bf16[256,1280]{1,0:T(8,128)(2,1)S(1)}, bf16[256,1280]{1,0:T(8,128)(2,1)S(1)}, u32[]{:S(2)}, u32[]{:S(2)}) %collective-permute-start.9) | collective-permute-done | bytes 655392 | tf_op jit(solution)/shard_map/factor/ppermute | solution.py:17
  136.2 1.5 factor.9
  137.7 0.1 collective-permute-start.12
  137.8 0.9 multiply_add_fusion.1
  138.8 0.1 pad_maximum_fusion
  138.8 0.8 broadcast_in_dim.9
  139.7 8.2 %all-to-all-start.2 = ((f32[16,64,128]{2,1,0:T(8,128)}), f32[16,64,128]{2,1,0:T(8,128)}, u32[]{:S(2)}, u32[]{:S(2)}) async-start(f32[16,64,128]{2,1,0:T(8,128)} %broadcast_in_dim.9), calls=%async_computation.2 | async-start | bytes 1048576 | tf_op jit(solution)/shard_map/backward/all_to_all | solution.py:566
  148.0 8.7 %collective-permute-done.12.came = bf16[256,1280]{1,0:T(8,128)(2,1)} collective-permute-done((bf16[256,1280]{1,0:T(8,128)(2,1)}, bf16[256,1280]{1,0:T(8,128)(2,1)}, u32[]{:S(2)}, u32[]{:S(2)}) %collective-permute-start.12) | collective-permute-done | bytes 655392 | tf_op jit(solution)/shard_map/factor/ppermute | solution.py:17
  156.7 1.8 %slice_add_fusion.mine = f32[256,512]{1,0:T(8,128)} fusion(f32[256,1280]{1,0:T(8,128)S(1)} %factor.6.rest_3_.here, bf16[256,1280]{1,0:T(8,128)(2,1)} %collective-permute-done.12.came), kind=kLoop, calls=%fused_computation | loop fusion | flops 262144 | bytes 1310720 | tf_op jit(solution)/shard_map/factor/add | solution.py:572
  158.5 5.0 %collective-permute-start.13 = (f32[256,512]{1,0:T(8,128)}, f32[256,512]{1,0:T(8,128)}, u32[]{:S(2)}, u32[]{:S(2)}) collective-permute-start(f32[256,512]{1,0:T(8,128)} %slice_add_fusion.mine), channel_id=1, source_target_pairs={{0,1},{1,0},{2,3},{3,2},{4,5},{5,4},{6,7},{7,6},{8,9},{9,8},{10,11... | collective-permute-start | bytes 1572872 | tf_op jit(solution)/shard_map/factor/ppermute | solution.py:22
  163.5 0.1 broadcast_compare_fusion
  163.6 1.5 all-to-all-done.2.after
  165.1 1.1 reduce_sum.9
  166.3 1.6 fusion.2
  167.8 2.2 %factor.10.done = f32[512,1024]{1,0:T(8,128)} custom-call(s32[7]{0:T(128)S(1)} %copy-done.17, f32[512,1024]{1,0:T(8,128)S(1)} %bitcast.17, f32[256,1280]{1,0:T(8,128)S(1)} %factor.6.rest_3_.here, bf16[256,1280]{1,0:T(8,128)(2,1)} %collective-permute-done.12.came, f32[16,64,128]{2,1,0:T(8,128)} %all-to-all-done.2.after), custom_call_target="tpu_custom_call" | custom-call | bytes 2359296 | tf_op jit(solution)/shard_map/factor/pallas_call | solution.py:225
  170.1 2.4 %factor.11 = f32[512,1024]{1,0:T(8,128)} custom-call(s32[7]{0:T(128)S(1)} %copy-done.17, f32[512,1024]{1,0:T(8,128)S(1)} %bitcast.18, f32[256,512]{1,0:T(8,128)} %slice_add_fusion.mine, f32[256,512]{1,0:T(8,128)} %collective-permute-done.13.sib, f32[512,1024]{1,0:T(8,128)} %factor.10.done), custom_call_target="tpu_custom_call", output_to_operand_aliasing={{}: (4, {})} | custom-call | bytes 1572864 | tf_op jit(solution)/shard_map/factor/pallas_call | solution.py:225
  (55 shorter events, 0.3 us)
Async XLA Ops:
  9.8 8.7 %copy-start.21 = (bf16[64,5120]{1,0:T(8,128)(2,1)S(1)}, bf16[64,5120]{1,0:T(8,128)(2,1)}, u32[]{:S(2)}) copy-start(bf16[64,5120]{1,0:T(8,128)(2,1)} %get-tuple-element.17.after) | copy-start | bytes 1966084
  9.8 14.4 %copy-start.22 = (bf16[64,4096]{1,0:T(8,128)(2,1)S(1)}, bf16[64,4096]{1,0:T(8,128)(2,1)}, u32[]{:S(2)}) copy-start(bf16[64,4096]{1,0:T(8,128)(2,1)} %get-tuple-element.22) | copy-start | bytes 1572868
  9.8 65.3 %all-to-all-start = ((bf16[16,136,512]{2,1,0:T(8,128)(2,1)}), bf16[16,136,512]{2,1,0:T(8,128)(2,1)S(1)}, u32[]{:S(2)}, u32[]{:S(2)}) async-start(bf16[16,136,512]{2,1,0:T(8,128)(2,1)} %get-tuple-element.18), calls=%async_computation | async-start | bytes 4456448 | tf_op jit(solution)/shard_map/columns/all_to_all | solution.py:528
  18.5 30.3 %collective-permute-start = (bf16[64,5120]{1,0:T(8,128)(2,1)S(1)}, bf16[64,5120]{1,0:T(8,128)(2,1)S(1)}, u32[]{:S(2)}, u32[]{:S(2)}) collective-permute-start(bf16[64,5120]{1,0:T(8,128)(2,1)S(1)} %copy-done.21), channel_id=1, source_target_pairs={{0,240},{16,0},{32,16},{48,32},{64,48},{80,64},{96,80},{112,96},{1... | collective-permute-start | bytes 1966088 | tf_op jit(solution)/shard_map/weights/ppermute | solution.py:17
  24.2 41.7 %collective-permute-start.2 = (bf16[64,4096]{1,0:T(8,128)(2,1)}, bf16[64,4096]{1,0:T(8,128)(2,1)}, u32[]{:S(2)}, u32[]{:S(2)}) collective-permute-start(bf16[64,4096]{1,0:T(8,128)(2,1)} %get-tuple-element.21), channel_id=1, source_target_pairs={{0,16},{16,32},{32,48},{48,64},{64,80},{80,96},{96,112},{112,128},... | collective-permute-start | bytes 1572872 | tf_op jit(solution)/shard_map/weights/ppermute | solution.py:17
  24.2 43.7 %collective-permute-start.4 = (bf16[64,4096]{1,0:T(8,128)(2,1)S(1)}, bf16[64,4096]{1,0:T(8,128)(2,1)}, u32[]{:S(2)}, u32[]{:S(2)}) collective-permute-start(bf16[64,4096]{1,0:T(8,128)(2,1)S(1)} %copy-done.22), channel_id=1, source_target_pairs={{0,32},{16,48},{32,64},{48,80},{64,96},{80,112},{96,128},{112,144}... | collective-permute-start | bytes 1572872 | tf_op jit(solution)/shard_map/weights/ppermute | solution.py:17
  48.8 19.1 %copy-start.19 = (bf16[64,5120]{1,0:T(8,128)(2,1)}, bf16[64,5120]{1,0:T(8,128)(2,1)S(1)}, u32[]{:S(2)}) copy-start(bf16[64,5120]{1,0:T(8,128)(2,1)S(1)} %collective-permute-done.dm.u1o.u1s.refs_14_) | copy-start | bytes 1966084
  48.8 19.2 %collective-permute-start.1 = (bf16[64,5120]{1,0:T(8,128)(2,1)S(1)}, bf16[64,5120]{1,0:T(8,128)(2,1)S(1)}, u32[]{:S(2)}, u32[]{:S(2)}) collective-permute-start(bf16[64,5120]{1,0:T(8,128)(2,1)S(1)} %collective-permute-done.dm.u1o.u1s.refs_14_), channel_id=1, source_target_pairs={{0,1},{1,0},{2,3},{3,2},{4,5},{5,4},{6,7},{7,6},{8,9},{9,8},{10,11... | collective-permute-start | bytes 1966088 | tf_op jit(solution)/shard_map/weights/ppermute | solution.py:22
  65.9 9.2 %collective-permute-start.3 = (bf16[64,4096]{1,0:T(8,128)(2,1)}, bf16[64,4096]{1,0:T(8,128)(2,1)S(1)}, u32[]{:S(2)}, u32[]{:S(2)}) collective-permute-start(bf16[64,4096]{1,0:T(8,128)(2,1)} %collective-permute-done.2.refs_10_), channel_id=1, source_target_pairs={{0,1},{1,0},{2,3},{3,2},{4,5},{5,4},{6,7},{7,6},{8,9},{9,8},{10,11... | collective-permute-start | bytes 1572872 | tf_op jit(solution)/shard_map/weights/ppermute | solution.py:22
  67.9 7.2 %collective-permute-start.5 = (bf16[64,4096]{1,0:T(8,128)(2,1)}, bf16[64,4096]{1,0:T(8,128)(2,1)S(1)}, u32[]{:S(2)}, u32[]{:S(2)}) collective-permute-start(bf16[64,4096]{1,0:T(8,128)(2,1)} %collective-permute-done.4.refs_12_), channel_id=1, source_target_pairs={{0,1},{1,0},{2,3},{3,2},{4,5},{5,4},{6,7},{7,6},{8,9},{9,8},{10,11... | collective-permute-start | bytes 1572872 | tf_op jit(solution)/shard_map/weights/ppermute | solution.py:22
  68.0 0.8 copy-start.20
  75.0 0.8 copy-start.1
  75.0 1.0 copy-start.2
  76.0 24.5 %collective-permute-start.6 = (bf16[16,136,512]{2,1,0:T(8,128)(2,1)S(1)}, bf16[16,136,512]{2,1,0:T(8,128)(2,1)}, u32[]{:S(2)}, u32[]{:S(2)}) collective-permute-start(bf16[16,136,512]{2,1,0:T(8,128)(2,1)S(1)} %columns.1.own), channel_id=1, source_target_pairs={{0,1},{1,0},{2,3},{3,2},{4,5},{5,4},{6,7},{7,6},{8,9},{9,8},{10,11... | collective-permute-start | bytes 6684680 | tf_op jit(solution)/shard_map/columns/ppermute | solution.py:22
  76.5 32.0 %all-to-all-start.1 = ((bf16[16,128,128]{2,1,0:T(8,128)(2,1)}), bf16[16,128,128]{2,1,0:T(8,128)(2,1)}, u32[]{:S(2)}, u32[]{:S(2)}) async-start(bf16[16,128,128]{2,1,0:T(8,128)(2,1)} %gates.3.rest_0_), calls=%async_computation.1 | async-start | bytes 1048576 | tf_op jit(solution)/shard_map/columns/all_to_all | solution.py:530
  82.8 17.8 %copy-start.17 = (s32[7]{0:T(128)S(1)}, s32[7]{0:T(128)}, u32[]{:S(2)}) copy-start(s32[7]{0:T(128)} %stack.53.where) | copy-start | bytes 88
  90.3 17.0 %collective-permute-start.7 = (f32[128,128]{1,0:T(8,128)}, f32[128,128]{1,0:T(8,128)S(1)}, u32[]{:S(2)}, u32[]{:S(2)}) collective-permute-start(f32[128,128]{1,0:T(8,128)} %get-tuple-element.27), channel_id=1, source_target_pairs={{0,16},{16,32},{32,48},{48,64},{64,80},{80,96},{96,112},{112,128},... | collective-permute-start | bytes 196616 | tf_op jit(solution)/shard_map/backward/ppermute | solution.py:17
  100.6 7.3 %collective-permute-start.8 = (f32[128,128]{1,0:T(8,128)}, f32[128,128]{1,0:T(8,128)S(1)}, u32[]{:S(2)}, u32[]{:S(2)}) collective-permute-start(f32[128,128]{1,0:T(8,128)} %get-tuple-element.28), channel_id=1, source_target_pairs={{0,32},{16,48},{32,64},{48,80},{64,96},{80,112},{96,128},{112,144}... | collective-permute-start | bytes 196616 | tf_op jit(solution)/shard_map/backward/ppermute | solution.py:17
  100.6 0.9 copy-start.7
  107.2 0.6 copy-start.9
  107.9 0.6 copy-start.11
  108.5 0.9 copy-start.3
  109.4 0.9 copy-start.5
  110.3 0.8 copy-start.10
  111.2 0.8 copy-start.12
  112.0 6.5 %copy-start.6 = (f32[1,3,64,128]{3,2,1,0:T(8,128)S(1)}, f32[1,3,64,128]{3,2,1,0:T(8,128)}, u32[]{:S(2)}) copy-start(f32[1,3,64,128]{3,2,1,0:T(8,128)} %q0.1) | copy-start | bytes 294916
  112.0 6.5 %copy-start.8 = (f32[192,128]{1,0:T(8,128)S(1)}, f32[192,128]{1,0:T(8,128)}, u32[]{:S(2)}) copy-start(f32[192,128]{1,0:T(8,128)} %get-tuple-element.23.rest_0_.proj) | copy-start | bytes 294916
  112.0 6.5 %copy-start.18 = (f32[128,64]{1,0:T(8,128)S(1)}, f32[128,64]{1,0:T(8,128)}, u32[]{:S(2)}) copy-start(f32[128,64]{1,0:T(8,128)} %get-tuple-element.26.m0) | copy-start | bytes 98308
  112.0 13.3 %copy-start.4 = (bf16[128,512]{1,0:T(8,128)(2,1)S(1)}, bf16[128,512]{1,0:T(8,128)(2,1)}, u32[]{:S(2)}) copy-start(bf16[128,512]{1,0:T(8,128)(2,1)} %get-tuple-element.24.rest_1_) | copy-start | bytes 393220
  118.3 18.0 %collective-permute-start.9 = (bf16[256,1280]{1,0:T(8,128)(2,1)S(1)}, bf16[256,1280]{1,0:T(8,128)(2,1)S(1)}, u32[]{:S(2)}, u32[]{:S(2)}) collective-permute-start(bf16[256,1280]{1,0:T(8,128)(2,1)S(1)} %factor.7.rest_0_), channel_id=1, source_target_pairs={{0,16},{16,32},{32,48},{48,64},{64,80},{80,96},{96,112},{112,128},... | collective-permute-start | bytes 1966088 | tf_op jit(solution)/shard_map/factor/ppermute | solution.py:17
  119.5 11.9 %copy-start.13 = (f32[64,64]{1,0:T(8,128)}, f32[64,64]{1,0:T(8,128)S(1)}, u32[]{:S(2)}) copy-start(f32[64,64]{1,0:T(8,128)S(1)} %get-tuple-element.29.rest_3_) | copy-start | bytes 49156
  119.5 11.9 %collective-permute-start.10 = (f32[64,64]{1,0:T(8,128)S(1)}, f32[64,64]{1,0:T(8,128)S(1)}, u32[]{:S(2)}, u32[]{:S(2)}) collective-permute-start(f32[64,64]{1,0:T(8,128)S(1)} %get-tuple-element.30), channel_id=1, source_target_pairs={{0,240},{16,0},{32,16},{48,32},{64,48},{80,64},{96,80},{112,96},{1... | collective-permute-start | bytes 49160 | tf_op jit(solution)/shard_map/backward/ppermute | solution.py:17
  123.0 8.5 %collective-permute-start.11 = (f32[64,64]{1,0:T(8,128)S(1)}, f32[64,64]{1,0:T(8,128)S(1)}, u32[]{:S(2)}, u32[]{:S(2)}) collective-permute-start(f32[64,64]{1,0:T(8,128)S(1)} %get-tuple-element.31), channel_id=1, source_target_pairs={{0,224},{16,240},{32,0},{48,16},{64,32},{80,48},{96,64},{112,80},{... | collective-permute-start | bytes 49160 | tf_op jit(solution)/shard_map/backward/ppermute | solution.py:17
  131.4 6.3 %copy-start.15 = (f32[64,64]{1,0:T(8,128)}, f32[64,64]{1,0:T(8,128)S(1)}, u32[]{:S(2)}) copy-start(f32[64,64]{1,0:T(8,128)S(1)} %collective-permute-done.10.rest_0_) | copy-start | bytes 49156
  131.5 6.4 %copy-start.14 = (f32[64,64]{1,0:T(8,128)S(1)}, f32[64,64]{1,0:T(8,128)}, u32[]{:S(2)}) copy-start(f32[64,64]{1,0:T(8,128)} %copy-done.13) | copy-start | bytes 49156
  131.5 6.3 %copy-start.16 = (f32[64,64]{1,0:T(8,128)}, f32[64,64]{1,0:T(8,128)S(1)}, u32[]{:S(2)}) copy-start(f32[64,64]{1,0:T(8,128)S(1)} %collective-permute-done.11.rest_1_) | copy-start | bytes 49156
  137.7 30.1 %copy-start = (f32[1,512,1024]{2,1,0:T(8,128)S(1)}, f32[1,512,1024]{2,1,0:T(8,128)}, u32[]{:S(2)}) copy-start(f32[1,512,1024]{2,1,0:T(8,128)} %param.14) | copy-start | bytes 6291460
  137.7 18.9 %collective-permute-start.12 = (bf16[256,1280]{1,0:T(8,128)(2,1)}, bf16[256,1280]{1,0:T(8,128)(2,1)}, u32[]{:S(2)}, u32[]{:S(2)}) collective-permute-start(bf16[256,1280]{1,0:T(8,128)(2,1)} %factor.9), channel_id=1, source_target_pairs={{0,16},{16,32},{32,48},{48,64},{64,80},{80,96},{96,112},{112,128},... | collective-permute-start | bytes 1966088 | tf_op jit(solution)/shard_map/factor/ppermute | solution.py:17
  139.7 25.4 %all-to-all-start.2 = ((f32[16,64,128]{2,1,0:T(8,128)}), f32[16,64,128]{2,1,0:T(8,128)}, u32[]{:S(2)}, u32[]{:S(2)}) async-start(f32[16,64,128]{2,1,0:T(8,128)} %broadcast_in_dim.9), calls=%async_computation.2 | async-start | bytes 1048576 | tf_op jit(solution)/shard_map/backward/all_to_all | solution.py:566
  158.5 11.6 %collective-permute-start.13 = (f32[256,512]{1,0:T(8,128)}, f32[256,512]{1,0:T(8,128)}, u32[]{:S(2)}, u32[]{:S(2)}) collective-permute-start(f32[256,512]{1,0:T(8,128)} %slice_add_fusion.mine), channel_id=1, source_target_pairs={{0,1},{1,0},{2,3},{3,2},{4,5},{5,4},{6,7},{7,6},{8,9},{9,8},{10,11... | collective-permute-start | bytes 1572872 | tf_op jit(solution)/shard_map/factor/ppermute | solution.py:22

commit v5 on v4

--- a/solution.py
+++ b/solution.py
@@ -22,6 +22,11 @@
     return lax.ppermute(block, "dp", [(i, i ^ 1) for i in range(count)])
 
 
+def swap_chips(block):
+    count = lax.axis_size("dp")
+    return lax.ppermute(block, "dp", [(i, i ^ 4) for i in range(count)])
+
+
 def nt(a, b):
     return lax.dot_general(a, b, (((1,), (1,)), ((), ())), preferred_element_type=F32)
 
@@ -30,7 +35,7 @@
     return lax.dot_general(a, b, (((0,), (0,)), ((), ())), preferred_element_type=F32)
 
 
-def call(kernel, where, operands, in_specs, outs, out_specs, grid, scratch, cost, aliases={}):
+def call(kernel, where, operands, in_specs, outs, out_specs, grid, scratch=(), aliases={}):
     spec = pltpu.PrefetchScalarGridSpec(
         num_scalar_prefetch=1,
         grid=grid,
@@ -38,14 +43,13 @@
         out_specs=out_specs,
         scratch_shapes=list(scratch),
     )
-    flops, moved = cost
     return pl.pallas_call(
         kernel,
         grid_spec=spec,
         out_shape=outs,
         input_output_aliases=aliases,
         compiler_params=pltpu.CompilerParams(dimension_semantics=("arbitrary",) * len(grid)),
-        cost_estimate=pl.CostEstimate(flops=flops, transcendentals=0, bytes_accessed=moved),
+        cost_estimate=pl.CostEstimate(flops=0, transcendentals=0, bytes_accessed=0),
     )(where, *operands)
 
 
@@ -66,10 +70,10 @@
     )(x, *after)
 
 
-CHIP, CORE, SEC, C0, F1, B1, B2 = range(7)
-
-
-def split_kernel(where, x, down, ids, after, out, gate, acc):
+CHIP, CORE, SEC, C0, F1, B1, B2, PAIR = range(8)
+
+
+def split_kernel(where, x, down, ids, out, gate, acc):
     i = pl.program_id(0)
     pieces, _, cols = out.shape
     tok, rank = gate.shape
@@ -92,7 +96,7 @@
         gate[...] = (z * jax.nn.sigmoid(z)).astype(BF16)
 
 
-def split(where, x, adapter_down, doc_ids, pieces, extra, after):
+def split(where, x, adapter_down, doc_ids, pieces, extra):
     tok, width = x.shape
     rank = adapter_down.shape[2]
     cols = width // pieces
@@ -101,12 +105,11 @@
     return call(
         split_kernel,
         where,
-        (x, adapter_down, doc_ids, after),
+        (x, adapter_down, doc_ids),
         [
             pl.BlockSpec((tok, each), lambda i, w: (0, i)),
             pl.BlockSpec((1, 1, rank, each), lambda i, w: (w[C0], 0, 0, i)),
             pl.BlockSpec(doc_ids.shape, lambda i, w: (0, 0)),
-            ANY,
         ],
         [
             jax.ShapeDtypeStruct((pieces, tok + extra, cols), BF16),
@@ -118,11 +121,10 @@
         ],
         (grid,),
         [pltpu.VMEM((tok, rank), F32)],
-        (2 * x.size * rank, 5 * x.size),
-    )
-
-
-def pack_kernel(where, up_f, down_f, up_b1, up_b2, ahead, behind1, behind2):
+    )
+
+
+def pack_kernel(where, up_f, down_f, up_b1, up_b2, after, ahead, behind1, behind2):
     cols = up_f.shape[3]
     ahead[:, :cols] = up_f[0, 0]
     ahead[:, cols:] = down_f[0, 0]
@@ -130,31 +132,32 @@
     behind2[...] = up_b2[0, 0]
 
 
-def pack(where, adapter_down, adapter_up, block):
+def pack(where, adapter_down, adapter_up, block, after):
     rank, width = adapter_down.shape[2:]
     half = width // 2
-    part = lambda span: pl.BlockSpec((1, 1, rank, half), lambda i, w: (w[span], 0, 0, w[CORE]))
-    shapes = ((rank, block + half), (rank, half), (rank, half))
+    part = lambda span: pl.BlockSpec(
+        (1, 1, rank, half // 2), lambda i, w: (w[span], 0, 0, 2 * w[CORE] + w[PAIR])
+    )
+    shapes = ((rank, block + half), (rank, half // 2), (rank, half // 2))
     return call(
         pack_kernel,
         where,
-        (adapter_up, adapter_down, adapter_up, adapter_up),
+        (adapter_up, adapter_down, adapter_up, adapter_up, after),
         [
             pl.BlockSpec((1, 1, rank, block), lambda i, w: (w[F1], 0, 0, w[CHIP])),
-            part(F1),
+            pl.BlockSpec((1, 1, rank, half), lambda i, w: (w[F1], 0, 0, w[CORE])),
             part(B1),
             part(B2),
+            pl.BlockSpec(after.shape, lambda i, w: (0, 0)),
         ],
         [jax.ShapeDtypeStruct(shape, BF16) for shape in shapes],
         [pl.BlockSpec(shape, lambda i, w: (0, 0)) for shape in shapes],
         (1,),
-        (),
-        (0, 8 * rank * half * 2),
     )
 
 
 def gate_kernel(
-    where, xm, xs, um, us, dm, ds, gate0, u0o, u0s, u1o, u1s, sent, ups_o, ups_s, acc
+    where, xm, xs, um, us, dm, ds, gate0, u0o, u0s, u1o, u1s, after, sent, ups_o, ups_s, acc
 ):
     i = pl.program_id(0)
     rank = gate0.shape[1]
@@ -179,7 +182,7 @@
             sent[k] = both
 
 
-def gates(where, x, adapter_up, ahead_mine, ahead_sib, gate0, replicas, rows):
+def gates(where, x, adapter_up, ahead_mine, ahead_sib, gate0, replicas, rows, after):
     tok, width = x.shape
     rank = gate0.shape[1]
     each = ahead_mine.shape[1] - width // 2
@@ -200,12 +203,13 @@
         where,
         (
             x, x, adapter_up, adapter_up, ahead_mine, ahead_sib, gate0,
-            adapter_up, adapter_up, ahead_mine, ahead_mine,
+            adapter_up, adapter_up, ahead_mine, ahead_mine, after,
         ),
         [
             x_spec(mine), x_spec(sib), u_spec(mine), u_spec(sib), d_spec, d_spec,
             pl.BlockSpec((tok, rank), lambda i, w: (0, 0)),
             u0(mine), u0(sib), u1(mine), u1(sib),
+            pl.BlockSpec((16, 128), lambda i, w: (0, 0)),
         ],
         [jax.ShapeDtypeStruct(shape, BF16) for shape in shapes],
         [
@@ -215,7 +219,6 @@
         ],
         (grid,),
         [pltpu.VMEM((tok, rank), F32)],
-        (4 * x.size * rank, 5 * x.size),
     )
 
 
@@ -226,16 +229,24 @@
         kernel,
         in_specs=[pl.BlockSpec(memory_space=pltpu.SMEM)]
         + [vmem] * len(operands)
-        + [ANY] * len(after),
+        + [vmem] * len(after),
         out_specs=out_specs or out_vmem,
         out_shape=outs,
         scratch_shapes=list(scratch),
         input_output_aliases=aliases,
         compiler_params=pltpu.CompilerParams(vmem_limit_bytes=24 << 20),
-        cost_estimate=pl.CostEstimate(
-            flops=0, transcendentals=0, bytes_accessed=2 * sum(x.size for x in operands)
-        ),
+        cost_estimate=pl.CostEstimate(flops=0, transcendentals=0, bytes_accessed=0),
     )(where, *operands, *after)
+
+
+def join_kernel(where, a, b, out):
+    out[:a.shape[0]] = a[...]
+    out[a.shape[0]:] = b[...]
+
+
+def join(where, a, b):
+    shape = (a.shape[0] + b.shape[0], a.shape[1])
+    return local(join_kernel, where, (a, b), jax.ShapeDtypeStruct(shape, a.dtype))
 
 
 def scale_columns(own, tok):
@@ -261,9 +272,9 @@
     hlf = rows // 2
     per = 4
     if step == 2:
-        out, acc = rest[-2:]
+        out, token, acc = rest[-3:]
     else:
-        out = acc = rest[-1]
+        acc, token = rest[-2:]
     columns = scale_columns(own, tok)
 
     for i in range(replicas // per):
@@ -279,24 +290,29 @@
             scale = [jnp.broadcast_to(columns[:, k:k + 1], (tok, rows)) for k in ks]
             return (jnp.concatenate(scale, axis=0) * act).astype(BF16)
 
-        def put(lo, hi, val):
+        def put(lo, val):
+            hi = lo + val.shape[1]
             acc[:, lo:hi] = val if i == 0 else acc[:, lo:hi] + val
 
         r = rebuilt(own, ups_own if step else None)
         q = rebuilt(other, ups_oth if step else None)
-        put(0, rows, tn(r[:, :hlf], r))
-        put(rows, rows + hlf, tn(r[:, hlf:], r[:, hlf:]))
+        put(0, tn(r[:, :hlf], r))
+        put(rows, tn(r[:, hlf:], r[:, hlf:]))
 
         @pl.when(core == 0)
         def _():
-            put(rows + hlf, 2 * rows + hlf, tn(r[:, :hlf], q))
+            put(rows + hlf, tn(r[:, :hlf], q))
 
         @pl.when(core == 1)
         def _():
-            put(rows + hlf, 2 * rows + hlf, tn(q[:, hlf:], r))
-
+            put(rows + hlf, tn(q[:, hlf:], r))
+
+    token[...] = jnp.zeros_like(token)
     if step == 2:
         out[...] = acc[...].astype(BF16)
+
+
+TOKEN = jax.ShapeDtypeStruct((8, 128), F32)
 
 
 def gram(step, where, own, other, ups=(), after=()):
@@ -306,14 +322,14 @@
         functools.partial(gram_kernel, step),
         where,
         (own, other, *ups),
-        jax.ShapeDtypeStruct(packed, BF16 if step == 2 else F32),
+        [jax.ShapeDtypeStruct(packed, BF16 if step == 2 else F32), TOKEN],
         [pltpu.VMEM(packed, F32)] if step == 2 else [],
         after,
     )
 
 
 def project_kernel(where, *refs):
-    ins, stash, (proj, m0, by1, by2) = refs[:16], refs[16], refs[17:]
+    ins, stash, (proj, m0, by1, by2) = refs[:14], refs[14], refs[16:]
     i = pl.program_id(0)
     rank = stash.shape[2]
 
@@ -324,16 +340,16 @@
         by1[:rank] = stash[0, 1]
         by2[:rank] = stash[0, 2]
 
-    for g, u, d, d1, u2, b1, b2, a in (ins[0::2], ins[1::2]):
-        two = jnp.concatenate([b1[...], b2[...]], axis=0)
+    for g, u, d, d1, u2, b, a in (ins[0::2], ins[1::2]):
+        two = b[...]
         proj[:rank] += nt(u[0, 0], g[...])
         proj[rank:] += nt(two, g[...])
         m0[...] += nt(two, d[0, 0])
-        by1[rank:, :rank] += nt(b1[...], d1[0, 0])
+        by1[rank:, :rank] += nt(b[:rank], d1[0, 0])
         by2[rank:, :rank] += nt(u2[0, 0], a[...])
 
 
-def project(where, grad, adapter_down, adapter_up, b1, b1s, b2, b2s, ahead, ahead_sib, stashed):
+def project(where, grad, adapter_down, adapter_up, b, b_sib, ahead, ahead_sib, stashed, after):
     tok, width = grad.shape
     rank = adapter_up.shape[2]
     each = ahead.shape[1] - width // 2
@@ -350,6 +366,8 @@
 
     g_spec = lambda side: pl.BlockSpec((tok, each), lambda i, w: (0, side(w) * grid + i))
     got = lambda skip: pl.BlockSpec((rank, each), lambda i, w: (0, i + skip))
+    per = grid // 2
+    quarter = pl.BlockSpec((2 * rank, each), lambda i, w: ((i // per + w[PAIR]) % 2, i % per))
     one = lambda w: 1
     shapes = ((3 * rank, tok), (2 * rank, rank), (2 * rank, tok), (2 * rank, tok))
     return call(
@@ -358,21 +376,20 @@
         (
             grad, grad, adapter_up, adapter_up, adapter_down, adapter_down,
             adapter_down, adapter_down, adapter_up, adapter_up,
-            b1, b1s, b2, b2s, ahead, ahead_sib, stashed,
+            b, b_sib, ahead, ahead_sib, stashed, after,
         ),
         [g_spec(mine), g_spec(sib)]
         + weights(one)
         + weights(one)
         + weights(lambda w: w[B1])
         + weights(lambda w: w[B2])
-        + [got(0)] * 4
+        + [quarter] * 2
         + [got(1)] * 2
-        + [pl.BlockSpec(stashed.shape, lambda i, w: (0, 0, 0, 0))],
+        + [pl.BlockSpec(stashed.shape, lambda i, w: (0, 0, 0, 0))]
+        + [pl.BlockSpec(after.shape, lambda i, w: (0, 0))],
         [jax.ShapeDtypeStruct(shape, F32) for shape in shapes],
         [pl.BlockSpec(shape, lambda i, w: (0, 0)) for shape in shapes],
         (grid,),
-        (),
-        (14 * grad.size * rank, 12 * grad.size),
     )
 
 
@@ -409,12 +426,59 @@
     )
 
 
-def merge_kernel(where, a, b, *rest):
-    rest[-1][...] = (a[...] + b[...].astype(F32)).astype(BF16)
+def merge_kernel(where, a, b, after, out, token):
+    out[...] = (a[...] + b[...].astype(F32)).astype(BF16)
+    token[...] = jnp.zeros_like(token)
 
 
 def merge(where, a, b, after):
-    return local(merge_kernel, where, (a, b), jax.ShapeDtypeStruct(a.shape, BF16), (), after)
+    return local(
+        merge_kernel, where, (a, b), [jax.ShapeDtypeStruct(a.shape, BF16), TOKEN], (), (after,)
+    )
+
+
+def curvature_kernel(where, outer0, outer1, outer2, out, token):
+    rank = outer0.shape[0]
+    f1 = where[B1].astype(F32)
+    f2 = where[B2].astype(F32)
+    zero = outer1[...] * (1.0 - f1) + outer2[...] * (1.0 - f2)
+    one = outer0[...] + outer1[...] * f1 + outer2[...] * f2
+    both = jnp.concatenate([zero, one], axis=1)
+    for k in range(out.shape[0]):
+        out[k] = both
+    token[...] = jnp.zeros_like(token)
+
+
+def curvature(where, outers, replicas):
+    rank = outers[0].shape[0]
+    return local(
+        curvature_kernel, where, outers,
+        [jax.ShapeDtypeStruct((replicas, rank, 2 * rank), F32), TOKEN],
+    )
+
+
+def statistics_kernel(tokens, where, old, parts, after, out):
+    rank = old.shape[2]
+    total = parts[0]
+    for k in range(1, parts.shape[0]):
+        total = total + parts[k]
+    later = where[B1] + where[B2]
+    for span, held in enumerate((2 - later, 1 + later)):
+        held = jnp.full((rank, rank), held.astype(F32), F32)
+        was = old[span, 0]
+        share = total[:, span * rank:(span + 1) * rank] / (jnp.maximum(held, 1.0) * tokens)
+        out[span, 0] = jnp.where(held > 0.0, 0.75 * was + 0.25 * share, was)
+
+
+def statistics(where, old, parts, tokens, after):
+    return local(
+        functools.partial(statistics_kernel, tokens),
+        where,
+        (old, parts),
+        jax.ShapeDtypeStruct(old.shape, F32),
+        (),
+        (after,),
+    )
 
 
 def put_rows(factor_scale, old, out, buf, sems, first_col, pieces):
@@ -436,6 +500,19 @@
         copy.wait()
 
 
+def add_kernel(cut, where, here, came, after, out):
+    out[...] = here[:, cut:] + came[:, cut:].astype(F32)
+
+
+def cross_part(where, here, came, after):
+    hlf, width = here.shape
+    cut = 3 * hlf
+    return local(
+        functools.partial(add_kernel, cut), where, (here, came),
+        jax.ShapeDtypeStruct((hlf, width - cut), F32), (), (after,),
+    )
+
+
 def square_kernel(factor_scale, where, old, here, came, after, out, buf, sems):
     hlf = here.shape[0]
     rows = 2 * hlf
@@ -452,7 +529,7 @@
     )
 
 
-def cross_kernel(factor_scale, where, old, mine, sib, done, out, buf, sems):
+def cross_kernel(factor_scale, where, old, mine, sib, done, out, token, buf, sems):
     core = where[CORE]
     hlf, rows = mine.shape
 
@@ -471,19 +548,28 @@
             )
         )
 
+    token[...] = jnp.zeros_like(token)
+
 
 def update(factor_scale, where, old, here, came, mine, sib, after):
     total = old.shape[0]
     shape = jax.ShapeDtypeStruct(old.shape, F32)
     scratch = [pltpu.VMEM((total, total), F32), pltpu.SemaphoreType.DMA((2,))]
+    vmem = pl.BlockSpec(memory_space=pltpu.VMEM)
     done = local(
         functools.partial(square_kernel, factor_scale), where, (old, here, came), shape, scratch,
         (after,), out_specs=ANY,
     )
-    return local(
-        functools.partial(cross_kernel, factor_scale), where, (old, mine, sib), shape, scratch,
-        (done,), {4: 0}, ANY,
-    )
+    return pl.pallas_call(
+        functools.partial(cross_kernel, factor_scale),
+        in_specs=[pl.BlockSpec(memory_space=pltpu.SMEM)] + [vmem] * 3 + [ANY],
+        out_specs=[ANY, vmem],
+        out_shape=[shape, TOKEN],
+        scratch_shapes=scratch,
+        input_output_aliases={4: 0},
+        compiler_params=pltpu.CompilerParams(vmem_limit_bytes=24 << 20),
+        cost_estimate=pl.CostEstimate(flops=0, transcendentals=0, bytes_accessed=0),
+    )(where, old, mine, sib, done)
 
 
 def shards(
@@ -506,23 +592,24 @@
     f1 = first((sec + sections - 1) % sections) + (sec == 0).astype(jnp.int32)
     b1 = (sec + 1 < sections).astype(jnp.int32)
     b2 = (sec + 2 < sections).astype(jnp.int32)
-    where = jnp.stack([rep // 2, rep % 2, sec, first(sec), f1, b1, b2]).astype(jnp.int32)
+    where = jnp.stack(
+        [rep // 2, rep % 2, sec, first(sec), f1, b1, b2, rep // 4 % 2]
+    ).astype(jnp.int32)
 
     with jax.named_scope("weights"):
-        ahead, behind1, behind2 = pack(where, adapter_down, adapter_up, block)
-        pieces, gate0 = split(where, x0, adapter_down, doc_ids, replicas, 8, ahead)
+        pieces, gate0 = split(where, x0, adapter_down, doc_ids, replicas, 8)
+        ahead, behind1, behind2 = pack(where, adapter_down, adapter_up, block, gate0)
         ahead = shift(ahead, "section", -1)
         ahead_sib = swap_cores(ahead)
-        behind1 = shift(behind1, "section", 1)
-        behind2 = shift(behind2, "section", 2)
-        behind1_sib = swap_cores(behind1)
-        behind2_sib = swap_cores(behind2)
+        behind = join(
+            where, shift(behind1, "section", 1), shift(behind2, "section", 2)
+        )
+        behind_pair = swap_chips(behind)
 
     with jax.named_scope("gates"):
         sent, ups_own, ups_oth = gates(
-            where, x0, adapter_up, ahead, ahead_sib, gate0, replicas, rows
+            where, x0, adapter_up, ahead, ahead_sib, gate0, replicas, rows, behind_pair
         )
-        sent = tie(sent, behind1_sib, behind2_sib)
 
     with jax.named_scope("columns"):
         own = tie(lax.all_to_all(pieces, "dp", 0, 0), sent, space=pltpu.VMEM)
@@ -530,62 +617,42 @@
         got = lax.all_to_all(sent, "dp", 0, 0)
 
     with jax.named_scope("backward"):
+        behind = join(where, behind, behind_pair)
+        behind_sib = swap_cores(behind)
         proj, m0, by1, by2 = project(
-            where, returning[0], adapter_down, adapter_up, behind1, behind1_sib, behind2,
-            behind2_sib, ahead, ahead_sib, stashed,
+            where, returning[0], adapter_down, adapter_up, behind, behind_sib, ahead, ahead_sib,
+            stashed, gate0,
         )
         by1 = shift(by1, "section", 1)
         by2 = shift(by2, "section", 2)
 
     with jax.named_scope("factor"):
         ups = (got, ups_own, ups_oth)
-        step0 = gram(0, where, own, other, (), (proj,))
-        step2 = gram(2, where, own, other, ups, (step0, by1, by2))
+        step2, token2 = gram(2, where, own, other, ups, (by1, by2))
         from2 = shift(step2, "section", 1)
+        step1, token1 = gram(1, where, own, other, ups, (token2,))
 
     with jax.named_scope("backward"):
-        outer0, outer1, outer2 = back(where, proj, m0, by1, by2, stashed, step2)
-
+        outer0, outer1, outer2 = back(where, proj, m0, by1, by2, stashed, token1)
         outer1 = shift(outer1, "section", -1)
         outer2 = shift(outer2, "section", -2)
+        share, token4 = curvature(where, (outer0, outer1, outer2), replicas)
+        shares = lax.all_to_all(share, "dp", 0, 0)
 
     with jax.named_scope("factor"):
-        step1 = gram(1, where, own, other, ups, (outer0,))
-        from1 = shift(merge(where, step1, from2, (outer1, outer2)), "section", 1)
-
-    with jax.named_scope("backward"):
-        g1 = b1.astype(F32)
-        g2 = b2.astype(F32)
-        curv = jnp.concatenate(
-            [
-                outer1 * (1.0 - g1) + outer2 * (1.0 - g2),
-                outer0 + outer1 * g1 + outer2 * g2,
-            ],
-            axis=1,
-        )
-        curv_all = lax.all_to_all(
-            jnp.broadcast_to(curv[None], (replicas,) + curv.shape), "dp", 0, 0
-        )
-
-    with jax.named_scope("factor"):
-        cut = rows + rows // 2
-        mine = step0[:, cut:] + from1[:, cut:].astype(F32)
+        from1, token3 = merge(where, step1, from2, token4)
+        from1 = shift(from1, "section", 1)
+        step0, _ = gram(0, where, own, other, (), (token3,))
+        mine = cross_part(where, step0, from1, shares)
         sib = swap_cores(mine)
         factor_scale = 0.25 / (steps_count * tokens)
-        input_factor_new = update(
-            factor_scale, where, input_factor[0], step0, from1, mine, sib, curv_all
-        )[None]
+        input_factor_new, last = update(
+            factor_scale, where, input_factor[0], step0, from1, mine, sib, shares
+        )
 
     with jax.named_scope("backward"):
-        curv_total = jnp.sum(curv_all, axis=0)
-        curv_total = jnp.stack([curv_total[:, :rank], curv_total[:, rank:]])
-        step_totals = jnp.stack([2.0 - g1 - g2, 1.0 + g1 + g2])
-        divisor = (jnp.maximum(step_totals, 1.0) * tokens)[:, None, None]
-        updated = 0.75 * output_factor[:, 0] + 0.25 * curv_total / divisor
-        output_factor_new = jnp.where(
-            (step_totals > 0.0)[:, None, None], updated, output_factor[:, 0]
-        )[:, None]
-    return (input_factor_new, output_factor_new)
+        output_factor_new = statistics(where, output_factor, shares, tokens, last)
+    return (input_factor_new[None], output_factor_new)
 
 
 def solution(mesh):

time: 174 us -> 162 us (0.931)
  starting transfers between devices: 54.1 us -> 42.3 us
  waiting for transfers between devices: 55.4 us -> 62.1 us
  other arithmetic: 5.61 us -> 0 us
  local copies, waits for them, and re-layouts: 9.07 us -> 4.65 us
  Pallas kernels: 47.4 us -> 51.3 us
    ppermute x9, waiting for transfers between devices: 53.9 us -> 39.2 us  [shift(): lax.ppermute(block, axis, [(i, (i + distance) % count) for i in range(cou...]
    ppermute x0 -> x1, waiting for transfers between devices: none -> 11.3 us  [swap_chips(): return lax.ppermute(block, 'dp', [(i, i ^ 4) for i in range(count)])]
    ppermute x9, starting transfers between devices: 22.1 us -> 11.6 us  [shift(): lax.ppermute(block, axis, [(i, (i + distance) % count) for i in range(cou...]
    all_to_all x1, waiting for transfers between devices: 1.51 us -> 10.4 us  [shards(): shares = lax.all_to_all(share, 'dp', 0, 0)]
    ppermute x5 -> x4, starting transfers between devices: 8.74 us -> 4.06 us  [swap_cores(): return lax.ppermute(block, 'dp', [(i, i ^ 1) for i in range(count)])]
    unnamed x46 -> x32, local copies, waits for them, and re-layouts: 7.47 us -> 4.03 us
    add x2 -> x0, other arithmetic: 2.75 us -> none  [the longest x1 1.83 us: shards(): mine = step0[:, cut:] + from1[:, cut:].astype(F32)]
    ppermute x0 -> x1, starting transfers between devices: none -> 2.43 us  [swap_chips(): return lax.ppermute(block, 'dp', [(i, i ^ 4) for i in range(count)])]
  transfers between devices with their start and end apart: 17 -> 17, of which waited for: 5 -> 9; matrix products, arithmetic and copies ran while one was open for 4% -> 0% of each run, Pallas kernels for 17% -> 21%
where the time goes in v5:
time: 162 us; the launch traced here: 161 us
  waiting for transfers between devices  62.1 us (38%)
  Pallas kernels  51.3 us (32%)
  starting transfers between devices  42.3 us (26%)
  local copies, waits for them, and re-layouts  4.65 us (3%)
    ppermute x9, waiting for transfers between devices, shift(): lax.ppermute(block, axis, [(i, (i + distance) % count) for i in range(cou...  39.2 us
    pallas_call x11, Pallas kernels, local(): pl.pallas_call(kernel, in_specs=[pl.BlockSpec(memory_space=pltpu.SMEM)] +...  27.5 us
    pallas_call x4, Pallas kernels, call(): pl.pallas_call(kernel, grid_spec=spec, out_shape=outs, input_output_alias...  22.1 us
    ppermute x9, starting transfers between devices, shift(): lax.ppermute(block, axis, [(i, (i + distance) % count) for i in range(cou...  11.6 us
    ppermute x1, waiting for transfers between devices, swap_chips(): return lax.ppermute(block, 'dp', [(i, i ^ 4) for i in range(count)])  11.3 us
    all_to_all x1, waiting for transfers between devices, shards(): shares = lax.all_to_all(share, 'dp', 0, 0)  10.4 us
    all_to_all x1, starting transfers between devices, shards(): shares = lax.all_to_all(share, 'dp', 0, 0)  8.98 us
    all_to_all x1, starting transfers between devices, shards(): own = tie(lax.all_to_all(pieces, 'dp', 0, 0), sent, space=pltpu.VMEM)  8.44 us
  transfers between devices with their start and end apart: 17, of which 9 were waited for; matrix products, arithmetic and copies ran while one was open for 0% of the time, Pallas kernels for 21%

profile of v5, /device:TPU:1, one launch (start us, length us, event | category | flops | bytes accessed | tf_op | source)
XLA Modules:
  0.0 161.4 jit_solution(16935782160626556826)
XLA Ops:
  0.7 0.6 stack.47.where
  1.3 5.2 %weights.3 = (bf16[16,136,512]{2,1,0:T(8,128)(2,1)}, bf16[128,64]{1,0:T(8,128)(2,1)}) custom-call(s32[8]{0:T(128)} %stack.47.where, bf16[128,8192]{1,0:T(8,128)(2,1)} %bitcast.14, bf16[2,1,64,8192]{3,2,1,0:T(8,128)(2,1)} %refs_7_.1, s32[16,128]{1,0:T(8,128)} %ids.1), custom_call_target="tpu_custom_call" | custom-call | tf_op jit(solution)/shard_map/weights/pallas_call | solution.py:46
  6.5 8.4 %all-to-all-start = ((bf16[16,136,512]{2,1,0:T(8,128)(2,1)}), bf16[16,136,512]{2,1,0:T(8,128)(2,1)S(1)}, u32[]{:S(2)}, u32[]{:S(2)}) async-start(bf16[16,136,512]{2,1,0:T(8,128)(2,1)} %get-tuple-element.28), calls=%async_computation | async-start | bytes 4456448 | tf_op jit(solution)/shard_map/columns/all_to_all | solution.py:615
  14.9 3.0 %weights.4 = (bf16[64,5120]{1,0:T(8,128)(2,1)}, bf16[64,2048]{1,0:T(8,128)(2,1)}, bf16[64,2048]{1,0:T(8,128)(2,1)}) custom-call(s32[8]{0:T(128)} %stack.47.where, bf16[2,1,64,8192]{3,2,1,0:T(8,128)(2,1)} %refs_9_.1, bf16[2,1,64,8192]{3,2,1,0:T(8,128)(2,1)} %refs_7_.1, bf16[2,1,64,8192]{3,2,1,0:T(8,128)(2,1)} %refs_9_.1, bf16[2,1,64,8192]{3,2,1,0:T(8,128)(2,1)} %refs_9_.1, ...), custom_call_target="tpu_custom_call" | custom-call | tf_op jit(solution)/shard_map/weights/pallas_call | solution.py:46
  17.9 5.7 %collective-permute-start = (bf16[64,5120]{1,0:T(8,128)(2,1)}, bf16[64,5120]{1,0:T(8,128)(2,1)S(1)}, u32[]{:S(2)}, u32[]{:S(2)}) collective-permute-start(bf16[64,5120]{1,0:T(8,128)(2,1)} %get-tuple-element.30), channel_id=1, source_target_pairs={{0,240},{16,0},{32,16},{48,32},{64,48},{80,64},{96,80},{112,96},{1... | collective-permute-start | bytes 1966088 | tf_op jit(solution)/shard_map/weights/ppermute | solution.py:17
  23.7 0.0 collective-permute-start.2
  23.7 0.0 collective-permute-start.3
  23.7 26.2 %collective-permute-done.dm.u1o.u1s.refs_12_ = bf16[64,5120]{1,0:T(8,128)(2,1)S(1)} collective-permute-done((bf16[64,5120]{1,0:T(8,128)(2,1)}, bf16[64,5120]{1,0:T(8,128)(2,1)S(1)}, u32[]{:S(2)}, u32[]{:S(2)}) %collective-permute-start) | collective-permute-done | bytes 655392 | tf_op jit(solution)/shard_map/weights/ppermute | solution.py:17
  49.9 1.1 collective-permute-start.1
  51.0 0.6 weights.5.a
  51.6 2.4 %collective-permute-start.4 = (bf16[128,2048]{1,0:T(8,128)(2,1)S(1)}, bf16[128,2048]{1,0:T(8,128)(2,1)S(1)}, u32[]{:S(2)}, u32[]{:S(2)}) collective-permute-start(bf16[128,2048]{1,0:T(8,128)(2,1)S(1)} %weights.5.a), channel_id=1, source_target_pairs={{0,4},{1,5},{2,6},{3,7},{4,0},{5,1},{6,2},{7,3},{8,12},{9,13},{10,... | collective-permute-start | bytes 1572872 | tf_op jit(solution)/shard_map/weights/ppermute | solution.py:27
  54.0 11.3 %collective-permute-done.4.after.b = bf16[128,2048]{1,0:T(8,128)(2,1)S(1)} collective-permute-done((bf16[128,2048]{1,0:T(8,128)(2,1)S(1)}, bf16[128,2048]{1,0:T(8,128)(2,1)S(1)}, u32[]{:S(2)}, u32[]{:S(2)}) %collective-permute-start.4) | collective-permute-done | bytes 524320 | tf_op jit(solution)/shard_map/weights/ppermute | solution.py:27
  65.4 0.8 copy-done.3
  66.1 6.3 %gates.1 = (bf16[16,128,128]{2,1,0:T(8,128)(2,1)}, bf16[128,512]{1,0:T(8,128)(2,1)}, bf16[128,512]{1,0:T(8,128)(2,1)}) custom-call(s32[8]{0:T(128)} %stack.47.where, bf16[128,8192]{1,0:T(8,128)(2,1)} %bitcast.15, bf16[128,8192]{1,0:T(8,128)(2,1)} %bitcast.16, bf16[2,1,64,8192]{3,2,1,0:T(8,128)(2,1)} %refs_9_.1, bf16[2,1,64,8192]{3,2,1,0:T(8,128)(2,1)} %refs_9_.1, ...), custom_call_target="tpu_custom_call" | custom-call | tf_op jit(solution)/shard_map/gates/pallas_call | solution.py:46
  72.5 0.0 copy-start.4
  72.5 1.5 collective-permute-start.5
  74.0 1.6 backward.5.refs_10_
  75.6 0.9 collective-permute-start.6
  76.5 6.8 %all-to-all-start.1 = ((bf16[16,128,128]{2,1,0:T(8,128)(2,1)}), bf16[16,128,128]{2,1,0:T(8,128)(2,1)S(1)}, u32[]{:S(2)}, u32[]{:S(2)}) async-start(bf16[16,128,128]{2,1,0:T(8,128)(2,1)} %get-tuple-element.33.rest_0_), calls=%async_computation.1 | async-start | bytes 1048576 | tf_op jit(solution)/shard_map/columns/all_to_all | solution.py:617
  83.4 7.6 %backward.6 = (f32[192,128]{1,0:T(8,128)}, f32[128,64]{1,0:T(8,128)}, f32[128,128]{1,0:T(8,128)}, f32[128,128]{1,0:T(8,128)}) custom-call(s32[8]{0:T(128)} %stack.47.where, bf16[128,8192]{1,0:T(8,128)(2,1)} %bitcast.18, bf16[128,8192]{1,0:T(8,128)(2,1)} %bitcast.19, bf16[2,1,64,8192]{3,2,1,0:T(8,128)(2,1)} %refs_9_.1, bf16[2,1,64,8192]{3,2,1,0:T(8,128)(2,1)} %refs_9_.1, ...), custom_call_target="tpu_custom_call" | custom-call | tf_op jit(solution)/shard_map/backward/pallas_call | solution.py:46
  91.0 2.2 %collective-permute-start.7 = (f32[128,128]{1,0:T(8,128)}, f32[128,128]{1,0:T(8,128)S(1)}, u32[]{:S(2)}, u32[]{:S(2)}) collective-permute-start(f32[128,128]{1,0:T(8,128)} %get-tuple-element.36), channel_id=1, source_target_pairs={{0,16},{16,32},{32,48},{48,64},{64,80},{80,96},{96,112},{112,128},... | collective-permute-start | bytes 196616 | tf_op jit(solution)/shard_map/backward/ppermute | solution.py:17
  93.2 1.3 all-to-all-done.1.rest_0_
  94.5 4.3 %collective-permute-done.7.rest_3_.by1 = f32[128,128]{1,0:T(8,128)S(1)} collective-permute-done((f32[128,128]{1,0:T(8,128)}, f32[128,128]{1,0:T(8,128)S(1)}, u32[]{:S(2)}, u32[]{:S(2)}) %collective-permute-start.7) | collective-permute-done | bytes 65568 | tf_op jit(solution)/shard_map/backward/ppermute | solution.py:17
  98.8 3.6 %collective-permute-done.8.rest_4_.by2 = f32[128,128]{1,0:T(8,128)S(1)} collective-permute-done((f32[128,128]{1,0:T(8,128)}, f32[128,128]{1,0:T(8,128)S(1)}, u32[]{:S(2)}, u32[]{:S(2)}) %collective-permute-start.8) | collective-permute-done | bytes 65568 | tf_op jit(solution)/shard_map/backward/ppermute | solution.py:17
  102.4 6.3 %factor.7 = (bf16[256,1280]{1,0:T(8,128)(2,1)S(1)}, f32[8,128]{1,0:T(8,128)S(1)}) custom-call(s32[8]{0:T(128)S(1)} %copy-done.11, bf16[16,136,512]{2,1,0:T(8,128)(2,1)S(1)} %columns.1.own, bf16[16,136,512]{2,1,0:T(8,128)(2,1)} %collective-permute-done.5.other, bf16[16,128,128]{2,1,0:T(8,128)(2,1)S(1)} %all-to-all-done.1.rest_0_, ...), custom_call_target="tpu_custom_call" | custom-call | tf_op jit(solution)/shard_map/factor/pallas_call | solution.py:228
  108.7 0.1 collective-permute-start.9
  108.8 0.0 copy-start.8
  108.8 0.0 copy-start.14
  108.8 6.1 %factor.8 = (f32[256,1280]{1,0:T(8,128)S(1)}, f32[8,128]{1,0:T(8,128)S(1)}) custom-call(s32[8]{0:T(128)S(1)} %copy-done.11, bf16[16,136,512]{2,1,0:T(8,128)(2,1)S(1)} %columns.1.own, bf16[16,136,512]{2,1,0:T(8,128)(2,1)} %collective-permute-done.5.other, bf16[16,128,128]{2,1,0:T(8,128)(2,1)S(1)} %all-to-all-done.1.rest_0_, bf16[128,512]{1,0:T(8,128)(2,1)S(1)} %copy-done.5, ...), custom_call_target="tpu_custom_call" | custom-call | tf_op jit(solution)/shard_map/factor/pallas_call | solution.py:228
  115.0 1.0 backward.7
  116.0 3.5 %collective-permute-start.10 = (f32[64,64]{1,0:T(8,128)S(1)}, f32[64,64]{1,0:T(8,128)S(1)}, u32[]{:S(2)}, u32[]{:S(2)}) collective-permute-start(f32[64,64]{1,0:T(8,128)S(1)} %get-tuple-element.45), channel_id=1, source_target_pairs={{0,240},{16,0},{32,16},{48,32},{64,48},{80,64},{96,80},{112,96},{1... | collective-permute-start | bytes 49160 | tf_op jit(solution)/shard_map/backward/ppermute | solution.py:17
  119.5 1.0 collective-permute-done.10.outer1
  120.6 2.9 %collective-permute-done.11.outer2 = f32[64,64]{1,0:T(8,128)S(1)} collective-permute-done((f32[64,64]{1,0:T(8,128)S(1)}, f32[64,64]{1,0:T(8,128)S(1)}, u32[]{:S(2)}, u32[]{:S(2)}) %collective-permute-start.11) | collective-permute-done | bytes 16416 | tf_op jit(solution)/shard_map/backward/ppermute | solution.py:17
  123.5 0.7 backward.8
  124.2 0.8 copy-done.7
  125.0 1.1 collective-permute-done.9.b
  126.1 1.5 factor.9
  127.6 9.0 %all-to-all-start.2 = ((f32[16,64,128]{2,1,0:T(8,128)}), f32[16,64,128]{2,1,0:T(8,128)S(1)}, u32[]{:S(2)}, u32[]{:S(2)}) async-start(f32[16,64,128]{2,1,0:T(8,128)} %copy-done.7), calls=%async_computation.2 | async-start | bytes 1048576 | tf_op jit(solution)/shard_map/backward/all_to_all | solution.py:640
  136.6 6.2 %factor.10 = (f32[256,1280]{1,0:T(8,128)S(1)}, f32[8,128]{1,0:T(8,128)}) custom-call(s32[8]{0:T(128)S(1)} %copy-done.11, bf16[16,136,512]{2,1,0:T(8,128)(2,1)S(1)} %columns.1.own, bf16[16,136,512]{2,1,0:T(8,128)(2,1)} %collective-permute-done.5.other, f32[8,128]{1,0:T(8,128)S(1)} %get-tuple-element.48.rest_0_), custom_call_target="tpu_custom_call" | custom-call | tf_op jit(solution)/shard_map/factor/pallas_call | solution.py:228
  142.8 1.1 copy-done.1
  143.8 10.4 %all-to-all-done.2.after.parts = f32[16,64,128]{2,1,0:T(8,128)S(1)} async-done(((f32[16,64,128]{2,1,0:T(8,128)}), f32[16,64,128]{2,1,0:T(8,128)S(1)}, u32[]{:S(2)}, u32[]{:S(2)}) %all-to-all-start.2) | async-done | bytes 524320 | tf_op jit(solution)/shard_map/backward/all_to_all | solution.py:640
  154.2 1.3 copy-done.2
  155.5 0.6 factor.11.mine
  156.1 0.5 collective-permute-start.13
  156.6 1.7 %factor.12.done = f32[512,1024]{1,0:T(8,128)} custom-call(s32[8]{0:T(128)S(1)} %copy-done.11, f32[512,1024]{1,0:T(8,128)S(1)} %bitcast.12, f32[256,1280]{1,0:T(8,128)S(1)} %copy-done.2, bf16[256,1280]{1,0:T(8,128)(2,1)S(1)} %collective-permute-done.12.came, f32[16,64,128]{2,1,0:T(8,128)S(1)} %all-to-all-done.2.after.parts), custom_call_target="tpu_custom_call" | custom-call | tf_op jit(solution)/shard_map/factor/pallas_call | solution.py:228
  158.3 0.0 copy-start.13
  158.3 1.7 %factor.13 = (f32[512,1024]{1,0:T(8,128)}, f32[8,128]{1,0:T(8,128)S(1)}) custom-call(s32[8]{0:T(128)S(1)} %copy-done.11, f32[512,1024]{1,0:T(8,128)S(1)} %bitcast.13, f32[256,512]{1,0:T(8,128)S(1)} %factor.11.mine, f32[256,512]{1,0:T(8,128)S(1)} %collective-permute-done.13.sib, f32[512,1024]{1,0:T(8,128)} %factor.12.done), custom_call_target="tpu_custom_call", output_to_operand_aliasing={{0}: (4, {})} | custom-call | tf_op jit(solution)/shard_map/factor/pallas_call | solution.py:563
  160.1 1.3 backward.9
  (36 shorter events, 0.1 us)
Async XLA Ops:
  6.5 65.9 %all-to-all-start = ((bf16[16,136,512]{2,1,0:T(8,128)(2,1)}), bf16[16,136,512]{2,1,0:T(8,128)(2,1)S(1)}, u32[]{:S(2)}, u32[]{:S(2)}) async-start(bf16[16,136,512]{2,1,0:T(8,128)(2,1)} %get-tuple-element.28), calls=%async_computation | async-start | bytes 4456448 | tf_op jit(solution)/shard_map/columns/all_to_all | solution.py:615
  14.9 36.0 %copy-start.9 = (s32[8]{0:T(128)S(1)}, s32[8]{0:T(128)}, u32[]{:S(2)}) copy-start(s32[8]{0:T(128)} %stack.47.where) | copy-start | bytes 100
  17.9 31.9 %collective-permute-start = (bf16[64,5120]{1,0:T(8,128)(2,1)}, bf16[64,5120]{1,0:T(8,128)(2,1)S(1)}, u32[]{:S(2)}, u32[]{:S(2)}) collective-permute-start(bf16[64,5120]{1,0:T(8,128)(2,1)} %get-tuple-element.30), channel_id=1, source_target_pairs={{0,240},{16,0},{32,16},{48,32},{64,48},{80,64},{96,80},{112,96},{1... | collective-permute-start | bytes 1966088 | tf_op jit(solution)/shard_map/weights/ppermute | solution.py:17
  23.7 27.3 %collective-permute-start.2 = (bf16[64,2048]{1,0:T(8,128)(2,1)}, bf16[64,2048]{1,0:T(8,128)(2,1)S(1)}, u32[]{:S(2)}, u32[]{:S(2)}) collective-permute-start(bf16[64,2048]{1,0:T(8,128)(2,1)} %get-tuple-element.31), channel_id=1, source_target_pairs={{0,16},{16,32},{32,48},{48,64},{64,80},{80,96},{96,112},{112,128},... | collective-permute-start | bytes 786440 | tf_op jit(solution)/shard_map/weights/ppermute | solution.py:17
  23.7 27.3 %collective-permute-start.3 = (bf16[64,2048]{1,0:T(8,128)(2,1)}, bf16[64,2048]{1,0:T(8,128)(2,1)S(1)}, u32[]{:S(2)}, u32[]{:S(2)}) collective-permute-start(bf16[64,2048]{1,0:T(8,128)(2,1)} %get-tuple-element.32), channel_id=1, source_target_pairs={{0,32},{16,48},{32,64},{48,80},{64,96},{80,112},{96,128},{112,144}... | collective-permute-start | bytes 786440 | tf_op jit(solution)/shard_map/weights/ppermute | solution.py:17
  49.9 15.5 %copy-start.15 = (bf16[64,5120]{1,0:T(8,128)(2,1)}, bf16[64,5120]{1,0:T(8,128)(2,1)S(1)}, u32[]{:S(2)}) copy-start(bf16[64,5120]{1,0:T(8,128)(2,1)S(1)} %collective-permute-done.dm.u1o.u1s.refs_12_) | copy-start | bytes 1966084
  49.9 15.5 %collective-permute-start.1 = (bf16[64,5120]{1,0:T(8,128)(2,1)S(1)}, bf16[64,5120]{1,0:T(8,128)(2,1)}, u32[]{:S(2)}, u32[]{:S(2)}) collective-permute-start(bf16[64,5120]{1,0:T(8,128)(2,1)S(1)} %collective-permute-done.dm.u1o.u1s.refs_12_), channel_id=1, source_target_pairs={{0,1},{1,0},{2,3},{3,2},{4,5},{5,4},{6,7},{7,6},{8,9},{9,8},{10,11... | collective-permute-start | bytes 1966088 | tf_op jit(solution)/shard_map/weights/ppermute | solution.py:22
  51.6 13.8 %collective-permute-start.4 = (bf16[128,2048]{1,0:T(8,128)(2,1)S(1)}, bf16[128,2048]{1,0:T(8,128)(2,1)S(1)}, u32[]{:S(2)}, u32[]{:S(2)}) collective-permute-start(bf16[128,2048]{1,0:T(8,128)(2,1)S(1)} %weights.5.a), channel_id=1, source_target_pairs={{0,4},{1,5},{2,6},{3,7},{4,0},{5,1},{6,2},{7,3},{8,12},{9,13},{10,... | collective-permute-start | bytes 1572872 | tf_op jit(solution)/shard_map/weights/ppermute | solution.py:27
  65.4 0.8 copy-start.3
  72.5 1.6 copy-start.4
  72.5 1.6 copy-start.10
  72.5 29.9 %collective-permute-start.5 = (bf16[16,136,512]{2,1,0:T(8,128)(2,1)S(1)}, bf16[16,136,512]{2,1,0:T(8,128)(2,1)}, u32[]{:S(2)}, u32[]{:S(2)}) collective-permute-start(bf16[16,136,512]{2,1,0:T(8,128)(2,1)S(1)} %columns.1.own), channel_id=1, source_target_pairs={{0,1},{1,0},{2,3},{3,2},{4,5},{5,4},{6,7},{7,6},{8,9},{9,8},{10,11... | collective-permute-start | bytes 6684680 | tf_op jit(solution)/shard_map/columns/ppermute | solution.py:22
  75.6 7.7 %collective-permute-start.6 = (bf16[256,2048]{1,0:T(8,128)(2,1)}, bf16[256,2048]{1,0:T(8,128)(2,1)}, u32[]{:S(2)}, u32[]{:S(2)}) collective-permute-start(bf16[256,2048]{1,0:T(8,128)(2,1)} %backward.5.refs_10_), channel_id=1, source_target_pairs={{0,1},{1,0},{2,3},{3,2},{4,5},{5,4},{6,7},{7,6},{8,9},{9,8},{10,11... | collective-permute-start | bytes 3145736 | tf_op jit(solution)/shard_map/backward/ppermute | solution.py:22
  76.5 17.9 %all-to-all-start.1 = ((bf16[16,128,128]{2,1,0:T(8,128)(2,1)}), bf16[16,128,128]{2,1,0:T(8,128)(2,1)S(1)}, u32[]{:S(2)}, u32[]{:S(2)}) async-start(bf16[16,128,128]{2,1,0:T(8,128)(2,1)} %get-tuple-element.33.rest_0_), calls=%async_computation.1 | async-start | bytes 1048576 | tf_op jit(solution)/shard_map/columns/all_to_all | solution.py:617
  83.3 19.0 %copy-start.5 = (bf16[128,512]{1,0:T(8,128)(2,1)S(1)}, bf16[128,512]{1,0:T(8,128)(2,1)}, u32[]{:S(2)}) copy-start(bf16[128,512]{1,0:T(8,128)(2,1)} %get-tuple-element.34.rest_1_) | copy-start | bytes 393220
  83.3 19.0 %copy-start.6 = (bf16[128,512]{1,0:T(8,128)(2,1)S(1)}, bf16[128,512]{1,0:T(8,128)(2,1)}, u32[]{:S(2)}) copy-start(bf16[128,512]{1,0:T(8,128)(2,1)} %get-tuple-element.35.rest_2_) | copy-start | bytes 393220
  83.3 19.0 %copy-start.11 = (s32[8]{0:T(128)S(1)}, s32[8]{0:T(128)}, u32[]{:S(2)}) copy-start(s32[8]{0:T(128)} %stack.47.where) | copy-start | bytes 100
  91.0 7.8 %collective-permute-start.7 = (f32[128,128]{1,0:T(8,128)}, f32[128,128]{1,0:T(8,128)S(1)}, u32[]{:S(2)}, u32[]{:S(2)}) collective-permute-start(f32[128,128]{1,0:T(8,128)} %get-tuple-element.36), channel_id=1, source_target_pairs={{0,16},{16,32},{32,48},{48,64},{64,80},{80,96},{96,112},{112,128},... | collective-permute-start | bytes 196616 | tf_op jit(solution)/shard_map/backward/ppermute | solution.py:17
  93.2 9.2 %collective-permute-start.8 = (f32[128,128]{1,0:T(8,128)}, f32[128,128]{1,0:T(8,128)S(1)}, u32[]{:S(2)}, u32[]{:S(2)}) collective-permute-start(f32[128,128]{1,0:T(8,128)} %get-tuple-element.37), channel_id=1, source_target_pairs={{0,32},{16,48},{32,64},{48,80},{64,96},{80,112},{96,128},{112,144}... | collective-permute-start | bytes 196616 | tf_op jit(solution)/shard_map/backward/ppermute | solution.py:17
  108.7 17.4 %collective-permute-start.9 = (bf16[256,1280]{1,0:T(8,128)(2,1)S(1)}, bf16[256,1280]{1,0:T(8,128)(2,1)S(1)}, u32[]{:S(2)}, u32[]{:S(2)}) collective-permute-start(bf16[256,1280]{1,0:T(8,128)(2,1)S(1)} %get-tuple-element.40), channel_id=1, source_target_pairs={{0,16},{16,32},{32,48},{48,64},{64,80},{80,96},{96,112},{112,128},... | collective-permute-start | bytes 1966088 | tf_op jit(solution)/shard_map/factor/ppermute | solution.py:17
  108.8 6.1 %copy-start.8 = (f32[1,3,64,128]{3,2,1,0:T(8,128)S(1)}, f32[1,3,64,128]{3,2,1,0:T(8,128)}, u32[]{:S(2)}) copy-start(f32[1,3,64,128]{3,2,1,0:T(8,128)} %q0.1) | copy-start | bytes 294916
  108.8 6.1 %copy-start.12 = (f32[192,128]{1,0:T(8,128)S(1)}, f32[192,128]{1,0:T(8,128)}, u32[]{:S(2)}) copy-start(f32[192,128]{1,0:T(8,128)} %get-tuple-element.41.proj) | copy-start | bytes 294916
  108.8 6.1 %copy-start.14 = (f32[128,64]{1,0:T(8,128)S(1)}, f32[128,64]{1,0:T(8,128)}, u32[]{:S(2)}) copy-start(f32[128,64]{1,0:T(8,128)} %get-tuple-element.42.m0) | copy-start | bytes 98308
  116.0 4.6 %collective-permute-start.10 = (f32[64,64]{1,0:T(8,128)S(1)}, f32[64,64]{1,0:T(8,128)S(1)}, u32[]{:S(2)}, u32[]{:S(2)}) collective-permute-start(f32[64,64]{1,0:T(8,128)S(1)} %get-tuple-element.45), channel_id=1, source_target_pairs={{0,240},{16,0},{32,16},{48,32},{64,48},{80,64},{96,80},{112,96},{1... | collective-permute-start | bytes 49160 | tf_op jit(solution)/shard_map/backward/ppermute | solution.py:17
  119.5 4.0 %collective-permute-start.11 = (f32[64,64]{1,0:T(8,128)S(1)}, f32[64,64]{1,0:T(8,128)S(1)}, u32[]{:S(2)}, u32[]{:S(2)}) collective-permute-start(f32[64,64]{1,0:T(8,128)S(1)} %get-tuple-element.46), channel_id=1, source_target_pairs={{0,224},{16,240},{32,0},{48,16},{64,32},{80,48},{96,64},{112,80},{... | collective-permute-start | bytes 49160 | tf_op jit(solution)/shard_map/backward/ppermute | solution.py:17
  124.2 0.8 copy-start.7
  127.6 26.6 %collective-permute-start.12 = (bf16[256,1280]{1,0:T(8,128)(2,1)}, bf16[256,1280]{1,0:T(8,128)(2,1)S(1)}, u32[]{:S(2)}, u32[]{:S(2)}) collective-permute-start(bf16[256,1280]{1,0:T(8,128)(2,1)} %get-tuple-element.50), channel_id=1, source_target_pairs={{0,16},{16,32},{32,48},{48,64},{64,80},{80,96},{96,112},{112,128},... | collective-permute-start | bytes 1966088 | tf_op jit(solution)/shard_map/factor/ppermute | solution.py:17
  127.6 26.6 %all-to-all-start.2 = ((f32[16,64,128]{2,1,0:T(8,128)}), f32[16,64,128]{2,1,0:T(8,128)S(1)}, u32[]{:S(2)}, u32[]{:S(2)}) async-start(f32[16,64,128]{2,1,0:T(8,128)} %copy-done.7), calls=%async_computation.2 | async-start | bytes 1048576 | tf_op jit(solution)/shard_map/backward/all_to_all | solution.py:640
  142.8 1.1 copy-start.1
  143.8 12.8 %copy-start = (f32[1,512,1024]{2,1,0:T(8,128)S(1)}, f32[1,512,1024]{2,1,0:T(8,128)}, u32[]{:S(2)}) copy-start(f32[1,512,1024]{2,1,0:T(8,128)} %param.14) | copy-start | bytes 6291460
  154.2 1.3 copy-start.2
  156.1 2.2 %collective-permute-start.13 = (f32[256,512]{1,0:T(8,128)S(1)}, f32[256,512]{1,0:T(8,128)S(1)}, u32[]{:S(2)}, u32[]{:S(2)}) collective-permute-start(f32[256,512]{1,0:T(8,128)S(1)} %factor.11.mine), channel_id=1, source_target_pairs={{0,1},{1,0},{2,3},{3,2},{4,5},{5,4},{6,7},{7,6},{8,9},{9,8},{10,11... | collective-permute-start | bytes 1572872 | tf_op jit(solution)/shard_map/factor/ppermute | solution.py:22
  158.3 1.8 %copy-start.13 = (f32[2,1,64,64]{3,2,1,0:T(8,128)S(1)}, f32[2,1,64,64]{3,2,1,0:T(8,128)}, u32[]{:S(2)}) copy-start(f32[2,1,64,64]{3,2,1,0:T(8,128)} %old.1) | copy-start | bytes 98308

commit v6 on v5

--- a/solution.py
+++ b/solution.py
@@ -156,69 +156,76 @@
     )
 
 
-def gate_kernel(
-    where, xm, xs, um, us, dm, ds, gate0, u0o, u0s, u1o, u1s, after, sent, ups_o, ups_s, acc
-):
-    i = pl.program_id(0)
-    rank = gate0.shape[1]
-
-    @pl.when(i == 0)
-    def _():
-        acc[...] = jnp.zeros_like(acc)
-        for out, zero, one in ((ups_o, u0o, u1o), (ups_s, u0s, u1s)):
-            out[:rank] = zero[0, 0]
-            out[rank:] = one[...]
-
-    for x, u, d in ((xm, um, dm), (xs, us, ds)):
-        add = jnp.dot(gate0[...], u[0, 0], preferred_element_type=F32)
-        acc[...] += nt((x[...].astype(F32) + add).astype(BF16), d[...])
-
-    @pl.when(i == pl.num_programs(0) - 1)
-    def _():
-        z = acc[...]
-        gate1 = (z * jax.nn.sigmoid(z)).astype(BF16)
-        both = jnp.concatenate([gate0[...], gate1], axis=1)
-        for k in range(sent.shape[0]):
-            sent[k] = both
-
-
-def gates(where, x, adapter_up, ahead_mine, ahead_sib, gate0, replicas, rows, after):
+def ahead_kernel(where, x, up, gate0, x1):
+    add = jnp.dot(gate0[...], up[0, 0], preferred_element_type=F32)
+    x1[...] = (x[...].astype(F32) + add).astype(BF16)
+
+
+def next_activation(where, x, adapter_up, gate0):
     tok, width = x.shape
     rank = gate0.shape[1]
-    each = ahead_mine.shape[1] - width // 2
-    grid = width // 2 // each
+    grid = 4
+    each = width // grid
+    return call(
+        ahead_kernel,
+        where,
+        (x, adapter_up, gate0),
+        [
+            pl.BlockSpec((tok, each), lambda i, w: (0, i)),
+            pl.BlockSpec((1, 1, rank, each), lambda i, w: (w[C0], 0, 0, i)),
+            pl.BlockSpec((tok, rank), lambda i, w: (0, 0)),
+        ],
+        jax.ShapeDtypeStruct((tok, width), BF16),
+        pl.BlockSpec((tok, each), lambda i, w: (0, i)),
+        (grid,),
+    )
+
+
+def gate_kernel(where, x1, mine, sib, gate0, sent):
+    core = where[CORE]
+    half = x1.shape[1] // 2
+    skip = mine.shape[1] - half
+    z = nt(x1[:, pl.ds(pl.multiple_of(core * half, half), half)], mine[:, skip:])
+    z += nt(x1[:, pl.ds(pl.multiple_of((1 - core) * half, half), half)], sib[:, skip:])
+    gate1 = (z * jax.nn.sigmoid(z)).astype(BF16)
+    both = jnp.concatenate([gate0[...], gate1], axis=1)
+    for k in range(sent.shape[0]):
+        sent[k] = both
+
+
+def gates(where, x1, ahead_mine, ahead_sib, gate0, replicas):
+    tok, rank = gate0.shape
+    return local(
+        gate_kernel,
+        where,
+        (x1, ahead_mine, ahead_sib, gate0),
+        jax.ShapeDtypeStruct((replicas, tok, 2 * rank), BF16),
+    )
+
+
+def columns_kernel(where, u0o, u0s, u1o, u1s, after, ups_o, ups_s):
+    rank = u1o.shape[0]
+    for out, zero, one in ((ups_o, u0o, u1o), (ups_s, u0s, u1s)):
+        out[:rank] = zero[0, 0]
+        out[rank:] = one[...]
+
+
+def up_columns(where, adapter_up, ahead, rows, after):
+    rank = ahead.shape[0]
     mine, sib = (lambda w: w[CORE]), (lambda w: 1 - w[CORE])
-    x_spec = lambda side: pl.BlockSpec((tok, each), lambda i, w: (0, side(w) * grid + i))
-    u_spec = lambda side: pl.BlockSpec(
-        (1, 1, rank, each), lambda i, w: (w[C0], 0, 0, side(w) * grid + i)
-    )
-    d_spec = pl.BlockSpec((rank, each), lambda i, w: (0, i + 1))
     u0 = lambda side: pl.BlockSpec(
         (1, 1, rank, rows), lambda i, w: (w[C0], 0, 0, 2 * w[CHIP] + side(w))
     )
     u1 = lambda side: pl.BlockSpec((rank, rows), lambda i, w: (0, side(w)))
-    shapes = ((replicas, tok, 2 * rank), (2 * rank, rows), (2 * rank, rows))
+    out = pl.BlockSpec((2 * rank, rows), lambda i, w: (0, 0))
     return call(
-        gate_kernel,
-        where,
-        (
-            x, x, adapter_up, adapter_up, ahead_mine, ahead_sib, gate0,
-            adapter_up, adapter_up, ahead_mine, ahead_mine, after,
-        ),
-        [
-            x_spec(mine), x_spec(sib), u_spec(mine), u_spec(sib), d_spec, d_spec,
-            pl.BlockSpec((tok, rank), lambda i, w: (0, 0)),
-            u0(mine), u0(sib), u1(mine), u1(sib),
-            pl.BlockSpec((16, 128), lambda i, w: (0, 0)),
-        ],
-        [jax.ShapeDtypeStruct(shape, BF16) for shape in shapes],
-        [
-            pl.BlockSpec(shapes[0], lambda i, w: (0, 0, 0)),
-            pl.BlockSpec(shapes[1], lambda i, w: (0, 0)),
-            pl.BlockSpec(shapes[2], lambda i, w: (0, 0)),
-        ],
-        (grid,),
-        [pltpu.VMEM((tok, rank), F32)],
+        columns_kernel,
+        where,
+        (adapter_up, adapter_up, ahead, ahead, after),
+        [u0(mine), u0(sib), u1(mine), u1(sib), ANY],
+        [jax.ShapeDtypeStruct((2 * rank, rows), BF16)] * 2,
+        [out, out],
+        (1,),
     )
 
 
@@ -239,14 +246,17 @@
     )(where, *operands, *after)
 
 
-def join_kernel(where, a, b, out):
+def join_kernel(where, a, b, *rest):
+    out = rest[-1]
     out[:a.shape[0]] = a[...]
     out[a.shape[0]:] = b[...]
 
 
-def join(where, a, b):
+def join(where, a, b, after=()):
     shape = (a.shape[0] + b.shape[0], a.shape[1])
-    return local(join_kernel, where, (a, b), jax.ShapeDtypeStruct(shape, a.dtype))
+    return local(
+        join_kernel, where, (a, b), jax.ShapeDtypeStruct(shape, a.dtype), (), after
+    )
 
 
 def scale_columns(own, tok):
@@ -600,54 +610,57 @@
         pieces, gate0 = split(where, x0, adapter_down, doc_ids, replicas, 8)
         ahead, behind1, behind2 = pack(where, adapter_down, adapter_up, block, gate0)
         ahead = shift(ahead, "section", -1)
+        behind1 = shift(behind1, "section", 1)
+        behind2 = shift(behind2, "section", 2)
+        ahead = tie(ahead, behind1, behind2, space=pltpu.VMEM)
         ahead_sib = swap_cores(ahead)
-        behind = join(
-            where, shift(behind1, "section", 1), shift(behind2, "section", 2)
-        )
+        behind = join(where, behind1, behind2)
         behind_pair = swap_chips(behind)
 
     with jax.named_scope("gates"):
-        sent, ups_own, ups_oth = gates(
-            where, x0, adapter_up, ahead, ahead_sib, gate0, replicas, rows, behind_pair
-        )
+        x1 = next_activation(where, x0, adapter_up, gate0)
+        sent = gates(where, x1, ahead, ahead_sib, gate0, replicas)
+        ups_own, ups_oth = up_columns(where, adapter_up, ahead, rows, sent)
 
     with jax.named_scope("columns"):
-        own = tie(lax.all_to_all(pieces, "dp", 0, 0), sent, space=pltpu.VMEM)
+        own = tie(lax.all_to_all(pieces, "dp", 0, 0), sent, ups_own, space=pltpu.VMEM)
         other = swap_cores(own)
         got = lax.all_to_all(sent, "dp", 0, 0)
 
+    with jax.named_scope("factor"):
+        ups = (got, ups_own, ups_oth)
+        step2, token2 = gram(2, where, own, other, ups)
+        from2 = shift(step2, "section", 1)
+        step1, token1 = gram(1, where, own, other, ups, (token2,))
+
     with jax.named_scope("backward"):
-        behind = join(where, behind, behind_pair)
+        behind = join(where, behind, behind_pair, (got,))
         behind_sib = swap_cores(behind)
         proj, m0, by1, by2 = project(
             where, returning[0], adapter_down, adapter_up, behind, behind_sib, ahead, ahead_sib,
-            stashed, gate0,
+            stashed, token1,
         )
         by1 = shift(by1, "section", 1)
         by2 = shift(by2, "section", 2)
 
     with jax.named_scope("factor"):
-        ups = (got, ups_own, ups_oth)
-        step2, token2 = gram(2, where, own, other, ups, (by1, by2))
-        from2 = shift(step2, "section", 1)
-        step1, token1 = gram(1, where, own, other, ups, (token2,))
+        from1, token3 = merge(where, step1, from2, m0)
+        from1 = shift(from1, "section", 1)
+        step0, token0 = gram(0, where, own, other, (), (token3,))
 
     with jax.named_scope("backward"):
-        outer0, outer1, outer2 = back(where, proj, m0, by1, by2, stashed, token1)
+        outer0, outer1, outer2 = back(where, proj, m0, by1, by2, stashed, token0)
         outer1 = shift(outer1, "section", -1)
         outer2 = shift(outer2, "section", -2)
         share, token4 = curvature(where, (outer0, outer1, outer2), replicas)
         shares = lax.all_to_all(share, "dp", 0, 0)
 
     with jax.named_scope("factor"):
-        from1, token3 = merge(where, step1, from2, token4)
-        from1 = shift(from1, "section", 1)
-        step0, _ = gram(0, where, own, other, (), (token3,))
-        mine = cross_part(where, step0, from1, shares)
+        mine = cross_part(where, step0, from1, token4)
         sib = swap_cores(mine)
         factor_scale = 0.25 / (steps_count * tokens)
         input_factor_new, last = update(
-            factor_scale, where, input_factor[0], step0, from1, mine, sib, shares
+            factor_scale, where, input_factor[0], step0, from1, mine, sib, token4
         )
 
     with jax.named_scope("backward"):

time: 162 us -> 174 us (1.074)
  local copies, waits for them, and re-layouts: 4.65 us -> 11.6 us
  Pallas kernels: 51.3 us -> 56.1 us
  starting transfers between devices: 42.3 us -> 38.2 us
  waiting for transfers between devices: 62.1 us -> 65.7 us
    all_to_all x1, waiting for transfers between devices: 1.27 us -> 8.61 us  [shards(): got = lax.all_to_all(sent, 'dp', 0, 0)]
    unnamed x32 -> x56, local copies, waits for them, and re-layouts: 4.03 us -> 10.9 us
    ppermute x9, waiting for transfers between devices: 39.2 us -> 44.2 us  [shift(): lax.ppermute(block, axis, [(i, (i + distance) % count) for i in range(cou...]
    all_to_all x1, waiting for transfers between devices: 10.4 us -> 5.96 us  [shards(): shares = lax.all_to_all(share, 'dp', 0, 0)]
    ppermute x1, waiting for transfers between devices: 11.3 us -> 6.97 us  [swap_chips(): return lax.ppermute(block, 'dp', [(i, i ^ 4) for i in range(count)])]
    all_to_all x1, starting transfers between devices: 8.98 us -> 4.82 us  [shards(): shares = lax.all_to_all(share, 'dp', 0, 0)]
    pallas_call x11 -> x12, Pallas kernels: 27.5 us -> 30.6 us  [local(): pl.pallas_call(kernel, in_specs=[pl.BlockSpec(memory_space=pltpu.SMEM)] +...]
    ppermute x4, starting transfers between devices: 4.06 us -> 6.45 us  [swap_cores(): return lax.ppermute(block, 'dp', [(i, i ^ 1) for i in range(count)])]
  transfers between devices with their start and end apart: 17 -> 17, of which waited for: 9 -> 9; matrix products, arithmetic and copies ran while one was open for 0% -> 0% of each run, Pallas kernels for 21% -> 27%
where the time goes in v6:
time: 174 us; the launch traced here: 173 us
  waiting for transfers between devices  65.7 us (38%)
  Pallas kernels  56.1 us (32%)
  starting transfers between devices  38.2 us (22%)
  local copies, waits for them, and re-layouts  11.6 us (7%)
    ppermute x9, waiting for transfers between devices, shift(): lax.ppermute(block, axis, [(i, (i + distance) % count) for i in range(cou...  44.2 us
    pallas_call x12, Pallas kernels, local(): pl.pallas_call(kernel, in_specs=[pl.BlockSpec(memory_space=pltpu.SMEM)] +...  30.6 us
    pallas_call x5, Pallas kernels, call(): pl.pallas_call(kernel, grid_spec=spec, out_shape=outs, input_output_alias...  23.1 us
    ppermute x9, starting transfers between devices, shift(): lax.ppermute(block, axis, [(i, (i + distance) % count) for i in range(cou...  11.8 us
    unnamed x56, local copies, waits for them, and re-layouts  10.9 us
    all_to_all x1, waiting for transfers between devices, shards(): got = lax.all_to_all(sent, 'dp', 0, 0)  8.61 us
    all_to_all x1, starting transfers between devices, shards(): lax.all_to_all(pieces, 'dp', 0, 0)  8.44 us
    ppermute x1, waiting for transfers between devices, swap_chips(): return lax.ppermute(block, 'dp', [(i, i ^ 4) for i in range(count)])  6.97 us
  transfers between devices with their start and end apart: 17, of which 9 were waited for; matrix products, arithmetic and copies ran while one was open for 0% of the time, Pallas kernels for 27%

profile of v6, /device:TPU:1, one launch (start us, length us, event | category | flops | bytes accessed | tf_op | source)
XLA Modules:
  0.0 172.7 jit_solution(14125859445256216790)
XLA Ops:
  0.7 0.7 stack.47.where
  1.4 5.2 %weights.4 = (bf16[16,136,512]{2,1,0:T(8,128)(2,1)}, bf16[128,64]{1,0:T(8,128)(2,1)}) custom-call(s32[8]{0:T(128)} %stack.47.where, bf16[128,8192]{1,0:T(8,128)(2,1)} %bitcast.16, bf16[2,1,64,8192]{3,2,1,0:T(8,128)(2,1)} %refs_7_.1, s32[16,128]{1,0:T(8,128)} %ids.1), custom_call_target="tpu_custom_call" | custom-call | tf_op jit(solution)/shard_map/weights/pallas_call | solution.py:46
  6.6 8.4 %all-to-all-start = ((bf16[16,136,512]{2,1,0:T(8,128)(2,1)}), bf16[16,136,512]{2,1,0:T(8,128)(2,1)S(1)}, u32[]{:S(2)}, u32[]{:S(2)}) async-start(bf16[16,136,512]{2,1,0:T(8,128)(2,1)} %get-tuple-element.28), calls=%async_computation | async-start | bytes 4456448 | tf_op jit(solution)/shard_map/columns/all_to_all | solution.py:626
  15.0 2.9 %weights.5 = (bf16[64,5120]{1,0:T(8,128)(2,1)}, bf16[64,2048]{1,0:T(8,128)(2,1)}, bf16[64,2048]{1,0:T(8,128)(2,1)}) custom-call(s32[8]{0:T(128)} %stack.47.where, bf16[2,1,64,8192]{3,2,1,0:T(8,128)(2,1)} %refs_9_.1, bf16[2,1,64,8192]{3,2,1,0:T(8,128)(2,1)} %refs_7_.1, bf16[2,1,64,8192]{3,2,1,0:T(8,128)(2,1)} %refs_9_.1, bf16[2,1,64,8192]{3,2,1,0:T(8,128)(2,1)} %refs_9_.1, ...), custom_call_target="tpu_custom_call" | custom-call | tf_op jit(solution)/shard_map/weights/pallas_call | solution.py:46
  17.9 5.7 %collective-permute-start = (bf16[64,5120]{1,0:T(8,128)(2,1)}, bf16[64,5120]{1,0:T(8,128)(2,1)S(1)}, u32[]{:S(2)}, u32[]{:S(2)}) collective-permute-start(bf16[64,5120]{1,0:T(8,128)(2,1)} %get-tuple-element.30), channel_id=1, source_target_pairs={{0,240},{16,0},{32,16},{48,32},{64,48},{80,64},{96,80},{112,96},{1... | collective-permute-start | bytes 1966088 | tf_op jit(solution)/shard_map/weights/ppermute | solution.py:17
  23.6 25.7 %collective-permute-done.1.rest_0_.a = bf16[64,2048]{1,0:T(8,128)(2,1)S(1)} collective-permute-done((bf16[64,2048]{1,0:T(8,128)(2,1)}, bf16[64,2048]{1,0:T(8,128)(2,1)S(1)}, u32[]{:S(2)}, u32[]{:S(2)}) %collective-permute-start.1) | collective-permute-done | bytes 262176 | tf_op jit(solution)/shard_map/weights/ppermute | solution.py:17
  49.3 0.3 collective-permute-done.x
  49.6 0.4 copy-done.11
  50.1 3.4 %collective-permute-start.3 = (bf16[64,5120]{1,0:T(8,128)(2,1)S(1)}, bf16[64,5120]{1,0:T(8,128)(2,1)S(1)}, u32[]{:S(2)}, u32[]{:S(2)}) collective-permute-start(bf16[64,5120]{1,0:T(8,128)(2,1)S(1)} %weights.6.mine.u1o.u1s.refs_12_), channel_id=1, source_target_pairs={{0,1},{1,0},{2,3},{3,2},{4,5},{5,4},{6,7},{7,6},{8,9},{9,8},{10,11... | collective-permute-start | bytes 1966088 | tf_op jit(solution)/shard_map/weights/ppermute | solution.py:22
  53.5 5.1 %gates.3.x1 = bf16[128,8192]{1,0:T(8,128)(2,1)} custom-call(s32[8]{0:T(128)} %stack.47.where, bf16[128,8192]{1,0:T(8,128)(2,1)} %bitcast.17, bf16[2,1,64,8192]{3,2,1,0:T(8,128)(2,1)} %refs_9_.1, bf16[128,64]{1,0:T(8,128)(2,1)} %get-tuple-element.29.gate0.after), custom_call_target="tpu_custom_call" | custom-call | tf_op jit(solution)/shard_map/gates/pallas_call | solution.py:46
  58.6 1.6 copy-done.1
  60.2 0.8 copy-done.18
  60.9 2.1 %gates.4.after.rest_0_ = bf16[16,128,128]{2,1,0:T(8,128)(2,1)} custom-call(s32[8]{0:T(128)S(1)} %copy-done.21, bf16[128,8192]{1,0:T(8,128)(2,1)S(1)} %copy-done.1, bf16[64,5120]{1,0:T(8,128)(2,1)S(1)} %weights.6.mine.u1o.u1s.refs_12_, bf16[64,5120]{1,0:T(8,128)(2,1)S(1)} %collective-permute-done.3.sib.refs_13_, bf16[128,64]{1,0:T(8,128)(2,1)S(1)} %copy-done.18), custom_call_target="tpu_custom_call" | custom-call | tf_op jit(solution)/shard_map/gates/pallas_call | solution.py:235
  63.1 2.3 %gates.5 = (bf16[128,512]{1,0:T(8,128)(2,1)}, bf16[128,512]{1,0:T(8,128)(2,1)}) custom-call(s32[8]{0:T(128)} %stack.47.where, bf16[2,1,64,8192]{3,2,1,0:T(8,128)(2,1)} %refs_9_.1, bf16[2,1,64,8192]{3,2,1,0:T(8,128)(2,1)} %refs_9_.1, bf16[64,5120]{1,0:T(8,128)(2,1)} %copy-done, bf16[64,5120]{1,0:T(8,128)(2,1)} %copy-done, ...), custom_call_target="tpu_custom_call" | custom-call | tf_op jit(solution)/shard_map/gates/pallas_call | solution.py:46
  65.4 0.9 copy-done.9
  66.4 0.9 copy-done.12
  67.3 0.6 weights.7.a
  68.1 6.6 %all-to-all-start.1 = ((bf16[16,128,128]{2,1,0:T(8,128)(2,1)}), bf16[16,128,128]{2,1,0:T(8,128)(2,1)S(1)}, u32[]{:S(2)}, u32[]{:S(2)}) async-start(bf16[16,128,128]{2,1,0:T(8,128)(2,1)} %gates.4.after.rest_0_), calls=%async_computation.1 | async-start | bytes 1048576 | tf_op jit(solution)/shard_map/columns/all_to_all | solution.py:628
  74.6 7.0 %collective-permute-done.6.b = bf16[128,2048]{1,0:T(8,128)(2,1)} collective-permute-done((bf16[128,2048]{1,0:T(8,128)(2,1)S(1)}, bf16[128,2048]{1,0:T(8,128)(2,1)}, u32[]{:S(2)}, u32[]{:S(2)}) %collective-permute-start.6) | collective-permute-done | bytes 524320 | tf_op jit(solution)/shard_map/weights/ppermute | solution.py:27
  81.6 8.6 %all-to-all-done.1.rest_0_ = bf16[16,128,128]{2,1,0:T(8,128)(2,1)S(1)} async-done(((bf16[16,128,128]{2,1,0:T(8,128)(2,1)}), bf16[16,128,128]{2,1,0:T(8,128)(2,1)S(1)}, u32[]{:S(2)}, u32[]{:S(2)}) %all-to-all-start.1) | async-done | bytes 524320 | tf_op jit(solution)/shard_map/columns/all_to_all | solution.py:628
  90.2 1.1 backward.5.refs_10_
  91.5 7.2 %factor.7 = (bf16[256,1280]{1,0:T(8,128)(2,1)}, f32[8,128]{1,0:T(8,128)S(1)}) custom-call(s32[8]{0:T(128)S(1)} %copy-done.22, bf16[16,136,512]{2,1,0:T(8,128)(2,1)S(1)} %columns.1.own, bf16[16,136,512]{2,1,0:T(8,128)(2,1)} %collective-permute-done.4.other, bf16[16,128,128]{2,1,0:T(8,128)(2,1)S(1)} %all-to-all-done.1.rest_0_, ...), custom_call_target="tpu_custom_call" | custom-call | tf_op jit(solution)/shard_map/factor/pallas_call | solution.py:235
  98.7 3.6 %collective-permute-start.5 = (bf16[256,1280]{1,0:T(8,128)(2,1)}, bf16[256,1280]{1,0:T(8,128)(2,1)}, u32[]{:S(2)}, u32[]{:S(2)}) collective-permute-start(bf16[256,1280]{1,0:T(8,128)(2,1)} %get-tuple-element.37), channel_id=1, source_target_pairs={{0,16},{16,32},{32,48},{48,64},{64,80},{80,96},{96,112},{112,128},... | collective-permute-start | bytes 1966088 | tf_op jit(solution)/shard_map/factor/ppermute | solution.py:17
  102.3 6.0 %factor.8 = (f32[256,1280]{1,0:T(8,128)S(1)}, f32[8,128]{1,0:T(8,128)S(1)}) custom-call(s32[8]{0:T(128)S(1)} %copy-done.22, bf16[16,136,512]{2,1,0:T(8,128)(2,1)S(1)} %columns.1.own, bf16[16,136,512]{2,1,0:T(8,128)(2,1)} %collective-permute-done.4.other, bf16[16,128,128]{2,1,0:T(8,128)(2,1)S(1)} %all-to-all-done.1.rest_0_, bf16[128,512]{1,0:T(8,128)(2,1)S(1)} %copy-done.10, ...), custom_call_target="tpu_custom_call" | custom-call | tf_op jit(solution)/shard_map/factor/pallas_call | solution.py:235
  108.3 1.0 copy-done.7
  109.4 0.6 copy-done.26
  110.0 1.0 copy-done.27
  111.0 7.6 %backward.6 = (f32[192,128]{1,0:T(8,128)}, f32[128,64]{1,0:T(8,128)}, f32[128,128]{1,0:T(8,128)}, f32[128,128]{1,0:T(8,128)}) custom-call(s32[8]{0:T(128)} %stack.47.where, bf16[128,8192]{1,0:T(8,128)(2,1)} %bitcast.14, bf16[128,8192]{1,0:T(8,128)(2,1)} %bitcast.15, bf16[2,1,64,8192]{3,2,1,0:T(8,128)(2,1)} %refs_9_.1, bf16[2,1,64,8192]{3,2,1,0:T(8,128)(2,1)} %refs_9_.1, ...), custom_call_target="tpu_custom_call" | custom-call | tf_op jit(solution)/shard_map/backward/pallas_call | solution.py:46
  118.6 0.6 collective-permute-done.5.b
  119.2 0.8 copy-done.19
  120.1 1.2 factor.9
  121.6 5.6 %factor.10 = (f32[256,1280]{1,0:T(8,128)S(1)}, f32[8,128]{1,0:T(8,128)S(1)}) custom-call(s32[8]{0:T(128)S(1)} %copy-done.23, bf16[16,136,512]{2,1,0:T(8,128)(2,1)S(1)} %columns.1.own, bf16[16,136,512]{2,1,0:T(8,128)(2,1)} %collective-permute-done.4.other, f32[8,128]{1,0:T(8,128)S(1)} %get-tuple-element.40.rest_0_), custom_call_target="tpu_custom_call" | custom-call | tf_op jit(solution)/shard_map/factor/pallas_call | solution.py:235
  127.3 13.9 %collective-permute-done.9.by1 = f32[128,128]{1,0:T(8,128)S(1)} collective-permute-done((f32[128,128]{1,0:T(8,128)}, f32[128,128]{1,0:T(8,128)S(1)}, u32[]{:S(2)}, u32[]{:S(2)}) %collective-permute-start.9) | collective-permute-done | bytes 65568 | tf_op jit(solution)/shard_map/backward/ppermute | solution.py:17
  141.2 1.0 backward.7
  142.2 2.3 %collective-permute-start.11 = (f32[64,64]{1,0:T(8,128)S(1)}, f32[64,64]{1,0:T(8,128)S(1)}, u32[]{:S(2)}, u32[]{:S(2)}) collective-permute-start(f32[64,64]{1,0:T(8,128)S(1)} %get-tuple-element.48), channel_id=1, source_target_pairs={{0,240},{16,0},{32,16},{48,32},{64,48},{80,64},{96,80},{112,96},{1... | collective-permute-start | bytes 49160 | tf_op jit(solution)/shard_map/backward/ppermute | solution.py:17
  144.5 2.0 %collective-permute-done.11.outer1 = f32[64,64]{1,0:T(8,128)S(1)} collective-permute-done((f32[64,64]{1,0:T(8,128)S(1)}, f32[64,64]{1,0:T(8,128)S(1)}, u32[]{:S(2)}, u32[]{:S(2)}) %collective-permute-start.11) | collective-permute-done | bytes 16416 | tf_op jit(solution)/shard_map/backward/ppermute | solution.py:17
  146.5 1.7 collective-permute-done.12.outer2
  148.2 0.7 backward.8
  148.9 0.8 copy-done.16
  149.7 1.4 factor.11.mine
  151.1 0.8 copy-done.5
  151.9 2.9 %collective-permute-start.13 = (f32[256,512]{1,0:T(8,128)}, f32[256,512]{1,0:T(8,128)}, u32[]{:S(2)}, u32[]{:S(2)}) collective-permute-start(f32[256,512]{1,0:T(8,128)} %factor.11.mine), channel_id=1, source_target_pairs={{0,1},{1,0},{2,3},{3,2},{4,5},{5,4},{6,7},{7,6},{8,9},{9,8},{10,11... | collective-permute-start | bytes 1572872 | tf_op jit(solution)/shard_map/factor/ppermute | solution.py:22
  154.8 4.8 %all-to-all-start.2 = ((f32[16,64,128]{2,1,0:T(8,128)}), f32[16,64,128]{2,1,0:T(8,128)}, u32[]{:S(2)}, u32[]{:S(2)}) async-start(f32[16,64,128]{2,1,0:T(8,128)} %copy-done.16), calls=%async_computation.2 | async-start | bytes 1048576 | tf_op jit(solution)/shard_map/backward/all_to_all | solution.py:656
  159.6 1.1 copy-done.6
  160.7 1.7 factor.12.done
  162.4 2.4 %factor.13 = (f32[512,1024]{1,0:T(8,128)}, f32[8,128]{1,0:T(8,128)S(1)}) custom-call(s32[8]{0:T(128)S(1)} %copy-done.23, f32[512,1024]{1,0:T(8,128)S(1)} %bitcast.13, f32[256,512]{1,0:T(8,128)} %factor.11.mine, f32[256,512]{1,0:T(8,128)} %collective-permute-done.13.sib, f32[512,1024]{1,0:T(8,128)} %factor.12.done), custom_call_target="tpu_custom_call", output_to_operand_aliasing={{0}: (4, {})} | custom-call | tf_op jit(solution)/shard_map/factor/pallas_call | solution.py:573
  164.9 6.0 %all-to-all-done.2.parts = f32[16,64,128]{2,1,0:T(8,128)} async-done(((f32[16,64,128]{2,1,0:T(8,128)}), f32[16,64,128]{2,1,0:T(8,128)}, u32[]{:S(2)}, u32[]{:S(2)}) %all-to-all-start.2) | async-done | bytes 524320 | tf_op jit(solution)/shard_map/backward/all_to_all | solution.py:656
  170.9 1.8 %backward.9 = f32[2,1,64,64]{3,2,1,0:T(8,128)} custom-call(s32[8]{0:T(128)S(1)} %copy-done.23, f32[2,1,64,64]{3,2,1,0:T(8,128)S(1)} %copy-done.25, f32[16,64,128]{2,1,0:T(8,128)} %all-to-all-done.2.parts, f32[8,128]{1,0:T(8,128)S(1)} %get-tuple-element.53.after), custom_call_target="tpu_custom_call" | custom-call | tf_op jit(solution)/shard_map/backward/pallas_call | solution.py:235
  (63 shorter events, 0.8 us)
Async XLA Ops:
  6.6 58.8 %all-to-all-start = ((bf16[16,136,512]{2,1,0:T(8,128)(2,1)}), bf16[16,136,512]{2,1,0:T(8,128)(2,1)S(1)}, u32[]{:S(2)}, u32[]{:S(2)}) async-start(bf16[16,136,512]{2,1,0:T(8,128)(2,1)} %get-tuple-element.28), calls=%async_computation | async-start | bytes 4456448 | tf_op jit(solution)/shard_map/columns/all_to_all | solution.py:626
  17.9 31.7 %collective-permute-start = (bf16[64,5120]{1,0:T(8,128)(2,1)}, bf16[64,5120]{1,0:T(8,128)(2,1)S(1)}, u32[]{:S(2)}, u32[]{:S(2)}) collective-permute-start(bf16[64,5120]{1,0:T(8,128)(2,1)} %get-tuple-element.30), channel_id=1, source_target_pairs={{0,240},{16,0},{32,16},{48,32},{64,48},{80,64},{96,80},{112,96},{1... | collective-permute-start | bytes 1966088 | tf_op jit(solution)/shard_map/weights/ppermute | solution.py:17
  23.6 25.7 %collective-permute-start.1 = (bf16[64,2048]{1,0:T(8,128)(2,1)}, bf16[64,2048]{1,0:T(8,128)(2,1)S(1)}, u32[]{:S(2)}, u32[]{:S(2)}) collective-permute-start(bf16[64,2048]{1,0:T(8,128)(2,1)} %get-tuple-element.31), channel_id=1, source_target_pairs={{0,16},{16,32},{32,48},{48,64},{64,80},{80,96},{96,112},{112,128},... | collective-permute-start | bytes 786440 | tf_op jit(solution)/shard_map/weights/ppermute | solution.py:17
  23.6 25.7 %collective-permute-start.2 = (bf16[64,2048]{1,0:T(8,128)(2,1)}, bf16[64,2048]{1,0:T(8,128)(2,1)S(1)}, u32[]{:S(2)}, u32[]{:S(2)}) collective-permute-start(bf16[64,2048]{1,0:T(8,128)(2,1)} %get-tuple-element.32), channel_id=1, source_target_pairs={{0,32},{16,48},{32,64},{48,80},{64,96},{80,112},{96,128},{112,144}... | collective-permute-start | bytes 786440 | tf_op jit(solution)/shard_map/weights/ppermute | solution.py:17
  49.3 0.7 copy-start.11
  49.3 0.8 copy-start.13
  50.1 8.5 %copy-start = (bf16[64,5120]{1,0:T(8,128)(2,1)}, bf16[64,5120]{1,0:T(8,128)(2,1)S(1)}, u32[]{:S(2)}) copy-start(bf16[64,5120]{1,0:T(8,128)(2,1)S(1)} %weights.6.mine.u1o.u1s.refs_12_) | copy-start | bytes 1966084
  50.1 8.5 %copy-start.21 = (s32[8]{0:T(128)S(1)}, s32[8]{0:T(128)}, u32[]{:S(2)}) copy-start(s32[8]{0:T(128)} %stack.47.where) | copy-start | bytes 100
  50.1 8.5 %collective-permute-start.3 = (bf16[64,5120]{1,0:T(8,128)(2,1)S(1)}, bf16[64,5120]{1,0:T(8,128)(2,1)S(1)}, u32[]{:S(2)}, u32[]{:S(2)}) collective-permute-start(bf16[64,5120]{1,0:T(8,128)(2,1)S(1)} %weights.6.mine.u1o.u1s.refs_12_), channel_id=1, source_target_pairs={{0,1},{1,0},{2,3},{3,2},{4,5},{5,4},{6,7},{7,6},{8,9},{9,8},{10,11... | collective-permute-start | bytes 1966088 | tf_op jit(solution)/shard_map/weights/ppermute | solution.py:22
  58.6 1.6 copy-start.1
  60.2 0.8 copy-start.18
  60.9 4.4 %copy-start.4 = (bf16[64,5120]{1,0:T(8,128)(2,1)}, bf16[64,5120]{1,0:T(8,128)(2,1)S(1)}, u32[]{:S(2)}) copy-start(bf16[64,5120]{1,0:T(8,128)(2,1)S(1)} %collective-permute-done.3.sib.refs_13_) | copy-start | bytes 1966084
  65.4 0.9 copy-start.9
  66.3 0.9 copy-start.12
  66.3 1.0 copy-start.14
  66.3 1.0 copy-start.22
  66.3 25.1 %collective-permute-start.4 = (bf16[16,136,512]{2,1,0:T(8,128)(2,1)S(1)}, bf16[16,136,512]{2,1,0:T(8,128)(2,1)}, u32[]{:S(2)}, u32[]{:S(2)}) collective-permute-start(bf16[16,136,512]{2,1,0:T(8,128)(2,1)S(1)} %columns.1.own), channel_id=1, source_target_pairs={{0,1},{1,0},{2,3},{3,2},{4,5},{5,4},{6,7},{7,6},{8,9},{9,8},{10,11... | collective-permute-start | bytes 6684680 | tf_op jit(solution)/shard_map/columns/ppermute | solution.py:22
  67.9 23.5 %copy-start.10 = (bf16[128,512]{1,0:T(8,128)(2,1)S(1)}, bf16[128,512]{1,0:T(8,128)(2,1)}, u32[]{:S(2)}) copy-start(bf16[128,512]{1,0:T(8,128)(2,1)} %get-tuple-element.33.rest_1_) | copy-start | bytes 393220
  67.9 23.5 %copy-start.15 = (bf16[128,512]{1,0:T(8,128)(2,1)S(1)}, bf16[128,512]{1,0:T(8,128)(2,1)}, u32[]{:S(2)}) copy-start(bf16[128,512]{1,0:T(8,128)(2,1)} %get-tuple-element.34.rest_2_) | copy-start | bytes 393220
  67.9 13.7 %collective-permute-start.6 = (bf16[128,2048]{1,0:T(8,128)(2,1)S(1)}, bf16[128,2048]{1,0:T(8,128)(2,1)}, u32[]{:S(2)}, u32[]{:S(2)}) collective-permute-start(bf16[128,2048]{1,0:T(8,128)(2,1)S(1)} %weights.7.a), channel_id=1, source_target_pairs={{0,4},{1,5},{2,6},{3,7},{4,0},{5,1},{6,2},{7,3},{8,12},{9,13},{10,... | collective-permute-start | bytes 1572872 | tf_op jit(solution)/shard_map/weights/ppermute | solution.py:27
  68.1 22.1 %all-to-all-start.1 = ((bf16[16,128,128]{2,1,0:T(8,128)(2,1)}), bf16[16,128,128]{2,1,0:T(8,128)(2,1)S(1)}, u32[]{:S(2)}, u32[]{:S(2)}) async-start(bf16[16,128,128]{2,1,0:T(8,128)(2,1)} %gates.4.after.rest_0_), calls=%async_computation.1 | async-start | bytes 1048576 | tf_op jit(solution)/shard_map/columns/all_to_all | solution.py:628
  91.3 7.4 %copy-start.3 = (bf16[256,2048]{1,0:T(8,128)(2,1)}, bf16[256,2048]{1,0:T(8,128)(2,1)S(1)}, u32[]{:S(2)}) copy-start(bf16[256,2048]{1,0:T(8,128)(2,1)S(1)} %backward.5.refs_10_) | copy-start | bytes 3145732
  91.3 18.6 %collective-permute-start.7 = (bf16[256,2048]{1,0:T(8,128)(2,1)S(1)}, bf16[256,2048]{1,0:T(8,128)(2,1)S(1)}, u32[]{:S(2)}, u32[]{:S(2)}) collective-permute-start(bf16[256,2048]{1,0:T(8,128)(2,1)S(1)} %backward.5.refs_10_), channel_id=1, source_target_pairs={{0,1},{1,0},{2,3},{3,2},{4,5},{5,4},{6,7},{7,6},{8,9},{9,8},{10,11... | collective-permute-start | bytes 3145736 | tf_op jit(solution)/shard_map/backward/ppermute | solution.py:22
  98.7 20.5 %collective-permute-start.5 = (bf16[256,1280]{1,0:T(8,128)(2,1)}, bf16[256,1280]{1,0:T(8,128)(2,1)}, u32[]{:S(2)}, u32[]{:S(2)}) collective-permute-start(bf16[256,1280]{1,0:T(8,128)(2,1)} %get-tuple-element.37), channel_id=1, source_target_pairs={{0,16},{16,32},{32,48},{48,64},{64,80},{80,96},{96,112},{112,128},... | collective-permute-start | bytes 1966088 | tf_op jit(solution)/shard_map/factor/ppermute | solution.py:17
  108.3 1.1 copy-start.7
  109.4 0.6 copy-start.26
  110.0 1.0 copy-start.27
  111.0 8.2 %copy-start.8 = (f32[256,1280]{1,0:T(8,128)S(1)}, f32[256,1280]{1,0:T(8,128)}, u32[]{:S(2)}) copy-start(f32[256,1280]{1,0:T(8,128)} %copy-done.7) | copy-start | bytes 3932164
  111.0 8.2 %copy-start.23 = (s32[8]{0:T(128)S(1)}, s32[8]{0:T(128)}, u32[]{:S(2)}) copy-start(s32[8]{0:T(128)} %stack.47.where) | copy-start | bytes 100
  119.2 0.8 copy-start.19
  121.3 28.4 %collective-permute-start.8 = (bf16[256,1280]{1,0:T(8,128)(2,1)S(1)}, bf16[256,1280]{1,0:T(8,128)(2,1)S(1)}, u32[]{:S(2)}, u32[]{:S(2)}) collective-permute-start(bf16[256,1280]{1,0:T(8,128)(2,1)S(1)} %get-tuple-element.42), channel_id=1, source_target_pairs={{0,16},{16,32},{32,48},{48,64},{64,80},{80,96},{96,112},{112,128},... | collective-permute-start | bytes 1966088 | tf_op jit(solution)/shard_map/factor/ppermute | solution.py:17
  121.4 19.8 %collective-permute-start.9 = (f32[128,128]{1,0:T(8,128)}, f32[128,128]{1,0:T(8,128)S(1)}, u32[]{:S(2)}, u32[]{:S(2)}) collective-permute-start(f32[128,128]{1,0:T(8,128)} %get-tuple-element.44), channel_id=1, source_target_pairs={{0,16},{16,32},{32,48},{48,64},{64,80},{80,96},{96,112},{112,128},... | collective-permute-start | bytes 196616 | tf_op jit(solution)/shard_map/backward/ppermute | solution.py:17
  121.5 19.7 %collective-permute-start.10 = (f32[128,128]{1,0:T(8,128)}, f32[128,128]{1,0:T(8,128)S(1)}, u32[]{:S(2)}, u32[]{:S(2)}) collective-permute-start(f32[128,128]{1,0:T(8,128)} %get-tuple-element.45), channel_id=1, source_target_pairs={{0,32},{16,48},{32,64},{48,80},{64,96},{80,112},{96,128},{112,144}... | collective-permute-start | bytes 196616 | tf_op jit(solution)/shard_map/backward/ppermute | solution.py:17
  121.6 19.6 %copy-start.17 = (f32[1,3,64,128]{3,2,1,0:T(8,128)S(1)}, f32[1,3,64,128]{3,2,1,0:T(8,128)}, u32[]{:S(2)}) copy-start(f32[1,3,64,128]{3,2,1,0:T(8,128)} %q0.1) | copy-start | bytes 294916
  121.6 19.6 %copy-start.20 = (f32[128,64]{1,0:T(8,128)S(1)}, f32[128,64]{1,0:T(8,128)}, u32[]{:S(2)}) copy-start(f32[128,64]{1,0:T(8,128)} %get-tuple-element.39.after.m0) | copy-start | bytes 98308
  121.6 19.6 %copy-start.24 = (f32[192,128]{1,0:T(8,128)S(1)}, f32[192,128]{1,0:T(8,128)}, u32[]{:S(2)}) copy-start(f32[192,128]{1,0:T(8,128)} %get-tuple-element.43.proj) | copy-start | bytes 294916
  127.2 32.4 %copy-start.2 = (f32[1,512,1024]{2,1,0:T(8,128)S(1)}, f32[1,512,1024]{2,1,0:T(8,128)}, u32[]{:S(2)}) copy-start(f32[1,512,1024]{2,1,0:T(8,128)} %param.14) | copy-start | bytes 6291460
  142.2 4.3 %collective-permute-start.11 = (f32[64,64]{1,0:T(8,128)S(1)}, f32[64,64]{1,0:T(8,128)S(1)}, u32[]{:S(2)}, u32[]{:S(2)}) collective-permute-start(f32[64,64]{1,0:T(8,128)S(1)} %get-tuple-element.48), channel_id=1, source_target_pairs={{0,240},{16,0},{32,16},{48,32},{64,48},{80,64},{96,80},{112,96},{1... | collective-permute-start | bytes 49160 | tf_op jit(solution)/shard_map/backward/ppermute | solution.py:17
  144.5 3.7 %collective-permute-start.12 = (f32[64,64]{1,0:T(8,128)S(1)}, f32[64,64]{1,0:T(8,128)S(1)}, u32[]{:S(2)}, u32[]{:S(2)}) collective-permute-start(f32[64,64]{1,0:T(8,128)S(1)} %get-tuple-element.49), channel_id=1, source_target_pairs={{0,224},{16,240},{32,0},{48,16},{64,32},{80,48},{96,64},{112,80},{... | collective-permute-start | bytes 49160 | tf_op jit(solution)/shard_map/backward/ppermute | solution.py:17
  148.9 0.8 copy-start.16
  151.1 0.8 copy-start.5
  151.9 10.5 %collective-permute-start.13 = (f32[256,512]{1,0:T(8,128)}, f32[256,512]{1,0:T(8,128)}, u32[]{:S(2)}, u32[]{:S(2)}) collective-permute-start(f32[256,512]{1,0:T(8,128)} %factor.11.mine), channel_id=1, source_target_pairs={{0,1},{1,0},{2,3},{3,2},{4,5},{5,4},{6,7},{7,6},{8,9},{9,8},{10,11... | collective-permute-start | bytes 1572872 | tf_op jit(solution)/shard_map/factor/ppermute | solution.py:22
  154.8 16.1 %all-to-all-start.2 = ((f32[16,64,128]{2,1,0:T(8,128)}), f32[16,64,128]{2,1,0:T(8,128)}, u32[]{:S(2)}, u32[]{:S(2)}) async-start(f32[16,64,128]{2,1,0:T(8,128)} %copy-done.16), calls=%async_computation.2 | async-start | bytes 1048576 | tf_op jit(solution)/shard_map/backward/all_to_all | solution.py:656
  159.6 1.1 copy-start.6
  162.4 8.4 %copy-start.25 = (f32[2,1,64,64]{3,2,1,0:T(8,128)S(1)}, f32[2,1,64,64]{3,2,1,0:T(8,128)}, u32[]{:S(2)}) copy-start(f32[2,1,64,64]{3,2,1,0:T(8,128)} %old.1) | copy-start | bytes 98308

commit v7 on v6

--- a/solution.py
+++ b/solution.py
@@ -10,6 +10,7 @@
 F32 = jnp.float32
 BF16 = jnp.bfloat16
 ANY = pl.BlockSpec(memory_space=pl.ANY)
+TOKEN = jax.ShapeDtypeStruct((8, 128), F32)
 
 
 def shift(block, axis, distance):
@@ -156,27 +157,49 @@
     )
 
 
-def ahead_kernel(where, x, up, gate0, x1):
+def ahead_kernel(where, x, up, gate0, u0o, u0s, x1, own, oth, token):
     add = jnp.dot(gate0[...], up[0, 0], preferred_element_type=F32)
     x1[...] = (x[...].astype(F32) + add).astype(BF16)
 
-
-def next_activation(where, x, adapter_up, gate0):
+    @pl.when(pl.program_id(0) == 0)
+    def _():
+        own[...] = u0o[0, 0]
+        oth[...] = u0s[0, 0]
+        token[...] = jnp.zeros_like(token)
+
+
+def next_activation(where, x, adapter_up, gate0, rows):
     tok, width = x.shape
     rank = gate0.shape[1]
     grid = 4
     each = width // grid
+    u0 = lambda side: pl.BlockSpec(
+        (1, 1, rank, rows), lambda i, w: (w[C0], 0, 0, 2 * w[CHIP] + side(w))
+    )
+    one = lambda shape: pl.BlockSpec(shape, lambda i, w: (0, 0))
     return call(
         ahead_kernel,
         where,
-        (x, adapter_up, gate0),
+        (x, adapter_up, gate0, adapter_up, adapter_up),
         [
             pl.BlockSpec((tok, each), lambda i, w: (0, i)),
             pl.BlockSpec((1, 1, rank, each), lambda i, w: (w[C0], 0, 0, i)),
-            pl.BlockSpec((tok, rank), lambda i, w: (0, 0)),
+            one((tok, rank)),
+            u0(lambda w: w[CORE]),
+            u0(lambda w: 1 - w[CORE]),
         ],
-        jax.ShapeDtypeStruct((tok, width), BF16),
-        pl.BlockSpec((tok, each), lambda i, w: (0, i)),
+        [
+            jax.ShapeDtypeStruct((tok, width), BF16),
+            jax.ShapeDtypeStruct((rank, rows), BF16),
+            jax.ShapeDtypeStruct((rank, rows), BF16),
+            TOKEN,
+        ],
+        [
+            pl.BlockSpec((tok, each), lambda i, w: (0, i)),
+            one((rank, rows)),
+            one((rank, rows)),
+            one(TOKEN.shape),
+        ],
         (grid,),
     )
 
@@ -200,32 +223,6 @@
         where,
         (x1, ahead_mine, ahead_sib, gate0),
         jax.ShapeDtypeStruct((replicas, tok, 2 * rank), BF16),
-    )
-
-
-def columns_kernel(where, u0o, u0s, u1o, u1s, after, ups_o, ups_s):
-    rank = u1o.shape[0]
-    for out, zero, one in ((ups_o, u0o, u1o), (ups_s, u0s, u1s)):
-        out[:rank] = zero[0, 0]
-        out[rank:] = one[...]
-
-
-def up_columns(where, adapter_up, ahead, rows, after):
-    rank = ahead.shape[0]
-    mine, sib = (lambda w: w[CORE]), (lambda w: 1 - w[CORE])
-    u0 = lambda side: pl.BlockSpec(
-        (1, 1, rank, rows), lambda i, w: (w[C0], 0, 0, 2 * w[CHIP] + side(w))
-    )
-    u1 = lambda side: pl.BlockSpec((rank, rows), lambda i, w: (0, side(w)))
-    out = pl.BlockSpec((2 * rank, rows), lambda i, w: (0, 0))
-    return call(
-        columns_kernel,
-        where,
-        (adapter_up, adapter_up, ahead, ahead, after),
-        [u0(mine), u0(sib), u1(mine), u1(sib), ANY],
-        [jax.ShapeDtypeStruct((2 * rank, rows), BF16)] * 2,
-        [out, out],
-        (1,),
     )
 
 
@@ -273,11 +270,16 @@
 
 
 def gram_kernel(step, where, own, other, *rest):
-    if step:
-        got, ups_own, ups_oth = rest[:3]
-    rest = rest[3 if step else 0:]
     core = where[CORE]
     replicas, long, rows = own.shape
+    if step:
+        got, up_own, up_oth, ahead = rest[:4]
+        ups_own, ups_oth = up_own[...], up_oth[...]
+    if step == 2:
+        one = lambda side: ahead[:, pl.ds(pl.multiple_of(side * rows, rows), rows)]
+        ups_own = jnp.concatenate([ups_own, one(core)], axis=0)
+        ups_oth = jnp.concatenate([ups_oth, one(1 - core)], axis=0)
+    rest = rest[4 if step else 0:]
     tok = long - 8
     hlf = rows // 2
     per = 4
@@ -293,9 +295,8 @@
         def rebuilt(ref, ups):
             act = jnp.concatenate([ref[k, :tok, :] for k in ks], axis=0).astype(F32)
             if step:
-                rank = ups.shape[0] // 2 * step
-                gate = jnp.concatenate([got[k] for k in ks], axis=0)[:, :rank]
-                add = jnp.dot(gate, ups[:rank], preferred_element_type=F32)
+                gate = jnp.concatenate([got[k] for k in ks], axis=0)[:, :ups.shape[0]]
+                add = jnp.dot(gate, ups, preferred_element_type=F32)
                 act = (act + add).astype(BF16).astype(F32)
             scale = [jnp.broadcast_to(columns[:, k:k + 1], (tok, rows)) for k in ks]
             return (jnp.concatenate(scale, axis=0) * act).astype(BF16)
@@ -320,9 +321,6 @@
     token[...] = jnp.zeros_like(token)
     if step == 2:
         out[...] = acc[...].astype(BF16)
-
-
-TOKEN = jax.ShapeDtypeStruct((8, 128), F32)
 
 
 def gram(step, where, own, other, ups=(), after=()):
@@ -436,14 +434,15 @@
     )
 
 
-def merge_kernel(where, a, b, after, out, token):
+def merge_kernel(where, a, b, *rest):
+    out, token = rest[-2:]
     out[...] = (a[...] + b[...].astype(F32)).astype(BF16)
     token[...] = jnp.zeros_like(token)
 
 
 def merge(where, a, b, after):
     return local(
-        merge_kernel, where, (a, b), [jax.ShapeDtypeStruct(a.shape, BF16), TOKEN], (), (after,)
+        merge_kernel, where, (a, b), [jax.ShapeDtypeStruct(a.shape, BF16), TOKEN], (), after
     )
 
 
@@ -612,51 +611,50 @@
         ahead = shift(ahead, "section", -1)
         behind1 = shift(behind1, "section", 1)
         behind2 = shift(behind2, "section", 2)
-        ahead = tie(ahead, behind1, behind2, space=pltpu.VMEM)
+        x1, up_own, up_oth, token5 = next_activation(where, x0, adapter_up, gate0, rows)
+        ahead = tie(ahead, behind1, behind2, token5, space=pltpu.VMEM)
         ahead_sib = swap_cores(ahead)
         behind = join(where, behind1, behind2)
         behind_pair = swap_chips(behind)
 
     with jax.named_scope("gates"):
-        x1 = next_activation(where, x0, adapter_up, gate0)
         sent = gates(where, x1, ahead, ahead_sib, gate0, replicas)
-        ups_own, ups_oth = up_columns(where, adapter_up, ahead, rows, sent)
 
     with jax.named_scope("columns"):
-        own = tie(lax.all_to_all(pieces, "dp", 0, 0), sent, ups_own, space=pltpu.VMEM)
+        own = tie(lax.all_to_all(pieces, "dp", 0, 0), sent, behind_pair, space=pltpu.VMEM)
         other = swap_cores(own)
         got = lax.all_to_all(sent, "dp", 0, 0)
 
     with jax.named_scope("factor"):
-        ups = (got, ups_own, ups_oth)
-        step2, token2 = gram(2, where, own, other, ups)
+        ups = (got, up_own, up_oth, ahead)
+        step0, token0 = gram(0, where, own, other)
+        step2, token2 = gram(2, where, own, other, ups, (token0,))
         from2 = shift(step2, "section", 1)
-        step1, token1 = gram(1, where, own, other, ups, (token2,))
 
     with jax.named_scope("backward"):
-        behind = join(where, behind, behind_pair, (got,))
+        behind = join(where, behind, behind_pair)
         behind_sib = swap_cores(behind)
         proj, m0, by1, by2 = project(
             where, returning[0], adapter_down, adapter_up, behind, behind_sib, ahead, ahead_sib,
-            stashed, token1,
+            stashed, token2,
         )
         by1 = shift(by1, "section", 1)
         by2 = shift(by2, "section", 2)
 
     with jax.named_scope("factor"):
-        from1, token3 = merge(where, step1, from2, m0)
+        step1, token1 = gram(1, where, own, other, ups, (m0,))
+        from1, token3 = merge(where, step1, from2, (token1, by1, by2))
         from1 = shift(from1, "section", 1)
-        step0, token0 = gram(0, where, own, other, (), (token3,))
 
     with jax.named_scope("backward"):
-        outer0, outer1, outer2 = back(where, proj, m0, by1, by2, stashed, token0)
+        outer0, outer1, outer2 = back(where, proj, m0, by1, by2, stashed, token3)
         outer1 = shift(outer1, "section", -1)
         outer2 = shift(outer2, "section", -2)
         share, token4 = curvature(where, (outer0, outer1, outer2), replicas)
         shares = lax.all_to_all(share, "dp", 0, 0)
 
     with jax.named_scope("factor"):
-        mine = cross_part(where, step0, from1, token4)
+        mine = cross_part(where, step0, from1, shares)
         sib = swap_cores(mine)
         factor_scale = 0.25 / (steps_count * tokens)
         input_factor_new, last = update(

time: 174 us -> 159 us (0.914)
  waiting for transfers between devices: 65.7 us -> 42.6 us
  blocking collectives: 0 us -> 21.8 us
  Pallas kernels: 56.1 us -> 51.4 us
  starting transfers between devices: 38.2 us -> 33.6 us
  local copies, waits for them, and re-layouts: 11.6 us -> 7.84 us
    all_to_all x0 -> x1, blocking collectives: none -> 21.8 us  [shards(): shares = lax.all_to_all(share, 'dp', 0, 0)]
    ppermute x9, waiting for transfers between devices: 44.2 us -> 30.5 us  [shift(): lax.ppermute(block, axis, [(i, (i + distance) % count) for i in range(cou...]
    all_to_all x1, waiting for transfers between devices: 8.61 us -> 0.71 us  [shards(): got = lax.all_to_all(sent, 'dp', 0, 0)]
    all_to_all x1 -> x0, waiting for transfers between devices: 5.96 us -> none  [shards(): shares = lax.all_to_all(share, 'dp', 0, 0)]
    all_to_all x1 -> x0, starting transfers between devices: 4.82 us -> none  [shards(): shares = lax.all_to_all(share, 'dp', 0, 0)]
    ppermute x1, waiting for transfers between devices: 6.97 us -> 11.1 us  [swap_chips(): return lax.ppermute(block, 'dp', [(i, i ^ 4) for i in range(count)])]
    unnamed x56 -> x50, local copies, waits for them, and re-layouts: 10.9 us -> 7.15 us
    pallas_call x5 -> x4, Pallas kernels: 23.1 us -> 20.9 us  [call(): pl.pallas_call(kernel, grid_spec=spec, out_shape=outs, input_output_alias...]
  transfers between devices with their start and end apart: 17 -> 16, of which waited for: 9 -> 9; matrix products, arithmetic and copies ran while one was open for 0% -> 0% of each run, Pallas kernels for 27% -> 26%
where the time goes in v7:
time: 159 us; the launch traced here: 158 us
  Pallas kernels  51.4 us (32%)
  waiting for transfers between devices  42.6 us (27%)
  starting transfers between devices  33.6 us (21%)
  blocking collectives  21.8 us (14%)
  local copies, waits for them, and re-layouts  7.84 us (5%)
    ppermute x9, waiting for transfers between devices, shift(): lax.ppermute(block, axis, [(i, (i + distance) % count) for i in range(cou...  30.5 us
    pallas_call x12, Pallas kernels, local(): pl.pallas_call(kernel, in_specs=[pl.BlockSpec(memory_space=pltpu.SMEM)] +...  28.8 us
    all_to_all x1, blocking collectives, shards(): shares = lax.all_to_all(share, 'dp', 0, 0)  21.8 us
    pallas_call x4, Pallas kernels, call(): pl.pallas_call(kernel, grid_spec=spec, out_shape=outs, input_output_alias...  20.9 us
    ppermute x9, starting transfers between devices, shift(): lax.ppermute(block, axis, [(i, (i + distance) % count) for i in range(cou...  13 us
    ppermute x1, waiting for transfers between devices, swap_chips(): return lax.ppermute(block, 'dp', [(i, i ^ 4) for i in range(count)])  11.1 us
    all_to_all x1, starting transfers between devices, shards(): lax.all_to_all(pieces, 'dp', 0, 0)  8.45 us
    unnamed x50, local copies, waits for them, and re-layouts  7.15 us
  transfers between devices with their start and end apart: 16, of which 9 were waited for; matrix products, arithmetic and copies ran while one was open for 0% of the time, Pallas kernels for 26%

profile of v7, /device:TPU:1, one launch (start us, length us, event | category | flops | bytes accessed | tf_op | source)
XLA Modules:
  0.0 158.4 jit_solution(7453172598189060528)
XLA Ops:
  0.7 0.7 stack.47.where
  1.4 5.2 %weights.5 = (bf16[16,136,512]{2,1,0:T(8,128)(2,1)}, bf16[128,64]{1,0:T(8,128)(2,1)}) custom-call(s32[8]{0:T(128)} %stack.47.where, bf16[128,8192]{1,0:T(8,128)(2,1)} %bitcast.16, bf16[2,1,64,8192]{3,2,1,0:T(8,128)(2,1)} %refs_7_.1, s32[16,128]{1,0:T(8,128)} %ids.1), custom_call_target="tpu_custom_call" | custom-call | tf_op jit(solution)/shard_map/weights/pallas_call | solution.py:47
  6.6 8.4 %all-to-all-start = ((bf16[16,136,512]{2,1,0:T(8,128)(2,1)}), bf16[16,136,512]{2,1,0:T(8,128)(2,1)S(1)}, u32[]{:S(2)}, u32[]{:S(2)}) async-start(bf16[16,136,512]{2,1,0:T(8,128)(2,1)} %get-tuple-element.30), calls=%async_computation | async-start | bytes 4456448 | tf_op jit(solution)/shard_map/columns/all_to_all | solution.py:624
  15.0 2.9 %weights.7 = (bf16[64,5120]{1,0:T(8,128)(2,1)}, bf16[64,2048]{1,0:T(8,128)(2,1)}, bf16[64,2048]{1,0:T(8,128)(2,1)}) custom-call(s32[8]{0:T(128)} %stack.47.where, bf16[2,1,64,8192]{3,2,1,0:T(8,128)(2,1)} %refs_9_.1, bf16[2,1,64,8192]{3,2,1,0:T(8,128)(2,1)} %refs_7_.1, bf16[2,1,64,8192]{3,2,1,0:T(8,128)(2,1)} %refs_9_.1, bf16[2,1,64,8192]{3,2,1,0:T(8,128)(2,1)} %refs_9_.1, ...), custom_call_target="tpu_custom_call" | custom-call | tf_op jit(solution)/shard_map/weights/pallas_call | solution.py:47
  17.9 5.7 %collective-permute-start = (bf16[64,5120]{1,0:T(8,128)(2,1)}, bf16[64,5120]{1,0:T(8,128)(2,1)S(1)}, u32[]{:S(2)}, u32[]{:S(2)}) collective-permute-start(bf16[64,5120]{1,0:T(8,128)(2,1)} %get-tuple-element.33), channel_id=1, source_target_pairs={{0,240},{16,0},{32,16},{48,32},{64,48},{80,64},{96,80},{112,96},{1... | collective-permute-start | bytes 1966088 | tf_op jit(solution)/shard_map/weights/ppermute | solution.py:18
  23.6 5.2 %weights.6 = (bf16[128,8192]{1,0:T(8,128)(2,1)}, bf16[64,512]{1,0:T(8,128)(2,1)}, bf16[64,512]{1,0:T(8,128)(2,1)}, f32[8,128]{1,0:T(8,128)}) custom-call(s32[8]{0:T(128)} %stack.47.where, bf16[128,8192]{1,0:T(8,128)(2,1)} %bitcast.17, bf16[2,1,64,8192]{3,2,1,0:T(8,128)(2,1)} %refs_9_.1, bf16[128,64]{1,0:T(8,128)(2,1)} %get-tuple-element.31.gate0.after, ...), custom_call_target="tpu_custom_call" | custom-call | tf_op jit(solution)/shard_map/weights/pallas_call | solution.py:47
  28.9 20.4 %collective-permute-done.1.rest_0_.a = bf16[64,2048]{1,0:T(8,128)(2,1)S(1)} collective-permute-done((bf16[64,2048]{1,0:T(8,128)(2,1)}, bf16[64,2048]{1,0:T(8,128)(2,1)S(1)}, u32[]{:S(2)}, u32[]{:S(2)}) %collective-permute-start.1) | collective-permute-done | bytes 262176 | tf_op jit(solution)/shard_map/weights/ppermute | solution.py:18
  49.3 0.3 collective-permute-done.x
  49.6 0.7 copy-done.23
  50.3 3.1 %collective-permute-start.3 = (bf16[64,5120]{1,0:T(8,128)(2,1)S(1)}, bf16[64,5120]{1,0:T(8,128)(2,1)S(1)}, u32[]{:S(2)}, u32[]{:S(2)}) collective-permute-start(bf16[64,5120]{1,0:T(8,128)(2,1)S(1)} %weights.8.mine.rest_3_.refs_12_), channel_id=1, source_target_pairs={{0,1},{1,0},{2,3},{3,2},{4,5},{5,4},{6,7},{7,6},{8,9},{9,8},{10,11... | collective-permute-start | bytes 1966088 | tf_op jit(solution)/shard_map/weights/ppermute | solution.py:23
  53.4 0.6 weights.9.a
  54.0 0.8 collective-permute-start.4
  54.8 0.3 collective-permute-done.3.sib.refs_13_
  55.1 1.3 gates.1.rest_0_
  56.5 11.1 %collective-permute-done.4.rest_1_.b = bf16[128,2048]{1,0:T(8,128)(2,1)S(1)} collective-permute-done((bf16[128,2048]{1,0:T(8,128)(2,1)S(1)}, bf16[128,2048]{1,0:T(8,128)(2,1)S(1)}, u32[]{:S(2)}, u32[]{:S(2)}) %collective-permute-start.4) | collective-permute-done | bytes 524320 | tf_op jit(solution)/shard_map/weights/ppermute | solution.py:28
  67.6 0.8 copy-done.10
  68.4 1.0 copy-done.11
  69.5 0.8 collective-permute-start.5
  70.3 5.9 %all-to-all-start.1 = ((bf16[16,128,128]{2,1,0:T(8,128)(2,1)}), bf16[16,128,128]{2,1,0:T(8,128)(2,1)S(1)}, u32[]{:S(2)}, u32[]{:S(2)}) async-start(bf16[16,128,128]{2,1,0:T(8,128)(2,1)} %copy-done.5), calls=%async_computation.1 | async-start | bytes 1048576 | tf_op jit(solution)/shard_map/columns/all_to_all | solution.py:626
  76.2 1.0 copy-done.8
  77.2 1.0 copy-done.12
  78.3 1.6 %backward.5.refs_10_ = bf16[256,2048]{1,0:T(8,128)(2,1)} custom-call(s32[8]{0:T(128)S(1)} %copy-done.19, bf16[128,2048]{1,0:T(8,128)(2,1)S(1)} %copy-done.8, bf16[128,2048]{1,0:T(8,128)(2,1)S(1)} %copy-done.12), custom_call_target="tpu_custom_call" | custom-call | tf_op jit(solution)/shard_map/backward/pallas_call | solution.py:232
  79.9 0.1 collective-permute-start.6
  80.0 5.6 %factor.7 = (f32[256,1280]{1,0:T(8,128)S(1)}, f32[8,128]{1,0:T(8,128)S(1)}) custom-call(s32[8]{0:T(128)S(1)} %copy-done.19, bf16[16,136,512]{2,1,0:T(8,128)(2,1)S(1)} %columns.1.own, bf16[16,136,512]{2,1,0:T(8,128)(2,1)} %collective-permute-done.5.other), custom_call_target="tpu_custom_call" | custom-call | tf_op jit(solution)/shard_map/factor/pallas_call | solution.py:232
  85.6 1.0 copy-done.3
  86.6 0.7 all-to-all-done.1.rest_0_
  87.3 7.1 %factor.8 = (bf16[256,1280]{1,0:T(8,128)(2,1)}, f32[8,128]{1,0:T(8,128)S(1)}) custom-call(s32[8]{0:T(128)S(1)} %copy-done.19, bf16[16,136,512]{2,1,0:T(8,128)(2,1)S(1)} %columns.1.own, bf16[16,136,512]{2,1,0:T(8,128)(2,1)} %collective-permute-done.5.other, bf16[16,128,128]{2,1,0:T(8,128)(2,1)S(1)} %all-to-all-done.1.rest_0_, bf16[64,512]{1,0:T(8,128)(2,1)S(1)} %copy-done.17, ...), custom_call_target="tpu_custom_call" | custom-call | tf_op jit(solution)/shard_map/factor/pallas_call | solution.py:232
  94.5 0.6 copy-done.24
  95.1 3.5 %collective-permute-start.7 = (bf16[256,1280]{1,0:T(8,128)(2,1)}, bf16[256,1280]{1,0:T(8,128)(2,1)}, u32[]{:S(2)}, u32[]{:S(2)}) collective-permute-start(bf16[256,1280]{1,0:T(8,128)(2,1)} %get-tuple-element.44), channel_id=1, source_target_pairs={{0,16},{16,32},{32,48},{48,64},{64,80},{80,96},{96,112},{112,128},... | collective-permute-start | bytes 1966088 | tf_op jit(solution)/shard_map/factor/ppermute | solution.py:18
  98.6 7.6 %backward.6 = (f32[192,128]{1,0:T(8,128)}, f32[128,64]{1,0:T(8,128)}, f32[128,128]{1,0:T(8,128)}, f32[128,128]{1,0:T(8,128)}) custom-call(s32[8]{0:T(128)} %stack.47.where, bf16[128,8192]{1,0:T(8,128)(2,1)} %bitcast.14, bf16[128,8192]{1,0:T(8,128)(2,1)} %bitcast.15, bf16[2,1,64,8192]{3,2,1,0:T(8,128)(2,1)} %refs_9_.1, bf16[2,1,64,8192]{3,2,1,0:T(8,128)(2,1)} %refs_9_.1, ...), custom_call_target="tpu_custom_call" | custom-call | tf_op jit(solution)/shard_map/backward/pallas_call | solution.py:47
  106.2 0.1 collective-permute-start.8
  106.4 0.8 copy-done.15
  107.2 6.0 %factor.9 = (f32[256,1280]{1,0:T(8,128)S(1)}, f32[8,128]{1,0:T(8,128)S(1)}) custom-call(s32[8]{0:T(128)S(1)} %copy-done.20, bf16[16,136,512]{2,1,0:T(8,128)(2,1)S(1)} %columns.1.own, bf16[16,136,512]{2,1,0:T(8,128)(2,1)} %collective-permute-done.5.other, bf16[16,128,128]{2,1,0:T(8,128)(2,1)S(1)} %all-to-all-done.1.rest_0_, bf16[64,512]{1,0:T(8,128)(2,1)S(1)} %copy-done.17, ...), custom_call_target="tpu_custom_call" | custom-call | tf_op jit(solution)/shard_map/factor/pallas_call | solution.py:232
  113.3 2.5 %collective-permute-done.8.rest_1_.by1 = f32[128,128]{1,0:T(8,128)S(1)} collective-permute-done((f32[128,128]{1,0:T(8,128)}, f32[128,128]{1,0:T(8,128)S(1)}, u32[]{:S(2)}, u32[]{:S(2)}) %collective-permute-start.8) | collective-permute-done | bytes 65568 | tf_op jit(solution)/shard_map/backward/ppermute | solution.py:18
  115.8 3.3 %collective-permute-done.9.rest_2_.by2 = f32[128,128]{1,0:T(8,128)S(1)} collective-permute-done((f32[128,128]{1,0:T(8,128)}, f32[128,128]{1,0:T(8,128)S(1)}, u32[]{:S(2)}, u32[]{:S(2)}) %collective-permute-start.9) | collective-permute-done | bytes 65568 | tf_op jit(solution)/shard_map/backward/ppermute | solution.py:18
  119.1 1.3 factor.10
  120.4 0.1 collective-permute-start.10
  120.5 1.0 backward.7
  121.6 3.6 %collective-permute-start.11 = (f32[64,64]{1,0:T(8,128)S(1)}, f32[64,64]{1,0:T(8,128)S(1)}, u32[]{:S(2)}, u32[]{:S(2)}) collective-permute-start(f32[64,64]{1,0:T(8,128)S(1)} %get-tuple-element.52), channel_id=1, source_target_pairs={{0,240},{16,0},{32,16},{48,32},{64,48},{80,64},{96,80},{112,96},{1... | collective-permute-start | bytes 49160 | tf_op jit(solution)/shard_map/backward/ppermute | solution.py:18
  125.1 1.0 collective-permute-done.11.outer1
  126.1 2.9 %collective-permute-done.12.outer2 = f32[64,64]{1,0:T(8,128)S(1)} collective-permute-done((f32[64,64]{1,0:T(8,128)S(1)}, f32[64,64]{1,0:T(8,128)S(1)}, u32[]{:S(2)}, u32[]{:S(2)}) %collective-permute-start.12) | collective-permute-done | bytes 16416 | tf_op jit(solution)/shard_map/backward/ppermute | solution.py:18
  129.1 0.7 backward.8
  129.7 21.8 %all_to_all.15.after.parts = f32[16,64,128]{2,1,0:T(8,128)S(1)} all-to-all(f32[16,64,128]{2,1,0:T(8,128)S(1)} %get-tuple-element.54), channel_id=1, replica_groups=mesh['section'=16,'dp'=16] {'dp'}, dimensions={0} | all-to-all | bytes 1048576 | tf_op jit(solution)/shard_map/backward/all_to_all | solution.py:654
  151.6 0.6 factor.11.mine
  152.2 1.4 collective-permute-start.13
  153.6 1.7 %factor.12.done = f32[512,1024]{1,0:T(8,128)} custom-call(s32[8]{0:T(128)S(1)} %copy-done.20, f32[512,1024]{1,0:T(8,128)S(1)} %bitcast.12, f32[256,1280]{1,0:T(8,128)S(1)} %copy-done.4, bf16[256,1280]{1,0:T(8,128)(2,1)S(1)} %collective-permute-done.10.came, f32[8,128]{1,0:T(8,128)S(1)} %get-tuple-element.55.after), custom_call_target="tpu_custom_call" | custom-call | tf_op jit(solution)/shard_map/factor/pallas_call | solution.py:232
  155.3 1.7 %factor.13 = (f32[512,1024]{1,0:T(8,128)}, f32[8,128]{1,0:T(8,128)S(1)}) custom-call(s32[8]{0:T(128)S(1)} %copy-done.20, f32[512,1024]{1,0:T(8,128)S(1)} %bitcast.13, f32[256,512]{1,0:T(8,128)S(1)} %factor.11.mine, f32[256,512]{1,0:T(8,128)S(1)} %collective-permute-done.13.sib, f32[512,1024]{1,0:T(8,128)} %factor.12.done), custom_call_target="tpu_custom_call", output_to_operand_aliasing={{0}: (4, {})} | custom-call | tf_op jit(solution)/shard_map/factor/pallas_call | solution.py:572
  157.1 1.3 backward.9
  (55 shorter events, 0.2 us)
Async XLA Ops:
  6.6 61.9 %all-to-all-start = ((bf16[16,136,512]{2,1,0:T(8,128)(2,1)}), bf16[16,136,512]{2,1,0:T(8,128)(2,1)S(1)}, u32[]{:S(2)}, u32[]{:S(2)}) async-start(bf16[16,136,512]{2,1,0:T(8,128)(2,1)} %get-tuple-element.30), calls=%async_computation | async-start | bytes 4456448 | tf_op jit(solution)/shard_map/columns/all_to_all | solution.py:624
  17.9 31.7 %collective-permute-start = (bf16[64,5120]{1,0:T(8,128)(2,1)}, bf16[64,5120]{1,0:T(8,128)(2,1)S(1)}, u32[]{:S(2)}, u32[]{:S(2)}) collective-permute-start(bf16[64,5120]{1,0:T(8,128)(2,1)} %get-tuple-element.33), channel_id=1, source_target_pairs={{0,240},{16,0},{32,16},{48,32},{64,48},{80,64},{96,80},{112,96},{1... | collective-permute-start | bytes 1966088 | tf_op jit(solution)/shard_map/weights/ppermute | solution.py:18
  23.6 25.7 %collective-permute-start.1 = (bf16[64,2048]{1,0:T(8,128)(2,1)}, bf16[64,2048]{1,0:T(8,128)(2,1)S(1)}, u32[]{:S(2)}, u32[]{:S(2)}) collective-permute-start(bf16[64,2048]{1,0:T(8,128)(2,1)} %get-tuple-element.34), channel_id=1, source_target_pairs={{0,16},{16,32},{32,48},{48,64},{64,80},{80,96},{96,112},{112,128},... | collective-permute-start | bytes 786440 | tf_op jit(solution)/shard_map/weights/ppermute | solution.py:18
  23.6 29.8 %copy-start.19 = (s32[8]{0:T(128)S(1)}, s32[8]{0:T(128)}, u32[]{:S(2)}) copy-start(s32[8]{0:T(128)} %stack.47.where) | copy-start | bytes 100
  23.6 25.7 %collective-permute-start.2 = (bf16[64,2048]{1,0:T(8,128)(2,1)}, bf16[64,2048]{1,0:T(8,128)(2,1)S(1)}, u32[]{:S(2)}, u32[]{:S(2)}) collective-permute-start(bf16[64,2048]{1,0:T(8,128)(2,1)} %get-tuple-element.35), channel_id=1, source_target_pairs={{0,32},{16,48},{32,64},{48,80},{64,96},{80,112},{96,128},{112,144}... | collective-permute-start | bytes 786440 | tf_op jit(solution)/shard_map/weights/ppermute | solution.py:18
  28.9 26.3 %copy-start.9 = (bf16[128,8192]{1,0:T(8,128)(2,1)S(1)}, bf16[128,8192]{1,0:T(8,128)(2,1)}, u32[]{:S(2)}) copy-start(bf16[128,8192]{1,0:T(8,128)(2,1)} %get-tuple-element.32.x1) | copy-start | bytes 6291460
  28.9 26.3 %copy-start.14 = (bf16[128,64]{1,0:T(8,128)(2,1)S(1)}, bf16[128,64]{1,0:T(8,128)(2,1)}, u32[]{:S(2)}) copy-start(bf16[128,64]{1,0:T(8,128)(2,1)} %get-tuple-element.31.gate0.after) | copy-start | bytes 49156
  49.6 0.7 copy-start.23
  50.3 37.0 %copy-start = (bf16[64,5120]{1,0:T(8,128)(2,1)}, bf16[64,5120]{1,0:T(8,128)(2,1)S(1)}, u32[]{:S(2)}) copy-start(bf16[64,5120]{1,0:T(8,128)(2,1)S(1)} %weights.8.mine.rest_3_.refs_12_) | copy-start | bytes 1966084
  50.3 4.8 %collective-permute-start.3 = (bf16[64,5120]{1,0:T(8,128)(2,1)S(1)}, bf16[64,5120]{1,0:T(8,128)(2,1)S(1)}, u32[]{:S(2)}, u32[]{:S(2)}) collective-permute-start(bf16[64,5120]{1,0:T(8,128)(2,1)S(1)} %weights.8.mine.rest_3_.refs_12_), channel_id=1, source_target_pairs={{0,1},{1,0},{2,3},{3,2},{4,5},{5,4},{6,7},{7,6},{8,9},{9,8},{10,11... | collective-permute-start | bytes 1966088 | tf_op jit(solution)/shard_map/weights/ppermute | solution.py:23
  54.0 2.5 %copy-start.7 = (bf16[128,2048]{1,0:T(8,128)(2,1)}, bf16[128,2048]{1,0:T(8,128)(2,1)S(1)}, u32[]{:S(2)}) copy-start(bf16[128,2048]{1,0:T(8,128)(2,1)S(1)} %weights.9.a) | copy-start | bytes 1572868
  54.0 13.6 %collective-permute-start.4 = (bf16[128,2048]{1,0:T(8,128)(2,1)S(1)}, bf16[128,2048]{1,0:T(8,128)(2,1)S(1)}, u32[]{:S(2)}, u32[]{:S(2)}) collective-permute-start(bf16[128,2048]{1,0:T(8,128)(2,1)S(1)} %weights.9.a), channel_id=1, source_target_pairs={{0,4},{1,5},{2,6},{3,7},{4,0},{5,1},{6,2},{7,3},{8,12},{9,13},{10,... | collective-permute-start | bytes 1572872 | tf_op jit(solution)/shard_map/weights/ppermute | solution.py:28
  55.1 1.4 copy-start.6
  56.5 13.0 %copy-start.5 = (bf16[16,128,128]{2,1,0:T(8,128)(2,1)}, bf16[16,128,128]{2,1,0:T(8,128)(2,1)S(1)}, u32[]{:S(2)}) copy-start(bf16[16,128,128]{2,1,0:T(8,128)(2,1)S(1)} %gates.1.rest_0_) | copy-start | bytes 1572868
  67.6 0.8 copy-start.10
  68.4 1.0 copy-start.11
  69.5 10.5 %collective-permute-start.5 = (bf16[16,136,512]{2,1,0:T(8,128)(2,1)S(1)}, bf16[16,136,512]{2,1,0:T(8,128)(2,1)}, u32[]{:S(2)}, u32[]{:S(2)}) collective-permute-start(bf16[16,136,512]{2,1,0:T(8,128)(2,1)S(1)} %columns.1.own), channel_id=1, source_target_pairs={{0,1},{1,0},{2,3},{3,2},{4,5},{5,4},{6,7},{7,6},{8,9},{9,8},{10,11... | collective-permute-start | bytes 6684680 | tf_op jit(solution)/shard_map/columns/ppermute | solution.py:23
  70.3 17.1 %all-to-all-start.1 = ((bf16[16,128,128]{2,1,0:T(8,128)(2,1)}), bf16[16,128,128]{2,1,0:T(8,128)(2,1)S(1)}, u32[]{:S(2)}, u32[]{:S(2)}) async-start(bf16[16,128,128]{2,1,0:T(8,128)(2,1)} %copy-done.5), calls=%async_computation.1 | async-start | bytes 1048576 | tf_op jit(solution)/shard_map/columns/all_to_all | solution.py:626
  76.2 1.0 copy-start.8
  77.2 1.0 copy-start.12
  79.9 7.5 %copy-start.17 = (bf16[64,512]{1,0:T(8,128)(2,1)S(1)}, bf16[64,512]{1,0:T(8,128)(2,1)}, u32[]{:S(2)}) copy-start(bf16[64,512]{1,0:T(8,128)(2,1)} %get-tuple-element.38.rest_1_) | copy-start | bytes 196612
  79.9 7.5 %copy-start.18 = (bf16[64,512]{1,0:T(8,128)(2,1)S(1)}, bf16[64,512]{1,0:T(8,128)(2,1)}, u32[]{:S(2)}) copy-start(bf16[64,512]{1,0:T(8,128)(2,1)} %get-tuple-element.39.rest_2_) | copy-start | bytes 196612
  79.9 18.7 %collective-permute-start.6 = (bf16[256,2048]{1,0:T(8,128)(2,1)}, bf16[256,2048]{1,0:T(8,128)(2,1)}, u32[]{:S(2)}, u32[]{:S(2)}) collective-permute-start(bf16[256,2048]{1,0:T(8,128)(2,1)} %backward.5.refs_10_), channel_id=1, source_target_pairs={{0,1},{1,0},{2,3},{3,2},{4,5},{5,4},{6,7},{7,6},{8,9},{9,8},{10,11... | collective-permute-start | bytes 3145736 | tf_op jit(solution)/shard_map/backward/ppermute | solution.py:23
  85.6 1.1 copy-start.3
  94.5 0.6 copy-start.24
  95.1 24.0 %collective-permute-start.7 = (bf16[256,1280]{1,0:T(8,128)(2,1)}, bf16[256,1280]{1,0:T(8,128)(2,1)}, u32[]{:S(2)}, u32[]{:S(2)}) collective-permute-start(bf16[256,1280]{1,0:T(8,128)(2,1)} %get-tuple-element.44), channel_id=1, source_target_pairs={{0,16},{16,32},{32,48},{48,64},{64,80},{80,96},{96,112},{112,128},... | collective-permute-start | bytes 1966088 | tf_op jit(solution)/shard_map/factor/ppermute | solution.py:18
  98.6 7.8 %copy-start.1 = (bf16[64,5120]{1,0:T(8,128)(2,1)S(1)}, bf16[64,5120]{1,0:T(8,128)(2,1)}, u32[]{:S(2)}) copy-start(bf16[64,5120]{1,0:T(8,128)(2,1)} %copy-done) | copy-start | bytes 1966084
  98.6 7.8 %copy-start.20 = (s32[8]{0:T(128)S(1)}, s32[8]{0:T(128)}, u32[]{:S(2)}) copy-start(s32[8]{0:T(128)} %stack.47.where) | copy-start | bytes 100
  106.2 9.6 %collective-permute-start.8 = (f32[128,128]{1,0:T(8,128)}, f32[128,128]{1,0:T(8,128)S(1)}, u32[]{:S(2)}, u32[]{:S(2)}) collective-permute-start(f32[128,128]{1,0:T(8,128)} %get-tuple-element.46), channel_id=1, source_target_pairs={{0,16},{16,32},{32,48},{48,64},{64,80},{80,96},{96,112},{112,128},... | collective-permute-start | bytes 196616 | tf_op jit(solution)/shard_map/backward/ppermute | solution.py:18
  106.3 12.8 %collective-permute-start.9 = (f32[128,128]{1,0:T(8,128)}, f32[128,128]{1,0:T(8,128)S(1)}, u32[]{:S(2)}, u32[]{:S(2)}) collective-permute-start(f32[128,128]{1,0:T(8,128)} %get-tuple-element.47), channel_id=1, source_target_pairs={{0,32},{16,48},{32,64},{48,80},{64,96},{80,112},{96,128},{112,144}... | collective-permute-start | bytes 196616 | tf_op jit(solution)/shard_map/backward/ppermute | solution.py:18
  106.4 0.8 copy-start.15
  113.3 7.2 %copy-start.13 = (f32[1,3,64,128]{3,2,1,0:T(8,128)S(1)}, f32[1,3,64,128]{3,2,1,0:T(8,128)}, u32[]{:S(2)}) copy-start(f32[1,3,64,128]{3,2,1,0:T(8,128)} %q0.1) | copy-start | bytes 294916
  113.3 7.2 %copy-start.16 = (f32[128,64]{1,0:T(8,128)S(1)}, f32[128,64]{1,0:T(8,128)}, u32[]{:S(2)}) copy-start(f32[128,64]{1,0:T(8,128)} %get-tuple-element.42.rest_4_.m0) | copy-start | bytes 98308
  113.3 7.2 %copy-start.21 = (f32[192,128]{1,0:T(8,128)S(1)}, f32[192,128]{1,0:T(8,128)}, u32[]{:S(2)}) copy-start(f32[192,128]{1,0:T(8,128)} %get-tuple-element.49.proj) | copy-start | bytes 294916
  113.3 38.3 %copy-start.4 = (f32[256,1280]{1,0:T(8,128)S(1)}, f32[256,1280]{1,0:T(8,128)}, u32[]{:S(2)}) copy-start(f32[256,1280]{1,0:T(8,128)} %copy-done.3) | copy-start | bytes 3932164
  120.4 31.2 %collective-permute-start.10 = (bf16[256,1280]{1,0:T(8,128)(2,1)S(1)}, bf16[256,1280]{1,0:T(8,128)(2,1)S(1)}, u32[]{:S(2)}, u32[]{:S(2)}) collective-permute-start(bf16[256,1280]{1,0:T(8,128)(2,1)S(1)} %get-tuple-element.48), channel_id=1, source_target_pairs={{0,16},{16,32},{32,48},{48,64},{64,80},{80,96},{96,112},{112,128},... | collective-permute-start | bytes 1966088 | tf_op jit(solution)/shard_map/factor/ppermute | solution.py:18
  121.6 32.0 %copy-start.2 = (f32[1,512,1024]{2,1,0:T(8,128)S(1)}, f32[1,512,1024]{2,1,0:T(8,128)}, u32[]{:S(2)}) copy-start(f32[1,512,1024]{2,1,0:T(8,128)} %param.14) | copy-start | bytes 6291460
  121.6 4.6 %collective-permute-start.11 = (f32[64,64]{1,0:T(8,128)S(1)}, f32[64,64]{1,0:T(8,128)S(1)}, u32[]{:S(2)}, u32[]{:S(2)}) collective-permute-start(f32[64,64]{1,0:T(8,128)S(1)} %get-tuple-element.52), channel_id=1, source_target_pairs={{0,240},{16,0},{32,16},{48,32},{64,48},{80,64},{96,80},{112,96},{1... | collective-permute-start | bytes 49160 | tf_op jit(solution)/shard_map/backward/ppermute | solution.py:18
  125.1 4.0 %collective-permute-start.12 = (f32[64,64]{1,0:T(8,128)S(1)}, f32[64,64]{1,0:T(8,128)S(1)}, u32[]{:S(2)}, u32[]{:S(2)}) collective-permute-start(f32[64,64]{1,0:T(8,128)S(1)} %get-tuple-element.53), channel_id=1, source_target_pairs={{0,224},{16,240},{32,0},{48,16},{64,32},{80,48},{96,64},{112,80},{... | collective-permute-start | bytes 49160 | tf_op jit(solution)/shard_map/backward/ppermute | solution.py:18
  152.2 3.1 %collective-permute-start.13 = (f32[256,512]{1,0:T(8,128)S(1)}, f32[256,512]{1,0:T(8,128)S(1)}, u32[]{:S(2)}, u32[]{:S(2)}) collective-permute-start(f32[256,512]{1,0:T(8,128)S(1)} %factor.11.mine), channel_id=1, source_target_pairs={{0,1},{1,0},{2,3},{3,2},{4,5},{5,4},{6,7},{7,6},{8,9},{9,8},{10,11... | collective-permute-start | bytes 1572872 | tf_op jit(solution)/shard_map/factor/ppermute | solution.py:23
  155.3 1.8 %copy-start.22 = (f32[2,1,64,64]{3,2,1,0:T(8,128)S(1)}, f32[2,1,64,64]{3,2,1,0:T(8,128)}, u32[]{:S(2)}) copy-start(f32[2,1,64,64]{3,2,1,0:T(8,128)} %old.1) | copy-start | bytes 98308

commit v8 on v7

--- a/solution.py
+++ b/solution.py
@@ -101,7 +101,7 @@
     tok, width = x.shape
     rank = adapter_down.shape[2]
     cols = width // pieces
-    grid = 4
+    grid = 8
     each = width // grid
     return call(
         split_kernel,
@@ -621,7 +621,7 @@
         sent = gates(where, x1, ahead, ahead_sib, gate0, replicas)
 
     with jax.named_scope("columns"):
-        own = tie(lax.all_to_all(pieces, "dp", 0, 0), sent, behind_pair, space=pltpu.VMEM)
+        own = tie(lax.all_to_all(pieces, "dp", 0, 0), sent, space=pltpu.VMEM)
         other = swap_cores(own)
         got = lax.all_to_all(sent, "dp", 0, 0)
 
@@ -632,7 +632,7 @@
         from2 = shift(step2, "section", 1)
 
     with jax.named_scope("backward"):
-        behind = join(where, behind, behind_pair)
+        behind = join(where, behind, behind_pair, (token0,))
         behind_sib = swap_cores(behind)
         proj, m0, by1, by2 = project(
             where, returning[0], adapter_down, adapter_up, behind, behind_sib, ahead, ahead_sib,

time: 159 us -> 156 us (0.981)
  Pallas kernels: 51.4 us -> 55.8 us
  blocking collectives: 21.8 us -> 17.5 us
  waiting for transfers between devices: 42.6 us -> 40.2 us
    ppermute x1, waiting for transfers between devices: 11.1 us -> 0.01 us  [swap_chips(): return lax.ppermute(block, 'dp', [(i, i ^ 4) for i in range(count)])]
    all_to_all x1, waiting for transfers between devices: 0.71 us -> 5.63 us  [shards(): got = lax.all_to_all(sent, 'dp', 0, 0)]
    all_to_all x1, blocking collectives: 21.8 us -> 17.5 us  [shards(): shares = lax.all_to_all(share, 'dp', 0, 0)]
    ppermute x9, waiting for transfers between devices: 30.5 us -> 32.9 us  [shift(): lax.ppermute(block, axis, [(i, (i + distance) % count) for i in range(cou...]
    pallas_call x12, Pallas kernels: 28.8 us -> 31 us  [local(): pl.pallas_call(kernel, in_specs=[pl.BlockSpec(memory_space=pltpu.SMEM)] +...]
    pallas_call x4, Pallas kernels: 20.9 us -> 23 us  [call(): pl.pallas_call(kernel, grid_spec=spec, out_shape=outs, input_output_alias...]
    unnamed x50 -> x38, local copies, waits for them, and re-layouts: 7.15 us -> 5.64 us
  transfers between devices with their start and end apart: 16 -> 16, of which waited for: 9 -> 9; matrix products, arithmetic and copies ran while one was open for 0% -> 0% of each run, Pallas kernels for 26% -> 28%
where the time goes in v8:
time: 156 us; the launch traced here: 155 us
  Pallas kernels  55.8 us (36%)
  waiting for transfers between devices  40.2 us (26%)
  starting transfers between devices  34.4 us (22%)
  blocking collectives  17.5 us (11%)
  local copies, waits for them, and re-layouts  6.3 us (4%)
    ppermute x9, waiting for transfers between devices, shift(): lax.ppermute(block, axis, [(i, (i + distance) % count) for i in range(cou...  32.9 us
    pallas_call x12, Pallas kernels, local(): pl.pallas_call(kernel, in_specs=[pl.BlockSpec(memory_space=pltpu.SMEM)] +...  31 us
    pallas_call x4, Pallas kernels, call(): pl.pallas_call(kernel, grid_spec=spec, out_shape=outs, input_output_alias...  23 us
    all_to_all x1, blocking collectives, shards(): shares = lax.all_to_all(share, 'dp', 0, 0)  17.5 us
    ppermute x9, starting transfers between devices, shift(): lax.ppermute(block, axis, [(i, (i + distance) % count) for i in range(cou...  12.5 us
    all_to_all x1, starting transfers between devices, shards(): own = tie(lax.all_to_all(pieces, 'dp', 0, 0), sent, space=pltpu.VMEM)  8.45 us
    all_to_all x1, starting transfers between devices, shards(): got = lax.all_to_all(sent, 'dp', 0, 0)  6.7 us
    ppermute x4, starting transfers between devices, swap_cores(): return lax.ppermute(block, 'dp', [(i, i ^ 1) for i in range(count)])  5.94 us
  transfers between devices with their start and end apart: 16, of which 9 were waited for; matrix products, arithmetic and copies ran while one was open for 0% of the time, Pallas kernels for 28%

profile of v8, /device:TPU:1, one launch (start us, length us, event | category | flops | bytes accessed | tf_op | source)
XLA Modules:
  0.0 155.1 jit_solution(8841363163135993237)
XLA Ops:
  0.7 0.7 stack.47.where
  1.4 7.3 %weights.5 = (bf16[16,136,512]{2,1,0:T(8,128)(2,1)}, bf16[128,64]{1,0:T(8,128)(2,1)}) custom-call(s32[8]{0:T(128)} %stack.47.where, bf16[128,8192]{1,0:T(8,128)(2,1)} %bitcast.16, bf16[2,1,64,8192]{3,2,1,0:T(8,128)(2,1)} %refs_7_.1, s32[16,128]{1,0:T(8,128)} %ids.1), custom_call_target="tpu_custom_call" | custom-call | tf_op jit(solution)/shard_map/weights/pallas_call | solution.py:47
  8.6 8.4 %all-to-all-start = ((bf16[16,136,512]{2,1,0:T(8,128)(2,1)}), bf16[16,136,512]{2,1,0:T(8,128)(2,1)S(1)}, u32[]{:S(2)}, u32[]{:S(2)}) async-start(bf16[16,136,512]{2,1,0:T(8,128)(2,1)} %get-tuple-element.30), calls=%async_computation | async-start | bytes 4456448 | tf_op jit(solution)/shard_map/columns/all_to_all | solution.py:624
  17.1 2.9 %weights.7 = (bf16[64,5120]{1,0:T(8,128)(2,1)}, bf16[64,2048]{1,0:T(8,128)(2,1)}, bf16[64,2048]{1,0:T(8,128)(2,1)}) custom-call(s32[8]{0:T(128)} %stack.47.where, bf16[2,1,64,8192]{3,2,1,0:T(8,128)(2,1)} %refs_9_.1, bf16[2,1,64,8192]{3,2,1,0:T(8,128)(2,1)} %refs_7_.1, bf16[2,1,64,8192]{3,2,1,0:T(8,128)(2,1)} %refs_9_.1, bf16[2,1,64,8192]{3,2,1,0:T(8,128)(2,1)} %refs_9_.1, ...), custom_call_target="tpu_custom_call" | custom-call | tf_op jit(solution)/shard_map/weights/pallas_call | solution.py:47
  20.0 5.7 %collective-permute-start = (bf16[64,5120]{1,0:T(8,128)(2,1)}, bf16[64,5120]{1,0:T(8,128)(2,1)S(1)}, u32[]{:S(2)}, u32[]{:S(2)}) collective-permute-start(bf16[64,5120]{1,0:T(8,128)(2,1)} %get-tuple-element.33), channel_id=1, source_target_pairs={{0,240},{16,0},{32,16},{48,32},{64,48},{80,64},{96,80},{112,96},{1... | collective-permute-start | bytes 1966088 | tf_op jit(solution)/shard_map/weights/ppermute | solution.py:18
  25.7 5.2 %weights.6 = (bf16[128,8192]{1,0:T(8,128)(2,1)}, bf16[64,512]{1,0:T(8,128)(2,1)}, bf16[64,512]{1,0:T(8,128)(2,1)}, f32[8,128]{1,0:T(8,128)}) custom-call(s32[8]{0:T(128)} %stack.47.where, bf16[128,8192]{1,0:T(8,128)(2,1)} %bitcast.17, bf16[2,1,64,8192]{3,2,1,0:T(8,128)(2,1)} %refs_9_.1, bf16[128,64]{1,0:T(8,128)(2,1)} %get-tuple-element.31.gate0.after, ...), custom_call_target="tpu_custom_call" | custom-call | tf_op jit(solution)/shard_map/weights/pallas_call | solution.py:47
  30.9 20.4 %collective-permute-done.1.rest_0_.a = bf16[64,2048]{1,0:T(8,128)(2,1)S(1)} collective-permute-done((bf16[64,2048]{1,0:T(8,128)(2,1)}, bf16[64,2048]{1,0:T(8,128)(2,1)S(1)}, u32[]{:S(2)}, u32[]{:S(2)}) %collective-permute-start.1) | collective-permute-done | bytes 262176 | tf_op jit(solution)/shard_map/weights/ppermute | solution.py:18
  51.4 0.3 collective-permute-done.x
  51.7 0.7 copy-done.17
  52.4 3.1 %collective-permute-start.3 = (bf16[64,5120]{1,0:T(8,128)(2,1)S(1)}, bf16[64,5120]{1,0:T(8,128)(2,1)S(1)}, u32[]{:S(2)}, u32[]{:S(2)}) collective-permute-start(bf16[64,5120]{1,0:T(8,128)(2,1)S(1)} %weights.8.mine.rest_3_.refs_12_), channel_id=1, source_target_pairs={{0,1},{1,0},{2,3},{3,2},{4,5},{5,4},{6,7},{7,6},{8,9},{9,8},{10,11... | collective-permute-start | bytes 1966088 | tf_op jit(solution)/shard_map/weights/ppermute | solution.py:23
  55.4 1.7 %collective-permute-done.3.sib.refs_13_ = bf16[64,5120]{1,0:T(8,128)(2,1)S(1)} collective-permute-done((bf16[64,5120]{1,0:T(8,128)(2,1)S(1)}, bf16[64,5120]{1,0:T(8,128)(2,1)S(1)}, u32[]{:S(2)}, u32[]{:S(2)}) %collective-permute-start.3) | collective-permute-done | bytes 655392 | tf_op jit(solution)/shard_map/weights/ppermute | solution.py:23
  57.2 1.6 %copy-done.6 = bf16[128,8192]{1,0:T(8,128)(2,1)S(1)} copy-done((bf16[128,8192]{1,0:T(8,128)(2,1)S(1)}, bf16[128,8192]{1,0:T(8,128)(2,1)}, u32[]{:S(2)}) %copy-start.6) | copy-done | bytes 2097176
  58.8 2.2 %gates.1.rest_0_ = bf16[16,128,128]{2,1,0:T(8,128)(2,1)} custom-call(s32[8]{0:T(128)S(1)} %copy-done.13, bf16[128,8192]{1,0:T(8,128)(2,1)S(1)} %copy-done.6, bf16[64,5120]{1,0:T(8,128)(2,1)S(1)} %weights.8.mine.rest_3_.refs_12_, bf16[64,5120]{1,0:T(8,128)(2,1)S(1)} %collective-permute-done.3.sib.refs_13_, bf16[128,64]{1,0:T(8,128)(2,1)S(1)} %copy-done.8), custom_call_target="tpu_custom_call" | custom-call | tf_op jit(solution)/shard_map/gates/pallas_call | solution.py:232
  60.9 0.8 copy-done.5
  61.8 0.4 collective-permute-start.4
  62.1 1.4 weights.9.a
  63.5 0.7 collective-permute-start.5
  64.2 6.7 %all-to-all-start.1 = ((bf16[16,128,128]{2,1,0:T(8,128)(2,1)}), bf16[16,128,128]{2,1,0:T(8,128)(2,1)S(1)}, u32[]{:S(2)}, u32[]{:S(2)}) async-start(bf16[16,128,128]{2,1,0:T(8,128)(2,1)} %gates.1.rest_0_), calls=%async_computation.1 | async-start | bytes 1048576 | tf_op jit(solution)/shard_map/columns/all_to_all | solution.py:626
  70.9 5.6 %factor.7 = (f32[256,1280]{1,0:T(8,128)S(1)}, f32[8,128]{1,0:T(8,128)S(1)}) custom-call(s32[8]{0:T(128)S(1)} %copy-done.13, bf16[16,136,512]{2,1,0:T(8,128)(2,1)S(1)} %columns.1.own, bf16[16,136,512]{2,1,0:T(8,128)(2,1)} %collective-permute-done.4.other), custom_call_target="tpu_custom_call" | custom-call | tf_op jit(solution)/shard_map/factor/pallas_call | solution.py:232
  76.5 0.0 copy-start.3
  76.5 1.0 copy-done.3
  77.6 2.3 %backward.5.refs_10_ = bf16[256,2048]{1,0:T(8,128)(2,1)} custom-call(s32[8]{0:T(128)S(1)} %copy-done.13, bf16[128,2048]{1,0:T(8,128)(2,1)} %weights.9.a, bf16[128,2048]{1,0:T(8,128)(2,1)} %collective-permute-done.5.b, f32[8,128]{1,0:T(8,128)S(1)} %get-tuple-element.40.rest_0_.rest_4_), custom_call_target="tpu_custom_call" | custom-call | tf_op jit(solution)/shard_map/backward/pallas_call | solution.py:232
  79.9 1.1 collective-permute-start.6
  81.0 5.6 %all-to-all-done.1.rest_0_ = bf16[16,128,128]{2,1,0:T(8,128)(2,1)S(1)} async-done(((bf16[16,128,128]{2,1,0:T(8,128)(2,1)}), bf16[16,128,128]{2,1,0:T(8,128)(2,1)S(1)}, u32[]{:S(2)}, u32[]{:S(2)}) %all-to-all-start.1) | async-done | bytes 524320 | tf_op jit(solution)/shard_map/columns/all_to_all | solution.py:626
  86.6 7.1 %factor.8 = (bf16[256,1280]{1,0:T(8,128)(2,1)}, f32[8,128]{1,0:T(8,128)S(1)}) custom-call(s32[8]{0:T(128)S(1)} %copy-done.13, bf16[16,136,512]{2,1,0:T(8,128)(2,1)S(1)} %columns.1.own, bf16[16,136,512]{2,1,0:T(8,128)(2,1)} %collective-permute-done.4.other, bf16[16,128,128]{2,1,0:T(8,128)(2,1)S(1)} %all-to-all-done.1.rest_0_, bf16[64,512]{1,0:T(8,128)(2,1)S(1)} %copy-done.11, ...), custom_call_target="tpu_custom_call" | custom-call | tf_op jit(solution)/shard_map/factor/pallas_call | solution.py:232
  93.7 0.6 copy-done.18
  94.3 3.0 %collective-permute-start.7 = (bf16[256,1280]{1,0:T(8,128)(2,1)}, bf16[256,1280]{1,0:T(8,128)(2,1)}, u32[]{:S(2)}, u32[]{:S(2)}) collective-permute-start(bf16[256,1280]{1,0:T(8,128)(2,1)} %get-tuple-element.44), channel_id=1, source_target_pairs={{0,16},{16,32},{32,48},{48,64},{64,80},{80,96},{96,112},{112,128},... | collective-permute-start | bytes 1966088 | tf_op jit(solution)/shard_map/factor/ppermute | solution.py:18
  97.4 7.6 %backward.6 = (f32[192,128]{1,0:T(8,128)}, f32[128,64]{1,0:T(8,128)}, f32[128,128]{1,0:T(8,128)}, f32[128,128]{1,0:T(8,128)}) custom-call(s32[8]{0:T(128)} %stack.47.where, bf16[128,8192]{1,0:T(8,128)(2,1)} %bitcast.14, bf16[128,8192]{1,0:T(8,128)(2,1)} %bitcast.15, bf16[2,1,64,8192]{3,2,1,0:T(8,128)(2,1)} %refs_9_.1, bf16[2,1,64,8192]{3,2,1,0:T(8,128)(2,1)} %refs_9_.1, ...), custom_call_target="tpu_custom_call" | custom-call | tf_op jit(solution)/shard_map/backward/pallas_call | solution.py:47
  105.0 0.1 collective-permute-start.8
  105.1 0.1 collective-permute-start.9
  105.2 0.8 copy-done.9
  106.0 6.0 %factor.9 = (f32[256,1280]{1,0:T(8,128)S(1)}, f32[8,128]{1,0:T(8,128)S(1)}) custom-call(s32[8]{0:T(128)S(1)} %copy-done.14, bf16[16,136,512]{2,1,0:T(8,128)(2,1)S(1)} %columns.1.own, bf16[16,136,512]{2,1,0:T(8,128)(2,1)} %collective-permute-done.4.other, bf16[16,128,128]{2,1,0:T(8,128)(2,1)S(1)} %all-to-all-done.1.rest_0_, bf16[64,512]{1,0:T(8,128)(2,1)S(1)} %copy-done.11, ...), custom_call_target="tpu_custom_call" | custom-call | tf_op jit(solution)/shard_map/factor/pallas_call | solution.py:232
  112.1 2.9 %collective-permute-done.7.b = bf16[256,1280]{1,0:T(8,128)(2,1)} collective-permute-done((bf16[256,1280]{1,0:T(8,128)(2,1)}, bf16[256,1280]{1,0:T(8,128)(2,1)}, u32[]{:S(2)}, u32[]{:S(2)}) %collective-permute-start.7) | collective-permute-done | bytes 655392 | tf_op jit(solution)/shard_map/factor/ppermute | solution.py:18
  115.0 1.2 collective-permute-done.8.rest_1_.by1
  116.2 4.1 %collective-permute-done.9.rest_2_.by2 = f32[128,128]{1,0:T(8,128)S(1)} collective-permute-done((f32[128,128]{1,0:T(8,128)}, f32[128,128]{1,0:T(8,128)S(1)}, u32[]{:S(2)}, u32[]{:S(2)}) %collective-permute-start.9) | collective-permute-done | bytes 65568 | tf_op jit(solution)/shard_map/backward/ppermute | solution.py:18
  120.2 1.2 factor.10
  121.5 0.1 collective-permute-start.10
  121.6 1.0 backward.7
  122.6 3.6 %collective-permute-start.11 = (f32[64,64]{1,0:T(8,128)S(1)}, f32[64,64]{1,0:T(8,128)S(1)}, u32[]{:S(2)}, u32[]{:S(2)}) collective-permute-start(f32[64,64]{1,0:T(8,128)S(1)} %get-tuple-element.52), channel_id=1, source_target_pairs={{0,240},{16,0},{32,16},{48,32},{64,48},{80,64},{96,80},{112,96},{1... | collective-permute-start | bytes 49160 | tf_op jit(solution)/shard_map/backward/ppermute | solution.py:18
  126.2 1.0 collective-permute-done.11.outer1
  127.2 2.9 %collective-permute-done.12.outer2 = f32[64,64]{1,0:T(8,128)S(1)} collective-permute-done((f32[64,64]{1,0:T(8,128)S(1)}, f32[64,64]{1,0:T(8,128)S(1)}, u32[]{:S(2)}, u32[]{:S(2)}) %collective-permute-start.12) | collective-permute-done | bytes 16416 | tf_op jit(solution)/shard_map/backward/ppermute | solution.py:18
  130.2 0.7 backward.8
  130.8 17.5 %all_to_all.15.after.parts = f32[16,64,128]{2,1,0:T(8,128)S(1)} all-to-all(f32[16,64,128]{2,1,0:T(8,128)S(1)} %get-tuple-element.54), channel_id=1, replica_groups=mesh['section'=16,'dp'=16] {'dp'}, dimensions={0} | all-to-all | bytes 1048576 | tf_op jit(solution)/shard_map/backward/all_to_all | solution.py:654
  148.3 0.6 factor.11.mine
  148.9 1.4 collective-permute-start.13
  150.3 1.7 %factor.12.done = f32[512,1024]{1,0:T(8,128)} custom-call(s32[8]{0:T(128)S(1)} %copy-done.14, f32[512,1024]{1,0:T(8,128)S(1)} %bitcast.12, f32[256,1280]{1,0:T(8,128)S(1)} %copy-done.4, bf16[256,1280]{1,0:T(8,128)(2,1)S(1)} %collective-permute-done.10.came, f32[8,128]{1,0:T(8,128)S(1)} %get-tuple-element.55.after), custom_call_target="tpu_custom_call" | custom-call | tf_op jit(solution)/shard_map/factor/pallas_call | solution.py:232
  152.1 1.8 %factor.13 = (f32[512,1024]{1,0:T(8,128)}, f32[8,128]{1,0:T(8,128)S(1)}) custom-call(s32[8]{0:T(128)S(1)} %copy-done.14, f32[512,1024]{1,0:T(8,128)S(1)} %bitcast.13, f32[256,512]{1,0:T(8,128)S(1)} %factor.11.mine, f32[256,512]{1,0:T(8,128)S(1)} %collective-permute-done.13.sib, f32[512,1024]{1,0:T(8,128)} %factor.12.done), custom_call_target="tpu_custom_call", output_to_operand_aliasing={{0}: (4, {})} | custom-call | tf_op jit(solution)/shard_map/factor/pallas_call | solution.py:572
  153.8 1.3 backward.9
  (43 shorter events, 0.1 us)
Async XLA Ops:
  8.6 53.1 %all-to-all-start = ((bf16[16,136,512]{2,1,0:T(8,128)(2,1)}), bf16[16,136,512]{2,1,0:T(8,128)(2,1)S(1)}, u32[]{:S(2)}, u32[]{:S(2)}) async-start(bf16[16,136,512]{2,1,0:T(8,128)(2,1)} %get-tuple-element.30), calls=%async_computation | async-start | bytes 4456448 | tf_op jit(solution)/shard_map/columns/all_to_all | solution.py:624
  20.0 31.7 %collective-permute-start = (bf16[64,5120]{1,0:T(8,128)(2,1)}, bf16[64,5120]{1,0:T(8,128)(2,1)S(1)}, u32[]{:S(2)}, u32[]{:S(2)}) collective-permute-start(bf16[64,5120]{1,0:T(8,128)(2,1)} %get-tuple-element.33), channel_id=1, source_target_pairs={{0,240},{16,0},{32,16},{48,32},{64,48},{80,64},{96,80},{112,96},{1... | collective-permute-start | bytes 1966088 | tf_op jit(solution)/shard_map/weights/ppermute | solution.py:18
  25.7 25.7 %collective-permute-start.1 = (bf16[64,2048]{1,0:T(8,128)(2,1)}, bf16[64,2048]{1,0:T(8,128)(2,1)S(1)}, u32[]{:S(2)}, u32[]{:S(2)}) collective-permute-start(bf16[64,2048]{1,0:T(8,128)(2,1)} %get-tuple-element.34), channel_id=1, source_target_pairs={{0,16},{16,32},{32,48},{48,64},{64,80},{80,96},{96,112},{112,128},... | collective-permute-start | bytes 786440 | tf_op jit(solution)/shard_map/weights/ppermute | solution.py:18
  25.7 31.5 %copy-start.8 = (bf16[128,64]{1,0:T(8,128)(2,1)S(1)}, bf16[128,64]{1,0:T(8,128)(2,1)}, u32[]{:S(2)}) copy-start(bf16[128,64]{1,0:T(8,128)(2,1)} %get-tuple-element.31.gate0.after) | copy-start | bytes 49156
  25.7 31.5 %copy-start.13 = (s32[8]{0:T(128)S(1)}, s32[8]{0:T(128)}, u32[]{:S(2)}) copy-start(s32[8]{0:T(128)} %stack.47.where) | copy-start | bytes 100
  25.7 25.7 %collective-permute-start.2 = (bf16[64,2048]{1,0:T(8,128)(2,1)}, bf16[64,2048]{1,0:T(8,128)(2,1)S(1)}, u32[]{:S(2)}, u32[]{:S(2)}) collective-permute-start(bf16[64,2048]{1,0:T(8,128)(2,1)} %get-tuple-element.35), channel_id=1, source_target_pairs={{0,32},{16,48},{32,64},{48,80},{64,96},{80,112},{96,128},{112,144}... | collective-permute-start | bytes 786440 | tf_op jit(solution)/shard_map/weights/ppermute | solution.py:18
  51.7 0.7 copy-start.17
  52.4 34.2 %copy-start = (bf16[64,5120]{1,0:T(8,128)(2,1)}, bf16[64,5120]{1,0:T(8,128)(2,1)S(1)}, u32[]{:S(2)}) copy-start(bf16[64,5120]{1,0:T(8,128)(2,1)S(1)} %weights.8.mine.rest_3_.refs_12_) | copy-start | bytes 1966084
  52.4 4.8 %collective-permute-start.3 = (bf16[64,5120]{1,0:T(8,128)(2,1)S(1)}, bf16[64,5120]{1,0:T(8,128)(2,1)S(1)}, u32[]{:S(2)}, u32[]{:S(2)}) collective-permute-start(bf16[64,5120]{1,0:T(8,128)(2,1)S(1)} %weights.8.mine.rest_3_.refs_12_), channel_id=1, source_target_pairs={{0,1},{1,0},{2,3},{3,2},{4,5},{5,4},{6,7},{7,6},{8,9},{9,8},{10,11... | collective-permute-start | bytes 1966088 | tf_op jit(solution)/shard_map/weights/ppermute | solution.py:23
  57.2 1.6 %copy-start.6 = (bf16[128,8192]{1,0:T(8,128)(2,1)S(1)}, bf16[128,8192]{1,0:T(8,128)(2,1)}, u32[]{:S(2)}) copy-start(bf16[128,8192]{1,0:T(8,128)(2,1)} %get-tuple-element.32.x1) | copy-start | bytes 6291460
  60.9 0.8 copy-start.5
  61.8 9.2 %collective-permute-start.4 = (bf16[16,136,512]{2,1,0:T(8,128)(2,1)S(1)}, bf16[16,136,512]{2,1,0:T(8,128)(2,1)}, u32[]{:S(2)}, u32[]{:S(2)}) collective-permute-start(bf16[16,136,512]{2,1,0:T(8,128)(2,1)S(1)} %columns.1.own), channel_id=1, source_target_pairs={{0,1},{1,0},{2,3},{3,2},{4,5},{5,4},{6,7},{7,6},{8,9},{9,8},{10,11... | collective-permute-start | bytes 6684680 | tf_op jit(solution)/shard_map/columns/ppermute | solution.py:23
  63.5 14.1 %collective-permute-start.5 = (bf16[128,2048]{1,0:T(8,128)(2,1)}, bf16[128,2048]{1,0:T(8,128)(2,1)}, u32[]{:S(2)}, u32[]{:S(2)}) collective-permute-start(bf16[128,2048]{1,0:T(8,128)(2,1)} %weights.9.a), channel_id=1, source_target_pairs={{0,4},{1,5},{2,6},{3,7},{4,0},{5,1},{6,2},{7,3},{8,12},{9,13},{10,... | collective-permute-start | bytes 1572872 | tf_op jit(solution)/shard_map/weights/ppermute | solution.py:28
  64.2 22.4 %all-to-all-start.1 = ((bf16[16,128,128]{2,1,0:T(8,128)(2,1)}), bf16[16,128,128]{2,1,0:T(8,128)(2,1)S(1)}, u32[]{:S(2)}, u32[]{:S(2)}) async-start(bf16[16,128,128]{2,1,0:T(8,128)(2,1)} %gates.1.rest_0_), calls=%async_computation.1 | async-start | bytes 1048576 | tf_op jit(solution)/shard_map/columns/all_to_all | solution.py:626
  76.5 1.1 copy-start.3
  77.6 9.0 %copy-start.11 = (bf16[64,512]{1,0:T(8,128)(2,1)S(1)}, bf16[64,512]{1,0:T(8,128)(2,1)}, u32[]{:S(2)}) copy-start(bf16[64,512]{1,0:T(8,128)(2,1)} %get-tuple-element.38.rest_1_) | copy-start | bytes 196612
  77.6 9.0 %copy-start.12 = (bf16[64,512]{1,0:T(8,128)(2,1)S(1)}, bf16[64,512]{1,0:T(8,128)(2,1)}, u32[]{:S(2)}) copy-start(bf16[64,512]{1,0:T(8,128)(2,1)} %get-tuple-element.39.rest_2_) | copy-start | bytes 196612
  79.9 17.5 %collective-permute-start.6 = (bf16[256,2048]{1,0:T(8,128)(2,1)}, bf16[256,2048]{1,0:T(8,128)(2,1)}, u32[]{:S(2)}, u32[]{:S(2)}) collective-permute-start(bf16[256,2048]{1,0:T(8,128)(2,1)} %backward.5.refs_10_), channel_id=1, source_target_pairs={{0,1},{1,0},{2,3},{3,2},{4,5},{5,4},{6,7},{7,6},{8,9},{9,8},{10,11... | collective-permute-start | bytes 3145736 | tf_op jit(solution)/shard_map/backward/ppermute | solution.py:23
  93.7 0.6 copy-start.18
  94.3 20.7 %collective-permute-start.7 = (bf16[256,1280]{1,0:T(8,128)(2,1)}, bf16[256,1280]{1,0:T(8,128)(2,1)}, u32[]{:S(2)}, u32[]{:S(2)}) collective-permute-start(bf16[256,1280]{1,0:T(8,128)(2,1)} %get-tuple-element.44), channel_id=1, source_target_pairs={{0,16},{16,32},{32,48},{48,64},{64,80},{80,96},{96,112},{112,128},... | collective-permute-start | bytes 1966088 | tf_op jit(solution)/shard_map/factor/ppermute | solution.py:18
  97.4 7.8 %copy-start.1 = (bf16[64,5120]{1,0:T(8,128)(2,1)S(1)}, bf16[64,5120]{1,0:T(8,128)(2,1)}, u32[]{:S(2)}) copy-start(bf16[64,5120]{1,0:T(8,128)(2,1)} %copy-done) | copy-start | bytes 1966084
  97.4 7.8 %copy-start.14 = (s32[8]{0:T(128)S(1)}, s32[8]{0:T(128)}, u32[]{:S(2)}) copy-start(s32[8]{0:T(128)} %stack.47.where) | copy-start | bytes 100
  105.0 11.2 %collective-permute-start.8 = (f32[128,128]{1,0:T(8,128)}, f32[128,128]{1,0:T(8,128)S(1)}, u32[]{:S(2)}, u32[]{:S(2)}) collective-permute-start(f32[128,128]{1,0:T(8,128)} %get-tuple-element.46), channel_id=1, source_target_pairs={{0,16},{16,32},{32,48},{48,64},{64,80},{80,96},{96,112},{112,128},... | collective-permute-start | bytes 196616 | tf_op jit(solution)/shard_map/backward/ppermute | solution.py:18
  105.1 15.2 %collective-permute-start.9 = (f32[128,128]{1,0:T(8,128)}, f32[128,128]{1,0:T(8,128)S(1)}, u32[]{:S(2)}, u32[]{:S(2)}) collective-permute-start(f32[128,128]{1,0:T(8,128)} %get-tuple-element.47), channel_id=1, source_target_pairs={{0,32},{16,48},{32,64},{48,80},{64,96},{80,112},{96,128},{112,144}... | collective-permute-start | bytes 196616 | tf_op jit(solution)/shard_map/backward/ppermute | solution.py:18
  105.2 0.8 copy-start.9
  112.0 9.5 %copy-start.7 = (f32[1,3,64,128]{3,2,1,0:T(8,128)S(1)}, f32[1,3,64,128]{3,2,1,0:T(8,128)}, u32[]{:S(2)}) copy-start(f32[1,3,64,128]{3,2,1,0:T(8,128)} %q0.1) | copy-start | bytes 294916
  112.0 9.5 %copy-start.10 = (f32[128,64]{1,0:T(8,128)S(1)}, f32[128,64]{1,0:T(8,128)}, u32[]{:S(2)}) copy-start(f32[128,64]{1,0:T(8,128)} %get-tuple-element.42.rest_4_.m0) | copy-start | bytes 98308
  112.0 9.5 %copy-start.15 = (f32[192,128]{1,0:T(8,128)S(1)}, f32[192,128]{1,0:T(8,128)}, u32[]{:S(2)}) copy-start(f32[192,128]{1,0:T(8,128)} %get-tuple-element.49.proj) | copy-start | bytes 294916
  112.1 36.3 %copy-start.4 = (f32[256,1280]{1,0:T(8,128)S(1)}, f32[256,1280]{1,0:T(8,128)}, u32[]{:S(2)}) copy-start(f32[256,1280]{1,0:T(8,128)} %copy-done.3) | copy-start | bytes 3932164
  121.5 26.8 %collective-permute-start.10 = (bf16[256,1280]{1,0:T(8,128)(2,1)S(1)}, bf16[256,1280]{1,0:T(8,128)(2,1)S(1)}, u32[]{:S(2)}, u32[]{:S(2)}) collective-permute-start(bf16[256,1280]{1,0:T(8,128)(2,1)S(1)} %get-tuple-element.48), channel_id=1, source_target_pairs={{0,16},{16,32},{32,48},{48,64},{64,80},{80,96},{96,112},{112,128},... | collective-permute-start | bytes 1966088 | tf_op jit(solution)/shard_map/factor/ppermute | solution.py:18
  122.6 27.7 %copy-start.2 = (f32[1,512,1024]{2,1,0:T(8,128)S(1)}, f32[1,512,1024]{2,1,0:T(8,128)}, u32[]{:S(2)}) copy-start(f32[1,512,1024]{2,1,0:T(8,128)} %param.14) | copy-start | bytes 6291460
  122.6 4.6 %collective-permute-start.11 = (f32[64,64]{1,0:T(8,128)S(1)}, f32[64,64]{1,0:T(8,128)S(1)}, u32[]{:S(2)}, u32[]{:S(2)}) collective-permute-start(f32[64,64]{1,0:T(8,128)S(1)} %get-tuple-element.52), channel_id=1, source_target_pairs={{0,240},{16,0},{32,16},{48,32},{64,48},{80,64},{96,80},{112,96},{1... | collective-permute-start | bytes 49160 | tf_op jit(solution)/shard_map/backward/ppermute | solution.py:18
  126.2 4.0 %collective-permute-start.12 = (f32[64,64]{1,0:T(8,128)S(1)}, f32[64,64]{1,0:T(8,128)S(1)}, u32[]{:S(2)}, u32[]{:S(2)}) collective-permute-start(f32[64,64]{1,0:T(8,128)S(1)} %get-tuple-element.53), channel_id=1, source_target_pairs={{0,224},{16,240},{32,0},{48,16},{64,32},{80,48},{96,64},{112,80},{... | collective-permute-start | bytes 49160 | tf_op jit(solution)/shard_map/backward/ppermute | solution.py:18
  148.9 3.1 %collective-permute-start.13 = (f32[256,512]{1,0:T(8,128)S(1)}, f32[256,512]{1,0:T(8,128)S(1)}, u32[]{:S(2)}, u32[]{:S(2)}) collective-permute-start(f32[256,512]{1,0:T(8,128)S(1)} %factor.11.mine), channel_id=1, source_target_pairs={{0,1},{1,0},{2,3},{3,2},{4,5},{5,4},{6,7},{7,6},{8,9},{9,8},{10,11... | collective-permute-start | bytes 1572872 | tf_op jit(solution)/shard_map/factor/ppermute | solution.py:23
  152.0 1.8 %copy-start.16 = (f32[2,1,64,64]{3,2,1,0:T(8,128)S(1)}, f32[2,1,64,64]{3,2,1,0:T(8,128)}, u32[]{:S(2)}) copy-start(f32[2,1,64,64]{3,2,1,0:T(8,128)} %old.1) | copy-start | bytes 98308

commit v9 on v8

--- a/solution.py
+++ b/solution.py
@@ -101,7 +101,7 @@
     tok, width = x.shape
     rank = adapter_down.shape[2]
     cols = width // pieces
-    grid = 8
+    grid = 4
     each = width // grid
     return call(
         split_kernel,
@@ -204,7 +204,7 @@
     )
 
 
-def gate_kernel(where, x1, mine, sib, gate0, sent):
+def gate_kernel(where, x1, mine, sib, gate0, after, sent):
     core = where[CORE]
     half = x1.shape[1] // 2
     skip = mine.shape[1] - half
@@ -216,13 +216,15 @@
         sent[k] = both
 
 
-def gates(where, x1, ahead_mine, ahead_sib, gate0, replicas):
+def gates(where, x1, ahead_mine, ahead_sib, gate0, replicas, after):
     tok, rank = gate0.shape
     return local(
         gate_kernel,
         where,
         (x1, ahead_mine, ahead_sib, gate0),
         jax.ShapeDtypeStruct((replicas, tok, 2 * rank), BF16),
+        (),
+        (after,),
     )
 
 
@@ -297,7 +299,7 @@
             if step:
                 gate = jnp.concatenate([got[k] for k in ks], axis=0)[:, :ups.shape[0]]
                 add = jnp.dot(gate, ups, preferred_element_type=F32)
-                act = (act + add).astype(BF16).astype(F32)
+                act = act + add
             scale = [jnp.broadcast_to(columns[:, k:k + 1], (tok, rows)) for k in ks]
             return (jnp.concatenate(scale, axis=0) * act).astype(BF16)
 
@@ -618,7 +620,7 @@
         behind_pair = swap_chips(behind)
 
     with jax.named_scope("gates"):
-        sent = gates(where, x1, ahead, ahead_sib, gate0, replicas)
+        sent = gates(where, x1, ahead, ahead_sib, gate0, replicas, behind)
 
     with jax.named_scope("columns"):
         own = tie(lax.all_to_all(pieces, "dp", 0, 0), sent, space=pltpu.VMEM)

time: 156 us -> 151 us (0.968)
  Pallas kernels: 55.8 us -> 52.1 us
  waiting for transfers between devices: 40.2 us -> 36.7 us
  local copies, waits for them, and re-layouts: 6.3 us -> 8.32 us
    pallas_call x4, Pallas kernels: 23 us -> 20.9 us  [call(): pl.pallas_call(kernel, grid_spec=spec, out_shape=outs, input_output_alias...]
    unnamed x38 -> x50, local copies, waits for them, and re-layouts: 5.64 us -> 7.63 us
    ppermute x9, waiting for transfers between devices: 32.9 us -> 31 us  [shift(): lax.ppermute(block, axis, [(i, (i + distance) % count) for i in range(cou...]
    ppermute x4, waiting for transfers between devices: 1.73 us -> 0.01 us  [swap_cores(): return lax.ppermute(block, 'dp', [(i, i ^ 1) for i in range(count)])]
  transfers between devices with their start and end apart: 16 -> 16, of which waited for: 9 -> 8; matrix products, arithmetic and copies ran while one was open for 0% -> 0% of each run, Pallas kernels for 28% -> 28%
where the time goes in v9:
time: 151 us; the launch traced here: 150 us
  Pallas kernels  52.1 us (35%)
  waiting for transfers between devices  36.7 us (24%)
  starting transfers between devices  34.4 us (23%)
  blocking collectives  17.5 us (12%)
  local copies, waits for them, and re-layouts  8.32 us (6%)
    ppermute x9, waiting for transfers between devices, shift(): lax.ppermute(block, axis, [(i, (i + distance) % count) for i in range(cou...  31 us
    pallas_call x12, Pallas kernels, local(): pl.pallas_call(kernel, in_specs=[pl.BlockSpec(memory_space=pltpu.SMEM)] +...  29.5 us
    pallas_call x4, Pallas kernels, call(): pl.pallas_call(kernel, grid_spec=spec, out_shape=outs, input_output_alias...  20.9 us
    all_to_all x1, blocking collectives, shards(): shares = lax.all_to_all(share, 'dp', 0, 0)  17.5 us
    ppermute x9, starting transfers between devices, shift(): lax.ppermute(block, axis, [(i, (i + distance) % count) for i in range(cou...  12.7 us
    all_to_all x1, starting transfers between devices, shards(): own = tie(lax.all_to_all(pieces, 'dp', 0, 0), sent, space=pltpu.VMEM)  8.45 us
    unnamed x50, local copies, waits for them, and re-layouts  7.63 us
    all_to_all x1, starting transfers between devices, shards(): got = lax.all_to_all(sent, 'dp', 0, 0)  6.87 us
  transfers between devices with their start and end apart: 16, of which 8 were waited for; matrix products, arithmetic and copies ran while one was open for 0% of the time, Pallas kernels for 28%

profile of v9, /device:TPU:1, one launch (start us, length us, event | category | flops | bytes accessed | tf_op | source)
XLA Modules:
  0.0 150.1 jit_solution(933371715563060127)
XLA Ops:
  0.7 0.7 stack.47.where
  1.4 5.2 %weights.5 = (bf16[16,136,512]{2,1,0:T(8,128)(2,1)}, bf16[128,64]{1,0:T(8,128)(2,1)}) custom-call(s32[8]{0:T(128)} %stack.47.where, bf16[128,8192]{1,0:T(8,128)(2,1)} %bitcast.16, bf16[2,1,64,8192]{3,2,1,0:T(8,128)(2,1)} %refs_7_.1, s32[16,128]{1,0:T(8,128)} %ids.1), custom_call_target="tpu_custom_call" | custom-call | tf_op jit(solution)/shard_map/weights/pallas_call | solution.py:47
  6.6 8.4 %all-to-all-start = ((bf16[16,136,512]{2,1,0:T(8,128)(2,1)}), bf16[16,136,512]{2,1,0:T(8,128)(2,1)S(1)}, u32[]{:S(2)}, u32[]{:S(2)}) async-start(bf16[16,136,512]{2,1,0:T(8,128)(2,1)} %get-tuple-element.30), calls=%async_computation | async-start | bytes 4456448 | tf_op jit(solution)/shard_map/columns/all_to_all | solution.py:626
  15.0 2.9 %weights.7 = (bf16[64,5120]{1,0:T(8,128)(2,1)}, bf16[64,2048]{1,0:T(8,128)(2,1)}, bf16[64,2048]{1,0:T(8,128)(2,1)}) custom-call(s32[8]{0:T(128)} %stack.47.where, bf16[2,1,64,8192]{3,2,1,0:T(8,128)(2,1)} %refs_9_.1, bf16[2,1,64,8192]{3,2,1,0:T(8,128)(2,1)} %refs_7_.1, bf16[2,1,64,8192]{3,2,1,0:T(8,128)(2,1)} %refs_9_.1, bf16[2,1,64,8192]{3,2,1,0:T(8,128)(2,1)} %refs_9_.1, ...), custom_call_target="tpu_custom_call" | custom-call | tf_op jit(solution)/shard_map/weights/pallas_call | solution.py:47
  17.9 5.7 %collective-permute-start = (bf16[64,5120]{1,0:T(8,128)(2,1)}, bf16[64,5120]{1,0:T(8,128)(2,1)S(1)}, u32[]{:S(2)}, u32[]{:S(2)}) collective-permute-start(bf16[64,5120]{1,0:T(8,128)(2,1)} %get-tuple-element.33), channel_id=1, source_target_pairs={{0,240},{16,0},{32,16},{48,32},{64,48},{80,64},{96,80},{112,96},{1... | collective-permute-start | bytes 1966088 | tf_op jit(solution)/shard_map/weights/ppermute | solution.py:18
  23.7 5.2 %weights.6 = (bf16[128,8192]{1,0:T(8,128)(2,1)}, bf16[64,512]{1,0:T(8,128)(2,1)}, bf16[64,512]{1,0:T(8,128)(2,1)}, f32[8,128]{1,0:T(8,128)}) custom-call(s32[8]{0:T(128)} %stack.47.where, bf16[128,8192]{1,0:T(8,128)(2,1)} %bitcast.17, bf16[2,1,64,8192]{3,2,1,0:T(8,128)(2,1)} %refs_9_.1, bf16[128,64]{1,0:T(8,128)(2,1)} %get-tuple-element.31.gate0.after, ...), custom_call_target="tpu_custom_call" | custom-call | tf_op jit(solution)/shard_map/weights/pallas_call | solution.py:47
  28.9 20.5 %collective-permute-done.1.rest_0_.a = bf16[64,2048]{1,0:T(8,128)(2,1)S(1)} collective-permute-done((bf16[64,2048]{1,0:T(8,128)(2,1)}, bf16[64,2048]{1,0:T(8,128)(2,1)S(1)}, u32[]{:S(2)}, u32[]{:S(2)}) %collective-permute-start.1) | collective-permute-done | bytes 262176 | tf_op jit(solution)/shard_map/weights/ppermute | solution.py:18
  49.3 0.3 collective-permute-done.x
  49.6 0.7 copy-done.23
  50.3 3.2 %collective-permute-start.3 = (bf16[64,5120]{1,0:T(8,128)(2,1)S(1)}, bf16[64,5120]{1,0:T(8,128)(2,1)S(1)}, u32[]{:S(2)}, u32[]{:S(2)}) collective-permute-start(bf16[64,5120]{1,0:T(8,128)(2,1)S(1)} %weights.8.mine.rest_3_.refs_12_), channel_id=1, source_target_pairs={{0,1},{1,0},{2,3},{3,2},{4,5},{5,4},{6,7},{7,6},{8,9},{9,8},{10,11... | collective-permute-start | bytes 1966088 | tf_op jit(solution)/shard_map/weights/ppermute | solution.py:23
  53.5 0.9 copy-done.8
  54.5 0.9 copy-done.10
  55.4 0.6 weights.9.after.a
  56.0 2.1 %gates.1.rest_0_ = bf16[16,128,128]{2,1,0:T(8,128)(2,1)} custom-call(s32[8]{0:T(128)S(1)} %copy-done.19, bf16[128,8192]{1,0:T(8,128)(2,1)S(1)} %copy-done.6, bf16[64,5120]{1,0:T(8,128)(2,1)S(1)} %weights.8.mine.rest_3_.refs_12_, bf16[64,5120]{1,0:T(8,128)(2,1)S(1)} %collective-permute-done.3.sib.refs_13_, bf16[128,64]{1,0:T(8,128)(2,1)S(1)} %copy-done.12, ...), custom_call_target="tpu_custom_call" | custom-call | tf_op jit(solution)/shard_map/gates/pallas_call | solution.py:234
  58.2 0.8 copy-done.5
  59.0 0.2 collective-permute-start.4
  59.2 0.7 collective-permute-start.5
  59.9 6.9 %all-to-all-start.1 = ((bf16[16,128,128]{2,1,0:T(8,128)(2,1)}), bf16[16,128,128]{2,1,0:T(8,128)(2,1)}, u32[]{:S(2)}, u32[]{:S(2)}) async-start(bf16[16,128,128]{2,1,0:T(8,128)(2,1)} %gates.1.rest_0_), calls=%async_computation.1 | async-start | bytes 1048576 | tf_op jit(solution)/shard_map/columns/all_to_all | solution.py:628
  66.8 5.6 %factor.7 = (f32[256,1280]{1,0:T(8,128)S(1)}, f32[8,128]{1,0:T(8,128)S(1)}) custom-call(s32[8]{0:T(128)S(1)} %copy-done.19, bf16[16,136,512]{2,1,0:T(8,128)(2,1)S(1)} %columns.1.own, bf16[16,136,512]{2,1,0:T(8,128)(2,1)} %collective-permute-done.4.other), custom_call_target="tpu_custom_call" | custom-call | tf_op jit(solution)/shard_map/factor/pallas_call | solution.py:234
  72.4 1.0 copy-done.3
  73.4 2.1 %backward.5.refs_10_ = bf16[256,2048]{1,0:T(8,128)(2,1)} custom-call(s32[8]{0:T(128)S(1)} %copy-done.19, bf16[128,2048]{1,0:T(8,128)(2,1)S(1)} %weights.9.after.a, bf16[128,2048]{1,0:T(8,128)(2,1)} %collective-permute-done.5.b, f32[8,128]{1,0:T(8,128)S(1)} %get-tuple-element.40.rest_0_.rest_4_), custom_call_target="tpu_custom_call" | custom-call | tf_op jit(solution)/shard_map/backward/pallas_call | solution.py:234
  75.6 0.9 collective-permute-start.6
  76.5 5.6 %all-to-all-done.1.rest_0_ = bf16[16,128,128]{2,1,0:T(8,128)(2,1)} async-done(((bf16[16,128,128]{2,1,0:T(8,128)(2,1)}), bf16[16,128,128]{2,1,0:T(8,128)(2,1)}, u32[]{:S(2)}, u32[]{:S(2)}) %all-to-all-start.1) | async-done | bytes 524320 | tf_op jit(solution)/shard_map/columns/all_to_all | solution.py:628
  82.1 7.1 %factor.8 = (bf16[256,1280]{1,0:T(8,128)(2,1)}, f32[8,128]{1,0:T(8,128)S(1)}) custom-call(s32[8]{0:T(128)S(1)} %copy-done.19, bf16[16,136,512]{2,1,0:T(8,128)(2,1)S(1)} %columns.1.own, bf16[16,136,512]{2,1,0:T(8,128)(2,1)} %collective-permute-done.4.other, bf16[16,128,128]{2,1,0:T(8,128)(2,1)} %all-to-all-done.1.rest_0_, bf16[64,512]{1,0:T(8,128)(2,1)S(1)} %copy-done.15, ...), custom_call_target="tpu_custom_call" | custom-call | tf_op jit(solution)/shard_map/factor/pallas_call | solution.py:234
  89.2 0.6 copy-done.24
  89.8 3.2 %collective-permute-start.7 = (bf16[256,1280]{1,0:T(8,128)(2,1)}, bf16[256,1280]{1,0:T(8,128)(2,1)S(1)}, u32[]{:S(2)}, u32[]{:S(2)}) collective-permute-start(bf16[256,1280]{1,0:T(8,128)(2,1)} %get-tuple-element.44), channel_id=1, source_target_pairs={{0,16},{16,32},{32,48},{48,64},{64,80},{80,96},{96,112},{112,128},... | collective-permute-start | bytes 1966088 | tf_op jit(solution)/shard_map/factor/ppermute | solution.py:18
  93.0 7.6 %backward.6 = (f32[192,128]{1,0:T(8,128)}, f32[128,64]{1,0:T(8,128)}, f32[128,128]{1,0:T(8,128)}, f32[128,128]{1,0:T(8,128)}) custom-call(s32[8]{0:T(128)} %stack.47.where, bf16[128,8192]{1,0:T(8,128)(2,1)} %bitcast.14, bf16[128,8192]{1,0:T(8,128)(2,1)} %bitcast.15, bf16[2,1,64,8192]{3,2,1,0:T(8,128)(2,1)} %refs_9_.1, bf16[2,1,64,8192]{3,2,1,0:T(8,128)(2,1)} %refs_9_.1, ...), custom_call_target="tpu_custom_call" | custom-call | tf_op jit(solution)/shard_map/backward/pallas_call | solution.py:47
  100.6 0.1 collective-permute-start.8
  100.8 0.8 copy-done.13
  101.7 0.8 copy-done.16
  102.5 0.8 copy-done.18
  103.3 6.0 %factor.9 = (f32[256,1280]{1,0:T(8,128)S(1)}, f32[8,128]{1,0:T(8,128)S(1)}) custom-call(s32[8]{0:T(128)S(1)} %copy-done.20, bf16[16,136,512]{2,1,0:T(8,128)(2,1)S(1)} %columns.1.own, bf16[16,136,512]{2,1,0:T(8,128)(2,1)} %collective-permute-done.4.other, bf16[16,128,128]{2,1,0:T(8,128)(2,1)} %all-to-all-done.1.rest_0_, bf16[64,512]{1,0:T(8,128)(2,1)S(1)} %copy-done.16, ...), custom_call_target="tpu_custom_call" | custom-call | tf_op jit(solution)/shard_map/factor/pallas_call | solution.py:234
  109.4 1.1 collective-permute-done.7.b
  110.4 1.1 collective-permute-done.8.rest_1_.by1
  111.5 4.2 %collective-permute-done.9.rest_2_.by2 = f32[128,128]{1,0:T(8,128)S(1)} collective-permute-done((f32[128,128]{1,0:T(8,128)}, f32[128,128]{1,0:T(8,128)S(1)}, u32[]{:S(2)}, u32[]{:S(2)}) %collective-permute-start.9) | collective-permute-done | bytes 65568 | tf_op jit(solution)/shard_map/backward/ppermute | solution.py:18
  115.7 0.7 factor.10
  116.4 0.1 collective-permute-start.10
  116.6 1.0 backward.7
  117.6 3.6 %collective-permute-start.11 = (f32[64,64]{1,0:T(8,128)S(1)}, f32[64,64]{1,0:T(8,128)S(1)}, u32[]{:S(2)}, u32[]{:S(2)}) collective-permute-start(f32[64,64]{1,0:T(8,128)S(1)} %get-tuple-element.52), channel_id=1, source_target_pairs={{0,240},{16,0},{32,16},{48,32},{64,48},{80,64},{96,80},{112,96},{1... | collective-permute-start | bytes 49160 | tf_op jit(solution)/shard_map/backward/ppermute | solution.py:18
  121.2 1.0 collective-permute-done.11.outer1
  122.2 2.9 %collective-permute-done.12.outer2 = f32[64,64]{1,0:T(8,128)S(1)} collective-permute-done((f32[64,64]{1,0:T(8,128)S(1)}, f32[64,64]{1,0:T(8,128)S(1)}, u32[]{:S(2)}, u32[]{:S(2)}) %collective-permute-start.12) | collective-permute-done | bytes 16416 | tf_op jit(solution)/shard_map/backward/ppermute | solution.py:18
  125.1 0.7 backward.8
  125.8 17.5 %all_to_all.15.after.parts = f32[16,64,128]{2,1,0:T(8,128)S(1)} all-to-all(f32[16,64,128]{2,1,0:T(8,128)S(1)} %get-tuple-element.54), channel_id=1, replica_groups=mesh['section'=16,'dp'=16] {'dp'}, dimensions={0} | all-to-all | bytes 1048576 | tf_op jit(solution)/shard_map/backward/all_to_all | solution.py:656
  143.3 0.6 factor.11.mine
  143.9 1.4 collective-permute-start.13
  145.3 1.7 %factor.12.done = f32[512,1024]{1,0:T(8,128)} custom-call(s32[8]{0:T(128)S(1)} %copy-done.20, f32[512,1024]{1,0:T(8,128)S(1)} %bitcast.12, f32[256,1280]{1,0:T(8,128)S(1)} %copy-done.4, bf16[256,1280]{1,0:T(8,128)(2,1)S(1)} %collective-permute-done.10.came, f32[8,128]{1,0:T(8,128)S(1)} %get-tuple-element.55.after), custom_call_target="tpu_custom_call" | custom-call | tf_op jit(solution)/shard_map/factor/pallas_call | solution.py:234
  147.0 1.7 %factor.13 = (f32[512,1024]{1,0:T(8,128)}, f32[8,128]{1,0:T(8,128)S(1)}) custom-call(s32[8]{0:T(128)S(1)} %copy-done.20, f32[512,1024]{1,0:T(8,128)S(1)} %bitcast.13, f32[256,512]{1,0:T(8,128)S(1)} %factor.11.mine, f32[256,512]{1,0:T(8,128)S(1)} %collective-permute-done.13.sib, f32[512,1024]{1,0:T(8,128)} %factor.12.done), custom_call_target="tpu_custom_call", output_to_operand_aliasing={{0}: (4, {})} | custom-call | tf_op jit(solution)/shard_map/factor/pallas_call | solution.py:574
  148.8 1.3 backward.9
  (55 shorter events, 0.2 us)
Async XLA Ops:
  6.6 52.4 %all-to-all-start = ((bf16[16,136,512]{2,1,0:T(8,128)(2,1)}), bf16[16,136,512]{2,1,0:T(8,128)(2,1)S(1)}, u32[]{:S(2)}, u32[]{:S(2)}) async-start(bf16[16,136,512]{2,1,0:T(8,128)(2,1)} %get-tuple-element.30), calls=%async_computation | async-start | bytes 4456448 | tf_op jit(solution)/shard_map/columns/all_to_all | solution.py:626
  17.9 31.7 %collective-permute-start = (bf16[64,5120]{1,0:T(8,128)(2,1)}, bf16[64,5120]{1,0:T(8,128)(2,1)S(1)}, u32[]{:S(2)}, u32[]{:S(2)}) collective-permute-start(bf16[64,5120]{1,0:T(8,128)(2,1)} %get-tuple-element.33), channel_id=1, source_target_pairs={{0,240},{16,0},{32,16},{48,32},{64,48},{80,64},{96,80},{112,96},{1... | collective-permute-start | bytes 1966088 | tf_op jit(solution)/shard_map/weights/ppermute | solution.py:18
  23.6 25.7 %collective-permute-start.1 = (bf16[64,2048]{1,0:T(8,128)(2,1)}, bf16[64,2048]{1,0:T(8,128)(2,1)S(1)}, u32[]{:S(2)}, u32[]{:S(2)}) collective-permute-start(bf16[64,2048]{1,0:T(8,128)(2,1)} %get-tuple-element.34), channel_id=1, source_target_pairs={{0,16},{16,32},{32,48},{48,64},{64,80},{80,96},{96,112},{112,128},... | collective-permute-start | bytes 786440 | tf_op jit(solution)/shard_map/weights/ppermute | solution.py:18
  23.6 29.9 %copy-start.19 = (s32[8]{0:T(128)S(1)}, s32[8]{0:T(128)}, u32[]{:S(2)}) copy-start(s32[8]{0:T(128)} %stack.47.where) | copy-start | bytes 100
  23.6 25.7 %collective-permute-start.2 = (bf16[64,2048]{1,0:T(8,128)(2,1)}, bf16[64,2048]{1,0:T(8,128)(2,1)S(1)}, u32[]{:S(2)}, u32[]{:S(2)}) collective-permute-start(bf16[64,2048]{1,0:T(8,128)(2,1)} %get-tuple-element.35), channel_id=1, source_target_pairs={{0,32},{16,48},{32,64},{48,80},{64,96},{80,112},{96,128},{112,144}... | collective-permute-start | bytes 786440 | tf_op jit(solution)/shard_map/weights/ppermute | solution.py:18
  23.6 32.4 %copy-start.12 = (bf16[128,64]{1,0:T(8,128)(2,1)S(1)}, bf16[128,64]{1,0:T(8,128)(2,1)}, u32[]{:S(2)}) copy-start(bf16[128,64]{1,0:T(8,128)(2,1)} %get-tuple-element.31.gate0.after) | copy-start | bytes 49156
  28.9 27.2 %copy-start.6 = (bf16[128,8192]{1,0:T(8,128)(2,1)S(1)}, bf16[128,8192]{1,0:T(8,128)(2,1)}, u32[]{:S(2)}) copy-start(bf16[128,8192]{1,0:T(8,128)(2,1)} %get-tuple-element.32.x1) | copy-start | bytes 6291460
  49.3 1.0 copy-start.7
  49.3 1.0 copy-start.9
  49.6 0.7 copy-start.23
  50.3 31.8 %copy-start = (bf16[64,5120]{1,0:T(8,128)(2,1)}, bf16[64,5120]{1,0:T(8,128)(2,1)S(1)}, u32[]{:S(2)}) copy-start(bf16[64,5120]{1,0:T(8,128)(2,1)S(1)} %weights.8.mine.rest_3_.refs_12_) | copy-start | bytes 1966084
  50.3 5.7 %collective-permute-start.3 = (bf16[64,5120]{1,0:T(8,128)(2,1)S(1)}, bf16[64,5120]{1,0:T(8,128)(2,1)S(1)}, u32[]{:S(2)}, u32[]{:S(2)}) collective-permute-start(bf16[64,5120]{1,0:T(8,128)(2,1)S(1)} %weights.8.mine.rest_3_.refs_12_), channel_id=1, source_target_pairs={{0,1},{1,0},{2,3},{3,2},{4,5},{5,4},{6,7},{7,6},{8,9},{9,8},{10,11... | collective-permute-start | bytes 1966088 | tf_op jit(solution)/shard_map/weights/ppermute | solution.py:23
  53.5 1.0 copy-start.8
  54.5 0.9 copy-start.10
  58.2 0.8 copy-start.5
  59.0 7.8 %collective-permute-start.4 = (bf16[16,136,512]{2,1,0:T(8,128)(2,1)S(1)}, bf16[16,136,512]{2,1,0:T(8,128)(2,1)}, u32[]{:S(2)}, u32[]{:S(2)}) collective-permute-start(bf16[16,136,512]{2,1,0:T(8,128)(2,1)S(1)} %columns.1.own), channel_id=1, source_target_pairs={{0,1},{1,0},{2,3},{3,2},{4,5},{5,4},{6,7},{7,6},{8,9},{9,8},{10,11... | collective-permute-start | bytes 6684680 | tf_op jit(solution)/shard_map/columns/ppermute | solution.py:23
  59.2 14.2 %collective-permute-start.5 = (bf16[128,2048]{1,0:T(8,128)(2,1)S(1)}, bf16[128,2048]{1,0:T(8,128)(2,1)}, u32[]{:S(2)}, u32[]{:S(2)}) collective-permute-start(bf16[128,2048]{1,0:T(8,128)(2,1)S(1)} %weights.9.after.a), channel_id=1, source_target_pairs={{0,4},{1,5},{2,6},{3,7},{4,0},{5,1},{6,2},{7,3},{8,12},{9,13},{10,... | collective-permute-start | bytes 1572872 | tf_op jit(solution)/shard_map/weights/ppermute | solution.py:28
  59.9 22.2 %all-to-all-start.1 = ((bf16[16,128,128]{2,1,0:T(8,128)(2,1)}), bf16[16,128,128]{2,1,0:T(8,128)(2,1)}, u32[]{:S(2)}, u32[]{:S(2)}) async-start(bf16[16,128,128]{2,1,0:T(8,128)(2,1)} %gates.1.rest_0_), calls=%async_computation.1 | async-start | bytes 1048576 | tf_op jit(solution)/shard_map/columns/all_to_all | solution.py:628
  72.4 1.1 copy-start.3
  73.4 8.7 %copy-start.15 = (bf16[64,512]{1,0:T(8,128)(2,1)S(1)}, bf16[64,512]{1,0:T(8,128)(2,1)}, u32[]{:S(2)}) copy-start(bf16[64,512]{1,0:T(8,128)(2,1)} %get-tuple-element.38.rest_1_) | copy-start | bytes 196612
  73.4 8.7 %copy-start.17 = (bf16[64,512]{1,0:T(8,128)(2,1)S(1)}, bf16[64,512]{1,0:T(8,128)(2,1)}, u32[]{:S(2)}) copy-start(bf16[64,512]{1,0:T(8,128)(2,1)} %get-tuple-element.39.rest_2_) | copy-start | bytes 196612
  75.6 17.5 %collective-permute-start.6 = (bf16[256,2048]{1,0:T(8,128)(2,1)}, bf16[256,2048]{1,0:T(8,128)(2,1)}, u32[]{:S(2)}, u32[]{:S(2)}) collective-permute-start(bf16[256,2048]{1,0:T(8,128)(2,1)} %backward.5.refs_10_), channel_id=1, source_target_pairs={{0,1},{1,0},{2,3},{3,2},{4,5},{5,4},{6,7},{7,6},{8,9},{9,8},{10,11... | collective-permute-start | bytes 3145736 | tf_op jit(solution)/shard_map/backward/ppermute | solution.py:23
  89.2 0.6 copy-start.24
  89.8 20.6 %collective-permute-start.7 = (bf16[256,1280]{1,0:T(8,128)(2,1)}, bf16[256,1280]{1,0:T(8,128)(2,1)S(1)}, u32[]{:S(2)}, u32[]{:S(2)}) collective-permute-start(bf16[256,1280]{1,0:T(8,128)(2,1)} %get-tuple-element.44), channel_id=1, source_target_pairs={{0,16},{16,32},{32,48},{48,64},{64,80},{80,96},{96,112},{112,128},... | collective-permute-start | bytes 1966088 | tf_op jit(solution)/shard_map/factor/ppermute | solution.py:18
  93.0 7.8 %copy-start.1 = (bf16[64,5120]{1,0:T(8,128)(2,1)S(1)}, bf16[64,5120]{1,0:T(8,128)(2,1)}, u32[]{:S(2)}) copy-start(bf16[64,5120]{1,0:T(8,128)(2,1)} %copy-done) | copy-start | bytes 1966084
  93.0 7.8 %copy-start.20 = (s32[8]{0:T(128)S(1)}, s32[8]{0:T(128)}, u32[]{:S(2)}) copy-start(s32[8]{0:T(128)} %stack.47.where) | copy-start | bytes 100
  100.6 10.9 %collective-permute-start.8 = (f32[128,128]{1,0:T(8,128)}, f32[128,128]{1,0:T(8,128)S(1)}, u32[]{:S(2)}, u32[]{:S(2)}) collective-permute-start(f32[128,128]{1,0:T(8,128)} %get-tuple-element.46), channel_id=1, source_target_pairs={{0,16},{16,32},{32,48},{48,64},{64,80},{80,96},{96,112},{112,128},... | collective-permute-start | bytes 196616 | tf_op jit(solution)/shard_map/backward/ppermute | solution.py:18
  100.7 15.0 %collective-permute-start.9 = (f32[128,128]{1,0:T(8,128)}, f32[128,128]{1,0:T(8,128)S(1)}, u32[]{:S(2)}, u32[]{:S(2)}) collective-permute-start(f32[128,128]{1,0:T(8,128)} %get-tuple-element.47), channel_id=1, source_target_pairs={{0,32},{16,48},{32,64},{48,80},{64,96},{80,112},{96,128},{112,144}... | collective-permute-start | bytes 196616 | tf_op jit(solution)/shard_map/backward/ppermute | solution.py:18
  100.8 0.8 copy-start.13
  101.7 0.8 copy-start.16
  102.5 0.8 copy-start.18
  109.3 7.2 %copy-start.11 = (f32[1,3,64,128]{3,2,1,0:T(8,128)S(1)}, f32[1,3,64,128]{3,2,1,0:T(8,128)}, u32[]{:S(2)}) copy-start(f32[1,3,64,128]{3,2,1,0:T(8,128)} %q0.1) | copy-start | bytes 294916
  109.3 7.2 %copy-start.14 = (f32[128,64]{1,0:T(8,128)S(1)}, f32[128,64]{1,0:T(8,128)}, u32[]{:S(2)}) copy-start(f32[128,64]{1,0:T(8,128)} %get-tuple-element.42.rest_4_.m0) | copy-start | bytes 98308
  109.3 7.2 %copy-start.21 = (f32[192,128]{1,0:T(8,128)S(1)}, f32[192,128]{1,0:T(8,128)}, u32[]{:S(2)}) copy-start(f32[192,128]{1,0:T(8,128)} %get-tuple-element.49.proj) | copy-start | bytes 294916
  109.4 33.9 %copy-start.4 = (f32[256,1280]{1,0:T(8,128)S(1)}, f32[256,1280]{1,0:T(8,128)}, u32[]{:S(2)}) copy-start(f32[256,1280]{1,0:T(8,128)} %copy-done.3) | copy-start | bytes 3932164
  116.4 26.8 %collective-permute-start.10 = (bf16[256,1280]{1,0:T(8,128)(2,1)S(1)}, bf16[256,1280]{1,0:T(8,128)(2,1)S(1)}, u32[]{:S(2)}, u32[]{:S(2)}) collective-permute-start(bf16[256,1280]{1,0:T(8,128)(2,1)S(1)} %get-tuple-element.48), channel_id=1, source_target_pairs={{0,16},{16,32},{32,48},{48,64},{64,80},{80,96},{96,112},{112,128},... | collective-permute-start | bytes 1966088 | tf_op jit(solution)/shard_map/factor/ppermute | solution.py:18
  117.6 27.7 %copy-start.2 = (f32[1,512,1024]{2,1,0:T(8,128)S(1)}, f32[1,512,1024]{2,1,0:T(8,128)}, u32[]{:S(2)}) copy-start(f32[1,512,1024]{2,1,0:T(8,128)} %param.14) | copy-start | bytes 6291460
  117.6 4.6 %collective-permute-start.11 = (f32[64,64]{1,0:T(8,128)S(1)}, f32[64,64]{1,0:T(8,128)S(1)}, u32[]{:S(2)}, u32[]{:S(2)}) collective-permute-start(f32[64,64]{1,0:T(8,128)S(1)} %get-tuple-element.52), channel_id=1, source_target_pairs={{0,240},{16,0},{32,16},{48,32},{64,48},{80,64},{96,80},{112,96},{1... | collective-permute-start | bytes 49160 | tf_op jit(solution)/shard_map/backward/ppermute | solution.py:18
  121.2 4.0 %collective-permute-start.12 = (f32[64,64]{1,0:T(8,128)S(1)}, f32[64,64]{1,0:T(8,128)S(1)}, u32[]{:S(2)}, u32[]{:S(2)}) collective-permute-start(f32[64,64]{1,0:T(8,128)S(1)} %get-tuple-element.53), channel_id=1, source_target_pairs={{0,224},{16,240},{32,0},{48,16},{64,32},{80,48},{96,64},{112,80},{... | collective-permute-start | bytes 49160 | tf_op jit(solution)/shard_map/backward/ppermute | solution.py:18
  143.9 3.1 %collective-permute-start.13 = (f32[256,512]{1,0:T(8,128)S(1)}, f32[256,512]{1,0:T(8,128)S(1)}, u32[]{:S(2)}, u32[]{:S(2)}) collective-permute-start(f32[256,512]{1,0:T(8,128)S(1)} %factor.11.mine), channel_id=1, source_target_pairs={{0,1},{1,0},{2,3},{3,2},{4,5},{5,4},{6,7},{7,6},{8,9},{9,8},{10,11... | collective-permute-start | bytes 1572872 | tf_op jit(solution)/shard_map/factor/ppermute | solution.py:23
  147.0 1.8 %copy-start.22 = (f32[2,1,64,64]{3,2,1,0:T(8,128)S(1)}, f32[2,1,64,64]{3,2,1,0:T(8,128)}, u32[]{:S(2)}) copy-start(f32[2,1,64,64]{3,2,1,0:T(8,128)} %old.1) | copy-start | bytes 98308

commit v10 on v9

--- a/solution.py
+++ b/solution.py
@@ -126,26 +126,26 @@
 
 
 def pack_kernel(where, up_f, down_f, up_b1, up_b2, after, ahead, behind1, behind2):
-    cols = up_f.shape[3]
-    ahead[:, :cols] = up_f[0, 0]
-    ahead[:, cols:] = down_f[0, 0]
+    half = down_f.shape[3]
+    ahead[:, :half] = down_f[0, 0]
+    ahead[:, half:] = up_f[0, 0]
     behind1[...] = up_b1[0, 0]
     behind2[...] = up_b2[0, 0]
 
 
-def pack(where, adapter_down, adapter_up, block, after):
+def pack(where, adapter_down, adapter_up, rows, after):
     rank, width = adapter_down.shape[2:]
     half = width // 2
     part = lambda span: pl.BlockSpec(
         (1, 1, rank, half // 2), lambda i, w: (w[span], 0, 0, 2 * w[CORE] + w[PAIR])
     )
-    shapes = ((rank, block + half), (rank, half // 2), (rank, half // 2))
+    shapes = ((rank, half + rows), (rank, half // 2), (rank, half // 2))
     return call(
         pack_kernel,
         where,
         (adapter_up, adapter_down, adapter_up, adapter_up, after),
         [
-            pl.BlockSpec((1, 1, rank, block), lambda i, w: (w[F1], 0, 0, w[CHIP])),
+            pl.BlockSpec((1, 1, rank, rows), lambda i, w: (w[F1], 0, 0, 2 * w[CHIP] + w[CORE])),
             pl.BlockSpec((1, 1, rank, half), lambda i, w: (w[F1], 0, 0, w[CORE])),
             part(B1),
             part(B2),
@@ -207,9 +207,8 @@
 def gate_kernel(where, x1, mine, sib, gate0, after, sent):
     core = where[CORE]
     half = x1.shape[1] // 2
-    skip = mine.shape[1] - half
-    z = nt(x1[:, pl.ds(pl.multiple_of(core * half, half), half)], mine[:, skip:])
-    z += nt(x1[:, pl.ds(pl.multiple_of((1 - core) * half, half), half)], sib[:, skip:])
+    z = nt(x1[:, pl.ds(pl.multiple_of(core * half, half), half)], mine[:, :half])
+    z += nt(x1[:, pl.ds(pl.multiple_of((1 - core) * half, half), half)], sib[:, :half])
     gate1 = (z * jax.nn.sigmoid(z)).astype(BF16)
     both = jnp.concatenate([gate0[...], gate1], axis=1)
     for k in range(sent.shape[0]):
@@ -275,13 +274,12 @@
     core = where[CORE]
     replicas, long, rows = own.shape
     if step:
-        got, up_own, up_oth, ahead = rest[:4]
+        got, up_own, up_oth, ahead, ahead_sib = rest[:5]
         ups_own, ups_oth = up_own[...], up_oth[...]
     if step == 2:
-        one = lambda side: ahead[:, pl.ds(pl.multiple_of(side * rows, rows), rows)]
-        ups_own = jnp.concatenate([ups_own, one(core)], axis=0)
-        ups_oth = jnp.concatenate([ups_oth, one(1 - core)], axis=0)
-    rest = rest[4 if step else 0:]
+        ups_own = jnp.concatenate([ups_own, ahead[:, ahead.shape[1] - rows:]], axis=0)
+        ups_oth = jnp.concatenate([ups_oth, ahead_sib[:, ahead.shape[1] - rows:]], axis=0)
+    rest = rest[5 if step else 0:]
     tok = long - 8
     hlf = rows // 2
     per = 4
@@ -362,8 +360,8 @@
 def project(where, grad, adapter_down, adapter_up, b, b_sib, ahead, ahead_sib, stashed, after):
     tok, width = grad.shape
     rank = adapter_up.shape[2]
-    each = ahead.shape[1] - width // 2
-    grid = width // 2 // each
+    grid = 4
+    each = width // 2 // grid
     mine, sib = (lambda w: w[CORE]), (lambda w: 1 - w[CORE])
 
     def half(span, side):
@@ -375,7 +373,7 @@
         return [half(span, mine), half(span, sib)]
 
     g_spec = lambda side: pl.BlockSpec((tok, each), lambda i, w: (0, side(w) * grid + i))
-    got = lambda skip: pl.BlockSpec((rank, each), lambda i, w: (0, i + skip))
+    got = pl.BlockSpec((rank, each), lambda i, w: (0, i))
     per = grid // 2
     quarter = pl.BlockSpec((2 * rank, each), lambda i, w: ((i // per + w[PAIR]) % 2, i % per))
     one = lambda w: 1
@@ -394,7 +392,7 @@
         + weights(lambda w: w[B1])
         + weights(lambda w: w[B2])
         + [quarter] * 2
-        + [got(1)] * 2
+        + [got] * 2
         + [pl.BlockSpec(stashed.shape, lambda i, w: (0, 0, 0, 0))]
         + [pl.BlockSpec(after.shape, lambda i, w: (0, 0))],
         [jax.ShapeDtypeStruct(shape, F32) for shape in shapes],
@@ -609,7 +607,7 @@
 
     with jax.named_scope("weights"):
         pieces, gate0 = split(where, x0, adapter_down, doc_ids, replicas, 8)
-        ahead, behind1, behind2 = pack(where, adapter_down, adapter_up, block, gate0)
+        ahead, behind1, behind2 = pack(where, adapter_down, adapter_up, rows, gate0)
         ahead = shift(ahead, "section", -1)
         behind1 = shift(behind1, "section", 1)
         behind2 = shift(behind2, "section", 2)
@@ -628,7 +626,7 @@
         got = lax.all_to_all(sent, "dp", 0, 0)
 
     with jax.named_scope("factor"):
-        ups = (got, up_own, up_oth, ahead)
+        ups = (got, up_own, up_oth, ahead, ahead_sib)
         step0, token0 = gram(0, where, own, other)
         step2, token2 = gram(2, where, own, other, ups, (token0,))
         from2 = shift(step2, "section", 1)

time: 151 us -> 153 us (1.013)
  waiting for transfers between devices: 36.7 us -> 34.9 us
    all_to_all x1, waiting for transfers between devices: 5.63 us -> 3.71 us  [shards(): got = lax.all_to_all(sent, 'dp', 0, 0)]
    ppermute x9, starting transfers between devices: 12.7 us -> 14.5 us  [shift(): lax.ppermute(block, axis, [(i, (i + distance) % count) for i in range(cou...]
    unnamed x50 -> x52, local copies, waits for them, and re-layouts: 7.63 us -> 8.4 us
  transfers between devices with their start and end apart: 16 -> 16, of which waited for: 8 -> 8; matrix products, arithmetic and copies ran while one was open for 0% -> 0% of each run, Pallas kernels for 28% -> 29%
where the time goes in v10:
time: 153 us; the launch traced here: 152 us
  Pallas kernels  53.6 us (35%)
  starting transfers between devices  35.7 us (23%)
  waiting for transfers between devices  34.9 us (23%)
  blocking collectives  18.1 us (12%)
  local copies, waits for them, and re-layouts  9.06 us (6%)
    pallas_call x12, Pallas kernels, local(): pl.pallas_call(kernel, in_specs=[pl.BlockSpec(memory_space=pltpu.SMEM)] +...  30.9 us
    ppermute x9, waiting for transfers between devices, shift(): lax.ppermute(block, axis, [(i, (i + distance) % count) for i in range(cou...  30.3 us
    pallas_call x4, Pallas kernels, call(): pl.pallas_call(kernel, grid_spec=spec, out_shape=outs, input_output_alias...  20.9 us
    all_to_all x1, blocking collectives, shards(): shares = lax.all_to_all(share, 'dp', 0, 0)  18.1 us
    ppermute x9, starting transfers between devices, shift(): lax.ppermute(block, axis, [(i, (i + distance) % count) for i in range(cou...  14.5 us
    all_to_all x1, starting transfers between devices, shards(): own = tie(lax.all_to_all(pieces, 'dp', 0, 0), sent, space=pltpu.VMEM)  8.44 us
    unnamed x52, local copies, waits for them, and re-layouts  8.4 us
    ppermute x4, starting transfers between devices, swap_cores(): return lax.ppermute(block, 'dp', [(i, i ^ 1) for i in range(count)])  6.68 us
  transfers between devices with their start and end apart: 16, of which 8 were waited for; matrix products, arithmetic and copies ran while one was open for 0% of the time, Pallas kernels for 29%

profile of v10, /device:TPU:1, one launch (start us, length us, event | category | flops | bytes accessed | tf_op | source)
XLA Modules:
  0.0 152.3 jit_solution(4695590008700766514)
XLA Ops:
  0.7 0.7 stack.47.where
  1.4 5.2 %weights.5 = (bf16[16,136,512]{2,1,0:T(8,128)(2,1)}, bf16[128,64]{1,0:T(8,128)(2,1)}) custom-call(s32[8]{0:T(128)} %stack.47.where, bf16[128,8192]{1,0:T(8,128)(2,1)} %bitcast.16, bf16[2,1,64,8192]{3,2,1,0:T(8,128)(2,1)} %refs_7_.1, s32[16,128]{1,0:T(8,128)} %ids.1), custom_call_target="tpu_custom_call" | custom-call | tf_op jit(solution)/shard_map/weights/pallas_call | solution.py:47
  6.6 8.4 %all-to-all-start = ((bf16[16,136,512]{2,1,0:T(8,128)(2,1)}), bf16[16,136,512]{2,1,0:T(8,128)(2,1)S(1)}, u32[]{:S(2)}, u32[]{:S(2)}) async-start(bf16[16,136,512]{2,1,0:T(8,128)(2,1)} %get-tuple-element.30), calls=%async_computation | async-start | bytes 4456448 | tf_op jit(solution)/shard_map/columns/all_to_all | solution.py:624
  15.0 2.9 %weights.7 = (bf16[64,4608]{1,0:T(8,128)(2,1)}, bf16[64,2048]{1,0:T(8,128)(2,1)}, bf16[64,2048]{1,0:T(8,128)(2,1)}) custom-call(s32[8]{0:T(128)} %stack.47.where, bf16[2,1,64,8192]{3,2,1,0:T(8,128)(2,1)} %refs_9_.1, bf16[2,1,64,8192]{3,2,1,0:T(8,128)(2,1)} %refs_7_.1, bf16[2,1,64,8192]{3,2,1,0:T(8,128)(2,1)} %refs_9_.1, bf16[2,1,64,8192]{3,2,1,0:T(8,128)(2,1)} %refs_9_.1, ...), custom_call_target="tpu_custom_call" | custom-call | tf_op jit(solution)/shard_map/weights/pallas_call | solution.py:47
  17.9 5.7 %collective-permute-start = (bf16[64,4608]{1,0:T(8,128)(2,1)}, bf16[64,4608]{1,0:T(8,128)(2,1)S(1)}, u32[]{:S(2)}, u32[]{:S(2)}) collective-permute-start(bf16[64,4608]{1,0:T(8,128)(2,1)} %get-tuple-element.33), channel_id=1, source_target_pairs={{0,240},{16,0},{32,16},{48,32},{64,48},{80,64},{96,80},{112,96},{1... | collective-permute-start | bytes 1769480 | tf_op jit(solution)/shard_map/weights/ppermute | solution.py:18
  23.6 5.2 %weights.6 = (bf16[128,8192]{1,0:T(8,128)(2,1)}, bf16[64,512]{1,0:T(8,128)(2,1)}, bf16[64,512]{1,0:T(8,128)(2,1)}, f32[8,128]{1,0:T(8,128)}) custom-call(s32[8]{0:T(128)} %stack.47.where, bf16[128,8192]{1,0:T(8,128)(2,1)} %bitcast.17, bf16[2,1,64,8192]{3,2,1,0:T(8,128)(2,1)} %refs_9_.1, bf16[128,64]{1,0:T(8,128)(2,1)} %get-tuple-element.31.gate0.after, ...), custom_call_target="tpu_custom_call" | custom-call | tf_op jit(solution)/shard_map/weights/pallas_call | solution.py:47
  28.9 20.6 %collective-permute-done.1.rest_0_.a = bf16[64,2048]{1,0:T(8,128)(2,1)S(1)} collective-permute-done((bf16[64,2048]{1,0:T(8,128)(2,1)}, bf16[64,2048]{1,0:T(8,128)(2,1)S(1)}, u32[]{:S(2)}, u32[]{:S(2)}) %collective-permute-start.1) | collective-permute-done | bytes 262176 | tf_op jit(solution)/shard_map/weights/ppermute | solution.py:18
  49.5 0.7 copy-done.24
  50.2 0.7 copy-done.10
  50.9 0.7 copy-done.12
  51.6 3.2 %collective-permute-start.3 = (bf16[64,4608]{1,0:T(8,128)(2,1)S(1)}, bf16[64,4608]{1,0:T(8,128)(2,1)S(1)}, u32[]{:S(2)}, u32[]{:S(2)}) collective-permute-start(bf16[64,4608]{1,0:T(8,128)(2,1)S(1)} %weights.8.mine.rest_3_.refs_12_), channel_id=1, source_target_pairs={{0,1},{1,0},{2,3},{3,2},{4,5},{5,4},{6,7},{7,6},{8,9},{9,8},{10,11... | collective-permute-start | bytes 1769480 | tf_op jit(solution)/shard_map/weights/ppermute | solution.py:23
  54.8 0.9 copy-done.11
  55.7 0.9 copy-done.13
  56.7 1.4 weights.9.after.a
  58.1 2.1 %gates.1.rest_0_ = bf16[16,128,128]{2,1,0:T(8,128)(2,1)S(1)} custom-call(s32[8]{0:T(128)S(1)} %copy-done.20, bf16[128,8192]{1,0:T(8,128)(2,1)S(1)} %copy-done.9, bf16[64,4608]{1,0:T(8,128)(2,1)S(1)} %weights.8.mine.rest_3_.refs_12_, bf16[64,4608]{1,0:T(8,128)(2,1)S(1)} %collective-permute-done.3.sib.rest_4_.refs_13_, bf16[128,64]{1,0:T(8,128)(2,1)S(1)} %copy-done.15, ...), custom_call_target="tpu_custom_call" | custom-call | tf_op jit(solution)/shard_map/gates/pallas_call | solution.py:233
  60.2 0.8 copy-done.7
  61.0 1.0 copy-done.8
  62.1 0.2 collective-permute-start.4
  62.2 6.0 %all-to-all-start.1 = ((bf16[16,128,128]{2,1,0:T(8,128)(2,1)}), bf16[16,128,128]{2,1,0:T(8,128)(2,1)}, u32[]{:S(2)}, u32[]{:S(2)}) async-start(bf16[16,128,128]{2,1,0:T(8,128)(2,1)} %copy-done.7), calls=%async_computation.1 | async-start | bytes 1048576 | tf_op jit(solution)/shard_map/columns/all_to_all | solution.py:626
  68.2 5.6 %factor.7 = (f32[256,1280]{1,0:T(8,128)S(1)}, f32[8,128]{1,0:T(8,128)S(1)}) custom-call(s32[8]{0:T(128)S(1)} %copy-done.20, bf16[16,136,512]{2,1,0:T(8,128)(2,1)S(1)} %columns.1.own, bf16[16,136,512]{2,1,0:T(8,128)(2,1)} %collective-permute-done.4.other), custom_call_target="tpu_custom_call" | custom-call | tf_op jit(solution)/shard_map/factor/pallas_call | solution.py:233
  73.8 1.0 copy-done.5
  74.9 0.8 collective-permute-done.5.b
  75.7 2.3 %backward.5.refs_10_ = bf16[256,2048]{1,0:T(8,128)(2,1)} custom-call(s32[8]{0:T(128)S(1)} %copy-done.20, bf16[128,2048]{1,0:T(8,128)(2,1)} %weights.9.after.a, bf16[128,2048]{1,0:T(8,128)(2,1)} %collective-permute-done.5.b, f32[8,128]{1,0:T(8,128)S(1)} %get-tuple-element.40.rest_0_.rest_5_), custom_call_target="tpu_custom_call" | custom-call | tf_op jit(solution)/shard_map/backward/pallas_call | solution.py:233
  78.0 1.9 %collective-permute-start.6 = (bf16[256,2048]{1,0:T(8,128)(2,1)}, bf16[256,2048]{1,0:T(8,128)(2,1)}, u32[]{:S(2)}, u32[]{:S(2)}) collective-permute-start(bf16[256,2048]{1,0:T(8,128)(2,1)} %backward.5.refs_10_), channel_id=1, source_target_pairs={{0,1},{1,0},{2,3},{3,2},{4,5},{5,4},{6,7},{7,6},{8,9},{9,8},{10,11... | collective-permute-start | bytes 3145736 | tf_op jit(solution)/shard_map/backward/ppermute | solution.py:23
  79.9 3.7 %all-to-all-done.1.rest_0_ = bf16[16,128,128]{2,1,0:T(8,128)(2,1)} async-done(((bf16[16,128,128]{2,1,0:T(8,128)(2,1)}), bf16[16,128,128]{2,1,0:T(8,128)(2,1)}, u32[]{:S(2)}, u32[]{:S(2)}) %all-to-all-start.1) | async-done | bytes 524320 | tf_op jit(solution)/shard_map/columns/all_to_all | solution.py:626
  83.6 7.1 %factor.8 = (bf16[256,1280]{1,0:T(8,128)(2,1)}, f32[8,128]{1,0:T(8,128)S(1)}) custom-call(s32[8]{0:T(128)S(1)} %copy-done.20, bf16[16,136,512]{2,1,0:T(8,128)(2,1)S(1)} %columns.1.own, bf16[16,136,512]{2,1,0:T(8,128)(2,1)} %collective-permute-done.4.other, bf16[16,128,128]{2,1,0:T(8,128)(2,1)} %all-to-all-done.1.rest_0_, bf16[64,512]{1,0:T(8,128)(2,1)S(1)} %copy-done.16, ...), custom_call_target="tpu_custom_call" | custom-call | tf_op jit(solution)/shard_map/factor/pallas_call | solution.py:233
  90.7 0.6 copy-done.25
  91.3 5.0 %collective-permute-start.7 = (bf16[256,1280]{1,0:T(8,128)(2,1)}, bf16[256,1280]{1,0:T(8,128)(2,1)}, u32[]{:S(2)}, u32[]{:S(2)}) collective-permute-start(bf16[256,1280]{1,0:T(8,128)(2,1)} %get-tuple-element.44), channel_id=1, source_target_pairs={{0,16},{16,32},{32,48},{48,64},{64,80},{80,96},{96,112},{112,128},... | collective-permute-start | bytes 1966088 | tf_op jit(solution)/shard_map/factor/ppermute | solution.py:18
  96.3 7.6 %backward.6 = (f32[192,128]{1,0:T(8,128)}, f32[128,64]{1,0:T(8,128)}, f32[128,128]{1,0:T(8,128)}, f32[128,128]{1,0:T(8,128)}) custom-call(s32[8]{0:T(128)} %stack.47.where, bf16[128,8192]{1,0:T(8,128)(2,1)} %bitcast.14, bf16[128,8192]{1,0:T(8,128)(2,1)} %bitcast.15, bf16[2,1,64,8192]{3,2,1,0:T(8,128)(2,1)} %refs_9_.1, bf16[2,1,64,8192]{3,2,1,0:T(8,128)(2,1)} %refs_9_.1, ...), custom_call_target="tpu_custom_call" | custom-call | tf_op jit(solution)/shard_map/backward/pallas_call | solution.py:47
  103.9 0.1 collective-permute-start.8
  104.2 0.8 copy-done.18
  105.0 6.0 %factor.9 = (f32[256,1280]{1,0:T(8,128)S(1)}, f32[8,128]{1,0:T(8,128)S(1)}) custom-call(s32[8]{0:T(128)S(1)} %copy-done.21, bf16[16,136,512]{2,1,0:T(8,128)(2,1)S(1)} %columns.1.own, bf16[16,136,512]{2,1,0:T(8,128)(2,1)} %collective-permute-done.4.other, bf16[16,128,128]{2,1,0:T(8,128)(2,1)} %all-to-all-done.1.rest_0_, bf16[64,512]{1,0:T(8,128)(2,1)S(1)} %copy-done.16, ...), custom_call_target="tpu_custom_call" | custom-call | tf_op jit(solution)/shard_map/factor/pallas_call | solution.py:233
  111.0 0.5 collective-permute-done.7.b
  111.5 2.4 %collective-permute-done.8.rest_1_.by1 = f32[128,128]{1,0:T(8,128)S(1)} collective-permute-done((f32[128,128]{1,0:T(8,128)}, f32[128,128]{1,0:T(8,128)S(1)}, u32[]{:S(2)}, u32[]{:S(2)}) %collective-permute-start.8) | collective-permute-done | bytes 65568 | tf_op jit(solution)/shard_map/backward/ppermute | solution.py:18
  113.9 2.9 %collective-permute-done.9.rest_2_.by2 = f32[128,128]{1,0:T(8,128)S(1)} collective-permute-done((f32[128,128]{1,0:T(8,128)}, f32[128,128]{1,0:T(8,128)S(1)}, u32[]{:S(2)}, u32[]{:S(2)}) %collective-permute-start.9) | collective-permute-done | bytes 65568 | tf_op jit(solution)/shard_map/backward/ppermute | solution.py:18
  116.8 1.2 factor.10
  118.0 0.1 collective-permute-start.10
  118.1 1.0 backward.7
  119.2 3.6 %collective-permute-start.11 = (f32[64,64]{1,0:T(8,128)S(1)}, f32[64,64]{1,0:T(8,128)S(1)}, u32[]{:S(2)}, u32[]{:S(2)}) collective-permute-start(f32[64,64]{1,0:T(8,128)S(1)} %get-tuple-element.52), channel_id=1, source_target_pairs={{0,240},{16,0},{32,16},{48,32},{64,48},{80,64},{96,80},{112,96},{1... | collective-permute-start | bytes 49160 | tf_op jit(solution)/shard_map/backward/ppermute | solution.py:18
  122.7 1.0 collective-permute-done.11.outer1
  123.8 2.9 %collective-permute-done.12.outer2 = f32[64,64]{1,0:T(8,128)S(1)} collective-permute-done((f32[64,64]{1,0:T(8,128)S(1)}, f32[64,64]{1,0:T(8,128)S(1)}, u32[]{:S(2)}, u32[]{:S(2)}) %collective-permute-start.12) | collective-permute-done | bytes 16416 | tf_op jit(solution)/shard_map/backward/ppermute | solution.py:18
  126.7 0.7 backward.8
  127.4 18.1 %all_to_all.15.after.parts = f32[16,64,128]{2,1,0:T(8,128)S(1)} all-to-all(f32[16,64,128]{2,1,0:T(8,128)S(1)} %get-tuple-element.54), channel_id=1, replica_groups=mesh['section'=16,'dp'=16] {'dp'}, dimensions={0} | all-to-all | bytes 1048576 | tf_op jit(solution)/shard_map/backward/all_to_all | solution.py:654
  145.5 0.6 factor.11.mine
  146.1 1.4 collective-permute-start.13
  147.5 1.7 %factor.12.done = f32[512,1024]{1,0:T(8,128)} custom-call(s32[8]{0:T(128)S(1)} %copy-done.21, f32[512,1024]{1,0:T(8,128)S(1)} %bitcast.12, f32[256,1280]{1,0:T(8,128)S(1)} %copy-done.6, bf16[256,1280]{1,0:T(8,128)(2,1)S(1)} %collective-permute-done.10.came, f32[8,128]{1,0:T(8,128)S(1)} %get-tuple-element.55.after), custom_call_target="tpu_custom_call" | custom-call | tf_op jit(solution)/shard_map/factor/pallas_call | solution.py:233
  149.3 1.7 %factor.13 = (f32[512,1024]{1,0:T(8,128)}, f32[8,128]{1,0:T(8,128)S(1)}) custom-call(s32[8]{0:T(128)S(1)} %copy-done.21, f32[512,1024]{1,0:T(8,128)S(1)} %bitcast.13, f32[256,512]{1,0:T(8,128)S(1)} %factor.11.mine, f32[256,512]{1,0:T(8,128)S(1)} %collective-permute-done.13.sib, f32[512,1024]{1,0:T(8,128)} %factor.12.done), custom_call_target="tpu_custom_call", output_to_operand_aliasing={{0}: (4, {})} | custom-call | tf_op jit(solution)/shard_map/factor/pallas_call | solution.py:572
  151.0 1.3 backward.9
  (57 shorter events, 0.2 us)
Async XLA Ops:
  6.6 54.5 %all-to-all-start = ((bf16[16,136,512]{2,1,0:T(8,128)(2,1)}), bf16[16,136,512]{2,1,0:T(8,128)(2,1)S(1)}, u32[]{:S(2)}, u32[]{:S(2)}) async-start(bf16[16,136,512]{2,1,0:T(8,128)(2,1)} %get-tuple-element.30), calls=%async_computation | async-start | bytes 4456448 | tf_op jit(solution)/shard_map/columns/all_to_all | solution.py:624
  17.9 31.6 %collective-permute-start = (bf16[64,4608]{1,0:T(8,128)(2,1)}, bf16[64,4608]{1,0:T(8,128)(2,1)S(1)}, u32[]{:S(2)}, u32[]{:S(2)}) collective-permute-start(bf16[64,4608]{1,0:T(8,128)(2,1)} %get-tuple-element.33), channel_id=1, source_target_pairs={{0,240},{16,0},{32,16},{48,32},{64,48},{80,64},{96,80},{112,96},{1... | collective-permute-start | bytes 1769480 | tf_op jit(solution)/shard_map/weights/ppermute | solution.py:18
  23.6 25.9 %collective-permute-start.1 = (bf16[64,2048]{1,0:T(8,128)(2,1)}, bf16[64,2048]{1,0:T(8,128)(2,1)S(1)}, u32[]{:S(2)}, u32[]{:S(2)}) collective-permute-start(bf16[64,2048]{1,0:T(8,128)(2,1)} %get-tuple-element.34), channel_id=1, source_target_pairs={{0,16},{16,32},{32,48},{48,64},{64,80},{80,96},{96,112},{112,128},... | collective-permute-start | bytes 786440 | tf_op jit(solution)/shard_map/weights/ppermute | solution.py:18
  23.6 31.2 %copy-start.20 = (s32[8]{0:T(128)S(1)}, s32[8]{0:T(128)}, u32[]{:S(2)}) copy-start(s32[8]{0:T(128)} %stack.47.where) | copy-start | bytes 100
  23.6 25.9 %collective-permute-start.2 = (bf16[64,2048]{1,0:T(8,128)(2,1)}, bf16[64,2048]{1,0:T(8,128)(2,1)S(1)}, u32[]{:S(2)}, u32[]{:S(2)}) collective-permute-start(bf16[64,2048]{1,0:T(8,128)(2,1)} %get-tuple-element.35), channel_id=1, source_target_pairs={{0,32},{16,48},{32,64},{48,80},{64,96},{80,112},{96,128},{112,144}... | collective-permute-start | bytes 786440 | tf_op jit(solution)/shard_map/weights/ppermute | solution.py:18
  23.6 34.5 %copy-start.15 = (bf16[128,64]{1,0:T(8,128)(2,1)S(1)}, bf16[128,64]{1,0:T(8,128)(2,1)}, u32[]{:S(2)}) copy-start(bf16[128,64]{1,0:T(8,128)(2,1)} %get-tuple-element.31.gate0.after) | copy-start | bytes 49156
  28.8 29.2 %copy-start.9 = (bf16[128,8192]{1,0:T(8,128)(2,1)S(1)}, bf16[128,8192]{1,0:T(8,128)(2,1)}, u32[]{:S(2)}) copy-start(bf16[128,8192]{1,0:T(8,128)(2,1)} %get-tuple-element.32.x1) | copy-start | bytes 6291460
  49.5 0.7 copy-start.24
  50.2 0.7 copy-start.10
  50.9 0.7 copy-start.12
  51.6 32.0 %copy-start = (bf16[64,4608]{1,0:T(8,128)(2,1)}, bf16[64,4608]{1,0:T(8,128)(2,1)S(1)}, u32[]{:S(2)}) copy-start(bf16[64,4608]{1,0:T(8,128)(2,1)S(1)} %weights.8.mine.rest_3_.refs_12_) | copy-start | bytes 1769476
  51.6 6.5 %collective-permute-start.3 = (bf16[64,4608]{1,0:T(8,128)(2,1)S(1)}, bf16[64,4608]{1,0:T(8,128)(2,1)S(1)}, u32[]{:S(2)}, u32[]{:S(2)}) collective-permute-start(bf16[64,4608]{1,0:T(8,128)(2,1)S(1)} %weights.8.mine.rest_3_.refs_12_), channel_id=1, source_target_pairs={{0,1},{1,0},{2,3},{3,2},{4,5},{5,4},{6,7},{7,6},{8,9},{9,8},{10,11... | collective-permute-start | bytes 1769480 | tf_op jit(solution)/shard_map/weights/ppermute | solution.py:23
  54.8 1.0 copy-start.11
  55.7 0.9 copy-start.13
  58.1 25.5 %copy-start.2 = (bf16[64,4608]{1,0:T(8,128)(2,1)}, bf16[64,4608]{1,0:T(8,128)(2,1)S(1)}, u32[]{:S(2)}) copy-start(bf16[64,4608]{1,0:T(8,128)(2,1)S(1)} %collective-permute-done.3.sib.rest_4_.refs_13_) | copy-start | bytes 1769476
  60.2 0.8 copy-start.7
  61.0 1.0 copy-start.8
  62.1 6.2 %collective-permute-start.4 = (bf16[16,136,512]{2,1,0:T(8,128)(2,1)S(1)}, bf16[16,136,512]{2,1,0:T(8,128)(2,1)}, u32[]{:S(2)}, u32[]{:S(2)}) collective-permute-start(bf16[16,136,512]{2,1,0:T(8,128)(2,1)S(1)} %columns.1.own), channel_id=1, source_target_pairs={{0,1},{1,0},{2,3},{3,2},{4,5},{5,4},{6,7},{7,6},{8,9},{9,8},{10,11... | collective-permute-start | bytes 6684680 | tf_op jit(solution)/shard_map/columns/ppermute | solution.py:23
  62.2 13.5 %collective-permute-start.5 = (bf16[128,2048]{1,0:T(8,128)(2,1)}, bf16[128,2048]{1,0:T(8,128)(2,1)}, u32[]{:S(2)}, u32[]{:S(2)}) collective-permute-start(bf16[128,2048]{1,0:T(8,128)(2,1)} %weights.9.after.a), channel_id=1, source_target_pairs={{0,4},{1,5},{2,6},{3,7},{4,0},{5,1},{6,2},{7,3},{8,12},{9,13},{10,... | collective-permute-start | bytes 1572872 | tf_op jit(solution)/shard_map/weights/ppermute | solution.py:28
  62.2 21.4 %all-to-all-start.1 = ((bf16[16,128,128]{2,1,0:T(8,128)(2,1)}), bf16[16,128,128]{2,1,0:T(8,128)(2,1)}, u32[]{:S(2)}, u32[]{:S(2)}) async-start(bf16[16,128,128]{2,1,0:T(8,128)(2,1)} %copy-done.7), calls=%async_computation.1 | async-start | bytes 1048576 | tf_op jit(solution)/shard_map/columns/all_to_all | solution.py:626
  73.8 1.1 copy-start.5
  74.9 8.7 %copy-start.16 = (bf16[64,512]{1,0:T(8,128)(2,1)S(1)}, bf16[64,512]{1,0:T(8,128)(2,1)}, u32[]{:S(2)}) copy-start(bf16[64,512]{1,0:T(8,128)(2,1)} %get-tuple-element.38.rest_1_) | copy-start | bytes 196612
  74.9 8.7 %copy-start.17 = (bf16[64,512]{1,0:T(8,128)(2,1)S(1)}, bf16[64,512]{1,0:T(8,128)(2,1)}, u32[]{:S(2)}) copy-start(bf16[64,512]{1,0:T(8,128)(2,1)} %get-tuple-element.39.rest_2_) | copy-start | bytes 196612
  78.0 18.3 %collective-permute-start.6 = (bf16[256,2048]{1,0:T(8,128)(2,1)}, bf16[256,2048]{1,0:T(8,128)(2,1)}, u32[]{:S(2)}, u32[]{:S(2)}) collective-permute-start(bf16[256,2048]{1,0:T(8,128)(2,1)} %backward.5.refs_10_), channel_id=1, source_target_pairs={{0,1},{1,0},{2,3},{3,2},{4,5},{5,4},{6,7},{7,6},{8,9},{9,8},{10,11... | collective-permute-start | bytes 3145736 | tf_op jit(solution)/shard_map/backward/ppermute | solution.py:23
  90.7 0.6 copy-start.25
  91.3 20.2 %collective-permute-start.7 = (bf16[256,1280]{1,0:T(8,128)(2,1)}, bf16[256,1280]{1,0:T(8,128)(2,1)}, u32[]{:S(2)}, u32[]{:S(2)}) collective-permute-start(bf16[256,1280]{1,0:T(8,128)(2,1)} %get-tuple-element.44), channel_id=1, source_target_pairs={{0,16},{16,32},{32,48},{48,64},{64,80},{80,96},{96,112},{112,128},... | collective-permute-start | bytes 1966088 | tf_op jit(solution)/shard_map/factor/ppermute | solution.py:18
  96.3 7.8 %copy-start.1 = (bf16[64,4608]{1,0:T(8,128)(2,1)S(1)}, bf16[64,4608]{1,0:T(8,128)(2,1)}, u32[]{:S(2)}) copy-start(bf16[64,4608]{1,0:T(8,128)(2,1)} %copy-done) | copy-start | bytes 1769476
  96.3 7.8 %copy-start.3 = (bf16[64,4608]{1,0:T(8,128)(2,1)S(1)}, bf16[64,4608]{1,0:T(8,128)(2,1)}, u32[]{:S(2)}) copy-start(bf16[64,4608]{1,0:T(8,128)(2,1)} %copy-done.2) | copy-start | bytes 1769476
  96.3 7.8 %copy-start.21 = (s32[8]{0:T(128)S(1)}, s32[8]{0:T(128)}, u32[]{:S(2)}) copy-start(s32[8]{0:T(128)} %stack.47.where) | copy-start | bytes 100
  103.9 9.9 %collective-permute-start.8 = (f32[128,128]{1,0:T(8,128)}, f32[128,128]{1,0:T(8,128)S(1)}, u32[]{:S(2)}, u32[]{:S(2)}) collective-permute-start(f32[128,128]{1,0:T(8,128)} %get-tuple-element.46), channel_id=1, source_target_pairs={{0,16},{16,32},{32,48},{48,64},{64,80},{80,96},{96,112},{112,128},... | collective-permute-start | bytes 196616 | tf_op jit(solution)/shard_map/backward/ppermute | solution.py:18
  104.0 12.7 %collective-permute-start.9 = (f32[128,128]{1,0:T(8,128)}, f32[128,128]{1,0:T(8,128)S(1)}, u32[]{:S(2)}, u32[]{:S(2)}) collective-permute-start(f32[128,128]{1,0:T(8,128)} %get-tuple-element.47), channel_id=1, source_target_pairs={{0,32},{16,48},{32,64},{48,80},{64,96},{80,112},{96,128},{112,144}... | collective-permute-start | bytes 196616 | tf_op jit(solution)/shard_map/backward/ppermute | solution.py:18
  104.2 0.8 copy-start.18
  111.0 7.1 %copy-start.14 = (f32[1,3,64,128]{3,2,1,0:T(8,128)S(1)}, f32[1,3,64,128]{3,2,1,0:T(8,128)}, u32[]{:S(2)}) copy-start(f32[1,3,64,128]{3,2,1,0:T(8,128)} %q0.1) | copy-start | bytes 294916
  111.0 7.1 %copy-start.19 = (f32[128,64]{1,0:T(8,128)S(1)}, f32[128,64]{1,0:T(8,128)}, u32[]{:S(2)}) copy-start(f32[128,64]{1,0:T(8,128)} %get-tuple-element.42.rest_5_.m0) | copy-start | bytes 98308
  111.0 7.1 %copy-start.22 = (f32[192,128]{1,0:T(8,128)S(1)}, f32[192,128]{1,0:T(8,128)}, u32[]{:S(2)}) copy-start(f32[192,128]{1,0:T(8,128)} %get-tuple-element.49.proj) | copy-start | bytes 294916
  111.0 34.5 %copy-start.6 = (f32[256,1280]{1,0:T(8,128)S(1)}, f32[256,1280]{1,0:T(8,128)}, u32[]{:S(2)}) copy-start(f32[256,1280]{1,0:T(8,128)} %copy-done.5) | copy-start | bytes 3932164
  118.0 27.5 %collective-permute-start.10 = (bf16[256,1280]{1,0:T(8,128)(2,1)S(1)}, bf16[256,1280]{1,0:T(8,128)(2,1)S(1)}, u32[]{:S(2)}, u32[]{:S(2)}) collective-permute-start(bf16[256,1280]{1,0:T(8,128)(2,1)S(1)} %get-tuple-element.48), channel_id=1, source_target_pairs={{0,16},{16,32},{32,48},{48,64},{64,80},{80,96},{96,112},{112,128},... | collective-permute-start | bytes 1966088 | tf_op jit(solution)/shard_map/factor/ppermute | solution.py:18
  119.2 28.4 %copy-start.4 = (f32[1,512,1024]{2,1,0:T(8,128)S(1)}, f32[1,512,1024]{2,1,0:T(8,128)}, u32[]{:S(2)}) copy-start(f32[1,512,1024]{2,1,0:T(8,128)} %param.14) | copy-start | bytes 6291460
  119.2 4.6 %collective-permute-start.11 = (f32[64,64]{1,0:T(8,128)S(1)}, f32[64,64]{1,0:T(8,128)S(1)}, u32[]{:S(2)}, u32[]{:S(2)}) collective-permute-start(f32[64,64]{1,0:T(8,128)S(1)} %get-tuple-element.52), channel_id=1, source_target_pairs={{0,240},{16,0},{32,16},{48,32},{64,48},{80,64},{96,80},{112,96},{1... | collective-permute-start | bytes 49160 | tf_op jit(solution)/shard_map/backward/ppermute | solution.py:18
  122.7 4.0 %collective-permute-start.12 = (f32[64,64]{1,0:T(8,128)S(1)}, f32[64,64]{1,0:T(8,128)S(1)}, u32[]{:S(2)}, u32[]{:S(2)}) collective-permute-start(f32[64,64]{1,0:T(8,128)S(1)} %get-tuple-element.53), channel_id=1, source_target_pairs={{0,224},{16,240},{32,0},{48,16},{64,32},{80,48},{96,64},{112,80},{... | collective-permute-start | bytes 49160 | tf_op jit(solution)/shard_map/backward/ppermute | solution.py:18
  146.1 3.1 %collective-permute-start.13 = (f32[256,512]{1,0:T(8,128)S(1)}, f32[256,512]{1,0:T(8,128)S(1)}, u32[]{:S(2)}, u32[]{:S(2)}) collective-permute-start(f32[256,512]{1,0:T(8,128)S(1)} %factor.11.mine), channel_id=1, source_target_pairs={{0,1},{1,0},{2,3},{3,2},{4,5},{5,4},{6,7},{7,6},{8,9},{9,8},{10,11... | collective-permute-start | bytes 1572872 | tf_op jit(solution)/shard_map/factor/ppermute | solution.py:23
  149.2 1.8 %copy-start.23 = (f32[2,1,64,64]{3,2,1,0:T(8,128)S(1)}, f32[2,1,64,64]{3,2,1,0:T(8,128)}, u32[]{:S(2)}) copy-start(f32[2,1,64,64]{3,2,1,0:T(8,128)} %old.1) | copy-start | bytes 98308

commit v11 on v9

--- a/solution.py
+++ b/solution.py
@@ -101,7 +101,7 @@
     tok, width = x.shape
     rank = adapter_down.shape[2]
     cols = width // pieces
-    grid = 4
+    grid = 2
     each = width // grid
     return call(
         split_kernel,

time: 151 us -> 150 us (level)
  transfers between devices with their start and end apart: 16 -> 16, of which waited for: 8 -> 8; matrix products, arithmetic and copies ran while one was open for 0% -> 0% of each run, Pallas kernels for 28% -> 29%
where the time goes in v11:
time: 150 us; the launch traced here: 149 us
  Pallas kernels  51 us (34%)
  waiting for transfers between devices  36.7 us (24%)
  starting transfers between devices  34.4 us (23%)
  blocking collectives  17.5 us (12%)
  local copies, waits for them, and re-layouts  8.32 us (6%)
    ppermute x9, waiting for transfers between devices, shift(): lax.ppermute(block, axis, [(i, (i + distance) % count) for i in range(cou...  31 us
    pallas_call x12, Pallas kernels, local(): pl.pallas_call(kernel, in_specs=[pl.BlockSpec(memory_space=pltpu.SMEM)] +...  29.5 us
    pallas_call x4, Pallas kernels, call(): pl.pallas_call(kernel, grid_spec=spec, out_shape=outs, input_output_alias...  19.7 us
    all_to_all x1, blocking collectives, shards(): shares = lax.all_to_all(share, 'dp', 0, 0)  17.5 us
    ppermute x9, starting transfers between devices, shift(): lax.ppermute(block, axis, [(i, (i + distance) % count) for i in range(cou...  12.7 us
    all_to_all x1, starting transfers between devices, shards(): own = tie(lax.all_to_all(pieces, 'dp', 0, 0), sent, space=pltpu.VMEM)  8.45 us
    unnamed x50, local copies, waits for them, and re-layouts  7.63 us
    all_to_all x1, starting transfers between devices, shards(): got = lax.all_to_all(sent, 'dp', 0, 0)  6.87 us
  transfers between devices with their start and end apart: 16, of which 8 were waited for; matrix products, arithmetic and copies ran while one was open for 0% of the time, Pallas kernels for 29%

profile of v11, /device:TPU:1, one launch (start us, length us, event | category | flops | bytes accessed | tf_op | source)
XLA Modules:
  0.0 148.9 jit_solution(6435676091096362950)
XLA Ops:
  0.7 0.7 stack.47.where
  1.4 4.0 %weights.5 = (bf16[16,136,512]{2,1,0:T(8,128)(2,1)}, bf16[128,64]{1,0:T(8,128)(2,1)}) custom-call(s32[8]{0:T(128)} %stack.47.where, bf16[128,8192]{1,0:T(8,128)(2,1)} %bitcast.16, bf16[2,1,64,8192]{3,2,1,0:T(8,128)(2,1)} %refs_7_.1, s32[16,128]{1,0:T(8,128)} %ids.1), custom_call_target="tpu_custom_call" | custom-call | tf_op jit(solution)/shard_map/weights/pallas_call | solution.py:47
  5.4 8.4 %all-to-all-start = ((bf16[16,136,512]{2,1,0:T(8,128)(2,1)}), bf16[16,136,512]{2,1,0:T(8,128)(2,1)S(1)}, u32[]{:S(2)}, u32[]{:S(2)}) async-start(bf16[16,136,512]{2,1,0:T(8,128)(2,1)} %get-tuple-element.30), calls=%async_computation | async-start | bytes 4456448 | tf_op jit(solution)/shard_map/columns/all_to_all | solution.py:626
  13.8 2.9 %weights.7 = (bf16[64,5120]{1,0:T(8,128)(2,1)}, bf16[64,2048]{1,0:T(8,128)(2,1)}, bf16[64,2048]{1,0:T(8,128)(2,1)}) custom-call(s32[8]{0:T(128)} %stack.47.where, bf16[2,1,64,8192]{3,2,1,0:T(8,128)(2,1)} %refs_9_.1, bf16[2,1,64,8192]{3,2,1,0:T(8,128)(2,1)} %refs_7_.1, bf16[2,1,64,8192]{3,2,1,0:T(8,128)(2,1)} %refs_9_.1, bf16[2,1,64,8192]{3,2,1,0:T(8,128)(2,1)} %refs_9_.1, ...), custom_call_target="tpu_custom_call" | custom-call | tf_op jit(solution)/shard_map/weights/pallas_call | solution.py:47
  16.8 5.7 %collective-permute-start = (bf16[64,5120]{1,0:T(8,128)(2,1)}, bf16[64,5120]{1,0:T(8,128)(2,1)S(1)}, u32[]{:S(2)}, u32[]{:S(2)}) collective-permute-start(bf16[64,5120]{1,0:T(8,128)(2,1)} %get-tuple-element.33), channel_id=1, source_target_pairs={{0,240},{16,0},{32,16},{48,32},{64,48},{80,64},{96,80},{112,96},{1... | collective-permute-start | bytes 1966088 | tf_op jit(solution)/shard_map/weights/ppermute | solution.py:18
  22.5 5.2 %weights.6 = (bf16[128,8192]{1,0:T(8,128)(2,1)}, bf16[64,512]{1,0:T(8,128)(2,1)}, bf16[64,512]{1,0:T(8,128)(2,1)}, f32[8,128]{1,0:T(8,128)}) custom-call(s32[8]{0:T(128)} %stack.47.where, bf16[128,8192]{1,0:T(8,128)(2,1)} %bitcast.17, bf16[2,1,64,8192]{3,2,1,0:T(8,128)(2,1)} %refs_9_.1, bf16[128,64]{1,0:T(8,128)(2,1)} %get-tuple-element.31.gate0.after, ...), custom_call_target="tpu_custom_call" | custom-call | tf_op jit(solution)/shard_map/weights/pallas_call | solution.py:47
  27.7 20.4 %collective-permute-done.1.rest_0_.a = bf16[64,2048]{1,0:T(8,128)(2,1)S(1)} collective-permute-done((bf16[64,2048]{1,0:T(8,128)(2,1)}, bf16[64,2048]{1,0:T(8,128)(2,1)S(1)}, u32[]{:S(2)}, u32[]{:S(2)}) %collective-permute-start.1) | collective-permute-done | bytes 262176 | tf_op jit(solution)/shard_map/weights/ppermute | solution.py:18
  48.1 0.3 collective-permute-done.x
  48.4 0.7 copy-done.23
  49.1 3.2 %collective-permute-start.3 = (bf16[64,5120]{1,0:T(8,128)(2,1)S(1)}, bf16[64,5120]{1,0:T(8,128)(2,1)S(1)}, u32[]{:S(2)}, u32[]{:S(2)}) collective-permute-start(bf16[64,5120]{1,0:T(8,128)(2,1)S(1)} %weights.8.mine.rest_3_.refs_12_), channel_id=1, source_target_pairs={{0,1},{1,0},{2,3},{3,2},{4,5},{5,4},{6,7},{7,6},{8,9},{9,8},{10,11... | collective-permute-start | bytes 1966088 | tf_op jit(solution)/shard_map/weights/ppermute | solution.py:23
  52.3 0.9 copy-done.8
  53.3 0.9 copy-done.10
  54.2 0.6 weights.9.after.a
  54.8 2.1 %gates.1.rest_0_ = bf16[16,128,128]{2,1,0:T(8,128)(2,1)} custom-call(s32[8]{0:T(128)S(1)} %copy-done.19, bf16[128,8192]{1,0:T(8,128)(2,1)S(1)} %copy-done.6, bf16[64,5120]{1,0:T(8,128)(2,1)S(1)} %weights.8.mine.rest_3_.refs_12_, bf16[64,5120]{1,0:T(8,128)(2,1)S(1)} %collective-permute-done.3.sib.refs_13_, bf16[128,64]{1,0:T(8,128)(2,1)S(1)} %copy-done.12, ...), custom_call_target="tpu_custom_call" | custom-call | tf_op jit(solution)/shard_map/gates/pallas_call | solution.py:234
  57.0 0.8 copy-done.5
  57.8 0.2 collective-permute-start.4
  58.0 0.7 collective-permute-start.5
  58.7 6.9 %all-to-all-start.1 = ((bf16[16,128,128]{2,1,0:T(8,128)(2,1)}), bf16[16,128,128]{2,1,0:T(8,128)(2,1)}, u32[]{:S(2)}, u32[]{:S(2)}) async-start(bf16[16,128,128]{2,1,0:T(8,128)(2,1)} %gates.1.rest_0_), calls=%async_computation.1 | async-start | bytes 1048576 | tf_op jit(solution)/shard_map/columns/all_to_all | solution.py:628
  65.6 5.6 %factor.7 = (f32[256,1280]{1,0:T(8,128)S(1)}, f32[8,128]{1,0:T(8,128)S(1)}) custom-call(s32[8]{0:T(128)S(1)} %copy-done.19, bf16[16,136,512]{2,1,0:T(8,128)(2,1)S(1)} %columns.1.own, bf16[16,136,512]{2,1,0:T(8,128)(2,1)} %collective-permute-done.4.other), custom_call_target="tpu_custom_call" | custom-call | tf_op jit(solution)/shard_map/factor/pallas_call | solution.py:234
  71.2 1.0 copy-done.3
  72.2 2.1 %backward.5.refs_10_ = bf16[256,2048]{1,0:T(8,128)(2,1)} custom-call(s32[8]{0:T(128)S(1)} %copy-done.19, bf16[128,2048]{1,0:T(8,128)(2,1)S(1)} %weights.9.after.a, bf16[128,2048]{1,0:T(8,128)(2,1)} %collective-permute-done.5.b, f32[8,128]{1,0:T(8,128)S(1)} %get-tuple-element.40.rest_0_.rest_4_), custom_call_target="tpu_custom_call" | custom-call | tf_op jit(solution)/shard_map/backward/pallas_call | solution.py:234
  74.4 0.9 collective-permute-start.6
  75.3 5.6 %all-to-all-done.1.rest_0_ = bf16[16,128,128]{2,1,0:T(8,128)(2,1)} async-done(((bf16[16,128,128]{2,1,0:T(8,128)(2,1)}), bf16[16,128,128]{2,1,0:T(8,128)(2,1)}, u32[]{:S(2)}, u32[]{:S(2)}) %all-to-all-start.1) | async-done | bytes 524320 | tf_op jit(solution)/shard_map/columns/all_to_all | solution.py:628
  80.9 7.1 %factor.8 = (bf16[256,1280]{1,0:T(8,128)(2,1)}, f32[8,128]{1,0:T(8,128)S(1)}) custom-call(s32[8]{0:T(128)S(1)} %copy-done.19, bf16[16,136,512]{2,1,0:T(8,128)(2,1)S(1)} %columns.1.own, bf16[16,136,512]{2,1,0:T(8,128)(2,1)} %collective-permute-done.4.other, bf16[16,128,128]{2,1,0:T(8,128)(2,1)} %all-to-all-done.1.rest_0_, bf16[64,512]{1,0:T(8,128)(2,1)S(1)} %copy-done.15, ...), custom_call_target="tpu_custom_call" | custom-call | tf_op jit(solution)/shard_map/factor/pallas_call | solution.py:234
  88.0 0.6 copy-done.24
  88.6 3.2 %collective-permute-start.7 = (bf16[256,1280]{1,0:T(8,128)(2,1)}, bf16[256,1280]{1,0:T(8,128)(2,1)S(1)}, u32[]{:S(2)}, u32[]{:S(2)}) collective-permute-start(bf16[256,1280]{1,0:T(8,128)(2,1)} %get-tuple-element.44), channel_id=1, source_target_pairs={{0,16},{16,32},{32,48},{48,64},{64,80},{80,96},{96,112},{112,128},... | collective-permute-start | bytes 1966088 | tf_op jit(solution)/shard_map/factor/ppermute | solution.py:18
  91.8 7.6 %backward.6 = (f32[192,128]{1,0:T(8,128)}, f32[128,64]{1,0:T(8,128)}, f32[128,128]{1,0:T(8,128)}, f32[128,128]{1,0:T(8,128)}) custom-call(s32[8]{0:T(128)} %stack.47.where, bf16[128,8192]{1,0:T(8,128)(2,1)} %bitcast.14, bf16[128,8192]{1,0:T(8,128)(2,1)} %bitcast.15, bf16[2,1,64,8192]{3,2,1,0:T(8,128)(2,1)} %refs_9_.1, bf16[2,1,64,8192]{3,2,1,0:T(8,128)(2,1)} %refs_9_.1, ...), custom_call_target="tpu_custom_call" | custom-call | tf_op jit(solution)/shard_map/backward/pallas_call | solution.py:47
  99.4 0.1 collective-permute-start.8
  99.6 0.8 copy-done.13
  100.5 0.8 copy-done.16
  101.3 0.8 copy-done.18
  102.2 6.0 %factor.9 = (f32[256,1280]{1,0:T(8,128)S(1)}, f32[8,128]{1,0:T(8,128)S(1)}) custom-call(s32[8]{0:T(128)S(1)} %copy-done.20, bf16[16,136,512]{2,1,0:T(8,128)(2,1)S(1)} %columns.1.own, bf16[16,136,512]{2,1,0:T(8,128)(2,1)} %collective-permute-done.4.other, bf16[16,128,128]{2,1,0:T(8,128)(2,1)} %all-to-all-done.1.rest_0_, bf16[64,512]{1,0:T(8,128)(2,1)S(1)} %copy-done.16, ...), custom_call_target="tpu_custom_call" | custom-call | tf_op jit(solution)/shard_map/factor/pallas_call | solution.py:234
  108.2 1.0 collective-permute-done.7.b
  109.2 1.1 collective-permute-done.8.rest_1_.by1
  110.4 4.2 %collective-permute-done.9.rest_2_.by2 = f32[128,128]{1,0:T(8,128)S(1)} collective-permute-done((f32[128,128]{1,0:T(8,128)}, f32[128,128]{1,0:T(8,128)S(1)}, u32[]{:S(2)}, u32[]{:S(2)}) %collective-permute-start.9) | collective-permute-done | bytes 65568 | tf_op jit(solution)/shard_map/backward/ppermute | solution.py:18
  114.5 0.7 factor.10
  115.2 0.1 collective-permute-start.10
  115.4 1.0 backward.7
  116.4 3.6 %collective-permute-start.11 = (f32[64,64]{1,0:T(8,128)S(1)}, f32[64,64]{1,0:T(8,128)S(1)}, u32[]{:S(2)}, u32[]{:S(2)}) collective-permute-start(f32[64,64]{1,0:T(8,128)S(1)} %get-tuple-element.52), channel_id=1, source_target_pairs={{0,240},{16,0},{32,16},{48,32},{64,48},{80,64},{96,80},{112,96},{1... | collective-permute-start | bytes 49160 | tf_op jit(solution)/shard_map/backward/ppermute | solution.py:18
  120.0 1.0 collective-permute-done.11.outer1
  121.0 2.9 %collective-permute-done.12.outer2 = f32[64,64]{1,0:T(8,128)S(1)} collective-permute-done((f32[64,64]{1,0:T(8,128)S(1)}, f32[64,64]{1,0:T(8,128)S(1)}, u32[]{:S(2)}, u32[]{:S(2)}) %collective-permute-start.12) | collective-permute-done | bytes 16416 | tf_op jit(solution)/shard_map/backward/ppermute | solution.py:18
  123.9 0.7 backward.8
  124.6 17.5 %all_to_all.15.after.parts = f32[16,64,128]{2,1,0:T(8,128)S(1)} all-to-all(f32[16,64,128]{2,1,0:T(8,128)S(1)} %get-tuple-element.54), channel_id=1, replica_groups=mesh['section'=16,'dp'=16] {'dp'}, dimensions={0} | all-to-all | bytes 1048576 | tf_op jit(solution)/shard_map/backward/all_to_all | solution.py:656
  142.1 0.6 factor.11.mine
  142.7 1.4 collective-permute-start.13
  144.1 1.7 %factor.12.done = f32[512,1024]{1,0:T(8,128)} custom-call(s32[8]{0:T(128)S(1)} %copy-done.20, f32[512,1024]{1,0:T(8,128)S(1)} %bitcast.12, f32[256,1280]{1,0:T(8,128)S(1)} %copy-done.4, bf16[256,1280]{1,0:T(8,128)(2,1)S(1)} %collective-permute-done.10.came, f32[8,128]{1,0:T(8,128)S(1)} %get-tuple-element.55.after), custom_call_target="tpu_custom_call" | custom-call | tf_op jit(solution)/shard_map/factor/pallas_call | solution.py:234
  145.8 1.7 %factor.13 = (f32[512,1024]{1,0:T(8,128)}, f32[8,128]{1,0:T(8,128)S(1)}) custom-call(s32[8]{0:T(128)S(1)} %copy-done.20, f32[512,1024]{1,0:T(8,128)S(1)} %bitcast.13, f32[256,512]{1,0:T(8,128)S(1)} %factor.11.mine, f32[256,512]{1,0:T(8,128)S(1)} %collective-permute-done.13.sib, f32[512,1024]{1,0:T(8,128)} %factor.12.done), custom_call_target="tpu_custom_call", output_to_operand_aliasing={{0}: (4, {})} | custom-call | tf_op jit(solution)/shard_map/factor/pallas_call | solution.py:574
  147.6 1.3 backward.9
  (55 shorter events, 0.2 us)
Async XLA Ops:
  5.4 52.4 %all-to-all-start = ((bf16[16,136,512]{2,1,0:T(8,128)(2,1)}), bf16[16,136,512]{2,1,0:T(8,128)(2,1)S(1)}, u32[]{:S(2)}, u32[]{:S(2)}) async-start(bf16[16,136,512]{2,1,0:T(8,128)(2,1)} %get-tuple-element.30), calls=%async_computation | async-start | bytes 4456448 | tf_op jit(solution)/shard_map/columns/all_to_all | solution.py:626
  16.8 31.7 %collective-permute-start = (bf16[64,5120]{1,0:T(8,128)(2,1)}, bf16[64,5120]{1,0:T(8,128)(2,1)S(1)}, u32[]{:S(2)}, u32[]{:S(2)}) collective-permute-start(bf16[64,5120]{1,0:T(8,128)(2,1)} %get-tuple-element.33), channel_id=1, source_target_pairs={{0,240},{16,0},{32,16},{48,32},{64,48},{80,64},{96,80},{112,96},{1... | collective-permute-start | bytes 1966088 | tf_op jit(solution)/shard_map/weights/ppermute | solution.py:18
  22.4 25.7 %collective-permute-start.1 = (bf16[64,2048]{1,0:T(8,128)(2,1)}, bf16[64,2048]{1,0:T(8,128)(2,1)S(1)}, u32[]{:S(2)}, u32[]{:S(2)}) collective-permute-start(bf16[64,2048]{1,0:T(8,128)(2,1)} %get-tuple-element.34), channel_id=1, source_target_pairs={{0,16},{16,32},{32,48},{48,64},{64,80},{80,96},{96,112},{112,128},... | collective-permute-start | bytes 786440 | tf_op jit(solution)/shard_map/weights/ppermute | solution.py:18
  22.5 29.9 %copy-start.19 = (s32[8]{0:T(128)S(1)}, s32[8]{0:T(128)}, u32[]{:S(2)}) copy-start(s32[8]{0:T(128)} %stack.47.where) | copy-start | bytes 100
  22.5 25.7 %collective-permute-start.2 = (bf16[64,2048]{1,0:T(8,128)(2,1)}, bf16[64,2048]{1,0:T(8,128)(2,1)S(1)}, u32[]{:S(2)}, u32[]{:S(2)}) collective-permute-start(bf16[64,2048]{1,0:T(8,128)(2,1)} %get-tuple-element.35), channel_id=1, source_target_pairs={{0,32},{16,48},{32,64},{48,80},{64,96},{80,112},{96,128},{112,144}... | collective-permute-start | bytes 786440 | tf_op jit(solution)/shard_map/weights/ppermute | solution.py:18
  22.5 32.4 %copy-start.12 = (bf16[128,64]{1,0:T(8,128)(2,1)S(1)}, bf16[128,64]{1,0:T(8,128)(2,1)}, u32[]{:S(2)}) copy-start(bf16[128,64]{1,0:T(8,128)(2,1)} %get-tuple-element.31.gate0.after) | copy-start | bytes 49156
  27.7 27.2 %copy-start.6 = (bf16[128,8192]{1,0:T(8,128)(2,1)S(1)}, bf16[128,8192]{1,0:T(8,128)(2,1)}, u32[]{:S(2)}) copy-start(bf16[128,8192]{1,0:T(8,128)(2,1)} %get-tuple-element.32.x1) | copy-start | bytes 6291460
  48.1 1.0 copy-start.7
  48.1 1.0 copy-start.9
  48.4 0.7 copy-start.23
  49.1 31.8 %copy-start = (bf16[64,5120]{1,0:T(8,128)(2,1)}, bf16[64,5120]{1,0:T(8,128)(2,1)S(1)}, u32[]{:S(2)}) copy-start(bf16[64,5120]{1,0:T(8,128)(2,1)S(1)} %weights.8.mine.rest_3_.refs_12_) | copy-start | bytes 1966084
  49.1 5.7 %collective-permute-start.3 = (bf16[64,5120]{1,0:T(8,128)(2,1)S(1)}, bf16[64,5120]{1,0:T(8,128)(2,1)S(1)}, u32[]{:S(2)}, u32[]{:S(2)}) collective-permute-start(bf16[64,5120]{1,0:T(8,128)(2,1)S(1)} %weights.8.mine.rest_3_.refs_12_), channel_id=1, source_target_pairs={{0,1},{1,0},{2,3},{3,2},{4,5},{5,4},{6,7},{7,6},{8,9},{9,8},{10,11... | collective-permute-start | bytes 1966088 | tf_op jit(solution)/shard_map/weights/ppermute | solution.py:23
  52.3 1.0 copy-start.8
  53.3 0.9 copy-start.10
  57.0 0.8 copy-start.5
  57.8 7.8 %collective-permute-start.4 = (bf16[16,136,512]{2,1,0:T(8,128)(2,1)S(1)}, bf16[16,136,512]{2,1,0:T(8,128)(2,1)}, u32[]{:S(2)}, u32[]{:S(2)}) collective-permute-start(bf16[16,136,512]{2,1,0:T(8,128)(2,1)S(1)} %columns.1.own), channel_id=1, source_target_pairs={{0,1},{1,0},{2,3},{3,2},{4,5},{5,4},{6,7},{7,6},{8,9},{9,8},{10,11... | collective-permute-start | bytes 6684680 | tf_op jit(solution)/shard_map/columns/ppermute | solution.py:23
  58.0 14.2 %collective-permute-start.5 = (bf16[128,2048]{1,0:T(8,128)(2,1)S(1)}, bf16[128,2048]{1,0:T(8,128)(2,1)}, u32[]{:S(2)}, u32[]{:S(2)}) collective-permute-start(bf16[128,2048]{1,0:T(8,128)(2,1)S(1)} %weights.9.after.a), channel_id=1, source_target_pairs={{0,4},{1,5},{2,6},{3,7},{4,0},{5,1},{6,2},{7,3},{8,12},{9,13},{10,... | collective-permute-start | bytes 1572872 | tf_op jit(solution)/shard_map/weights/ppermute | solution.py:28
  58.7 22.2 %all-to-all-start.1 = ((bf16[16,128,128]{2,1,0:T(8,128)(2,1)}), bf16[16,128,128]{2,1,0:T(8,128)(2,1)}, u32[]{:S(2)}, u32[]{:S(2)}) async-start(bf16[16,128,128]{2,1,0:T(8,128)(2,1)} %gates.1.rest_0_), calls=%async_computation.1 | async-start | bytes 1048576 | tf_op jit(solution)/shard_map/columns/all_to_all | solution.py:628
  71.2 1.1 copy-start.3
  72.2 8.7 %copy-start.15 = (bf16[64,512]{1,0:T(8,128)(2,1)S(1)}, bf16[64,512]{1,0:T(8,128)(2,1)}, u32[]{:S(2)}) copy-start(bf16[64,512]{1,0:T(8,128)(2,1)} %get-tuple-element.38.rest_1_) | copy-start | bytes 196612
  72.2 8.7 %copy-start.17 = (bf16[64,512]{1,0:T(8,128)(2,1)S(1)}, bf16[64,512]{1,0:T(8,128)(2,1)}, u32[]{:S(2)}) copy-start(bf16[64,512]{1,0:T(8,128)(2,1)} %get-tuple-element.39.rest_2_) | copy-start | bytes 196612
  74.4 17.5 %collective-permute-start.6 = (bf16[256,2048]{1,0:T(8,128)(2,1)}, bf16[256,2048]{1,0:T(8,128)(2,1)}, u32[]{:S(2)}, u32[]{:S(2)}) collective-permute-start(bf16[256,2048]{1,0:T(8,128)(2,1)} %backward.5.refs_10_), channel_id=1, source_target_pairs={{0,1},{1,0},{2,3},{3,2},{4,5},{5,4},{6,7},{7,6},{8,9},{9,8},{10,11... | collective-permute-start | bytes 3145736 | tf_op jit(solution)/shard_map/backward/ppermute | solution.py:23
  88.0 0.6 copy-start.24
  88.6 20.6 %collective-permute-start.7 = (bf16[256,1280]{1,0:T(8,128)(2,1)}, bf16[256,1280]{1,0:T(8,128)(2,1)S(1)}, u32[]{:S(2)}, u32[]{:S(2)}) collective-permute-start(bf16[256,1280]{1,0:T(8,128)(2,1)} %get-tuple-element.44), channel_id=1, source_target_pairs={{0,16},{16,32},{32,48},{48,64},{64,80},{80,96},{96,112},{112,128},... | collective-permute-start | bytes 1966088 | tf_op jit(solution)/shard_map/factor/ppermute | solution.py:18
  91.8 7.8 %copy-start.1 = (bf16[64,5120]{1,0:T(8,128)(2,1)S(1)}, bf16[64,5120]{1,0:T(8,128)(2,1)}, u32[]{:S(2)}) copy-start(bf16[64,5120]{1,0:T(8,128)(2,1)} %copy-done) | copy-start | bytes 1966084
  91.8 7.8 %copy-start.20 = (s32[8]{0:T(128)S(1)}, s32[8]{0:T(128)}, u32[]{:S(2)}) copy-start(s32[8]{0:T(128)} %stack.47.where) | copy-start | bytes 100
  99.4 10.9 %collective-permute-start.8 = (f32[128,128]{1,0:T(8,128)}, f32[128,128]{1,0:T(8,128)S(1)}, u32[]{:S(2)}, u32[]{:S(2)}) collective-permute-start(f32[128,128]{1,0:T(8,128)} %get-tuple-element.46), channel_id=1, source_target_pairs={{0,16},{16,32},{32,48},{48,64},{64,80},{80,96},{96,112},{112,128},... | collective-permute-start | bytes 196616 | tf_op jit(solution)/shard_map/backward/ppermute | solution.py:18
  99.5 15.0 %collective-permute-start.9 = (f32[128,128]{1,0:T(8,128)}, f32[128,128]{1,0:T(8,128)S(1)}, u32[]{:S(2)}, u32[]{:S(2)}) collective-permute-start(f32[128,128]{1,0:T(8,128)} %get-tuple-element.47), channel_id=1, source_target_pairs={{0,32},{16,48},{32,64},{48,80},{64,96},{80,112},{96,128},{112,144}... | collective-permute-start | bytes 196616 | tf_op jit(solution)/shard_map/backward/ppermute | solution.py:18
  99.6 0.8 copy-start.13
  100.5 0.8 copy-start.16
  101.3 0.8 copy-start.18
  108.2 7.2 %copy-start.11 = (f32[1,3,64,128]{3,2,1,0:T(8,128)S(1)}, f32[1,3,64,128]{3,2,1,0:T(8,128)}, u32[]{:S(2)}) copy-start(f32[1,3,64,128]{3,2,1,0:T(8,128)} %q0.1) | copy-start | bytes 294916
  108.2 7.2 %copy-start.14 = (f32[128,64]{1,0:T(8,128)S(1)}, f32[128,64]{1,0:T(8,128)}, u32[]{:S(2)}) copy-start(f32[128,64]{1,0:T(8,128)} %get-tuple-element.42.rest_4_.m0) | copy-start | bytes 98308
  108.2 7.2 %copy-start.21 = (f32[192,128]{1,0:T(8,128)S(1)}, f32[192,128]{1,0:T(8,128)}, u32[]{:S(2)}) copy-start(f32[192,128]{1,0:T(8,128)} %get-tuple-element.49.proj) | copy-start | bytes 294916
  108.2 33.9 %copy-start.4 = (f32[256,1280]{1,0:T(8,128)S(1)}, f32[256,1280]{1,0:T(8,128)}, u32[]{:S(2)}) copy-start(f32[256,1280]{1,0:T(8,128)} %copy-done.3) | copy-start | bytes 3932164
  115.2 26.9 %collective-permute-start.10 = (bf16[256,1280]{1,0:T(8,128)(2,1)S(1)}, bf16[256,1280]{1,0:T(8,128)(2,1)S(1)}, u32[]{:S(2)}, u32[]{:S(2)}) collective-permute-start(bf16[256,1280]{1,0:T(8,128)(2,1)S(1)} %get-tuple-element.48), channel_id=1, source_target_pairs={{0,16},{16,32},{32,48},{48,64},{64,80},{80,96},{96,112},{112,128},... | collective-permute-start | bytes 1966088 | tf_op jit(solution)/shard_map/factor/ppermute | solution.py:18
  116.4 27.7 %copy-start.2 = (f32[1,512,1024]{2,1,0:T(8,128)S(1)}, f32[1,512,1024]{2,1,0:T(8,128)}, u32[]{:S(2)}) copy-start(f32[1,512,1024]{2,1,0:T(8,128)} %param.14) | copy-start | bytes 6291460
  116.4 4.6 %collective-permute-start.11 = (f32[64,64]{1,0:T(8,128)S(1)}, f32[64,64]{1,0:T(8,128)S(1)}, u32[]{:S(2)}, u32[]{:S(2)}) collective-permute-start(f32[64,64]{1,0:T(8,128)S(1)} %get-tuple-element.52), channel_id=1, source_target_pairs={{0,240},{16,0},{32,16},{48,32},{64,48},{80,64},{96,80},{112,96},{1... | collective-permute-start | bytes 49160 | tf_op jit(solution)/shard_map/backward/ppermute | solution.py:18
  120.0 4.0 %collective-permute-start.12 = (f32[64,64]{1,0:T(8,128)S(1)}, f32[64,64]{1,0:T(8,128)S(1)}, u32[]{:S(2)}, u32[]{:S(2)}) collective-permute-start(f32[64,64]{1,0:T(8,128)S(1)} %get-tuple-element.53), channel_id=1, source_target_pairs={{0,224},{16,240},{32,0},{48,16},{64,32},{80,48},{96,64},{112,80},{... | collective-permute-start | bytes 49160 | tf_op jit(solution)/shard_map/backward/ppermute | solution.py:18
  142.7 3.1 %collective-permute-start.13 = (f32[256,512]{1,0:T(8,128)S(1)}, f32[256,512]{1,0:T(8,128)S(1)}, u32[]{:S(2)}, u32[]{:S(2)}) collective-permute-start(f32[256,512]{1,0:T(8,128)S(1)} %factor.11.mine), channel_id=1, source_target_pairs={{0,1},{1,0},{2,3},{3,2},{4,5},{5,4},{6,7},{7,6},{8,9},{9,8},{10,11... | collective-permute-start | bytes 1572872 | tf_op jit(solution)/shard_map/factor/ppermute | solution.py:23
  145.8 1.8 %copy-start.22 = (f32[2,1,64,64]{3,2,1,0:T(8,128)S(1)}, f32[2,1,64,64]{3,2,1,0:T(8,128)}, u32[]{:S(2)}) copy-start(f32[2,1,64,64]{3,2,1,0:T(8,128)} %old.1) | copy-start | bytes 98308
